TPU v7x, 32 devices: a whole 2x2x4 slice. The times are simulated.
32 devices in a mesh: blk: 8 (over z, y), uly: 4 (over x, core).
Axes of the slice: x: 2, y: 2, z: 4, core: 2. Of those that a mesh axis runs over, the one named last changes fastest.
Arguments:
- tokens: bfloat16 [6400, 1024], P(('blk', 'uly')), may hold values from -6 to 6
- cotangent: bfloat16 [6400, 1024], P(('blk', 'uly')), may hold values from -6 to 6
- noise_embed: bfloat16 [64, 1024], P(('blk', 'uly')), may hold values from -6 to 6
- frame_clip: int32 [64], replicated, may hold values from 0 to 8, as said below
- frame_index: int32 [64], replicated, may hold values from 0 to 31, as said below
- mod_weight: bfloat16 [1024, 6144], replicated, may hold values from -0.1875 to 0.1875
- mod_bias: bfloat16 [6144], replicated, may hold values from -3 to 3
- attn_weight: bfloat16 [1024, 3072], replicated, may hold values from -0.1875 to 0.1875
- attn_bias: bfloat16 [3072], replicated, may hold values from -3 to 3
- proj_weight: bfloat16 [1024, 1024], replicated, may hold values from -3 to 3
- proj_bias: bfloat16 [1024], replicated, may hold values from -3 to 3
- up_weight: bfloat16 [1024, 4096], replicated, may hold values from -0.1875 to 0.1875
- up_bias: bfloat16 [4096], replicated, may hold values from -3 to 3
- down_weight: bfloat16 [4096, 1024], replicated, may hold values from -0.09375 to 0.09375
- down_bias: bfloat16 [1024], replicated, may hold values from -3 to 3
Outputs:
- output: bfloat16 [6400, 1024], P(('blk', 'uly'))
- token_grad: float32 [6400, 1024], P(('blk', 'uly'))
- grad_mod_weight: float32 [1024, 6144], P(('blk', 'uly'))
- grad_mod_bias: float32 [6144], P(('blk', 'uly'))
- grad_attn_weight: float32 [1024, 3072], P(('blk', 'uly'))
- grad_attn_bias: float32 [3072], P(('blk', 'uly'))
- grad_proj_weight: float32 [1024, 1024], P(('blk', 'uly'))
- grad_proj_bias: float32 [1024], P(('blk', 'uly'))
- grad_up_weight: float32 [1024, 4096], P(('blk', 'uly'))
- grad_up_bias: float32 [4096], P(('blk', 'uly'))
- grad_down_weight: float32 [4096, 1024], P(('blk', 'uly'))
- grad_down_bias: float32 [1024], P(('blk', 'uly'))
Inputs may be any that keep to these rules, and one draw needn't show every extreme that they name: `frame_clip`: block b holds frames b * 8 to (b + 1) * 8 - 1. Of these, 4 consecutive frames, either the first or the last ones of the block, form one short clip with id b, and the other 4 frames belong to the one long clip, whose id is the number of blocks and which has frames in every block, 32 in all. `frame_index`: the frame's place within its clip, counting from 0 at the clip's first frame; the long clip's places rise with the frame number.
All inputs are finite; a program needn't handle non-finite values.
Results may differ from a plain program's by a relative error of at most 0.015.
The roundings to bfloat16 on the way count: a program that leaves them out, or rounds other values in their place, can miss the bound.
Values may be sent and summed in bfloat16 or wider, within the bound.
No kernel may reach another device: no remote copies, remote signals or barrier semaphores. Data moves between devices by JAX's collectives and lax.ppermute only.
A program may use at most 320 MiB of HBM per device.

v0:
```python
import math

import jax
import jax.numpy as jnp
from jax import lax
from jax.sharding import PartitionSpec as P

DH = 64
GRID = 10
FB = 8
PATCH = 100


GELU_C = 0.7978845608028654
GELU_K = 0.044715
NEG_BIG = -1e30


def layer_norm(values):
    center = values - jnp.mean(values, axis=-1, keepdims=True)
    inv_std = lax.rsqrt(jnp.mean(center * center, axis=-1, keepdims=True) + 1e-06)
    return (center * inv_std, inv_std)


def norm_back(grad, normed, inv_std):
    return inv_std * (
        grad
        - jnp.mean(grad, axis=-1, keepdims=True)
        - normed * jnp.mean(grad * normed, axis=-1, keepdims=True)
    )


def rope_table(time_pos, row_pos, col_pos):
    half = DH // 2
    n_time = DH // 8
    n_row = 3 * DH // 16
    pair = jnp.arange(half, dtype=jnp.int32)
    in_time = pair < n_time
    in_row = (pair >= n_time) & (pair < n_time + n_row)
    local = jnp.where(in_time, pair, jnp.where(in_row, pair - n_time, pair - n_time - n_row))
    total = jnp.where(in_time, n_time, n_row)
    frequency = jnp.exp(-math.log(10000.0) * local.astype(jnp.float32) / total.astype(jnp.float32))
    place = jnp.where(
        in_time[None, :],
        time_pos[:, None],
        jnp.where(in_row[None, :], row_pos[:, None], col_pos[:, None]),
    )
    angle = place.astype(jnp.float32) * frequency[None, :]
    return (jnp.cos(angle), jnp.sin(angle))


def rotate(values, cosine, sine, sign):
    rows = values.shape[0]
    pairs = values.reshape(rows, -1, DH // 2, 2)
    first = pairs[..., 0]
    second = pairs[..., 1]
    cos_part = cosine[:, None, :]
    sin_part = sign * sine[:, None, :]
    turned = jnp.stack(
        [first * cos_part - second * sin_part, first * sin_part + second * cos_part], axis=-1
    )
    return turned.reshape(values.shape)


def on_device(
    tokens,
    cotangent,
    noise_embed,
    frame_clip,
    frame_index,
    mod_weight,
    mod_bias,
    attn_weight,
    attn_bias,
    proj_weight,
    proj_bias,
    up_weight,
    up_bias,
    down_weight,
    down_bias,
):
    n_uly = lax.axis_size("uly")
    n_blk = lax.axis_size("blk")
    blk_index = lax.axis_index("blk")
    uly_index = lax.axis_index("uly")
    tok_dev, width = tokens.shape
    frames_dev = noise_embed.shape[0]
    block_tok = tok_dev * n_uly
    head_cols = width // n_uly
    heads_dev = head_cols // DH
    scale = 1.0 / math.sqrt(DH)
    patch = jnp.arange(PATCH, dtype=jnp.int32)
    row_of = patch // GRID
    col_of = patch % GRID
    block_clip = lax.dynamic_slice_in_dim(frame_clip, blk_index * FB, FB)
    block_time = lax.dynamic_slice_in_dim(frame_index, blk_index * FB, FB)
    own_time = lax.dynamic_slice_in_dim(block_time, uly_index * frames_dev, frames_dev)
    cos_own, sin_own = rope_table(
        jnp.repeat(own_time, PATCH), jnp.tile(row_of, frames_dev), jnp.tile(col_of, frames_dev)
    )
    cos_blk, sin_blk = rope_table(
        jnp.repeat(block_time, PATCH), jnp.tile(row_of, FB), jnp.tile(col_of, FB)
    )
    silu_noise = jax.nn.silu(noise_embed.astype(jnp.float32)).astype(jnp.bfloat16)
    mod = jnp.dot(silu_noise, mod_weight, preferred_element_type=jnp.float32) + mod_bias.astype(
        jnp.float32
    )
    shift1, scale1, gate1, shift2, scale2, gate2 = [
        mod[:, None, j * width : (j + 1) * width] for j in range(6)
    ]
    framed = tokens.astype(jnp.float32).reshape(frames_dev, PATCH, width)
    normed1, inv_std1 = layer_norm(framed)
    hidden1 = (normed1 * (1.0 + scale1) + shift1).astype(jnp.bfloat16).reshape(tok_dev, width)
    qkv = jnp.dot(hidden1, attn_weight, preferred_element_type=jnp.float32) + attn_bias.astype(
        jnp.float32
    )
    q_tok = rotate(qkv[:, :width], cos_own, sin_own, 1.0).astype(jnp.bfloat16)
    k_tok = rotate(qkv[:, width : 2 * width], cos_own, sin_own, 1.0).astype(jnp.bfloat16)
    v_tok = qkv[:, 2 * width :].astype(jnp.bfloat16)
    q_heads, k_heads, v_heads = (
        lax.all_to_all(q_tok, "uly", split_axis=1, concat_axis=0, tiled=True),
        lax.all_to_all(k_tok, "uly", split_axis=1, concat_axis=0, tiled=True),
        lax.all_to_all(v_tok, "uly", split_axis=1, concat_axis=0, tiled=True),
    )
    k_every, v_every = (
        lax.all_gather(k_heads, "blk", axis=0, tiled=True),
        lax.all_gather(v_heads, "blk", axis=0, tiled=True),
    )
    group = 2
    n_pieces = n_blk // group
    piece_rows = group * block_tok
    key_pieces = k_every.reshape(n_pieces, piece_rows, heads_dev, DH)
    value_pieces = v_every.reshape(n_pieces, piece_rows, heads_dev, DH)
    clip_pieces = jnp.repeat(frame_clip, PATCH).reshape(n_pieces, piece_rows)
    time_pieces = jnp.repeat(frame_index, PATCH).reshape(n_pieces, piece_rows)
    query_clip = jnp.repeat(block_clip, PATCH)
    query_time = jnp.repeat(block_time, PATCH)
    queries = q_heads.reshape(block_tok, heads_dev, DH)

    def piece_score(k_rows, clip_k, time_k):
        allowed = (query_clip[:, None] == clip_k[None, :]) & (
            time_k[None, :] <= query_time[:, None]
        )
        score = (
            jnp.einsum("qhd,khd->hqk", queries, k_rows, preferred_element_type=jnp.float32) * scale
        )
        return (allowed, jnp.where(allowed[None], score, NEG_BIG))

    def gather_stats(carry, pieces):
        top, total = carry
        k_rows, clip_k, time_k = pieces
        allowed, score = piece_score(k_rows, clip_k, time_k)
        new_top = jnp.maximum(top, jnp.max(score, axis=-1))
        expo = jnp.where(allowed[None], jnp.exp(score - new_top[..., None]), 0.0)
        total = total * jnp.exp(top - new_top) + jnp.sum(expo, axis=-1)
        return ((new_top, total), None)

    start_top = jnp.full((heads_dev, block_tok), NEG_BIG, jnp.float32)
    start_total = jnp.zeros((heads_dev, block_tok), jnp.float32)
    (top_all, total_all), _ = lax.scan(
        gather_stats, (start_top, start_total), (key_pieces, clip_pieces, time_pieces)
    )
    log_total = top_all + jnp.log(total_all)

    def mix_values(carry, pieces):
        acc_low, acc_exact = carry
        k_rows, v_rows, clip_k, time_k = pieces
        allowed, score = piece_score(k_rows, clip_k, time_k)
        prob = jnp.where(allowed[None], jnp.exp(score - log_total[..., None]), 0.0)
        acc_low = acc_low + jnp.einsum(
            "hqk,khd->qhd", prob.astype(jnp.bfloat16), v_rows, preferred_element_type=jnp.float32
        )
        acc_exact = acc_exact + jnp.einsum(
            "hqk,khd->qhd", prob, v_rows.astype(jnp.float32), preferred_element_type=jnp.float32
        )
        return ((acc_low, acc_exact), None)

    zero_rows = jnp.zeros((block_tok, heads_dev, DH), jnp.float32)
    (mixed_low, mixed_exact), _ = lax.scan(
        mix_values, (zero_rows, zero_rows), (key_pieces, value_pieces, clip_pieces, time_pieces)
    )
    attn_heads = mixed_low.reshape(block_tok, head_cols).astype(jnp.bfloat16)
    attn_tok = lax.all_to_all(attn_heads, "uly", split_axis=0, concat_axis=1, tiled=True)
    branch = (
        jnp.dot(attn_tok, proj_weight, preferred_element_type=jnp.float32)
        + proj_bias.astype(jnp.float32)
    ).reshape(frames_dev, PATCH, width)
    resid = framed + gate1 * branch
    normed2, inv_std2 = layer_norm(resid)
    hidden2 = (normed2 * (1.0 + scale2) + shift2).astype(jnp.bfloat16).reshape(tok_dev, width)
    pre = jnp.dot(hidden2, up_weight, preferred_element_type=jnp.float32) + up_bias.astype(
        jnp.float32
    )
    inner_tanh = jnp.tanh(GELU_C * (pre + GELU_K * pre * pre * pre))
    act = (0.5 * pre * (1.0 + inner_tanh)).astype(jnp.bfloat16)
    mlp = (
        jnp.dot(act, down_weight, preferred_element_type=jnp.float32)
        + down_bias.astype(jnp.float32)
    ).reshape(frames_dev, PATCH, width)
    output = (resid + gate2 * mlp).reshape(tok_dev, width).astype(jnp.bfloat16)
    dy_grad = cotangent.astype(jnp.float32).reshape(frames_dev, PATCH, width)
    gate2_grad = jnp.sum(dy_grad * mlp, axis=1)
    mlp_grad = (gate2 * dy_grad).astype(jnp.bfloat16).reshape(tok_dev, width)
    g_down_weight = jnp.einsum("tf,td->fd", act, mlp_grad, preferred_element_type=jnp.float32)
    g_down_bias = jnp.sum(mlp_grad.astype(jnp.float32), axis=0)
    act_grad = jnp.einsum("td,fd->tf", mlp_grad, down_weight, preferred_element_type=jnp.float32)
    slope = 0.5 * (1.0 + inner_tanh) + 0.5 * pre * (1.0 - inner_tanh * inner_tanh) * GELU_C * (
        1.0 + 3.0 * GELU_K * pre * pre
    )
    pre_grad = (act_grad * slope).astype(jnp.bfloat16)
    g_up_weight = jnp.einsum("td,tf->df", hidden2, pre_grad, preferred_element_type=jnp.float32)
    g_up_bias = jnp.sum(pre_grad.astype(jnp.float32), axis=0)
    hid2_grad = jnp.einsum(
        "tf,df->td", pre_grad, up_weight, preferred_element_type=jnp.float32
    ).reshape(frames_dev, PATCH, width)
    shift2_grad = jnp.sum(hid2_grad, axis=1)
    scale2_grad = jnp.sum(hid2_grad * normed2, axis=1)
    resid_grad = dy_grad + norm_back(hid2_grad * (1.0 + scale2), normed2, inv_std2)
    gate1_grad = jnp.sum(resid_grad * branch, axis=1)
    branch_grad = (gate1 * resid_grad).astype(jnp.bfloat16).reshape(tok_dev, width)
    g_proj_weight = jnp.einsum(
        "td,te->de", attn_tok, branch_grad, preferred_element_type=jnp.float32
    )
    g_proj_bias = jnp.sum(branch_grad.astype(jnp.float32), axis=0)
    attn_grad_tok = jnp.einsum(
        "te,de->td", branch_grad, proj_weight, preferred_element_type=jnp.float32
    ).astype(jnp.bfloat16)
    attn_grad = lax.all_to_all(
        attn_grad_tok, "uly", split_axis=1, concat_axis=0, tiled=True
    ).reshape(block_tok, heads_dev, DH)
    row_delta = jnp.einsum("qhd,qhd->hq", attn_grad.astype(jnp.float32), mixed_exact)

    def back_piece(query_acc, pieces):
        k_rows, v_rows, clip_k, time_k = pieces
        allowed, score = piece_score(k_rows, clip_k, time_k)
        prob = jnp.where(allowed[None], jnp.exp(score - log_total[..., None]), 0.0)
        prob_grad = jnp.einsum(
            "qhd,khd->hqk", attn_grad, v_rows, preferred_element_type=jnp.float32
        )
        score_grad = (prob * (prob_grad - row_delta[..., None])).astype(jnp.bfloat16)
        query_acc = (
            query_acc
            + jnp.einsum("hqk,khd->qhd", score_grad, k_rows, preferred_element_type=jnp.float32)
            * scale
        )
        key_rows = (
            jnp.einsum("hqk,qhd->khd", score_grad, queries, preferred_element_type=jnp.float32)
            * scale
        )
        value_rows = jnp.einsum(
            "hqk,qhd->khd", prob.astype(jnp.bfloat16), attn_grad, preferred_element_type=jnp.float32
        )
        return (query_acc, (key_rows, value_rows))

    query_grad, (key_terms, value_terms) = lax.scan(
        back_piece, zero_rows, (key_pieces, value_pieces, clip_pieces, time_pieces)
    )
    key_terms = key_terms.reshape(n_blk * block_tok, head_cols)
    value_terms = value_terms.reshape(n_blk * block_tok, head_cols)
    key_local, value_local = (
        lax.psum_scatter(
            key_terms.astype(jnp.bfloat16), "blk", scatter_dimension=0, tiled=True
        ).astype(jnp.float32),
        lax.psum_scatter(
            value_terms.astype(jnp.bfloat16), "blk", scatter_dimension=0, tiled=True
        ).astype(jnp.float32),
    )
    dq_heads = rotate(query_grad.reshape(block_tok, head_cols), cos_blk, sin_blk, -1.0).astype(
        jnp.bfloat16
    )
    dk_heads = rotate(key_local, cos_blk, sin_blk, -1.0).astype(jnp.bfloat16)
    dv_heads = value_local.astype(jnp.bfloat16)
    dq_tok, dk_tok, dv_tok = (
        lax.all_to_all(dq_heads, "uly", split_axis=0, concat_axis=1, tiled=True),
        lax.all_to_all(dk_heads, "uly", split_axis=0, concat_axis=1, tiled=True),
        lax.all_to_all(dv_heads, "uly", split_axis=0, concat_axis=1, tiled=True),
    )
    qkv_grad = jnp.concatenate([dq_tok, dk_tok, dv_tok], axis=1)
    g_attn_weight = jnp.einsum("td,te->de", hidden1, qkv_grad, preferred_element_type=jnp.float32)
    g_attn_bias = jnp.sum(qkv_grad.astype(jnp.float32), axis=0)
    hid1_grad = jnp.einsum(
        "te,de->td", qkv_grad, attn_weight, preferred_element_type=jnp.float32
    ).reshape(frames_dev, PATCH, width)
    shift1_grad = jnp.sum(hid1_grad, axis=1)
    scale1_grad = jnp.sum(hid1_grad * normed1, axis=1)
    token_grad = (resid_grad + norm_back(hid1_grad * (1.0 + scale1), normed1, inv_std1)).reshape(
        tok_dev, width
    )
    mod_grad = jnp.concatenate(
        [shift1_grad, scale1_grad, gate1_grad, shift2_grad, scale2_grad, gate2_grad], axis=1
    )
    g_mod_weight = jnp.einsum(
        "fd,fe->de",
        silu_noise.astype(jnp.float32),
        mod_grad,
        precision=lax.Precision.HIGHEST,
        preferred_element_type=jnp.float32,
    )
    g_mod_bias = jnp.sum(mod_grad, axis=0)
    (
        g_mod_weight,
        g_mod_bias,
        g_attn_weight,
        g_attn_bias,
        g_proj_weight,
        g_proj_bias,
        g_up_weight,
        g_up_bias,
        g_down_weight,
        g_down_bias,
    ) = (
        lax.psum_scatter(g_mod_weight, ("blk", "uly"), scatter_dimension=0, tiled=True),
        lax.psum_scatter(g_mod_bias, ("blk", "uly"), scatter_dimension=0, tiled=True),
        lax.psum_scatter(g_attn_weight, ("blk", "uly"), scatter_dimension=0, tiled=True),
        lax.psum_scatter(g_attn_bias, ("blk", "uly"), scatter_dimension=0, tiled=True),
        lax.psum_scatter(g_proj_weight, ("blk", "uly"), scatter_dimension=0, tiled=True),
        lax.psum_scatter(g_proj_bias, ("blk", "uly"), scatter_dimension=0, tiled=True),
        lax.psum_scatter(g_up_weight, ("blk", "uly"), scatter_dimension=0, tiled=True),
        lax.psum_scatter(g_up_bias, ("blk", "uly"), scatter_dimension=0, tiled=True),
        lax.psum_scatter(g_down_weight, ("blk", "uly"), scatter_dimension=0, tiled=True),
        lax.psum_scatter(g_down_bias, ("blk", "uly"), scatter_dimension=0, tiled=True),
    )
    return (
        output,
        token_grad,
        g_mod_weight,
        g_mod_bias,
        g_attn_weight,
        g_attn_bias,
        g_proj_weight,
        g_proj_bias,
        g_up_weight,
        g_up_bias,
        g_down_weight,
        g_down_bias,
    )


def solution(mesh):
    in_specs = (
        P(("blk", "uly"), None),
        P(("blk", "uly"), None),
        P(("blk", "uly"), None),
        P(),
        P(),
        P(),
        P(),
        P(),
        P(),
        P(),
        P(),
        P(),
        P(),
        P(),
        P(),
    )
    out_specs = (
        P(("blk", "uly"), None),
        P(("blk", "uly"), None),
        P(("blk", "uly"), None),
        P(("blk", "uly")),
        P(("blk", "uly"), None),
        P(("blk", "uly")),
        P(("blk", "uly"), None),
        P(("blk", "uly")),
        P(("blk", "uly"), None),
        P(("blk", "uly")),
        P(("blk", "uly"), None),
        P(("blk", "uly")),
    )
    return jax.shard_map(
        on_device, mesh=mesh, in_specs=in_specs, out_specs=out_specs, check_vma=False
    )
```

profile of v0, /device:TPU:4, one launch (start us, length us, event | category | flops | bytes accessed | tf_op | source)
XLA Modules:
  0.0 1707.8 jit_solution(14024680513358716793)
XLA Ops:
  44.5 10.9 all_to_all.131
  82.2 34.6 %all-gather.5.cloned.1.call-done = bf16[6400,256]{1,0:T(8,128)(2,1)} async-done(((bf16[800,256]{1,0:T(8,128)(2,1)}), bf16[6400,256]{1,0:T(8,128)(2,1)}) %all-gather.5.cloned.1.call-update) | async-done | bytes 3276816 | tf_op jit(solution)/shard_map/all_gather | solution.py:126
  137.5 112.8 %while.41 = (s32[]{:T(128)}, f32[4,800]{1,0:T(4,128)S(1)}, f32[4,800]{1,0:T(4,128)}, s32[4,1600]{1,0:T(4,128)S(1)}, s32[4,1600]{1,0:T(4,128)S(1)}, /*index=5*/bf...) while((s32[]{:T(128)}, f32[4,800]{1,0:T(4,128)S(1)}, ...), condition=%wide.region_5.6_spmd.clone, body=%wide.region_2.5_spmd.clone.sunk | while | flops 700176000 | bytes 46394932 | solution.py:160
  141.7 13.3 fusion.152
  154.9 10.4 select_reduce_fusion.2
  170.1 12.9 fusion.152
  183.1 10.4 select_reduce_fusion.2
  198.2 12.9 fusion.152
  211.2 10.4 select_reduce_fusion.2
  226.3 12.9 fusion.152
  239.3 10.4 select_reduce_fusion.2
  272.2 70.2 %while.42 = (s32[]{:T(128)}, f32[800,4,64]{0,2,1:T(8,128)}, f32[800,4,64]{0,2,1:T(8,128)S(1)}, bf16[4,1600,4,64]{1,3,2,0:T(8,128)(2,1)}, s32[4,1600]{1,0:T(4,128...) while((s32[]{:T(128)}, f32[800,4,64]{0,2,1:T(8,128)}, ...), condition=%wide.region_7.8_spmd.clone, body=%wide.region_6.7_spmd.clone.sunk | while | flops 1991219200 | bytes 60277552 | solution.py:179
  412.2 184.9 %while.43 = (s32[]{:T(128)}, f32[800,4,64]{0,2,1:T(8,128)S(1)}, bf16[4,1600,4,64]{1,3,2,0:T(8,128)(2,1)}, bf16[4,1600,4,64]{1,3,2,0:T(8,128)(2,1)}, bf16[4,1600,...) while((s32[]{:T(128)}, f32[800,4,64]{0,2,1:T(8,128)S(1)}, ...), condition=%wide.region_13.14_spmd.clone, body=%wide.region_12.13_spmd.clone.sunk | while | flops 3322624000 | bytes 147058464 | solution.py:255
  414.1 11.7 fusion.173
  435.6 12.5 fusion.174
  460.3 11.7 fusion.173
  481.8 12.5 fusion.174
  506.5 11.7 fusion.173
  527.9 12.5 fusion.174
  552.6 11.7 fusion.173
  574.1 12.5 fusion.174
  597.1 10.5 copy.115
  607.6 10.6 reshape.862
  618.3 10.6 copy.114
  644.4 48.4 %reduce-scatter.24.cloned.1.call-done = bf16[800,256]{1,0:T(8,128)(2,1)} async-done(((bf16[6400,256]{1,0:T(8,128)(2,1)}), bf16[800,256]{1,0:T(8,128)(2,1)}) %reduce-scatter.24.cloned.1.call-update) | async-done | bytes 409616 | tf_op jit(solution)/shard_map/reduce_scatter | solution.py:264
  696.3 75.6 %reduce-scatter.22.cloned.1.call-done = bf16[800,256]{1,0:T(8,128)(2,1)} async-done(((bf16[6400,256]{1,0:T(8,128)(2,1)}), bf16[800,256]{1,0:T(8,128)(2,1)}) %reduce-scatter.22.cloned.1.call-update) | async-done | bytes 409616
  861.6 13.4 fusion.79
  875.7 42.1 %all-reduce.5 = (f32[6144]{0:T(1024)S(1)}, f32[3072]{0:T(1024)S(1)}, f32[1024]{0:T(1024)S(1)}, f32[4096]{0:T(1024)S(1)}, f32[1024]{0:T(1024)S(1)}) all-reduce(f32[6144]{0:T(1024)S(1)} %reduce_sum.194, f32[3072]{0:T(1024)S(1)} %convert_reduce_fusion.1, f32[1024]{0:T(1024)S(1)} %copy-done.64, ...), channel_id=5, replica_groups=mesh['blk'=8,'uly'=4] {'blk','uly'}, use_global_device_ids=true, to_apply=%region_26.27.clone | all-reduce | flops 15360 | bytes 122880
  920.8 152.5 %reduce-scatter.14.cloned.1.call-done = f32[32,3072]{1,0:T(8,128)} async-done(((f32[1024,3072]{1,0:T(8,128)}), f32[32,3072]{1,0:T(8,128)}) %reduce-scatter.14.cloned.1.call-update) | async-done | bytes 393232 | tf_op jit(solution)/shard_map/reduce_scatter | solution.py:314
  1073.4 183.1 %reduce-scatter.20.cloned.1.call-done = f32[128,1024]{1,0:T(8,128)} async-done(((f32[4096,1024]{1,0:T(8,128)}), f32[128,1024]{1,0:T(8,128)}) %reduce-scatter.20.cloned.1.call-update) | async-done | bytes 524304 | tf_op jit(solution)/shard_map/reduce_scatter | solution.py:320
  1256.5 187.5 %reduce-scatter.18.cloned.1.call-done = f32[32,4096]{1,0:T(8,128)} async-done(((f32[1024,4096]{1,0:T(8,128)}), f32[32,4096]{1,0:T(8,128)}) %reduce-scatter.18.cloned.1.call-update) | async-done | bytes 524304 | tf_op jit(solution)/shard_map/reduce_scatter | solution.py:318
  1444.0 257.1 %reduce-scatter.12.cloned.1.call-done = f32[32,6144]{1,0:T(8,128)} async-done(((f32[1024,6144]{1,0:T(8,128)}), f32[32,6144]{1,0:T(8,128)}) %reduce-scatter.12.cloned.1.call-update) | async-done | bytes 786448 | tf_op jit(solution)/shard_map/reduce_scatter | solution.py:312
  (515 shorter events, 464.1 us)
Async XLA Ops:
  7.2 366.3 %copy-start = (bf16[1024,1024]{1,0:T(8,128)(2,1)S(1)}, bf16[1024,1024]{1,0:T(8,128)(2,1)}, u32[]{:S(2)}) copy-start(bf16[1024,1024]{1,0:T(8,128)(2,1)} %param.30) | copy-start | bytes 6291460
  7.2 109.6 %all-gather.5.cloned.1.call-start = ((), (), s32[]{:S(2)}) async-start(), calls=%async_computation.16 | async-start | bytes 3686400 | tf_op jit(solution)/shard_map/all_gather | solution.py:126
  7.3 29.8 %copy-start.71 = (f32[32]{0:T(128)}, f32[32]{0:T(128)S(1)}, u32[]{:S(2)}) copy-start(f32[32]{0:T(128)S(1)} %fusion.78) | copy-start | bytes 388
  7.3 29.7 %copy-start.73 = (pred[32]{0:T(512)(128)(4,1)}, pred[32]{0:T(512)(128)(4,1)S(1)}, u32[]{:S(2)}) copy-start(pred[32]{0:T(512)(128)(4,1)S(1)} %get-tuple-element.561) | copy-start | bytes 100
  7.3 29.7 %copy-start.75 = (pred[32]{0:T(512)(128)(4,1)}, pred[32]{0:T(512)(128)(4,1)S(1)}, u32[]{:S(2)}) copy-start(pred[32]{0:T(512)(128)(4,1)S(1)} %get-tuple-element.562) | copy-start | bytes 100
  55.4 19.2 %copy-start.79 = (s32[64]{0:T(128)S(1)}, s32[64]{0:T(128)}, u32[]{:S(2)}) copy-start(s32[64]{0:T(128)} %param.25) | copy-start | bytes 772
  55.4 19.3 %copy-start.78 = (s32[64]{0:T(128)S(1)}, s32[64]{0:T(128)}, u32[]{:S(2)}) copy-start(s32[64]{0:T(128)} %param.24) | copy-start | bytes 772
  59.3 11.1 all-to-all-start.2
  70.4 11.8 all-to-all-start
  74.5 175.8 %all-gather.3.cloned.1.call-start = ((), (), s32[]{:S(2)}) async-start(), calls=%async_computation.15 | async-start | bytes 3686400 | tf_op jit(solution)/shard_map/all_gather | solution.py:127
  342.4 18.7 %copy-start.4 = (f32[800,4,64]{0,2,1:T(8,128)}, f32[800,4,64]{0,2,1:T(8,128)S(1)}, u32[]{:S(2)}) copy-start(f32[800,4,64]{0,2,1:T(8,128)S(1)} %get-tuple-element.195) | copy-start | bytes 2457604
  342.4 13.8 copy-start.54
  347.0 16.3 copy-start.47
  349.1 23.2 %all-to-all-start.3 = ((bf16[4,200,256]{2,1,0:T(8,128)(2,1)}), bf16[4,200,256]{2,1,0:T(8,128)(2,1)}, u32[]{:S(2)}, u32[]{:S(2)}) async-start(bf16[4,200,256]{2,1,0:T(8,128)(2,1)} %copy.85), calls=%async_computation.3 | async-start | bytes 819200 | tf_op jit(solution)/shard_map/all_to_all | solution.py:183
  376.3 19.4 %copy-start.7 = (f32[200,1024]{1,0:T(8,128)}, f32[200,1024]{1,0:T(8,128)S(1)}, u32[]{:S(2)}) copy-start(f32[200,1024]{1,0:T(8,128)S(1)} %get-tuple-element.520) | copy-start | bytes 2457604
  376.4 19.4 %copy-start.52 = (f32[200]{0:T(256)}, f32[200]{0:T(256)S(1)}, u32[]{:S(2)}) copy-start(f32[200]{0:T(256)S(1)} %broadcast_multiply_fusion.4) | copy-start | bytes 2404
  376.6 19.1 %copy-start.56 = (f32[200]{0:T(256)}, f32[200]{0:T(256)S(1)}, u32[]{:S(2)}) copy-start(f32[200]{0:T(256)S(1)} %add_rsqrt_fusion) | copy-start | bytes 2404
  376.9 14.9 slice-start
  398.4 13.8 copy-start.66
  399.2 11.1 all-to-all-start.4
  402.6 290.2 %reduce-scatter.24.cloned.1.call-start = ((), (), s32[]{:S(2)}) async-start(), calls=%async_computation.23 | async-start | bytes 3686400 | tf_op jit(solution)/shard_map/reduce_scatter | solution.py:264
  618.2 153.7 %reduce-scatter.22.cloned.1.call-start = ((), (), s32[]{:S(2)}) async-start(), calls=%async_computation.22 | async-start | bytes 3686400
  639.1 281.7 %reduce-scatter.16.cloned.1.call-start = ((), (), s32[]{:S(2)}) async-start(), calls=%async_computation.19 | async-start | bytes 4325376 | tf_op jit(solution)/shard_map/reduce_scatter | solution.py:316
  692.8 85.9 %all-to-all-start.7 = ((bf16[4,200,256]{2,1,0:T(8,128)(2,1)}), bf16[4,200,256]{2,1,0:T(8,128)(2,1)S(1)}, u32[]{:S(2)}, u32[]{:S(2)}) async-start(bf16[4,200,256]{2,1,0:T(8,128)(2,1)} %bitcast.231), calls=%async_computation.7 | async-start | bytes 819200 | tf_op jit(solution)/shard_map/all_to_all | solution.py:276
  778.7 13.2 all-to-all-start.6
  783.8 23.0 %copy-start.39 = (bf16[200,1024]{1,0:T(8,128)(2,1)S(1)}, bf16[200,1024]{1,0:T(8,128)(2,1)}, u32[]{:S(2)}) copy-start(bf16[200,1024]{1,0:T(8,128)(2,1)} %copy-done.38) | copy-start | bytes 1228804
  791.9 13.8 all-to-all-start.5
  795.3 278.0 %reduce-scatter.14.cloned.1.call-start = ((), (), s32[]{:S(2)}) async-start(), calls=%async_computation.18 | async-start | bytes 12976128 | tf_op jit(solution)/shard_map/reduce_scatter | solution.py:314
  813.1 443.3 %reduce-scatter.20.cloned.1.call-start = ((), (), s32[]{:S(2)}) async-start(), calls=%async_computation.21 | async-start | bytes 17301504 | tf_op jit(solution)/shard_map/reduce_scatter | solution.py:320
  824.4 619.6 %reduce-scatter.18.cloned.1.call-start = ((), (), s32[]{:S(2)}) async-start(), calls=%async_computation.20 | async-start | bytes 17301504 | tf_op jit(solution)/shard_map/reduce_scatter | solution.py:318
  834.1 867.0 %reduce-scatter.12.cloned.1.call-start = ((), (), s32[]{:S(2)}) async-start(), calls=%async_computation.17 | async-start | bytes 25952256 | tf_op jit(solution)/shard_map/reduce_scatter | solution.py:312
  875.0 826.0 %copy-start.1 = (bf16[1024,1024]{1,0:T(8,128)(2,1)S(1)}, bf16[1024,1024]{1,0:T(8,128)(2,1)}, u32[]{:S(2)}) copy-start(bf16[1024,1024]{1,0:T(8,128)(2,1)} %param.30) | copy-start | bytes 6291460
  (94 other events, 459.0 us)
Sparse Core Ops, SparseCore 0:
  55.5 61.3 all-gather.4
  119.0 60.4 all-gather.2
  618.3 74.4 reduce-scatter.23
  696.7 75.1 reduce-scatter.21
  774.6 130.4 reduce-scatter.15
  911.6 161.7 reduce-scatter.13
  1076.3 180.1 reduce-scatter.19
  1259.4 184.4 reduce-scatter.17
  1452.1 248.9 reduce-scatter.11
where the time goes:
time: 1720 us; the launch traced here: 1710 us
  waiting for transfers between devices  972 us (57%)
  matrix products  376 us (22%)
  local copies, waits for them, and re-layouts  170 us (10%)
  other arithmetic  93.1 us (5%)
  blocking collectives  52.9 us (3%)
  starting transfers between devices  26.5 us (2%)
    reduce_scatter x1, waiting for transfers between devices, on_device(): lax.psum_scatter(g_mod_weight, ('blk', 'uly'), scatter_dimension=0, tiled...  257 us
    reduce_scatter x1, waiting for transfers between devices, on_device(): lax.psum_scatter(g_up_weight, ('blk', 'uly'), scatter_dimension=0, tiled=...  187 us
    reduce_scatter x1, waiting for transfers between devices, on_device(): lax.psum_scatter(g_down_weight, ('blk', 'uly'), scatter_dimension=0, tile...  183 us
    reduce_scatter x1, waiting for transfers between devices, on_device(): lax.psum_scatter(g_attn_weight, ('blk', 'uly'), scatter_dimension=0, tile...  153 us
    dot_general x12, matrix products, piece_score(): jnp.einsum('qhd,khd->hqk', queries, k_rows, preferred_element_type=jnp.fl...  131 us
    unnamed x10, waiting for transfers between devices  75.7 us
    unnamed x175, local copies, waits for them, and re-layouts  73.7 us
    dot_general x4, matrix products, back_piece(): jnp.einsum('qhd,khd->hqk', attn_grad, v_rows, preferred_element_type=jnp....  50 us
  transfers between devices with their start and end apart: 16, of which 12 were waited for; matrix products, arithmetic and copies ran while one was open for 15% of the time, Pallas kernels for 0%

commit v1 on v0

v1 whole, which is shorter than its diff:
```python
import functools
import math

import jax
import jax.numpy as jnp
import numpy as np
from jax import lax
from jax.experimental import pallas as pl
from jax.experimental.pallas import tpu as pltpu
from jax.sharding import PartitionSpec as P

DH = 64
GRID = 10
FB = 8
PATCH = 100
HALF = 64
LANES = 128

GELU_C = 0.7978845608028654
GELU_K = 0.044715
NEG_BIG = -1e30
MIB = 1 << 20

BF = jnp.bfloat16
F32 = jnp.float32


def round_up(value, step):
    return -(-value // step) * step


def lane_low(shape):
    return lax.broadcasted_iota(jnp.int32, shape, len(shape) - 1) < HALF


def first_frame(shape):
    return lax.broadcasted_iota(jnp.int32, shape, 0) < PATCH


def swap_halves(value):
    return pltpu.roll(value, HALF, 1)


def swap_pairs(value):
    even = lax.broadcasted_iota(jnp.int32, value.shape, 1) % 2 == 0
    return jnp.where(even, pltpu.roll(value, LANES - 1, 1), pltpu.roll(value, 1, 1))


def per_frame(shape, first, second):
    return jnp.where(first_frame(shape), jnp.broadcast_to(first, shape), jnp.broadcast_to(second, shape))


def frame_sums(value):
    head = first_frame(value.shape)
    one = jnp.sum(jnp.where(head, value, 0.0), axis=0, keepdims=True)
    two = jnp.sum(jnp.where(head, 0.0, value), axis=0, keepdims=True)
    return one, two


def norm_rows(values):
    center = values - jnp.mean(values, axis=-1, keepdims=True)
    inv_std = lax.rsqrt(jnp.mean(center * center, axis=-1, keepdims=True) + 1e-06)
    return center * inv_std, inv_std


def norm_back(grad, normed, inv_std):
    return inv_std * (
        grad
        - jnp.mean(grad, axis=-1, keepdims=True)
        - normed * jnp.mean(grad * normed, axis=-1, keepdims=True)
    )


def dot(left, right):
    return jnp.dot(left, right, preferred_element_type=F32)


def dot_lanes(left, right):
    return lax.dot_general(left, right, (((1,), (1,)), ((), ())), preferred_element_type=F32)


def dot_rows(left, right):
    return lax.dot_general(left, right, (((0,), (0,)), ((), ())), preferred_element_type=F32)


def split_pair(value, rows_top):
    rows = value.shape[0]
    top = value[:rows_top]
    bottom = jnp.concatenate(
        [value[rows_top:], jnp.zeros((2 * rows_top - rows, LANES), value.dtype)], axis=0
    )
    low = lane_low(top.shape)
    return jnp.where(low, top, swap_halves(bottom)), jnp.where(low, swap_halves(top), bottom)


def join_pair(one, two, rows):
    rows_top = one.shape[0]
    low = lane_low(one.shape)
    top = jnp.where(low, one, swap_halves(two))
    bottom = jnp.where(low, swap_halves(one), two)
    return jnp.concatenate([top, bottom[: rows - rows_top]], axis=0)


def smem():
    return pl.BlockSpec(memory_space=pltpu.SMEM)


def whole(shape):
    return pl.BlockSpec(shape, lambda *_: (0,) * len(shape))


def tokens_to_qkv(flags, tok_own, tok_oth, mods, weight, bias, tab_cos, tab_sin, time_cos, time_sin, lay):
    rows, width = tok_own.shape
    cols = lay.heads * DH

    def body(flag_ref, own_ref, oth_ref, mod_ref, w_ref, b_ref, tc_ref, ts_ref, qc_ref, qs_ref, hid_ref, long_ref, short_ref):
        step = pl.program_id(0)
        own_long = flag_ref[0]

        @pl.when(step == 0)
        def _():
            for src, base, slot in ((own_ref, 0, 1 - own_long), (oth_ref, 2, own_long)):
                normed, _ = norm_rows(src[...].astype(F32))
                shift = per_frame(normed.shape, mod_ref[base : base + 1, :width], mod_ref[base + 1 : base + 2, :width])
                scale = per_frame(
                    normed.shape, mod_ref[base : base + 1, width : 2 * width], mod_ref[base + 1 : base + 2, width : 2 * width]
                )
                hid_ref[slot] = (normed * (1.0 + scale) + shift).astype(BF)

        for slot, out_ref in ((0, long_ref), (1, short_ref)):
            acc = dot(hid_ref[slot], w_ref[...]) + b_ref[...]

            def rotated(pair):
                value = acc[:, pair * LANES : (pair + 1) * LANES]
                cosine = tc_ref[...] + per_frame(value.shape, qc_ref[2 * slot : 2 * slot + 1], qc_ref[2 * slot + 1 : 2 * slot + 2])
                sine = ts_ref[...] + per_frame(value.shape, qs_ref[2 * slot : 2 * slot + 1], qs_ref[2 * slot + 1 : 2 * slot + 2])
                return value * cosine + swap_pairs(value) * sine

            @pl.when(step == 0)
            def _():
                for pair in range(cols // LANES):
                    turned = rotated(pair)
                    out_ref[2 * pair, :rows, :HALF] = turned[:, :HALF].astype(BF)
                    out_ref[2 * pair + 1, :rows, :HALF] = swap_halves(turned)[:, :HALF].astype(BF)

            @pl.when(step == 1)
            def _():
                for pair in range(cols // LANES):
                    turned = rotated(pair)
                    out_ref[2 * pair, :rows, HALF:] = swap_halves(turned)[:, HALF:].astype(BF)
                    out_ref[2 * pair + 1, :rows, HALF:] = turned[:, HALF:].astype(BF)

            @pl.when(step == 2)
            def _():
                for pair in range(cols // LANES):
                    one, two = split_pair(acc[:, pair * LANES : (pair + 1) * LANES], lay.top)
                    out_ref[2 * pair, lay.vrow :, :] = one.astype(BF)
                    out_ref[2 * pair + 1, lay.vrow :, :] = two.astype(BF)

    packed = (lay.heads, lay.vrow + lay.top, LANES)
    return pl.pallas_call(
        body,
        grid_spec=pltpu.PrefetchScalarGridSpec(
            num_scalar_prefetch=1,
            grid=(3,),
            in_specs=[
                whole((rows, width)),
                whole((rows, width)),
                whole(mods.shape),
                pl.BlockSpec((width, cols), lambda j, f: (0, 2 * j + f[1])),
                pl.BlockSpec((1, cols), lambda j, f: (0, 2 * j + f[1])),
                whole(tab_cos.shape),
                whole(tab_sin.shape),
                whole(time_cos.shape),
                whole(time_sin.shape),
            ],
            out_specs=[whole((2, rows, width)), whole(packed), whole(packed)],
        ),
        out_shape=[
            jax.ShapeDtypeStruct((2, rows, width), BF),
            jax.ShapeDtypeStruct(packed, BF),
            jax.ShapeDtypeStruct(packed, BF),
        ],
        compiler_params=pltpu.CompilerParams(vmem_limit_bytes=40 * MIB),
        cost_estimate=pl.CostEstimate(flops=12 * rows * width * cols, bytes_accessed=12 * MIB, transcendentals=0),
        name="tokens_to_qkv",
    )(flags, tok_own, tok_oth, mods, weight, bias, tab_cos, tab_sin, time_cos, time_sin)


def unpack_values(ref, at, lay):
    part = ref[at, lay.vrow :, :].astype(F32)
    return jnp.concatenate([part, swap_halves(part)[: lay.rows - lay.top]], axis=0)


def diag_mask(shape, lay, core):
    key_row = lax.broadcasted_iota(jnp.int32, shape, 0)
    query = lax.broadcasted_iota(jnp.int32, shape, 1)
    own = (key_row < lay.rows) & ((key_row < PATCH) | (query >= PATCH))
    return own | ((key_row >= lay.rows) & (core == 1))


def load_keys(own_ref, oth_ref, group, lay):
    low = lane_low((lay.rows, LANES))
    halves = [
        jnp.where(low, unpack_values(ref, group, lay), ref[group, : lay.rows, :].astype(F32))
        for ref in (own_ref, oth_ref)
    ]
    return jnp.concatenate(halves, axis=0)


def load_query(own_ref, at, lay):
    value = swap_halves(own_ref[at, : lay.rows, :].astype(F32)) * (1.0 / math.sqrt(DH))
    return jnp.where(lane_low(value.shape), 0.0, value).astype(BF)


def fold_rows(value, op):
    return op(value.reshape(value.shape[0] // 8, 8, value.shape[1]), axis=0)


def attend(flags, own, oth, lay, long_clip):
    groups = own.shape[0]
    parts = lay.parts if long_clip else 1
    tile = 2 * lay.rows
    depth = groups if long_clip else 1

    def body(flag_ref, own_ref, oth_ref, o_ref, ot_ref, lse_ref, kv_ref, vt_ref, st_ref):
        core = flag_ref[2]
        part = flag_ref[3]

        def prepare(group, _):
            keys = load_keys(own_ref, oth_ref, group, lay)
            kv_ref[group] = keys.astype(BF)
            vt_ref[group] = keys.T[:HALF].astype(BF)
            return 0

        lax.fori_loop(0, groups, prepare, 0)
        if parts > 1:
            o_ref[...] = jnp.zeros_like(o_ref)

        def block(step, _):
            at = step * parts + part if parts > 1 else step
            slot = at if long_clip else 0
            query = load_query(own_ref, at, lay)

            def scores(kt, top):
                score = dot_lanes(kv_ref[kt], query)
                st_ref[kt] = score
                return jnp.maximum(top, fold_rows(score, jnp.max))

            top = jnp.full((8, lay.rows), NEG_BIG, F32)
            if long_clip:
                top = lax.fori_loop(0, at, scores, top)
            score = dot_lanes(kv_ref[at], query)
            score = jnp.where(diag_mask(score.shape, lay, core), score, NEG_BIG)
            st_ref[slot] = score
            top = jnp.max(jnp.maximum(top, fold_rows(score, jnp.max)), axis=0, keepdims=True)

            def mix(kt, carry):
                total, acc = carry
                expo = jnp.exp(st_ref[kt if long_clip else 0] - top)
                total = total + fold_rows(expo, jnp.sum)
                return total, acc + dot(vt_ref[kt], expo.astype(BF))

            zero = (jnp.zeros((8, lay.rows), F32), jnp.zeros((HALF, lay.rows), F32))
            if long_clip:
                total, acc = lax.fori_loop(0, at + 1, mix, zero)
            else:
                total, acc = mix(at, zero)
            total = jnp.sum(total, axis=0, keepdims=True)
            acc = acc / total
            ot_ref[at] = acc
            lse_ref[at] = jnp.broadcast_to(top + jnp.log(total), (8, lay.rows))
            out = jnp.concatenate([acc, jnp.zeros_like(acc)], axis=0).T
            o_ref[at] = split_pair(out, lay.top)[0].astype(BF)
            return 0

        lax.fori_loop(0, groups // parts, block, 0)

    vm = pl.BlockSpec(memory_space=pltpu.VMEM)
    pairs = groups * (groups + 1) // 2 if long_clip else groups
    return pl.pallas_call(
        body,
        in_specs=[smem(), vm, vm],
        out_specs=[vm, vm, vm],
        out_shape=[
            jax.ShapeDtypeStruct((groups, lay.top, LANES), BF),
            jax.ShapeDtypeStruct((groups, HALF, lay.rows), F32),
            jax.ShapeDtypeStruct((groups, 8, lay.rows), F32),
        ],
        scratch_shapes=[
            pltpu.VMEM((groups, tile, LANES), BF),
            pltpu.VMEM((groups, HALF, tile), BF),
            pltpu.VMEM((depth, tile, lay.rows), F32),
        ],
        compiler_params=pltpu.CompilerParams(vmem_limit_bytes=48 * MIB),
        cost_estimate=pl.CostEstimate(
            flops=pairs * 16 * tile * lay.rows * DH // parts, bytes_accessed=4 * MIB, transcendentals=pairs * tile * lay.rows
        ),
        name="attend_long" if long_clip else "attend_short",
    )(flags, own, oth)


def attend_back(flags, own, oth, d_out, ot, lse, tab_cos, tab_sin, time_cos, time_sin, lay, long_clip):
    groups = own.shape[0]
    parts = lay.parts if long_clip else 1
    tile = 2 * lay.rows

    def body(flag_ref, own_ref, oth_ref, do_ref, ot_ref, lse_ref, tc_ref, ts_ref, qc_ref, qs_ref, dq_ref, down_ref, doth_ref, kv_ref, kt_ref, acc_ref):
        core = flag_ref[2]
        part = flag_ref[3]

        def prepare(group, _):
            keys = load_keys(own_ref, oth_ref, group, lay)
            kv_ref[group] = keys.astype(BF)
            kt_ref[group] = keys.T[HALF:].astype(BF)
            acc_ref[group] = jnp.zeros((tile, LANES), F32)
            return 0

        lax.fori_loop(0, groups, prepare, 0)
        if parts > 1:
            dq_ref[...] = jnp.zeros_like(dq_ref)

        def block(step, _):
            at = step * parts + part if parts > 1 else step
            query = load_query(own_ref, at, lay)
            packed = do_ref[at].astype(F32)
            grad = jnp.concatenate([packed, swap_halves(packed)[: lay.rows - lay.top]], axis=0)
            grad = jnp.where(lane_low(grad.shape), grad, 0.0)
            delta = jnp.sum(grad.T[:HALF] * ot_ref[at], axis=0, keepdims=True)
            grad = grad.astype(BF)
            lse_row = lse_ref[at][0:1]

            def tile_back(kt, acc, mask):
                keys = kv_ref[kt]
                prob = jnp.exp(dot_lanes(keys, query) - lse_row)
                if mask is not None:
                    prob = jnp.where(mask, prob, 0.0)
                score_grad = (prob * (dot_lanes(keys, grad) - delta)).astype(BF)
                acc_ref[kt] += dot(score_grad, query) + dot(prob.astype(BF), grad)
                return acc + dot(kt_ref[kt], score_grad)

            acc = tile_back(at, jnp.zeros((HALF, lay.rows), F32), diag_mask((tile, lay.rows), lay, core))
            if long_clip:
                acc = lax.fori_loop(0, at, lambda kt, a: tile_back(kt, a, None), acc)
            acc = acc * (1.0 / math.sqrt(DH))
            dq = jnp.concatenate([acc, jnp.zeros_like(acc)], axis=0).T
            tab = at if long_clip else 0
            cosine = tc_ref[...] + per_frame(dq.shape, qc_ref[2 * tab], qc_ref[2 * tab + 1])
            sine = ts_ref[...] + per_frame(dq.shape, qs_ref[2 * tab], qs_ref[2 * tab + 1])
            dq_ref[at] = (dq * cosine - swap_pairs(dq) * sine).astype(BF)
            return 0

        lax.fori_loop(0, groups // parts, block, 0)

        def flush(group, _):
            down_ref[group] = acc_ref[group, : lay.rows]
            doth_ref[group] = acc_ref[group, lay.rows :].astype(BF)
            return 0

        lax.fori_loop(0, groups, flush, 0)

    vm = pl.BlockSpec(memory_space=pltpu.VMEM)
    pairs = groups * (groups + 1) // 2 if long_clip else groups
    return pl.pallas_call(
        body,
        in_specs=[smem()] + [vm] * 9,
        out_specs=[vm, vm, vm],
        out_shape=[
            jax.ShapeDtypeStruct((groups, lay.rows, LANES), BF),
            jax.ShapeDtypeStruct((groups, lay.rows, LANES), F32),
            jax.ShapeDtypeStruct((groups, lay.rows, LANES), BF),
        ],
        scratch_shapes=[
            pltpu.VMEM((groups, tile, LANES), BF),
            pltpu.VMEM((groups, HALF, tile), BF),
            pltpu.VMEM((groups, tile, LANES), F32),
        ],
        compiler_params=pltpu.CompilerParams(vmem_limit_bytes=48 * MIB),
        cost_estimate=pl.CostEstimate(
            flops=pairs * 40 * tile * lay.rows * DH // parts, bytes_accessed=6 * MIB, transcendentals=pairs * tile * lay.rows
        ),
        name="attend_back_long" if long_clip else "attend_back_short",
    )(flags, own, oth, d_out, ot, lse, tab_cos, tab_sin, time_cos, time_sin)


def finish_keys(dq, mine, theirs, tab_cos, tab_sin, time_cos, time_sin, lay, long_clip):
    groups = dq.shape[0]

    def body(dq_ref, a_ref, b_ref, tc_ref, ts_ref, qc_ref, qs_ref, out_ref):
        def one(group, _):
            both = a_ref[group] + b_ref[group].astype(F32)
            tab = group if long_clip else 0
            cosine = tc_ref[...] + per_frame(both.shape, qc_ref[2 * tab], qc_ref[2 * tab + 1])
            sine = ts_ref[...] + per_frame(both.shape, qs_ref[2 * tab], qs_ref[2 * tab + 1])
            keys = both * cosine - swap_pairs(both) * sine
            out_ref[group, : lay.rows, :] = jnp.where(lane_low(keys.shape), dq_ref[group].astype(F32), keys).astype(BF)
            out_ref[group, lay.vrow :, :] = split_pair(both, lay.top)[0].astype(BF)
            return 0

        lax.fori_loop(0, groups, one, 0)

    vm = pl.BlockSpec(memory_space=pltpu.VMEM)
    return pl.pallas_call(
        body,
        in_specs=[vm] * 7,
        out_specs=vm,
        out_shape=jax.ShapeDtypeStruct((groups, lay.vrow + lay.top, LANES), BF),
        compiler_params=pltpu.CompilerParams(vmem_limit_bytes=40 * MIB),
        cost_estimate=pl.CostEstimate(flops=groups * lay.rows * LANES * 10, bytes_accessed=3 * MIB, transcendentals=0),
        name="finish_keys",
    )(dq, mine, theirs, tab_cos, tab_sin, time_cos, time_sin)


def project_and_norm(flags, long_out, short_out, recv, weight, bias, tokens, mods, lay):
    rows, width = tokens.shape
    half = lay.heads * DH

    def body(flag_ref, long_ref, short_ref, recv_ref, w_ref, b_ref, tok_ref, mod_ref, branch_ref, resid_ref, normed_ref, inv_ref, hid_ref, att_ref):
        own_long = flag_ref[0]
        side = flag_ref[1]
        for pair in range(lay.heads // 2):
            kept = [
                jnp.where(own_long == 1, long_ref[2 * pair + k].astype(F32), short_ref[2 * pair + k].astype(F32)) for k in (0, 1)
            ]
            got = [recv_ref[2 * pair + k].astype(F32) for k in (0, 1)]
            lanes = slice(pair * LANES, (pair + 1) * LANES)
            att_ref[side, :, lanes] = join_pair(kept[0], kept[1], rows).astype(BF)
            att_ref[1 - side, :, lanes] = join_pair(got[0], got[1], rows).astype(BF)
        branch = dot(att_ref[0], w_ref[:half]) + dot(att_ref[1], w_ref[half:]) + b_ref[...]
        branch_ref[...] = branch
        gate = per_frame(branch.shape, mod_ref[0:1], mod_ref[1:2])
        resid = tok_ref[...].astype(F32) + gate * branch
        resid_ref[...] = resid
        normed, inv_std = norm_rows(resid)
        normed_ref[...] = normed
        inv_ref[...] = jnp.broadcast_to(inv_std, inv_ref.shape)
        shift = per_frame(branch.shape, mod_ref[2:3], mod_ref[3:4])
        scale = per_frame(branch.shape, mod_ref[4:5], mod_ref[5:6])
        hid_ref[...] = (normed * (1.0 + scale) + shift).astype(BF)

    vm = pl.BlockSpec(memory_space=pltpu.VMEM)
    full = jax.ShapeDtypeStruct((rows, width), F32)
    return pl.pallas_call(
        body,
        in_specs=[smem()] + [vm] * 7,
        out_specs=[vm] * 5,
        out_shape=[full, full, full, jax.ShapeDtypeStruct((rows, LANES), F32), jax.ShapeDtypeStruct((rows, width), BF)],
        scratch_shapes=[pltpu.VMEM((2, rows, half), BF)],
        compiler_params=pltpu.CompilerParams(vmem_limit_bytes=32 * MIB),
        cost_estimate=pl.CostEstimate(flops=2 * rows * width * width, bytes_accessed=6 * MIB, transcendentals=0),
        name="project_and_norm",
    )(flags, long_out, short_out, recv, weight, bias, tokens, mods)


def mlp_both(flags, hidden, mlp_grad, up_weight, up_bias, down_weight, lay, out_dtype, name):
    rows, width = hidden.shape
    ff = up_weight.shape[1]
    wide = 2 * LANES
    steps = ff // (2 * wide)

    def body(flag_ref, hid_ref, mg_ref, up_ref, ub_ref, dn_ref, actm_ref, actt_ref, pgm_ref, pgt_ref, bm_ref, bt_ref, mlp_ref, hg_ref, macc, hacc):
        step = pl.program_id(0)
        core = flag_ref[2]
        pre = dot(hid_ref[...], up_ref[...]) + ub_ref[...]
        tanh = jnp.tanh(GELU_C * (pre + GELU_K * pre * pre * pre))
        act = (0.5 * pre * (1.0 + tanh)).astype(BF)
        slope = 0.5 * (1.0 + tanh) + 0.5 * pre * (1.0 - tanh * tanh) * GELU_C * (1.0 + 3.0 * GELU_K * pre * pre)
        pre_low = (dot_lanes(mg_ref[...], dn_ref[...]) * slope).astype(BF)
        mlp = dot(act, dn_ref[...])
        back = dot_lanes(pre_low, up_ref[...])

        @pl.when(step == 0)
        def _():
            macc[...] = mlp
            hacc[...] = back

        @pl.when(step > 0)
        def _():
            macc[...] += mlp
            hacc[...] += back

        @pl.when(step == steps - 1)
        def _():
            mlp_ref[...] = macc[...].astype(mlp_ref.dtype)
            hg_ref[...] = hacc[...].astype(hg_ref.dtype)

        first = core == 0
        actm_ref[...] = jnp.where(first, act[:, :LANES], act[:, LANES:])
        actt_ref[...] = jnp.where(first, act[:, LANES:], act[:, :LANES])
        pgm_ref[...] = jnp.where(first, pre_low[:, :LANES], pre_low[:, LANES:])
        pgt_ref[...] = jnp.where(first, pre_low[:, LANES:], pre_low[:, :LANES])
        sums = jnp.sum(pre_low.astype(F32), axis=0, keepdims=True)
        bm_ref[...] = jnp.broadcast_to(jnp.where(first, sums[:, :LANES], sums[:, LANES:]), bm_ref.shape)
        bt_ref[...] = jnp.broadcast_to(jnp.where(first, sums[:, LANES:], sums[:, :LANES]), bt_ref.shape)

    quarter = ff // 4
    chunk = pl.BlockSpec((rows, LANES), lambda i, f: (0, i))
    bchunk = pl.BlockSpec((8, LANES), lambda i, f: (0, i))
    return pl.pallas_call(
        body,
        grid_spec=pltpu.PrefetchScalarGridSpec(
            num_scalar_prefetch=1,
            grid=(steps,),
            in_specs=[
                whole((rows, width)),
                whole((rows, width)),
                pl.BlockSpec((width, wide), lambda i, f: (0, 2 * i + f[1])),
                pl.BlockSpec((1, wide), lambda i, f: (0, 2 * i + f[1])),
                pl.BlockSpec((wide, width), lambda i, f: (2 * i + f[1], 0)),
            ],
            out_specs=[chunk, chunk, chunk, chunk, bchunk, bchunk, whole((rows, width)), whole((rows, width))],
            scratch_shapes=[pltpu.VMEM((rows, width), F32), pltpu.VMEM((rows, width), F32)],
        ),
        out_shape=[jax.ShapeDtypeStruct((rows, quarter), BF)] * 4
        + [jax.ShapeDtypeStruct((8, quarter), F32)] * 2
        + [jax.ShapeDtypeStruct((rows, width), out_dtype)] * 2,
        compiler_params=pltpu.CompilerParams(vmem_limit_bytes=32 * MIB),
        cost_estimate=pl.CostEstimate(flops=4 * rows * width * ff, bytes_accessed=12 * MIB, transcendentals=rows * ff // 2),
        name=name,
    )(flags, hidden, mlp_grad, up_weight, up_bias, down_weight)


def branch_back(flags, hid_own, hid_recv, cotangent, normed, inv_std, branch, mods, weight, lay):
    rows, width = normed.shape
    half = lay.heads * DH

    def body(flag_ref, a_ref, b_ref, dy_ref, n_ref, inv_ref, br_ref, mod_ref, w_ref, rg_ref, bg_ref, keep_ref, send_ref, sums_ref):
        side = flag_ref[1]
        hid = a_ref[...] + b_ref[...].astype(F32)
        norm = n_ref[...]
        scale = per_frame(hid.shape, mod_ref[4:5], mod_ref[5:6])
        resid = dy_ref[...].astype(F32) + norm_back(hid * (1.0 + scale), norm, inv_ref[:, 0:1])
        rg_ref[...] = resid
        gate = per_frame(hid.shape, mod_ref[0:1], mod_ref[1:2])
        low = (gate * resid).astype(BF)
        bg_ref[...] = low
        for out_ref, which in ((keep_ref, side), (send_ref, 1 - side)):
            grad = dot_lanes(low, w_ref[pl.ds(pl.multiple_of(which * half, half), half), :])
            for pair in range(lay.heads // 2):
                one, two = split_pair(grad[:, pair * LANES : (pair + 1) * LANES], lay.top)
                out_ref[2 * pair] = one.astype(BF)
                out_ref[2 * pair + 1] = two.astype(BF)
        sums_ref[0:1], sums_ref[1:2] = frame_sums(resid * br_ref[...])
        sums_ref[2:3], sums_ref[3:4] = frame_sums(hid)
        sums_ref[4:5], sums_ref[5:6] = frame_sums(hid * norm)
        sums_ref[6:7] = jnp.sum(low.astype(F32), axis=0, keepdims=True)
        sums_ref[7:8] = jnp.zeros((1, width), F32)

    vm = pl.BlockSpec(memory_space=pltpu.VMEM)
    packed = jax.ShapeDtypeStruct((lay.heads, lay.top, LANES), BF)
    return pl.pallas_call(
        body,
        in_specs=[smem()] + [vm] * 8,
        out_specs=[vm] * 5,
        out_shape=[
            jax.ShapeDtypeStruct((rows, width), F32),
            jax.ShapeDtypeStruct((rows, width), BF),
            packed,
            packed,
            jax.ShapeDtypeStruct((8, width), F32),
        ],
        compiler_params=pltpu.CompilerParams(vmem_limit_bytes=32 * MIB),
        cost_estimate=pl.CostEstimate(flops=2 * rows * width * width, bytes_accessed=8 * MIB, transcendentals=0),
        name="branch_back",
    )(flags, hid_own, hid_recv, cotangent, normed, inv_std, branch, mods, weight)


def qkv_back(flags, grads, tok_own, tok_oth, weight, lay, is_long):
    rows, width = tok_own.shape
    cols = lay.heads * DH
    half = cols // 2

    def body(flag_ref, g_ref, own_ref, oth_ref, w_ref, hid_ref, low_ref, gm_ref, gt_ref, bias_ref, sums_ref, q_ref, acc_ref):
        step = pl.program_id(0)
        core = flag_ref[2]

        @pl.when(step == 0)
        def _():
            for pair in range(lay.heads // 2):
                one, two = g_ref[2 * pair, :rows, :].astype(F32), g_ref[2 * pair + 1, :rows, :].astype(F32)
                low = lane_low(one.shape)
                lanes = slice(pair * LANES, (pair + 1) * LANES)
                q_ref[0, :, lanes] = jnp.where(low, one, swap_halves(two)).astype(BF)
                q_ref[1, :, lanes] = jnp.where(low, swap_halves(one), two).astype(BF)
                one, two = g_ref[2 * pair, lay.vrow :, :].astype(F32), g_ref[2 * pair + 1, lay.vrow :, :].astype(F32)
                q_ref[2, :, lanes] = join_pair(one, two, rows).astype(BF)

        value = q_ref[step]
        part = dot_lanes(value, w_ref[...])

        @pl.when(step == 0)
        def _():
            acc_ref[...] = part

        @pl.when(step > 0)
        def _():
            acc_ref[...] += part

        first = core == 0
        gm_ref[...] = jnp.where(first, value[:, :half], value[:, half:])
        gt_ref[...] = jnp.where(first, value[:, half:], value[:, :half])
        bias_ref[...] = jnp.broadcast_to(jnp.sum(value.astype(F32), axis=0, keepdims=True), bias_ref.shape)

        @pl.when(step == 2)
        def _():
            hid = acc_ref[...]
            hid_ref[...] = hid
            low_ref[...] = hid.astype(BF)
            mine = (flag_ref[0] == 1) if is_long else (flag_ref[0] == 0)
            normed, _ = norm_rows(jnp.where(mine, own_ref[...].astype(F32), oth_ref[...].astype(F32)))
            sums_ref[0:1], sums_ref[1:2] = frame_sums(hid)
            sums_ref[2:3], sums_ref[3:4] = frame_sums(hid * normed)
            sums_ref[4:8] = jnp.zeros((4, width), F32)

    return pl.pallas_call(
        body,
        grid_spec=pltpu.PrefetchScalarGridSpec(
            num_scalar_prefetch=1,
            grid=(3,),
            in_specs=[
                whole(grads.shape),
                whole((rows, width)),
                whole((rows, width)),
                pl.BlockSpec((width, cols), lambda j, f: (0, 2 * j + f[1])),
            ],
            out_specs=[
                whole((rows, width)),
                whole((rows, width)),
                pl.BlockSpec((rows, half), lambda j, f: (0, j)),
                pl.BlockSpec((rows, half), lambda j, f: (0, j)),
                pl.BlockSpec((8, cols), lambda j, f: (0, j)),
                whole((8, width)),
            ],
            scratch_shapes=[pltpu.VMEM((3, rows, cols), BF), pltpu.VMEM((rows, width), F32)],
        ),
        out_shape=[
            jax.ShapeDtypeStruct((rows, width), F32),
            jax.ShapeDtypeStruct((rows, width), BF),
            jax.ShapeDtypeStruct((rows, 3 * half), BF),
            jax.ShapeDtypeStruct((rows, 3 * half), BF),
            jax.ShapeDtypeStruct((8, 3 * cols), F32),
            jax.ShapeDtypeStruct((8, width), F32),
        ],
        compiler_params=pltpu.CompilerParams(vmem_limit_bytes=40 * MIB),
        cost_estimate=pl.CostEstimate(flops=6 * rows * width * cols, bytes_accessed=8 * MIB, transcendentals=0),
        name="qkv_back_long" if is_long else "qkv_back_short",
    )(flags, grads, tok_own, tok_oth, weight)


def token_back(flags, hid_long, hid_short, recv, tokens, resid_grad, mods, lay):
    rows, width = tokens.shape

    def body(flag_ref, l_ref, s_ref, r_ref, tok_ref, rg_ref, mod_ref, out_ref):
        hid = jnp.where(flag_ref[0] == 1, l_ref[...], s_ref[...]) + r_ref[...].astype(F32)
        normed, inv_std = norm_rows(tok_ref[...].astype(F32))
        scale = per_frame(hid.shape, mod_ref[0:1, width : 2 * width], mod_ref[1:2, width : 2 * width])
        out_ref[...] = rg_ref[...] + norm_back(hid * (1.0 + scale), normed, inv_std)

    vm = pl.BlockSpec(memory_space=pltpu.VMEM)
    return pl.pallas_call(
        body,
        in_specs=[smem()] + [vm] * 6,
        out_specs=vm,
        out_shape=jax.ShapeDtypeStruct((rows, width), F32),
        compiler_params=pltpu.CompilerParams(vmem_limit_bytes=32 * MIB),
        cost_estimate=pl.CostEstimate(flops=rows * width * 20, bytes_accessed=5 * MIB, transcendentals=0),
        name="token_back",
    )(flags, hid_long, hid_short, recv, tokens, resid_grad, mods)


def weight_grads(lefts, rights, n_blk, name):
    count = len(lefts)
    rows, depth = lefts[0].shape
    cols = rights[0].shape[1]
    tall = max(depth // n_blk, LANES)
    steps = depth // tall
    per = tall // (depth // n_blk)

    def body(*refs):
        out_ref = refs[-1]
        acc = dot_rows(refs[0][...], refs[count][...])
        for k in range(1, count):
            acc += dot_rows(refs[k][...], refs[count + k][...])
        out_ref[...] = acc.astype(BF).reshape(out_ref.shape)

    return pl.pallas_call(
        body,
        grid=(steps,),
        in_specs=[pl.BlockSpec((rows, tall), lambda i: (0, i))] * count + [whole((rows, cols))] * count,
        out_specs=pl.BlockSpec((per, tall // per, cols), lambda i: (i, 0, 0)),
        out_shape=jax.ShapeDtypeStruct((n_blk, depth // n_blk, cols), BF),
        compiler_params=pltpu.CompilerParams(vmem_limit_bytes=32 * MIB),
        cost_estimate=pl.CostEstimate(flops=2 * count * rows * depth * cols, bytes_accessed=6 * MIB, transcendentals=0),
        name=name,
    )(*lefts, *rights)


def head_weight_grads(longs, shorts, grad_long, grad_short, lay):
    rows, width = grad_long.shape
    pairs = lay.heads // 2

    def body(l_ref, s_ref, gl_ref, gs_ref, out_ref):
        for pair in range(pairs):
            acc = 0.0
            for ref, g_ref in ((l_ref, gl_ref), (s_ref, gs_ref)):
                left = join_pair(ref[2 * pair].astype(F32), ref[2 * pair + 1].astype(F32), rows).astype(BF)
                acc = acc + dot_rows(left, g_ref[...])
            out_ref[pair * LANES : (pair + 1) * LANES, :] = acc.astype(BF)

    vm = pl.BlockSpec(memory_space=pltpu.VMEM)
    return pl.pallas_call(
        body,
        in_specs=[vm] * 4,
        out_specs=vm,
        out_shape=jax.ShapeDtypeStruct((lay.heads * DH, width), BF),
        compiler_params=pltpu.CompilerParams(vmem_limit_bytes=32 * MIB),
        cost_estimate=pl.CostEstimate(flops=4 * rows * width * lay.heads * DH, bytes_accessed=3 * MIB, transcendentals=0),
        name="head_weight_grads",
    )(longs, shorts, grad_long, grad_short)


def rotary_static(frames):
    n_time, n_row = DH // 8, 3 * DH // 16
    cosine = np.zeros((frames * PATCH, LANES), np.float32)
    sine = np.zeros((frames * PATCH, LANES), np.float32)
    patch = np.arange(frames * PATCH) % PATCH
    for group, place in ((0, patch // GRID), (1, patch % GRID)):
        for j in range(n_row):
            freq = np.exp(np.float32(-math.log(10000.0)) * np.float32(j) / np.float32(n_row)).astype(np.float32)
            angle = (place.astype(np.float32) * freq).astype(np.float64)
            pair = n_time + group * n_row + j
            for head in (0, HALF):
                cosine[:, head + 2 * pair] = np.cos(angle)
                cosine[:, head + 2 * pair + 1] = np.cos(angle)
                sine[:, head + 2 * pair] = -np.sin(angle)
                sine[:, head + 2 * pair + 1] = np.sin(angle)
    return cosine, sine


def rotary_time(times):
    n_time = DH // 8
    lane = jnp.arange(LANES, dtype=jnp.int32)
    pair = (lane % HALF) // 2
    freq = jnp.exp(-math.log(10000.0) * pair.astype(F32) / float(n_time))
    angle = times.astype(F32)[:, None] * freq[None, :]
    live = (pair < n_time)[None, :]
    sign = jnp.where(lane % 2 == 0, -1.0, 1.0)[None, :]
    return jnp.where(live, jnp.cos(angle), 0.0), jnp.where(live, sign * jnp.sin(angle), 0.0)


class Layout:
    def __init__(self, rows, heads, parts):
        self.rows = rows
        self.heads = heads
        self.parts = parts
        self.top = round_up(-(-rows // 2), 16)
        self.vrow = round_up(rows, 16)


def on_device(
    tokens, cotangent, noise_embed, frame_clip, frame_index, mod_weight, mod_bias, attn_weight, attn_bias,
    proj_weight, proj_bias, up_weight, up_bias, down_weight, down_bias,
):
    n_uly = lax.axis_size("uly")
    n_blk = lax.axis_size("blk")
    blk = lax.axis_index("blk")
    uly = lax.axis_index("uly")
    rows, width = tokens.shape
    frames = noise_embed.shape[0]
    side, core = uly // 2, uly % 2
    heads = width // DH // 2
    parts = n_blk // heads
    lay = Layout(rows, heads, parts)
    dev = blk * n_uly + uly

    def swap_side(value):
        return lax.ppermute(value, "uly", [(i, i ^ 2) for i in range(n_uly)])

    def swap_core(value):
        return lax.ppermute(value, "uly", [(i, i ^ 1) for i in range(n_uly)])

    def spread(value):
        return lax.all_to_all(value, "blk", split_axis=0, concat_axis=0, tiled=True)

    def gather_all(value):
        many = lax.all_to_all(jnp.broadcast_to(value[None], (n_blk,) + value.shape), "blk", 0, 0, tiled=True)
        return lax.all_to_all(jnp.broadcast_to(many[None], (n_uly,) + many.shape), "uly", 0, 0, tiled=True)

    long_first = frame_clip[::FB] == n_blk
    own_long_b = lax.dynamic_index_in_dim(long_first, blk, 0, False) == (side == 0)
    own_long = own_long_b.astype(jnp.int32)
    flags = jnp.stack([own_long, side, core, blk // heads]).astype(jnp.int32)

    noise_oth = swap_side(noise_embed)
    tok_oth = swap_side(tokens)

    block_time = frame_index.reshape(n_blk, FB)
    head_time, tail_time = block_time[:, : FB // 2], block_time[:, FB // 2 :]
    long_times = lax.dynamic_slice_in_dim(jnp.where(long_first[:, None], head_time, tail_time), core * frames, frames, 1)
    short_times = lax.dynamic_slice_in_dim(jnp.where(long_first[:, None], tail_time, head_time), core * frames, frames, 1)
    short_times = lax.dynamic_index_in_dim(short_times, blk, 0, False)
    time_cos, time_sin = rotary_time(jnp.concatenate([lax.dynamic_index_in_dim(long_times, blk, 0, False), short_times]))
    long_cos, long_sin = rotary_time(long_times.reshape(-1))
    short_cos, short_sin = time_cos[frames:, None], time_sin[frames:, None]
    long_cos, long_sin = long_cos[:, None], long_sin[:, None]
    tab_cos, tab_sin = (jnp.asarray(t) for t in rotary_static(frames))

    noise = jnp.concatenate([noise_embed, noise_oth], axis=0).astype(F32)
    silu = jax.nn.silu(noise).astype(BF)
    mod = dot(silu, mod_weight) + mod_bias.astype(F32)
    own_mod = mod[:frames]
    gate2 = own_mod[:, 5 * width :]
    mid_mods = jnp.concatenate(
        [own_mod[:, 2 * width : 3 * width], own_mod[:, 3 * width : 4 * width], own_mod[:, 4 * width : 5 * width]], axis=0
    )
    mid_mods = jnp.concatenate([mid_mods, jnp.zeros((2, width), F32)], axis=0)
    gate2_rows = jnp.repeat(gate2, PATCH, axis=0)
    dy_grad = cotangent.astype(F32)
    mlp_grad = (gate2_rows * dy_grad).astype(BF)

    hidden1, qkv_long, qkv_short = tokens_to_qkv(
        flags, tokens, tok_oth, mod[:, : 2 * width], attn_weight, attn_bias.astype(F32)[None], tab_cos, tab_sin, time_cos, time_sin, lay
    )
    sent = jnp.concatenate([qkv_long] * parts, axis=0) if parts > 1 else qkv_long
    long_own = spread(sent)
    short_oth = swap_core(qkv_short)
    mlp_grad_oth = swap_side(mlp_grad)
    out_short, ot_short, lse_short = attend(flags, qkv_short, short_oth, lay, False)
    long_oth = swap_core(long_own)
    out_long_all, ot_long, lse_long = attend(flags, long_own, long_oth, lay, True)

    def own_part(value):
        if parts == 1:
            return value
        return lax.dynamic_slice_in_dim(value, (blk % parts) * heads, heads, 0)

    out_long = own_part(spread(out_long_all))
    out_recv = swap_side(jnp.where(own_long_b, out_short, out_long))
    branch, resid, normed2, inv2, hidden2 = project_and_norm(
        flags, out_long, out_short, out_recv, proj_weight, proj_bias.astype(F32)[None], tokens, mid_mods, lay
    )

    hidden2_oth = swap_side(hidden2)
    up_b = up_bias.astype(F32)[None]
    actm, actt, pgm, pgt, bm, bt, mlp_own, hid_own = mlp_both(
        flags, hidden2, mlp_grad, up_weight, up_b, down_weight, lay, F32, "mlp_own"
    )
    actm2, actt2, pgm2, pgt2, bm2, bt2, mlp_oth, hid_oth = mlp_both(
        flags, hidden2_oth, mlp_grad_oth, up_weight, up_b, down_weight, lay, BF, "mlp_other"
    )
    hid_recv = swap_side(hid_oth)

    resid_grad, branch_grad, do_keep, do_send, mid_sums = branch_back(
        flags, hid_own, hid_recv, cotangent, normed2, inv2, branch, mid_mods, proj_weight, lay
    )
    do_recv = swap_side(do_send)
    do_long = jnp.where(own_long_b, do_keep, do_recv)
    do_short = jnp.where(own_long_b, do_recv, do_keep)
    if parts > 1:
        hot = (jnp.arange(parts) == blk % parts)[:, None, None, None]
        do_sent = jnp.where(hot, do_long[None], 0).reshape((n_blk,) + do_long.shape[1:])
    else:
        do_sent = do_long
    do_all = spread(do_sent)

    dq_s, mine_s, theirs_s = attend_back(
        flags, qkv_short, short_oth, do_short, ot_short, lse_short, tab_cos, tab_sin, short_cos, short_sin, lay, False
    )
    grads_short = finish_keys(dq_s, mine_s, swap_core(theirs_s), tab_cos, tab_sin, short_cos, short_sin, lay, False)

    dq_l, mine_l, theirs_l = attend_back(
        flags, long_own, long_oth, do_all, ot_long, lse_long, tab_cos, tab_sin, long_cos, long_sin, lay, True
    )
    grads_all = spread(finish_keys(dq_l, mine_l, swap_core(theirs_l), tab_cos, tab_sin, long_cos, long_sin, lay, True))
    if parts > 1:
        grads_long = jnp.sum(grads_all.astype(F32).reshape((parts, heads) + grads_all.shape[1:]), axis=0).astype(BF)
    else:
        grads_long = grads_all

    hidS, hidS_low, gmS, gtS, abS, sumS = qkv_back(flags, grads_short, tokens, tok_oth, attn_weight, lay, False)
    hidL, hidL_low, gmL, gtL, abL, sumL = qkv_back(flags, grads_long, tokens, tok_oth, attn_weight, lay, True)
    hid1_recv = swap_side(jnp.where(own_long_b, hidS_low, hidL_low))
    token_grad = token_back(flags, hidL, hidS, hid1_recv, tokens, resid_grad, mod[:, : 2 * width], lay)

    mlp_recv = swap_side(mlp_oth)
    mlp = mlp_own + mlp_recv.astype(F32) + down_bias.astype(F32)[None]
    output = (resid + gate2_rows * mlp).astype(BF)
    gate2_grad = jnp.sum((dy_grad * mlp).reshape(frames, PATCH, width), axis=1)

    act_got, pg_got, act_got2, pg_got2 = (swap_core(v) for v in (actt, pgt, actt2, pgt2))
    hid_c, hid_c2, mg_c, mg_c2 = (swap_core(v) for v in (hidden2, hidden2_oth, mlp_grad, mlp_grad_oth))
    up_part = weight_grads([hidden2, hidden2_oth, hid_c, hid_c2], [pgm, pgm2, pg_got, pg_got2], n_blk, "up_grads")
    down_part = weight_grads([actm, actm2, act_got, act_got2], [mlp_grad, mlp_grad_oth, mg_c, mg_c2], n_blk, "down_grads")
    mlp_total = lax.psum_scatter(
        jnp.concatenate([up_part, down_part], axis=1), "blk", scatter_dimension=0, tiled=False
    )
    up_rows = up_part.shape[1]
    up_mine = mlp_total[:up_rows]
    down_mine = mlp_total[up_rows:].astype(F32)

    def to_rows(value):
        return lax.all_to_all(value.reshape((n_uly, value.shape[0] // n_uly) + value.shape[1:]), "uly", 0, 0, tiled=True)

    up_all = to_rows(up_mine)
    row_out = up_all.shape[1]
    ff = up_weight.shape[1]
    g_up_weight = jnp.swapaxes(up_all, 0, 1).reshape(row_out, n_uly, ff // (n_uly * LANES), LANES)
    g_up_weight = jnp.swapaxes(g_up_weight, 1, 2).reshape(row_out, ff).astype(F32)

    g = ff // (n_blk * n_uly)
    def down_home(index):
        b, u = divmod(index, n_uly)
        start = ((b * g // LANES) * n_uly + u) * LANES + (b * g) % LANES
        return start // g

    down_map = [(i, down_home(i)) for i in range(n_blk * n_uly)]
    if all(a == b for a, b in down_map):
        g_down_weight = down_mine
    else:
        g_down_weight = lax.ppermute(down_mine, ("blk", "uly"), down_map)

    branch_grad_oth = swap_side(branch_grad)
    bg_long = jnp.where(own_long_b, branch_grad, branch_grad_oth)
    bg_short = jnp.where(own_long_b, branch_grad_oth, branch_grad)
    proj_part = head_weight_grads(out_long, out_short, bg_long, bg_short, lay).reshape(2, -1, width)
    proj_got = swap_core(jnp.where(core == 0, proj_part[1], proj_part[0]))
    proj_half = jnp.where(core == 0, proj_part[0], proj_part[1]).astype(F32) + proj_got.astype(F32)
    proj_sum = jnp.sum(spread(proj_half.astype(BF).reshape(n_blk, -1, width)).astype(F32), axis=0)
    proj_map = [(b * n_uly + u, u * n_blk + b) for b in range(n_blk) for u in range(n_uly)]
    g_proj_weight = lax.ppermute(proj_sum, ("blk", "uly"), proj_map)

    h1_core = swap_core(hidden1)
    attn_part = weight_grads(
        [hidden1[0], hidden1[1], h1_core[0], h1_core[1]], [gmL, gmS, swap_core(gtL), swap_core(gtS)], n_blk, "attn_grads"
    )
    attn_sum = jnp.sum(spread(attn_part).astype(F32), axis=0)
    attn_all = to_rows(attn_sum)
    g_attn_weight = jnp.transpose(attn_all.reshape(n_uly, row_out, 3, -1), (1, 2, 0, 3)).reshape(row_out, 3 * width)

    down_b = jnp.sum(mlp_grad.astype(F32), axis=0, keepdims=True)
    early = jnp.concatenate(
        [mid_sums[0:2], mid_sums[2:6], gate2_grad, silu[:frames].astype(F32), down_b, mid_sums[6:7],
         (bm + bm2)[0:1], (bt + bt2)[0:1], jnp.zeros((2, width), F32)], axis=0,
    ).astype(BF)
    early_all = gather_all(early).astype(F32)
    late = jnp.concatenate(
        [sumL[:4], sumS[:4], jnp.pad((abL + abS)[0], (0, width // 2)).reshape(2, width), jnp.zeros((6, width), F32)], axis=0
    ).astype(BF)
    late_all = gather_all(late).astype(F32)

    own_long_all = (long_first[None, :] == (jnp.arange(n_uly) // 2 == 0)[:, None])[:, :, None, None]
    part_l, part_s = late_all[:, :, 0:4], late_all[:, :, 4:8]
    part_own = jnp.where(own_long_all, part_l, part_s)
    part_oth = jnp.where(own_long_all, part_s, part_l)
    first_all = part_own + jnp.concatenate([part_oth[2:], part_oth[:2]], axis=0)
    silu_all = early_all[:, :, 8:10].reshape(-1, width).astype(BF)
    silu_cols = lax.dynamic_slice_in_dim(silu_all, dev * (width // (n_blk * n_uly)), width // (n_blk * n_uly), 1)
    mod_all = jnp.concatenate(
        [first_all[:, :, 0:2], first_all[:, :, 2:4], early_all[:, :, 0:2], early_all[:, :, 2:4], early_all[:, :, 4:6], early_all[:, :, 6:8]],
        axis=-1,
    ).reshape(-1, 6 * width)
    g_mod_weight = dot_rows(silu_cols, mod_all.astype(BF))

    def cut(vector, start, size):
        return lax.dynamic_slice_in_dim(vector, start, size, 0)

    total_dev = n_blk * n_uly
    g_mod_bias = cut(jnp.sum(mod_all, axis=0), dev * (6 * width // total_dev), 6 * width // total_dev)
    early_sum = jnp.sum(early_all, axis=(0, 1))
    g_down_bias = cut(early_sum[10], dev * (width // total_dev), width // total_dev)
    g_proj_bias = cut(early_sum[11], dev * (width // total_dev), width // total_dev)
    up_by_uly = jnp.sum(early_all[:, :, 12:14], axis=1)
    up_quarter = up_by_uly[:, 0] + up_by_uly[:, 1].reshape(n_uly // 2, 2, width)[:, ::-1].reshape(n_uly, width)
    up_line = jnp.swapaxes(up_quarter.reshape(n_uly, -1, LANES), 0, 1).reshape(-1)
    g_up_bias = cut(up_line, dev * g, g)
    late_bias = jnp.sum(late_all[:, :, 8:10], axis=1).reshape(n_uly // 2, 2, 2 * width).sum(axis=1)[:, : 3 * width // 2]
    attn_line = jnp.swapaxes(late_bias.reshape(n_uly // 2, 3, width // 2), 0, 1).reshape(-1)
    g_attn_bias = cut(attn_line, dev * (3 * width // total_dev), 3 * width // total_dev)
    return (
        output, token_grad, g_mod_weight, g_mod_bias, g_attn_weight, g_attn_bias,
        g_proj_weight, g_proj_bias, g_up_weight, g_up_bias, g_down_weight, g_down_bias,
    )


def solution(mesh):
    row = P(("blk", "uly"), None)
    flat = P(("blk", "uly"))
    in_specs = (row, row, row) + (P(),) * 12
    out_specs = (row, row, row, flat, row, flat, row, flat, row, flat, row, flat)
    return jax.shard_map(on_device, mesh=mesh, in_specs=in_specs, out_specs=out_specs, check_vma=False)
```

time: 1720 us -> 448 us (0.26)
  waiting for transfers between devices: 972 us -> 86.9 us
  matrix products: 376 us -> 7.59 us
  Pallas kernels: 0 us -> 129 us
  local copies, waits for them, and re-layouts: 170 us -> 63.9 us
  other arithmetic: 93.1 us -> 39.4 us
  starting transfers between devices: 26.5 us -> 78.1 us
  blocking collectives: 52.9 us -> 22 us
    reduce_scatter x6 -> x1, waiting for transfers between devices: 829 us -> 0.01 us  [on_device(): lax.psum_scatter(jnp.concatenate([up_part, down_part], axis=1), 'blk', sc...]
    dot_general x50 -> x2, matrix products: 376 us -> 7.59 us  [the longest x1 6.33 us: dot(): return jnp.dot(left, right, preferred_element_type=F32)]
    pallas_call x0 -> x18, Pallas kernels: none -> 129 us  [the longest x2 30.6 us: attend_back(): pl.pallas_call(body, in_specs=[smem()] + [vm] * 9, out_specs=[vm, vm, vm]...]
    unnamed x10 -> x1, waiting for transfers between devices: 75.7 us -> 0.02 us
    unnamed x1 -> x0, blocking collectives: 42.1 us -> none
    reduce_sum x12 -> x9, other arithmetic: 50.9 us -> 13.7 us  [the longest x1 3.63 us: on_device(): jnp.sum(mod_all, axis=0)]
    ppermute x0 -> x27, waiting for transfers between devices: none -> 34.9 us  [the longest x10 25.7 us: swap_side(): return lax.ppermute(value, 'uly', [(i, i ^ 2) for i in range(n_uly)])]
    all_gather x2 -> x0, waiting for transfers between devices: 34.6 us -> none  [the longest x1 34.6 us: on_device(): lax.all_gather(k_heads, 'blk', axis=0, tiled=True)]
  transfers between devices with their start and end apart: 16 -> 39, of which waited for: 12 -> 14; matrix products, arithmetic and copies ran while one was open for 15% -> 16% of each run, Pallas kernels for 0% -> 28%
where the time goes in v1:
time: 448 us; the launch traced here: 443 us
  Pallas kernels  129 us (29%)
  waiting for transfers between devices  86.9 us (19%)
  starting transfers between devices  78.1 us (17%)
  local copies, waits for them, and re-layouts  63.9 us (14%)
  other arithmetic  39.4 us (9%)
  blocking collectives  22 us (5%)
  between operations  16 us (4%)
  matrix products  7.59 us (2%)
    unnamed x202, local copies, waits for them, and re-layouts  40.1 us
    all_to_all x5, waiting for transfers between devices, spread(): return lax.all_to_all(value, 'blk', split_axis=0, concat_axis=0, tiled=True)  36.3 us
    all_to_all x5, starting transfers between devices, spread(): return lax.all_to_all(value, 'blk', split_axis=0, concat_axis=0, tiled=True)  31.7 us
    pallas_call x2, Pallas kernels, attend_back(): pl.pallas_call(body, in_specs=[smem()] + [vm] * 9, out_specs=[vm, vm, vm]...  30.6 us
    pallas_call x2, Pallas kernels, attend(): pl.pallas_call(body, in_specs=[smem(), vm, vm], out_specs=[vm, vm, vm], o...  29.5 us
    ppermute x10, waiting for transfers between devices, swap_side(): return lax.ppermute(value, 'uly', [(i, i ^ 2) for i in range(n_uly)])  25.7 us
    pallas_call x2, Pallas kernels, mlp_both(): pl.pallas_call(body, grid_spec=pltpu.PrefetchScalarGridSpec(num_scalar_pr...  22.7 us
    all_to_all x1, blocking collectives, spread(): return lax.all_to_all(value, 'blk', split_axis=0, concat_axis=0, tiled=True)  22 us
  transfers between devices with their start and end apart: 39, of which 14 were waited for; matrix products, arithmetic and copies ran while one was open for 16% of the time, Pallas kernels for 28%

profile of v1, /device:TPU:4, one launch (start us, length us, event | category | flops | bytes accessed | tf_op | source)
XLA Modules:
  0.0 443.2 jit_solution(15387405806491239850)
XLA Ops:
  14.2 4.6 %collective-permute-done.1 = bf16[2,1024]{1,0:T(2,128)(2,1)S(1)} collective-permute-done((bf16[2,1024]{1,0:T(2,128)(2,1)}, bf16[2,1024]{1,0:T(2,128)(2,1)S(1)}, u32[]{:S(2)}, u32[]{:S(2)}) %collective-permute-start.1) | collective-permute-done | bytes 4128 | tf_op jit(solution)/shard_map/ppermute | solution.py:777
  18.7 6.3 %convolution_add_fusion = f32[4,6144]{1,0:T(4,128)S(1)} fusion(bf16[1024,6144]{1,0:T(8,128)(2,1)} %param.22, f32[6144]{0:T(1024)S(1)} %convert_element_type.125, bf16[2,1024]{1,0:T(2,128)(2,1)S(1)} %collective-permute-done.1, bf16[2,1024]{1,0:T(2,128)(2,1)} %param.19), kind=kOutput, calls=%fused_computation | convolution fusion | flops 50393088 | bytes 12713984 | tf_op jit(solution)/shard_map/dot_general | solution.py:75
  25.2 7.3 %tokens_to_qkv.1 = (bf16[2,200,1024]{2,1,0:T(8,128)(2,1)S(1)}, bf16[8,320,128]{2,1,0:T(8,128)(2,1)S(1)}, bf16[8,320,128]{2,1,0:T(8,128)(2,1)}) custom-call(s32[4]{0:T(128)S(1)} %pad_add_fusion.flag_ref, bf16[200,1024]{1,0:T(8,128)(2,1)S(1)} %copy-done.5, bf16[200,1024]{1,0:T(8,128)(2,1)S(1)} %collective-permute-done.oth_ref, f32[4,2048]{1,0:T(4,128)S(1)} %slice.198.mod_ref, ...), custom_call_target="tpu_custom_call" | custom-call | flops 1258291200 | bytes 12582912 | tf_op jit(solution)/shard_map/tokens_to_qkv/pallas_call | solution.py:161
  33.4 22.0 %all_to_all.60.own_ref = bf16[8,320,128]{2,1,0:T(8,128)(2,1)S(1)} all-to-all(bf16[8,320,128]{2,1,0:T(8,128)(2,1)S(1)} %get-tuple-element.65), channel_id=1, replica_groups=mesh['blk'=8,'uly'=4] {'blk'}, dimensions={0} | all-to-all | bytes 1310720 | tf_op jit(solution)/shard_map/all_to_all | solution.py:783
  58.4 21.2 %attend_long.1 = (bf16[8,112,128]{2,1,0:T(8,128)(2,1)}, f32[8,64,200]{2,1,0:T(8,128)S(1)}, f32[8,8,200]{2,1,0:T(8,128)S(1)}) custom-call(s32[4]{0:T(128)S(1)} %pad_add_fusion.flag_ref, bf16[8,320,128]{2,1,0:T(8,128)(2,1)S(1)} %all_to_all.60.own_ref, bf16[8,320,128]{2,1,0:T(8,128)(2,1)S(1)} %collective-permute-done.2.oth_ref), custom_call_target="tpu_custom_call" | custom-call | flops 2949120000 | bytes 4194304 | tf_op jit(solution)/shard_map/attend_long/pallas_call | solution.py:281
  81.0 4.4 all-to-all-start.1
  92.0 8.3 %attend_short.1 = (bf16[8,112,128]{2,1,0:T(8,128)(2,1)S(1)}, f32[8,64,200]{2,1,0:T(8,128)S(1)}, f32[8,8,200]{2,1,0:T(8,128)S(1)}) custom-call(s32[4]{0:T(128)S(1)} %copy-done.36, bf16[8,320,128]{2,1,0:T(8,128)(2,1)} %get-tuple-element.67.own_ref, bf16[8,320,128]{2,1,0:T(8,128)(2,1)} %collective-permute-done.3.oth_ref), custom_call_target="tpu_custom_call" | custom-call | flops 655360000 | bytes 4194304 | tf_op jit(solution)/shard_map/attend_short/pallas_call | solution.py:281
  125.3 11.4 %mlp_own.1 = (bf16[200,1024]{1,0:T(8,128)(2,1)S(1)}, bf16[200,1024]{1,0:T(8,128)(2,1)}, bf16[200,1024]{1,0:T(8,128)(2,1)S(1)}, bf16[200,1024]{1,0:T(8,128)(2,1)S...) custom-call(s32[4]{0:T(128)S(1)} %copy-done.37, ...), custom_call_target="tpu_custom_call" | custom-call | flops 3355443200 | bytes 12582912 | tf_op jit(solution)/shard_map/mlp_own/pallas_call | solution.py:499
  144.6 11.3 %mlp_other.1 = (bf16[200,1024]{1,0:T(8,128)(2,1)S(1)}, bf16[200,1024]{1,0:T(8,128)(2,1)S(1)}, bf16[200,1024]{1,0:T(8,128)(2,1)S(1)}, bf16[200,1024]{1,0:T(8,128)...) custom-call(s32[4]{0:T(128)S(1)} %copy-done.37, ...), custom_call_target="tpu_custom_call" | custom-call | flops 3355443200 | bytes 12582912 | tf_op jit(solution)/shard_map/mlp_other/pallas_call | solution.py:499
  159.2 17.2 %collective-permute-done.8.b_ref = bf16[200,1024]{1,0:T(8,128)(2,1)S(1)} collective-permute-done((bf16[200,1024]{1,0:T(8,128)(2,1)S(1)}, bf16[200,1024]{1,0:T(8,128)(2,1)S(1)}, u32[]{:S(2)}, u32[]{:S(2)}) %collective-permute-start.8) | collective-permute-done | bytes 409632 | tf_op jit(solution)/shard_map/ppermute | solution.py:777
  186.4 6.0 %all-to-all-start.4 = ((bf16[8,16,1024]{2,1,0:T(8,128)(2,1)}), bf16[8,16,1024]{2,1,0:T(8,128)(2,1)S(1)}, u32[]{:S(2)}, u32[]{:S(2)}) async-start(bf16[8,16,1024]{2,1,0:T(8,128)(2,1)} %broadcast_in_dim.153), calls=%async_computation.4 | async-start | bytes 524288 | tf_op jit(solution)/shard_map/all_to_all | solution.py:786
  195.6 5.5 %all-to-all-done.4 = bf16[8,16,1024]{2,1,0:T(8,128)(2,1)S(1)} async-done(((bf16[8,16,1024]{2,1,0:T(8,128)(2,1)}), bf16[8,16,1024]{2,1,0:T(8,128)(2,1)S(1)}, u32[]{:S(2)}, u32[]{:S(2)}) %all-to-all-start.4) | async-done | bytes 262176 | tf_op jit(solution)/shard_map/all_to_all | solution.py:786
  201.2 4.2 all-to-all-start.2
  206.4 6.6 %down_grads.1 = bf16[8,128,1024]{2,1,0:T(8,128)(2,1)S(1)} custom-call(bf16[200,1024]{1,0:T(8,128)(2,1)S(1)} %copy-done.53, bf16[200,1024]{1,0:T(8,128)(2,1)S(1)} %copy-done.55, bf16[200,1024]{1,0:T(8,128)(2,1)} %collective-permute-done.23.refs_2_, bf16[200,1024]{1,0:T(8,128)(2,1)} %collective-permute-done.24.refs_3_, ...), custom_call_target="tpu_custom_call" | custom-call | flops 1677721600 | bytes 6291456 | tf_op jit(solution)/shard_map/down_grads/pallas_call | solution.py:686
  213.0 6.3 %up_grads.1 = bf16[8,128,1024]{2,1,0:T(8,128)(2,1)S(1)} custom-call(bf16[200,1024]{1,0:T(8,128)(2,1)} %get-tuple-element.70.hid_ref.refs_0_, bf16[200,1024]{1,0:T(8,128)(2,1)S(1)} %copy-done.28, bf16[200,1024]{1,0:T(8,128)(2,1)} %collective-permute-done.19.refs_2_, bf16[200,1024]{1,0:T(8,128)(2,1)} %collective-permute-done.20.refs_3_, ...), custom_call_target="tpu_custom_call" | custom-call | flops 1677721600 | bytes 6291456 | tf_op jit(solution)/shard_map/up_grads/pallas_call | solution.py:686
  223.9 4.3 all-to-all-start.5
  230.3 21.2 %attend_back_long.1 = (bf16[8,200,128]{2,1,0:T(8,128)(2,1)S(1)}, f32[8,200,128]{2,1,0:T(8,128)S(1)}, bf16[8,200,128]{2,1,0:T(8,128)(2,1)}) custom-call(s32[4]{0:T(128)S(1)} %copy-done.38, bf16[8,320,128]{2,1,0:T(8,128)(2,1)S(1)} %copy-done.26, bf16[8,320,128]{2,1,0:T(8,128)(2,1)S(1)} %copy-done.45, bf16[8,112,128]{2,1,0:T(8,128)(2,1)S(1)} %all-to-all-done.2.do_ref, ...), custom_call_target="tpu_custom_call" | custom-call | flops 7372800000 | bytes 6291456 | tf_op jit(solution)/shard_map/attend_back_long/pallas_call | solution.py:364
  255.7 6.1 %all-to-all-start.3 = ((bf16[8,320,128]{2,1,0:T(8,128)(2,1)}), bf16[8,320,128]{2,1,0:T(8,128)(2,1)S(1)}, u32[]{:S(2)}, u32[]{:S(2)}) async-start(bf16[8,320,128]{2,1,0:T(8,128)(2,1)} %finish_keys.2), calls=%async_computation.3 | async-start | bytes 1310720 | tf_op jit(solution)/shard_map/all_to_all | solution.py:783
  269.3 10.4 %all-to-all-done.3.g_ref = bf16[8,320,128]{2,1,0:T(8,128)(2,1)S(1)} async-done(((bf16[8,320,128]{2,1,0:T(8,128)(2,1)}), bf16[8,320,128]{2,1,0:T(8,128)(2,1)S(1)}, u32[]{:S(2)}, u32[]{:S(2)}) %all-to-all-start.3) | async-done | bytes 655392 | tf_op jit(solution)/shard_map/all_to_all | solution.py:783
  279.8 4.6 %all-to-all-start.10 = ((bf16[8,32,1024]{2,1,0:T(8,128)(2,1)}), bf16[8,32,1024]{2,1,0:T(8,128)(2,1)}, u32[]{:S(2)}, u32[]{:S(2)}) async-start(bf16[8,32,1024]{2,1,0:T(8,128)(2,1)} %bitcast.21), calls=%async_computation.10 | async-start | bytes 1048576 | tf_op jit(solution)/shard_map/all_to_all | solution.py:783
  285.4 9.4 %attend_back_short.1 = (bf16[8,200,128]{2,1,0:T(8,128)(2,1)S(1)}, f32[8,200,128]{2,1,0:T(8,128)S(1)}, bf16[8,200,128]{2,1,0:T(8,128)(2,1)}) custom-call(s32[4]{0:T(128)S(1)} %copy-done.38, bf16[8,320,128]{2,1,0:T(8,128)(2,1)} %get-tuple-element.67.own_ref, bf16[8,320,128]{2,1,0:T(8,128)(2,1)} %collective-permute-done.3.oth_ref, ...), custom_call_target="tpu_custom_call" | custom-call | flops 1638400000 | bytes 6291456 | tf_op jit(solution)/shard_map/attend_back_short/pallas_call | solution.py:364
  303.9 4.0 qkv_back_short.1
  309.5 3.4 qkv_back_long.1
  316.2 6.0 %all-to-all-start.6 = ((bf16[8,16,1024]{2,1,0:T(8,128)(2,1)}), bf16[8,16,1024]{2,1,0:T(8,128)(2,1)}, u32[]{:S(2)}, u32[]{:S(2)}) async-start(bf16[8,16,1024]{2,1,0:T(8,128)(2,1)} %broadcast_in_dim.157), calls=%async_computation.6 | async-start | bytes 524288 | tf_op jit(solution)/shard_map/all_to_all | solution.py:786
  324.9 6.0 %all-to-all-done.6 = bf16[8,16,1024]{2,1,0:T(8,128)(2,1)} async-done(((bf16[8,16,1024]{2,1,0:T(8,128)(2,1)}), bf16[8,16,1024]{2,1,0:T(8,128)(2,1)}, u32[]{:S(2)}, u32[]{:S(2)}) %all-to-all-start.6) | async-done | bytes 262176 | tf_op jit(solution)/shard_map/all_to_all | solution.py:786
  332.9 4.3 all-to-all-start.7
  349.6 3.5 collective-permute-done.18
  353.1 6.3 %attn_grads.1 = bf16[8,128,768]{2,1,0:T(8,128)(2,1)} custom-call(bf16[200,1024]{1,0:T(8,128)(2,1)S(1)} %get-tuple-element.131.refs_0_, bf16[200,1024]{1,0:T(8,128)(2,1)S(1)} %get-tuple-element.130.refs_1_, bf16[200,1024]{1,0:T(8,128)(2,1)S(1)} %get-tuple-element.129.refs_2_, bf16[200,1024]{1,0:T(8,128)(2,1)S(1)} %get-tuple-element.128.refs_3_, ...), custom_call_target="tpu_custom_call" | custom-call | flops 1258291200 | bytes 6291456 | tf_op jit(solution)/shard_map/attn_grads/pallas_call | solution.py:686
  363.3 12.4 %all-to-all-start.8 = ((bf16[8,128,768]{2,1,0:T(8,128)(2,1)}), bf16[8,128,768]{2,1,0:T(8,128)(2,1)}, u32[]{:S(2)}, u32[]{:S(2)}) async-start(bf16[8,128,768]{2,1,0:T(8,128)(2,1)} %attn_grads.1), calls=%async_computation.8 | async-start | bytes 3145728 | tf_op jit(solution)/shard_map/all_to_all | solution.py:783
  381.2 3.6 fusion.22
  384.8 25.8 %all-to-all-done.8 = bf16[8,128,768]{2,1,0:T(8,128)(2,1)} async-done(((bf16[8,128,768]{2,1,0:T(8,128)(2,1)}), bf16[8,128,768]{2,1,0:T(8,128)(2,1)}, u32[]{:S(2)}, u32[]{:S(2)}) %all-to-all-start.8) | async-done | bytes 1572896 | tf_op jit(solution)/shard_map/all_to_all | solution.py:783
  413.0 3.7 all-to-all-start.9
  (373 shorter events, 149.6 us)
Async XLA Ops:
  7.2 17.9 %collective-permute-start = (bf16[200,1024]{1,0:T(8,128)(2,1)}, bf16[200,1024]{1,0:T(8,128)(2,1)S(1)}, u32[]{:S(2)}, u32[]{:S(2)}) collective-permute-start(bf16[200,1024]{1,0:T(8,128)(2,1)} %tok_ref.3), channel_id=1, source_target_pairs={{0,2},{1,3},{2,0},{3,1},{4,6},{5,7},{6,4},{7,5},{8,10},{9,11},{10,... | collective-permute-start | bytes 1228808 | tf_op jit(solution)/shard_map/ppermute | solution.py:777
  55.4 35.9 %collective-permute-start.3 = (bf16[8,320,128]{2,1,0:T(8,128)(2,1)}, bf16[8,320,128]{2,1,0:T(8,128)(2,1)}, u32[]{:S(2)}, u32[]{:S(2)}) collective-permute-start(bf16[8,320,128]{2,1,0:T(8,128)(2,1)} %get-tuple-element.67.own_ref), channel_id=1, source_target_pairs={{0,1},{1,0},{2,3},{3,2},{4,5},{5,4},{6,7},{7,6},{8,9},{9,8},{10,11... | collective-permute-start | bytes 1966088 | tf_op jit(solution)/shard_map/ppermute | solution.py:780
  81.0 21.4 %all-to-all-start.1 = ((bf16[8,112,128]{2,1,0:T(8,128)(2,1)}), bf16[8,112,128]{2,1,0:T(8,128)(2,1)S(1)}, u32[]{:S(2)}, u32[]{:S(2)}) async-start(bf16[8,112,128]{2,1,0:T(8,128)(2,1)} %get-tuple-element.66), calls=%async_computation.1 | async-start | bytes 458752 | tf_op jit(solution)/shard_map/all_to_all | solution.py:783
  89.8 28.5 %collective-permute-start.6 = (bf16[200,1024]{1,0:T(8,128)(2,1)}, bf16[200,1024]{1,0:T(8,128)(2,1)}, u32[]{:S(2)}, u32[]{:S(2)}) collective-permute-start(bf16[200,1024]{1,0:T(8,128)(2,1)} %get-tuple-element.119.mg_ref.refs_4_), channel_id=1, source_target_pairs={{0,2},{1,3},{2,0},{3,1},{4,6},{5,7},{6,4},{7,5},{8,10},{9,11},{10,... | collective-permute-start | bytes 1228808 | tf_op jit(solution)/shard_map/ppermute | solution.py:777
  111.2 81.2 %collective-permute-start.25 = (bf16[200,1024]{1,0:T(8,128)(2,1)}, bf16[200,1024]{1,0:T(8,128)(2,1)}, u32[]{:S(2)}, u32[]{:S(2)}) collective-permute-start(bf16[200,1024]{1,0:T(8,128)(2,1)} %get-tuple-element.119.mg_ref.refs_4_), channel_id=1, source_target_pairs={{0,1},{1,0},{2,3},{3,2},{4,5},{5,4},{6,7},{7,6},{8,9},{9,8},{10,11... | collective-permute-start | bytes 1228808 | tf_op jit(solution)/shard_map/ppermute | solution.py:780
  117.1 20.7 %collective-permute-start.5 = (bf16[200,1024]{1,0:T(8,128)(2,1)}, bf16[200,1024]{1,0:T(8,128)(2,1)S(1)}, u32[]{:S(2)}, u32[]{:S(2)}) collective-permute-start(bf16[200,1024]{1,0:T(8,128)(2,1)} %get-tuple-element.70.hid_ref.refs_0_), channel_id=1, source_target_pairs={{0,2},{1,3},{2,0},{3,1},{4,6},{5,7},{6,4},{7,5},{8,10},{9,11},{10,... | collective-permute-start | bytes 1228808 | tf_op jit(solution)/shard_map/ppermute | solution.py:777
  118.4 74.2 %collective-permute-start.26 = (bf16[200,1024]{1,0:T(8,128)(2,1)}, bf16[200,1024]{1,0:T(8,128)(2,1)}, u32[]{:S(2)}, u32[]{:S(2)}) collective-permute-start(bf16[200,1024]{1,0:T(8,128)(2,1)} %collective-permute-done.6.mg_ref.refs_5_), channel_id=1, source_target_pairs={{0,1},{1,0},{2,3},{3,2},{4,5},{5,4},{6,7},{7,6},{8,9},{9,8},{10,11... | collective-permute-start | bytes 1228808 | tf_op jit(solution)/shard_map/ppermute | solution.py:780
  137.5 55.6 %collective-permute-start.23 = (bf16[200,1024]{1,0:T(8,128)(2,1)}, bf16[200,1024]{1,0:T(8,128)(2,1)}, u32[]{:S(2)}, u32[]{:S(2)}) collective-permute-start(bf16[200,1024]{1,0:T(8,128)(2,1)} %get-tuple-element.116), channel_id=1, source_target_pairs={{0,1},{1,0},{2,3},{3,2},{4,5},{5,4},{6,7},{7,6},{8,9},{9,8},{10,11... | collective-permute-start | bytes 1228808 | tf_op jit(solution)/shard_map/ppermute | solution.py:780
  155.9 23.2 %collective-permute-start.7 = (bf16[200,1024]{1,0:T(8,128)(2,1)S(1)}, bf16[200,1024]{1,0:T(8,128)(2,1)S(1)}, u32[]{:S(2)}, u32[]{:S(2)}) collective-permute-start(bf16[200,1024]{1,0:T(8,128)(2,1)S(1)} %get-tuple-element.72), channel_id=1, source_target_pairs={{0,2},{1,3},{2,0},{3,1},{4,6},{5,7},{6,4},{7,5},{8,10},{9,11},{10,... | collective-permute-start | bytes 1228808 | tf_op jit(solution)/shard_map/ppermute | solution.py:777
  157.4 19.0 %collective-permute-start.8 = (bf16[200,1024]{1,0:T(8,128)(2,1)S(1)}, bf16[200,1024]{1,0:T(8,128)(2,1)S(1)}, u32[]{:S(2)}, u32[]{:S(2)}) collective-permute-start(bf16[200,1024]{1,0:T(8,128)(2,1)S(1)} %get-tuple-element.74), channel_id=1, source_target_pairs={{0,2},{1,3},{2,0},{3,1},{4,6},{5,7},{6,4},{7,5},{8,10},{9,11},{10,... | collective-permute-start | bytes 1228808 | tf_op jit(solution)/shard_map/ppermute | solution.py:777
  176.4 36.6 %collective-permute-start.19 = (bf16[200,1024]{1,0:T(8,128)(2,1)}, bf16[200,1024]{1,0:T(8,128)(2,1)}, u32[]{:S(2)}, u32[]{:S(2)}) collective-permute-start(bf16[200,1024]{1,0:T(8,128)(2,1)} %get-tuple-element.70.hid_ref.refs_0_), channel_id=1, source_target_pairs={{0,1},{1,0},{2,3},{3,2},{4,5},{5,4},{6,7},{7,6},{8,9},{9,8},{10,11... | collective-permute-start | bytes 1228808 | tf_op jit(solution)/shard_map/ppermute | solution.py:780
  179.0 14.1 %collective-permute-start.9 = (bf16[8,112,128]{2,1,0:T(8,128)(2,1)}, bf16[8,112,128]{2,1,0:T(8,128)(2,1)}, u32[]{:S(2)}, u32[]{:S(2)}) collective-permute-start(bf16[8,112,128]{2,1,0:T(8,128)(2,1)} %get-tuple-element.79), channel_id=1, source_target_pairs={{0,2},{1,3},{2,0},{3,1},{4,6},{5,7},{6,4},{7,5},{8,10},{9,11},{10,... | collective-permute-start | bytes 688136 | tf_op jit(solution)/shard_map/ppermute | solution.py:777
  186.4 14.7 %all-to-all-start.4 = ((bf16[8,16,1024]{2,1,0:T(8,128)(2,1)}), bf16[8,16,1024]{2,1,0:T(8,128)(2,1)S(1)}, u32[]{:S(2)}, u32[]{:S(2)}) async-start(bf16[8,16,1024]{2,1,0:T(8,128)(2,1)} %broadcast_in_dim.153), calls=%async_computation.4 | async-start | bytes 524288 | tf_op jit(solution)/shard_map/all_to_all | solution.py:786
  192.5 20.5 %collective-permute-start.21 = (bf16[200,1024]{1,0:T(8,128)(2,1)S(1)}, bf16[200,1024]{1,0:T(8,128)(2,1)}, u32[]{:S(2)}, u32[]{:S(2)}) collective-permute-start(bf16[200,1024]{1,0:T(8,128)(2,1)S(1)} %copy-done.49), channel_id=1, source_target_pairs={{0,1},{1,0},{2,3},{3,2},{4,5},{5,4},{6,7},{7,6},{8,9},{9,8},{10,11... | collective-permute-start | bytes 1228808 | tf_op jit(solution)/shard_map/ppermute | solution.py:780
  192.6 12.8 %collective-permute-start.24 = (bf16[200,1024]{1,0:T(8,128)(2,1)S(1)}, bf16[200,1024]{1,0:T(8,128)(2,1)}, u32[]{:S(2)}, u32[]{:S(2)}) collective-permute-start(bf16[200,1024]{1,0:T(8,128)(2,1)S(1)} %copy-done.57), channel_id=1, source_target_pairs={{0,1},{1,0},{2,3},{3,2},{4,5},{5,4},{6,7},{7,6},{8,9},{9,8},{10,11... | collective-permute-start | bytes 1228808 | tf_op jit(solution)/shard_map/ppermute | solution.py:780
  193.0 20.0 %collective-permute-start.22 = (bf16[200,1024]{1,0:T(8,128)(2,1)}, bf16[200,1024]{1,0:T(8,128)(2,1)}, u32[]{:S(2)}, u32[]{:S(2)}) collective-permute-start(bf16[200,1024]{1,0:T(8,128)(2,1)} %get-tuple-element.113), channel_id=1, source_target_pairs={{0,1},{1,0},{2,3},{3,2},{4,5},{5,4},{6,7},{7,6},{8,9},{9,8},{10,11... | collective-permute-start | bytes 1228808 | tf_op jit(solution)/shard_map/ppermute | solution.py:780
  193.1 19.9 %collective-permute-start.20 = (bf16[200,1024]{1,0:T(8,128)(2,1)S(1)}, bf16[200,1024]{1,0:T(8,128)(2,1)}, u32[]{:S(2)}, u32[]{:S(2)}) collective-permute-start(bf16[200,1024]{1,0:T(8,128)(2,1)S(1)} %copy-done.28), channel_id=1, source_target_pairs={{0,1},{1,0},{2,3},{3,2},{4,5},{5,4},{6,7},{7,6},{8,9},{9,8},{10,11... | collective-permute-start | bytes 1228808 | tf_op jit(solution)/shard_map/ppermute | solution.py:780
  201.2 20.7 %all-to-all-start.2 = ((bf16[8,112,128]{2,1,0:T(8,128)(2,1)}), bf16[8,112,128]{2,1,0:T(8,128)(2,1)S(1)}, u32[]{:S(2)}, u32[]{:S(2)}) async-start(bf16[8,112,128]{2,1,0:T(8,128)(2,1)} %get-tuple-element.137), calls=%async_computation.2 | async-start | bytes 458752 | tf_op jit(solution)/shard_map/all_to_all | solution.py:783
  205.3 215.8 %reduce-scatter.2.cloned.1.call-start = ((), (), s32[]{:S(2)}) async-start(), calls=%async_computation.13 | async-start | bytes 4718592 | tf_op jit(solution)/shard_map/reduce_scatter | solution.py:894
  223.9 31.8 %all-to-all-start.5 = ((bf16[4,8,16,1024]{3,2,1,0:T(8,128)(2,1)}), bf16[4,8,16,1024]{3,2,1,0:T(8,128)(2,1)}, u32[]{:S(2)}, u32[]{:S(2)}) async-start(bf16[4,8,16,1024]{3,2,1,0:T(8,128)(2,1)} %broadcast_in_dim.154), calls=%async_computation.5 | async-start | bytes 2097152 | tf_op jit(solution)/shard_map/all_to_all | solution.py:787
  252.0 12.0 %collective-permute-start.16 = (bf16[200,1024]{1,0:T(8,128)(2,1)}, bf16[200,1024]{1,0:T(8,128)(2,1)S(1)}, u32[]{:S(2)}, u32[]{:S(2)}) collective-permute-start(bf16[200,1024]{1,0:T(8,128)(2,1)} %get-tuple-element.109), channel_id=1, source_target_pairs={{0,2},{1,3},{2,0},{3,1},{4,6},{5,7},{6,4},{7,5},{8,10},{9,11},{10,... | collective-permute-start | bytes 1228808 | tf_op jit(solution)/shard_map/ppermute | solution.py:777
  255.7 24.1 %all-to-all-start.3 = ((bf16[8,320,128]{2,1,0:T(8,128)(2,1)}), bf16[8,320,128]{2,1,0:T(8,128)(2,1)S(1)}, u32[]{:S(2)}, u32[]{:S(2)}) async-start(bf16[8,320,128]{2,1,0:T(8,128)(2,1)} %finish_keys.2), calls=%async_computation.3 | async-start | bytes 1310720 | tf_op jit(solution)/shard_map/all_to_all | solution.py:783
  279.8 35.7 %all-to-all-start.10 = ((bf16[8,32,1024]{2,1,0:T(8,128)(2,1)}), bf16[8,32,1024]{2,1,0:T(8,128)(2,1)}, u32[]{:S(2)}, u32[]{:S(2)}) async-start(bf16[8,32,1024]{2,1,0:T(8,128)(2,1)} %bitcast.21), calls=%async_computation.10 | async-start | bytes 1048576 | tf_op jit(solution)/shard_map/all_to_all | solution.py:783
  295.7 26.5 %collective-permute-start.13 = (bf16[2,200,1024]{2,1,0:T(8,128)(2,1)S(1)}, bf16[2,200,1024]{2,1,0:T(8,128)(2,1)}, u32[]{:S(2)}, u32[]{:S(2)}) collective-permute-start(bf16[2,200,1024]{2,1,0:T(8,128)(2,1)S(1)} %copy-done.16), channel_id=1, source_target_pairs={{0,1},{1,0},{2,3},{3,2},{4,5},{5,4},{6,7},{7,6},{8,9},{9,8},{10,11... | collective-permute-start | bytes 2457608 | tf_op jit(solution)/shard_map/ppermute | solution.py:780
  316.2 14.7 %all-to-all-start.6 = ((bf16[8,16,1024]{2,1,0:T(8,128)(2,1)}), bf16[8,16,1024]{2,1,0:T(8,128)(2,1)}, u32[]{:S(2)}, u32[]{:S(2)}) async-start(bf16[8,16,1024]{2,1,0:T(8,128)(2,1)} %broadcast_in_dim.157), calls=%async_computation.6 | async-start | bytes 524288 | tf_op jit(solution)/shard_map/all_to_all | solution.py:786
  323.4 29.6 %collective-permute-start.15 = (bf16[200,768]{1,0:T(8,128)(2,1)}, bf16[200,768]{1,0:T(8,128)(2,1)}, u32[]{:S(2)}, u32[]{:S(2)}) collective-permute-start(bf16[200,768]{1,0:T(8,128)(2,1)} %get-tuple-element.108), channel_id=1, source_target_pairs={{0,1},{1,0},{2,3},{3,2},{4,5},{5,4},{6,7},{7,6},{8,9},{9,8},{10,11... | collective-permute-start | bytes 921608 | tf_op jit(solution)/shard_map/ppermute | solution.py:780
  332.9 30.4 %all-to-all-start.7 = ((bf16[4,8,16,1024]{3,2,1,0:T(8,128)(2,1)}), bf16[4,8,16,1024]{3,2,1,0:T(8,128)(2,1)}, u32[]{:S(2)}, u32[]{:S(2)}) async-start(bf16[4,8,16,1024]{3,2,1,0:T(8,128)(2,1)} %broadcast_in_dim.158), calls=%async_computation.7 | async-start | bytes 2097152 | tf_op jit(solution)/shard_map/all_to_all | solution.py:787
  338.0 23.2 %collective-permute-start.12 = (bf16[200,1024]{1,0:T(8,128)(2,1)}, bf16[200,1024]{1,0:T(8,128)(2,1)S(1)}, u32[]{:S(2)}, u32[]{:S(2)}) collective-permute-start(bf16[200,1024]{1,0:T(8,128)(2,1)} %broadcast_select_fusion.3), channel_id=1, source_target_pairs={{0,2},{1,3},{2,0},{3,1},{4,6},{5,7},{6,4},{7,5},{8,10},{9,11},{10,... | collective-permute-start | bytes 1228808 | tf_op jit(solution)/shard_map/ppermute | solution.py:777
  340.0 13.1 %collective-permute-start.14 = (bf16[200,768]{1,0:T(8,128)(2,1)}, bf16[200,768]{1,0:T(8,128)(2,1)}, u32[]{:S(2)}, u32[]{:S(2)}) collective-permute-start(bf16[200,768]{1,0:T(8,128)(2,1)} %copy-done.62), channel_id=1, source_target_pairs={{0,1},{1,0},{2,3},{3,2},{4,5},{5,4},{6,7},{7,6},{8,9},{9,8},{10,11... | collective-permute-start | bytes 921608 | tf_op jit(solution)/shard_map/ppermute | solution.py:780
  341.8 11.2 %collective-permute-start.18 = (f32[32,1024]{1,0:T(8,128)}, f32[32,1024]{1,0:T(8,128)}, u32[]{:S(2)}, u32[]{:S(2)}) collective-permute-start(f32[32,1024]{1,0:T(8,128)} %convert_reduce_fusion.1), channel_id=1, source_target_pairs={{0,0},{1,8},{2,16},{3,24},{4,1},{5,9},{6,17},{7,25},{8,2},{9,10},{... | collective-permute-start | bytes 393224 | tf_op jit(solution)/shard_map/ppermute | solution.py:930
  363.3 47.3 %all-to-all-start.8 = ((bf16[8,128,768]{2,1,0:T(8,128)(2,1)}), bf16[8,128,768]{2,1,0:T(8,128)(2,1)}, u32[]{:S(2)}, u32[]{:S(2)}) async-start(bf16[8,128,768]{2,1,0:T(8,128)(2,1)} %attn_grads.1), calls=%async_computation.8 | async-start | bytes 3145728 | tf_op jit(solution)/shard_map/all_to_all | solution.py:783
  413.0 10.9 %all-to-all-start.9 = ((f32[4,32,768]{2,1,0:T(8,128)}), f32[4,32,768]{2,1,0:T(8,128)S(1)}, u32[]{:S(2)}, u32[]{:S(2)}) async-start(f32[4,32,768]{2,1,0:T(8,128)} %bitcast.18), calls=%async_computation.9 | async-start | bytes 786432 | tf_op jit(solution)/shard_map/all_to_all | solution.py:902
  (105 other events, 782.0 us)
Sparse Core Ops, SparseCore 0:
  221.9 98.6 reduce-scatter.1

commit v2 on v1

v2 whole, which is shorter than its diff:
```python
import functools
import math

import jax
import jax.numpy as jnp
import numpy as np
from jax import lax
from jax.experimental import pallas as pl
from jax.experimental.pallas import tpu as pltpu
from jax.sharding import PartitionSpec as P

DH = 64
GRID = 10
FB = 8
PATCH = 100
HALF = 64
LANES = 128

GELU_C = 0.7978845608028654
GELU_K = 0.044715
NEG_BIG = -1e30
MIB = 1 << 20
UNROLL = 2
PACK = 24

BF = jnp.bfloat16
F32 = jnp.float32


def round_up(value, step):
    return -(-value // step) * step


def lane_low(shape):
    return lax.broadcasted_iota(jnp.int32, shape, len(shape) - 1) < HALF


def first_frame(shape):
    return lax.broadcasted_iota(jnp.int32, shape, 0) < PATCH


def swap_halves(value):
    return pltpu.roll(value, HALF, 1)


def swap_pairs(value):
    even = lax.broadcasted_iota(jnp.int32, value.shape, 1) % 2 == 0
    return jnp.where(even, pltpu.roll(value, LANES - 1, 1), pltpu.roll(value, 1, 1))


def per_frame(shape, first, second):
    return jnp.where(first_frame(shape), jnp.broadcast_to(first, shape), jnp.broadcast_to(second, shape))


def frame_sums(value):
    head = first_frame(value.shape)
    one = jnp.sum(jnp.where(head, value, 0.0), axis=0, keepdims=True)
    two = jnp.sum(jnp.where(head, 0.0, value), axis=0, keepdims=True)
    return one, two


def norm_rows(values):
    center = values - jnp.mean(values, axis=-1, keepdims=True)
    inv_std = lax.rsqrt(jnp.mean(center * center, axis=-1, keepdims=True) + 1e-06)
    return center * inv_std, inv_std


def norm_back(grad, normed, inv_std):
    return inv_std * (
        grad
        - jnp.mean(grad, axis=-1, keepdims=True)
        - normed * jnp.mean(grad * normed, axis=-1, keepdims=True)
    )


def dot(left, right):
    return jnp.dot(left, right, preferred_element_type=F32)


def dot_lanes(left, right):
    return lax.dot_general(left, right, (((1,), (1,)), ((), ())), preferred_element_type=F32)


def dot_rows(left, right):
    return lax.dot_general(left, right, (((0,), (0,)), ((), ())), preferred_element_type=F32)


def split_pair(value, rows_top):
    rows = value.shape[0]
    top = value[:rows_top]
    bottom = jnp.concatenate(
        [value[rows_top:], jnp.zeros((2 * rows_top - rows, LANES), value.dtype)], axis=0
    )
    low = lane_low(top.shape)
    return jnp.where(low, top, swap_halves(bottom)), jnp.where(low, swap_halves(top), bottom)


def join_pair(one, two, rows):
    rows_top = one.shape[0]
    low = lane_low(one.shape)
    top = jnp.where(low, one, swap_halves(two))
    bottom = jnp.where(low, swap_halves(one), two)
    return jnp.concatenate([top, bottom[: rows - rows_top]], axis=0)


def smem():
    return pl.BlockSpec(memory_space=pltpu.SMEM)


def whole(shape):
    return pl.BlockSpec(shape, lambda *_: (0,) * len(shape))


def kernel_call(body, flags, args, outs, *, specs=None, out_specs=None, grid=(1,), scratch=(), vmem=16, pins=(), out_pins=(), aliases=None, flops, name):
    specs = specs or [None] * len(args)
    out_specs = out_specs or [None] * len(outs)
    return pl.pallas_call(
        body,
        grid_spec=pltpu.PrefetchScalarGridSpec(
            num_scalar_prefetch=1,
            grid=grid,
            in_specs=[spec or whole(a.shape) for spec, a in zip(specs, args)],
            out_specs=[spec or whole(o.shape) for spec, o in zip(out_specs, outs)],
            scratch_shapes=list(scratch),
        ),
        out_shape=[pltpu.HBM(o.shape, o.dtype) if k in out_pins else o for k, o in enumerate(outs)],
        input_output_aliases=aliases or {},
        compiler_params=pltpu.CompilerParams(vmem_limit_bytes=vmem * MIB),
        cost_estimate=pl.CostEstimate(flops=flops // 4096, bytes_accessed=4096, transcendentals=0),
        name=name,
    )(flags, *[pltpu.with_memory_space_constraint(a, pltpu.HBM) if a.size >= MIB or k in pins else a for k, a in enumerate(args)])


def shape_of(dims, dtype):
    return jax.ShapeDtypeStruct(dims, dtype)


def tokens_to_qkv(flags, tok_own, tok_oth, mods, weight, bias, tab_cos, tab_sin, time_cos, time_sin, lay):
    rows, width = tok_own.shape
    cols = lay.heads * DH

    def body(flag_ref, own_ref, oth_ref, mod_ref, w_ref, b_ref, tc_ref, ts_ref, qc_ref, qs_ref, hid_ref, long_ref, short_ref):
        step = pl.program_id(0)
        own_long = flag_ref[0]

        @pl.when(step == 0)
        def _():
            for src, base, slot in ((own_ref, 0, 1 - own_long), (oth_ref, 2, own_long)):
                normed, _ = norm_rows(src[...].astype(F32))
                shift = per_frame(normed.shape, mod_ref[base : base + 1, :width], mod_ref[base + 1 : base + 2, :width])
                scale = per_frame(
                    normed.shape, mod_ref[base : base + 1, width : 2 * width], mod_ref[base + 1 : base + 2, width : 2 * width]
                )
                hid_ref[slot] = (normed * (1.0 + scale) + shift).astype(BF)

        for slot, out_ref in ((0, long_ref), (1, short_ref)):
            acc = dot(hid_ref[slot], w_ref[...]) + b_ref[...]

            def rotated(pair):
                value = acc[:, pair * LANES : (pair + 1) * LANES]
                cosine = tc_ref[...] + per_frame(value.shape, qc_ref[2 * slot : 2 * slot + 1], qc_ref[2 * slot + 1 : 2 * slot + 2])
                sine = ts_ref[...] + per_frame(value.shape, qs_ref[2 * slot : 2 * slot + 1], qs_ref[2 * slot + 1 : 2 * slot + 2])
                return value * cosine + swap_pairs(value) * sine

            @pl.when(step == 0)
            def _():
                for pair in range(cols // LANES):
                    turned = rotated(pair)
                    out_ref[2 * pair, :rows, :HALF] = turned[:, :HALF].astype(BF)
                    out_ref[2 * pair + 1, :rows, :HALF] = swap_halves(turned)[:, :HALF].astype(BF)

            @pl.when(step == 1)
            def _():
                for pair in range(cols // LANES):
                    turned = rotated(pair)
                    out_ref[2 * pair, :rows, HALF:] = swap_halves(turned)[:, HALF:].astype(BF)
                    out_ref[2 * pair + 1, :rows, HALF:] = turned[:, HALF:].astype(BF)

            @pl.when(step == 2)
            def _():
                for pair in range(cols // LANES):
                    one, two = split_pair(acc[:, pair * LANES : (pair + 1) * LANES], lay.top)
                    out_ref[2 * pair, lay.vrow :, :] = one.astype(BF)
                    out_ref[2 * pair + 1, lay.vrow :, :] = two.astype(BF)

    packed = (lay.heads, lay.vrow + lay.top, LANES)
    return kernel_call(
        body,
        flags,
        [tok_own, tok_oth, mods, weight, bias, tab_cos, tab_sin, time_cos, time_sin],
        [shape_of((2, rows, width), BF), shape_of(packed, BF), shape_of(packed, BF)],
        specs=[
            None, None, None,
            pl.BlockSpec((width, cols), lambda j, f: (0, 2 * j + f[1])),
            pl.BlockSpec((1, cols), lambda j, f: (0, 2 * j + f[1])),
            None, None, None, None,
        ],
        out_pins=(0,),
        grid=(3,),
        flops=12 * rows * width * cols,
        name="tokens_to_qkv",
    )


def unpack_values(ref, at, lay):
    part = ref[at, lay.vrow :, :].astype(F32)
    return jnp.concatenate([part, swap_halves(part)[: lay.rows - lay.top]], axis=0)


def hundreds(value):
    return (value * 1311) >> 17


def diag_mask(keys, queries, core):
    key = hundreds(lax.broadcasted_iota(jnp.int32, (keys, 1), 0)) ^ (2 * core)
    query = hundreds(lax.broadcasted_iota(jnp.int32, (1, queries), 1))
    query = ((query & 2) << 1) + (query & 1) + 2 * core
    return key <= query


def load_keys(own_ref, oth_ref, group, lay):
    low = lane_low((lay.rows, LANES))
    halves = [
        jnp.where(low, unpack_values(ref, group, lay), ref[group, : lay.rows, :].astype(F32))
        for ref in (own_ref, oth_ref)
    ]
    return jnp.concatenate(halves, axis=0)


def load_query(own_ref, at, lay):
    value = swap_halves(own_ref[at, : lay.rows, :].astype(F32)) * (1.0 / math.sqrt(DH))
    return jnp.where(lane_low(value.shape), 0.0, value)


def load_rows(load, groups):
    return jnp.concatenate([load(g) for g in groups], axis=0)


def fold_rows(value, op):
    return op(value.reshape(value.shape[0] // 8, 8, value.shape[1]), axis=0)


def unpack_rows(ref, at, lay):
    packed = ref[at].astype(F32)
    grad = jnp.concatenate([packed, swap_halves(packed)[: lay.rows - lay.top]], axis=0)
    return jnp.where(lane_low(grad.shape), grad, 0.0)


def attend(flags, own, oth, lay, long_clip):
    groups = own.shape[0]
    parts = lay.parts if long_clip else 1
    per = 2 if long_clip else 1
    count = groups // per
    keys, queries = 2 * lay.rows * per, lay.rows * per
    depth = count if long_clip else UNROLL

    def body(flag_ref, own_ref, oth_ref, o_ref, ot_ref, lse_ref, kv_ref, vt_ref, st_ref):
        core = flag_ref[2]
        part = flag_ref[3]

        def prepare(tile, slot):
            rows = jnp.concatenate([load_keys(own_ref, oth_ref, per * tile + k, lay) for k in range(per)], axis=0)
            kv_ref[slot] = rows.astype(BF)
            vt_ref[slot] = rows.T[:HALF].astype(BF)

        def block(at, slot):
            query = load_rows(lambda g: load_query(own_ref, g, lay), [per * at + k for k in range(per)]).astype(BF)

            def scores(kt, top):
                score = dot_lanes(kv_ref[kt], query)
                st_ref[kt] = score
                return jnp.maximum(top, fold_rows(score, jnp.max))

            top = jnp.full((8, queries), NEG_BIG, F32)
            if long_clip:
                top = lax.fori_loop(0, at, scores, top)
            score = dot_lanes(kv_ref[slot], query)
            score = jnp.where(diag_mask(keys, queries, core), score, NEG_BIG)
            st_ref[slot] = score
            top = jnp.max(jnp.maximum(top, fold_rows(score, jnp.max)), axis=0, keepdims=True)

            def mix(kt, carry):
                total, acc = carry
                expo = jnp.exp(st_ref[kt] - top)
                total = total + fold_rows(expo, jnp.sum)
                return total, acc + dot(vt_ref[kt], expo.astype(BF))

            zero = (jnp.zeros((8, queries), F32), jnp.zeros((HALF, queries), F32))
            if long_clip:
                total, acc = lax.fori_loop(0, at + 1, mix, zero)
            else:
                total, acc = mix(slot, zero)
            total = jnp.sum(total, axis=0, keepdims=True)
            acc = acc / total
            ot_ref[at] = acc
            lse_ref[at] = jnp.broadcast_to(top + jnp.log(total), (8, queries))
            out = jnp.concatenate([acc, jnp.zeros_like(acc)], axis=0).T
            for k in range(per):
                o_ref[per * at + k] = split_pair(out[k * lay.rows : (k + 1) * lay.rows], lay.top)[0].astype(BF)

        if long_clip:
            def prepare_loop(tile, _):
                prepare(tile, tile)
                return 0

            lax.fori_loop(0, count, prepare_loop, 0)
            if parts > 1:
                o_ref[...] = jnp.zeros_like(o_ref)

            def block_loop(step, _):
                at = step * parts + part if parts > 1 else step
                block(at, at)
                return 0

            lax.fori_loop(0, count // parts, block_loop, 0)
        else:
            def head_loop(step, _):
                for k in range(UNROLL):
                    prepare(UNROLL * step + k, k)
                for k in range(UNROLL):
                    block(UNROLL * step + k, k)
                return 0

            lax.fori_loop(0, count // UNROLL, head_loop, 0)

    pairs = count * (count + 1) // 2 if long_clip else count
    return kernel_call(
        body,
        flags,
        [own, oth],
        [
            shape_of((groups, lay.top, LANES), BF),
            shape_of((count, HALF, queries), F32),
            shape_of((count, 8, queries), F32),
        ],
        scratch=[
            pltpu.VMEM((depth, keys, LANES), BF),
            pltpu.VMEM((depth, HALF, keys), BF),
            pltpu.VMEM((depth, keys, queries), F32),
        ],
        out_pins=(1, 2),
        vmem=max(24, 3 * groups) if long_clip else 16,
        flops=pairs * 16 * keys * queries * DH // parts,
        name="attend_long" if long_clip else "attend_short",
    )


def attend_back(flags, own, oth, d_outs, ot, lse, tab_cos, tab_sin, time_cos, time_sin, lay, long_clip):
    groups = own.shape[0]
    parts = lay.parts if long_clip else 1
    per = 2 if long_clip else 1
    count = groups // per
    keys, queries = 2 * lay.rows * per, lay.rows * per
    depth = count if long_clip else UNROLL

    def body(flag_ref, own_ref, oth_ref, *refs):
        do_refs, refs = refs[: len(d_outs)], refs[len(d_outs) :]
        ot_ref, lse_ref, tc_ref, ts_ref, qc_ref, qs_ref, dq_ref, down_ref, doth_ref, kv_ref, kt_ref, acc_ref = refs
        own_long = flag_ref[0]
        core = flag_ref[2]
        part = flag_ref[3]

        def prepare(tile, slot):
            rows = jnp.concatenate([load_keys(own_ref, oth_ref, per * tile + k, lay) for k in range(per)], axis=0)
            kv_ref[slot] = rows.astype(BF)
            kt_ref[slot] = rows.T[HALF:].astype(BF)
            if long_clip:
                acc_ref[slot] = jnp.zeros((keys, LANES), F32)

        def block(at, slot):
            members = [per * at + k for k in range(per)]
            query = load_rows(lambda g: load_query(own_ref, g, lay), members).astype(BF)
            if long_clip:
                grad = load_rows(lambda g: unpack_rows(do_refs[0], g, lay), members)
            else:
                grad = load_rows(
                    lambda g: jnp.where(own_long == 1, unpack_rows(do_refs[1], g, lay), unpack_rows(do_refs[0], g, lay)), members
                )
            delta = jnp.sum(grad.T[:HALF] * ot_ref[at], axis=0, keepdims=True)
            grad = grad.astype(BF)
            lse_row = lse_ref[at][0:1]

            def tile_back(kt, acc, diag):
                tile = kv_ref[kt]
                prob = jnp.exp(dot_lanes(tile, query) - lse_row)
                if diag:
                    prob = jnp.where(diag_mask(keys, queries, core), prob, 0.0)
                score_grad = (prob * (dot_lanes(tile, grad) - delta)).astype(BF)
                both = dot(score_grad, query) + dot(prob.astype(BF), grad)
                if long_clip:
                    acc_ref[kt] += both
                else:
                    acc_ref[kt] = both
                return acc + dot(kt_ref[kt], score_grad)

            acc = tile_back(slot, jnp.zeros((HALF, queries), F32), True)
            if long_clip:
                acc = lax.fori_loop(0, at, lambda kt, a: tile_back(kt, a, False), acc)
            acc = acc * (1.0 / math.sqrt(DH))
            turned = jnp.concatenate([acc, jnp.zeros_like(acc)], axis=0).T
            for k, group in enumerate(members):
                dq = turned[k * lay.rows : (k + 1) * lay.rows]
                tab = group if long_clip else 0
                cosine = tc_ref[...] + per_frame(dq.shape, qc_ref[2 * tab], qc_ref[2 * tab + 1])
                sine = ts_ref[...] + per_frame(dq.shape, qs_ref[2 * tab], qs_ref[2 * tab + 1])
                dq_ref[group] = (dq * cosine - swap_pairs(dq) * sine).astype(BF)

        def flush(tile, slot):
            for k in range(per):
                down_ref[per * tile + k] = acc_ref[slot, 2 * k * lay.rows : (2 * k + 1) * lay.rows]
                doth_ref[per * tile + k] = acc_ref[slot, (2 * k + 1) * lay.rows : (2 * k + 2) * lay.rows].astype(BF)

        if long_clip:
            def prepare_loop(tile, _):
                prepare(tile, tile)
                return 0

            lax.fori_loop(0, count, prepare_loop, 0)
            if parts > 1:
                dq_ref[...] = jnp.zeros_like(dq_ref)

            def block_loop(step, _):
                at = step * parts + part if parts > 1 else step
                block(at, at)
                return 0

            lax.fori_loop(0, count // parts, block_loop, 0)

            def flush_loop(tile, _):
                flush(tile, tile)
                return 0

            lax.fori_loop(0, count, flush_loop, 0)
        else:
            def head_loop(step, _):
                for k in range(UNROLL):
                    prepare(UNROLL * step + k, k)
                for k in range(UNROLL):
                    block(UNROLL * step + k, k)
                for k in range(UNROLL):
                    flush(UNROLL * step + k, k)
                return 0

            lax.fori_loop(0, count // UNROLL, head_loop, 0)

    pairs = count * (count + 1) // 2 if long_clip else count
    return kernel_call(
        body,
        flags,
        [own, oth, *d_outs, ot, lse, tab_cos, tab_sin, time_cos, time_sin],
        [
            shape_of((groups, lay.rows, LANES), BF),
            shape_of((groups, lay.rows, LANES), F32),
            shape_of((groups, lay.rows, LANES), BF),
        ],
        scratch=[
            pltpu.VMEM((depth, keys, LANES), BF),
            pltpu.VMEM((depth, HALF, keys), BF),
            pltpu.VMEM((depth, keys, LANES), F32),
        ],
        out_pins=(0, 1),
        vmem=max(24, 3 * groups) if long_clip else 20,
        pins=(0, 1) + tuple(range(2 + len(d_outs), 8 + len(d_outs))),
        flops=pairs * 40 * keys * queries * DH // parts,
        name="attend_back_long" if long_clip else "attend_back_short",
    )


def finish_keys(flags, dq, mine, theirs, tab_cos, tab_sin, time_cos, time_sin, lay, long_clip):
    groups = dq.shape[0]

    def body(flag_ref, dq_ref, a_ref, b_ref, tc_ref, ts_ref, qc_ref, qs_ref, out_ref):
        def one(group, _):
            both = a_ref[group] + b_ref[group].astype(F32)
            tab = group if long_clip else 0
            cosine = tc_ref[...] + per_frame(both.shape, qc_ref[2 * tab], qc_ref[2 * tab + 1])
            sine = ts_ref[...] + per_frame(both.shape, qs_ref[2 * tab], qs_ref[2 * tab + 1])
            keys = both * cosine - swap_pairs(both) * sine
            out_ref[group, : lay.rows, :] = jnp.where(lane_low(keys.shape), dq_ref[group].astype(F32), keys).astype(BF)
            out_ref[group, lay.vrow :, :] = split_pair(both, lay.top)[0].astype(BF)
            return 0

        lax.fori_loop(0, groups, one, 0)

    return kernel_call(
        body,
        flags,
        [dq, mine, theirs, tab_cos, tab_sin, time_cos, time_sin],
        [shape_of((groups, lay.vrow + lay.top, LANES), BF)],
        pins=(0, 1),
        vmem=max(16, groups),
        flops=groups * lay.rows * LANES * 10,
        name="finish_keys",
    )[0]


def project_and_norm(flags, long_out, short_out, recv, weight, bias, tokens, mods, lay):
    rows, width = tokens.shape
    half = lay.heads * DH

    def body(flag_ref, long_ref, short_ref, recv_ref, w_ref, b_ref, tok_ref, mod_ref, branch_ref, resid_ref, normed_ref, inv_ref, hid_ref, att_ref):
        own_long = flag_ref[0]
        side = flag_ref[1]
        for pair in range(lay.heads // 2):
            kept = [
                jnp.where(own_long == 1, long_ref[2 * pair + k].astype(F32), short_ref[2 * pair + k].astype(F32)) for k in (0, 1)
            ]
            got = [recv_ref[2 * pair + k].astype(F32) for k in (0, 1)]
            lanes = slice(pair * LANES, (pair + 1) * LANES)
            att_ref[side, :, lanes] = join_pair(kept[0], kept[1], rows).astype(BF)
            att_ref[1 - side, :, lanes] = join_pair(got[0], got[1], rows).astype(BF)
        branch = dot(att_ref[0], w_ref[:half]) + dot(att_ref[1], w_ref[half:]) + b_ref[...]
        branch_ref[...] = branch
        gate = per_frame(branch.shape, mod_ref[0:1], mod_ref[1:2])
        resid = tok_ref[...].astype(F32) + gate * branch
        resid_ref[...] = resid
        normed, inv_std = norm_rows(resid)
        normed_ref[...] = normed
        inv_ref[...] = jnp.broadcast_to(inv_std, inv_ref.shape)
        shift = per_frame(branch.shape, mod_ref[2:3], mod_ref[3:4])
        scale = per_frame(branch.shape, mod_ref[4:5], mod_ref[5:6])
        hid_ref[...] = (normed * (1.0 + scale) + shift).astype(BF)

    full = shape_of((rows, width), F32)
    return kernel_call(
        body,
        flags,
        [long_out, short_out, recv, weight, bias, tokens, mods],
        [full, full, full, shape_of((rows, LANES), F32), shape_of((rows, width), BF)],
        scratch=[pltpu.VMEM((2, rows, half), BF)],
        out_pins=(0, 1, 2, 3),
        vmem=24,
        flops=2 * rows * width * width,
        name="project_and_norm",
    )


def mlp_both(flags, hidden, mlp_grad, up_weight, up_bias, down_weight, lay, out_dtype, name):
    rows, width = hidden.shape
    ff = up_weight.shape[1]
    wide = 2 * LANES
    chunks = 2
    steps = ff // (2 * wide * chunks)
    quarter = ff // 4

    def body(flag_ref, hid_ref, mg_ref, *refs):
        weights, outs = refs[: 3 * chunks], refs[3 * chunks :]
        mine_ref, send_ref, bm_ref, bt_ref, mlp_ref, hg_ref, macc, hacc = outs
        step = pl.program_id(0)
        first = flag_ref[2] == 0
        mlp, back = 0.0, 0.0
        for k in range(chunks):
            up_ref, ub_ref, dn_ref = weights[3 * k : 3 * k + 3]
            pre = dot(hid_ref[...], up_ref[...]) + ub_ref[...]
            tanh = jnp.tanh(GELU_C * (pre + GELU_K * pre * pre * pre))
            act = (0.5 * pre * (1.0 + tanh)).astype(BF)
            slope = 0.5 * (1.0 + tanh) + 0.5 * pre * (1.0 - tanh * tanh) * GELU_C * (1.0 + 3.0 * GELU_K * pre * pre)
            pre_low = (dot_lanes(mg_ref[...], dn_ref[...]) * slope).astype(BF)
            mlp = mlp + dot(act, dn_ref[...])
            back = back + dot_lanes(pre_low, up_ref[...])
            sums = jnp.sum(pre_low.astype(F32), axis=0, keepdims=True)
            lanes = slice(k * LANES, (k + 1) * LANES)
            for at, value in ((0, act), (1, pre_low)):
                mine_ref[at, :, lanes] = jnp.where(first, value[:, :LANES], value[:, LANES:])
                send_ref[at, :, lanes] = jnp.where(first, value[:, LANES:], value[:, :LANES])
            bm_ref[:, lanes] = jnp.broadcast_to(jnp.where(first, sums[:, :LANES], sums[:, LANES:]), (8, LANES))
            bt_ref[:, lanes] = jnp.broadcast_to(jnp.where(first, sums[:, LANES:], sums[:, :LANES]), (8, LANES))

        @pl.when(step == 0)
        def _():
            macc[...] = mlp
            hacc[...] = back

        @pl.when(step > 0)
        def _():
            macc[...] += mlp
            hacc[...] += back

        @pl.when(step == steps - 1)
        def _():
            mlp_ref[...] = macc[...].astype(mlp_ref.dtype)
            hg_ref[...] = hacc[...].astype(hg_ref.dtype)

    chunk = pl.BlockSpec((2, rows, chunks * LANES), lambda i, f: (0, 0, i))
    bchunk = pl.BlockSpec((8, chunks * LANES), lambda i, f: (0, i))
    weight_args, weight_specs = [], []
    for k in range(chunks):
        weight_args += [up_weight, up_bias, down_weight]
        weight_specs += [
            pl.BlockSpec((width, wide), lambda i, f, k=k: (0, 2 * (chunks * i + k) + f[1])),
            pl.BlockSpec((1, wide), lambda i, f, k=k: (0, 2 * (chunks * i + k) + f[1])),
            pl.BlockSpec((wide, width), lambda i, f, k=k: (2 * (chunks * i + k) + f[1], 0)),
        ]
    return kernel_call(
        body,
        flags,
        [hidden, mlp_grad, *weight_args],
        [shape_of((2, rows, quarter), BF)] * 2 + [shape_of((8, quarter), F32)] * 2 + [shape_of((rows, width), out_dtype)] * 2,
        specs=[None, None] + weight_specs,
        out_specs=[chunk, chunk, bchunk, bchunk, None, None],
        grid=(steps,),
        scratch=[pltpu.VMEM((rows, width), F32), pltpu.VMEM((rows, width), F32)],
        vmem=20,
        flops=4 * rows * width * ff,
        name=name,
    )


def scale_cotangent(flags, cotangent, gates):
    rows, width = cotangent.shape

    def body(flag_ref, dy_ref, g_ref, out_ref, sums_ref):
        low = (per_frame((rows, width), g_ref[0:1], g_ref[1:2]) * dy_ref[...].astype(F32)).astype(BF)
        out_ref[...] = low
        sums_ref[...] = jnp.broadcast_to(jnp.sum(low.astype(F32), axis=0, keepdims=True), sums_ref.shape)

    return kernel_call(
        body,
        flags,
        [cotangent, gates],
        [shape_of((rows, width), BF), shape_of((8, width), F32)],
        pins=(0,),
        flops=rows * width,
        name="scale_cotangent",
    )


def layer_output(flags, mlp_own, mlp_recv, bias, resid, cotangent, gates):
    rows, width = resid.shape

    def body(flag_ref, a_ref, b_ref, bias_ref, r_ref, dy_ref, g_ref, out_ref, sums_ref):
        mlp = a_ref[...] + b_ref[...].astype(F32) + bias_ref[...]
        out_ref[...] = (r_ref[...] + per_frame((rows, width), g_ref[0:1], g_ref[1:2]) * mlp).astype(BF)
        sums_ref[0:1], sums_ref[1:2] = frame_sums(dy_ref[...].astype(F32) * mlp)
        sums_ref[2:8] = jnp.zeros((6, width), F32)

    return kernel_call(
        body,
        flags,
        [mlp_own, mlp_recv, bias, resid, cotangent, gates],
        [shape_of((rows, width), BF), shape_of((8, width), F32)],
        pins=(0, 3, 4),
        flops=rows * width * 4,
        name="layer_output",
    )


def pack_rows(flags, n_blk, mid, gate2, silu, down_b, up_sums, sum_long, sum_short, bias_long, bias_short):
    width = mid.shape[1]
    cols = bias_long.shape[1]

    def body(flag_ref, mid_ref, g_ref, s_ref, d_ref, m1, m2, t1, t2, sl, ss, bl, bs, out_ref):
        bias = bl[0:1] + bs[0:1]
        bias = jnp.concatenate([bias, jnp.zeros((1, 2 * width - cols), F32)], axis=1)
        rows = jnp.concatenate(
            [mid_ref[0:6], g_ref[0:2], s_ref[...].astype(F32), d_ref[0:1], mid_ref[6:7], m1[0:1] + m2[0:1], t1[0:1] + t2[0:1],
             sl[0:4], ss[0:4], bias[:, :width], bias[:, width:]],
            axis=0,
        ).astype(BF)
        for k in range(n_blk):
            out_ref[k] = rows

    return kernel_call(
        body,
        flags,
        [mid, gate2, silu, down_b, *up_sums, sum_long, sum_short, bias_long, bias_short],
        [shape_of((n_blk, PACK, width), BF)],
        flops=width * PACK,
        name="pack_rows",
    )[0]


def branch_back(flags, hid_own, hid_recv, cotangent, normed, inv_std, branch, mods, weight, lay):
    rows, width = normed.shape
    half = lay.heads * DH

    def body(flag_ref, a_ref, b_ref, dy_ref, n_ref, inv_ref, br_ref, mod_ref, w_ref, rg_ref, bg_ref, keep_ref, send_ref, sums_ref):
        side = flag_ref[1]
        hid = a_ref[...] + b_ref[...].astype(F32)
        norm = n_ref[...]
        scale = per_frame(hid.shape, mod_ref[4:5], mod_ref[5:6])
        resid = dy_ref[...].astype(F32) + norm_back(hid * (1.0 + scale), norm, inv_ref[:, 0:1])
        rg_ref[...] = resid
        gate = per_frame(hid.shape, mod_ref[0:1], mod_ref[1:2])
        low = (gate * resid).astype(BF)
        bg_ref[...] = low
        for out_ref, which in ((keep_ref, side), (send_ref, 1 - side)):
            grad = dot_lanes(low, w_ref[pl.ds(pl.multiple_of(which * half, half), half), :])
            for pair in range(lay.heads // 2):
                one, two = split_pair(grad[:, pair * LANES : (pair + 1) * LANES], lay.top)
                out_ref[2 * pair] = one.astype(BF)
                out_ref[2 * pair + 1] = two.astype(BF)
        sums_ref[0:1], sums_ref[1:2] = frame_sums(resid * br_ref[...])
        sums_ref[2:3], sums_ref[3:4] = frame_sums(hid)
        sums_ref[4:5], sums_ref[5:6] = frame_sums(hid * norm)
        sums_ref[6:7] = jnp.sum(low.astype(F32), axis=0, keepdims=True)
        sums_ref[7:8] = jnp.zeros((1, width), F32)

    packed = shape_of((lay.heads, lay.top, LANES), BF)
    return kernel_call(
        body,
        flags,
        [hid_own, hid_recv, cotangent, normed, inv_std, branch, mods, weight],
        [shape_of((rows, width), F32), shape_of((rows, width), BF), packed, packed, shape_of((8, width), F32)],
        pins=(0, 2, 3, 4, 5, 6),
        out_pins=(0,),
        vmem=24,
        flops=2 * rows * width * width,
        name="branch_back",
    )


def qkv_back(flags, grads, tok_own, tok_oth, weight, lay, is_long):
    rows, width = tok_own.shape
    cols = lay.heads * DH
    half = cols // 2

    def body(flag_ref, g_ref, own_ref, oth_ref, w_ref, hid_ref, low_ref, gm_ref, gt_ref, bias_ref, sums_ref, q_ref, acc_ref):
        step = pl.program_id(0)
        core = flag_ref[2]

        @pl.when(step == 0)
        def _():
            for pair in range(lay.heads // 2):
                one, two = g_ref[2 * pair, :rows, :].astype(F32), g_ref[2 * pair + 1, :rows, :].astype(F32)
                low = lane_low(one.shape)
                lanes = slice(pair * LANES, (pair + 1) * LANES)
                q_ref[0, :, lanes] = jnp.where(low, one, swap_halves(two)).astype(BF)
                q_ref[1, :, lanes] = jnp.where(low, swap_halves(one), two).astype(BF)
                one, two = g_ref[2 * pair, lay.vrow :, :].astype(F32), g_ref[2 * pair + 1, lay.vrow :, :].astype(F32)
                q_ref[2, :, lanes] = join_pair(one, two, rows).astype(BF)

        value = q_ref[step]
        part = dot_lanes(value, w_ref[...])

        @pl.when(step == 0)
        def _():
            acc_ref[...] = part

        @pl.when(step > 0)
        def _():
            acc_ref[...] += part

        first = core == 0
        gm_ref[...] = jnp.where(first, value[:, :half], value[:, half:])
        gt_ref[...] = jnp.where(first, value[:, half:], value[:, :half])
        bias_ref[...] = jnp.broadcast_to(jnp.sum(value.astype(F32), axis=0, keepdims=True), bias_ref.shape)

        @pl.when(step == 2)
        def _():
            hid = acc_ref[...]
            hid_ref[...] = hid
            low_ref[...] = hid.astype(BF)
            mine = (flag_ref[0] == 1) if is_long else (flag_ref[0] == 0)
            normed, _ = norm_rows(jnp.where(mine, own_ref[...].astype(F32), oth_ref[...].astype(F32)))
            sums_ref[0:1], sums_ref[1:2] = frame_sums(hid)
            sums_ref[2:3], sums_ref[3:4] = frame_sums(hid * normed)
            sums_ref[4:8] = jnp.zeros((4, width), F32)

    return kernel_call(
        body,
        flags,
        [grads, tok_own, tok_oth, weight],
        [
            shape_of((rows, width), F32),
            shape_of((rows, width), BF),
            shape_of((rows, 3 * half), BF),
            shape_of((rows, 3 * half), BF),
            shape_of((8, 3 * cols), F32),
            shape_of((8, width), F32),
        ],
        specs=[None, None, None, pl.BlockSpec((width, cols), lambda j, f: (0, 2 * j + f[1]))],
        out_specs=[
            None, None,
            pl.BlockSpec((rows, half), lambda j, f: (0, j)),
            pl.BlockSpec((rows, half), lambda j, f: (0, j)),
            pl.BlockSpec((8, cols), lambda j, f: (0, j)),
            None,
        ],
        pins=(1, 2),
        out_pins=(0,),
        grid=(3,),
        scratch=[pltpu.VMEM((3, rows, cols), BF), pltpu.VMEM((rows, width), F32)],
        flops=6 * rows * width * cols,
        name="qkv_back_long" if is_long else "qkv_back_short",
    )


def token_back(flags, hid_long, hid_short, recv, tokens, resid_grad, mods, lay):
    rows, width = tokens.shape

    def body(flag_ref, l_ref, s_ref, r_ref, tok_ref, rg_ref, mod_ref, out_ref):
        hid = jnp.where(flag_ref[0] == 1, l_ref[...], s_ref[...]) + r_ref[...].astype(F32)
        normed, inv_std = norm_rows(tok_ref[...].astype(F32))
        scale = per_frame(hid.shape, mod_ref[0:1, width : 2 * width], mod_ref[1:2, width : 2 * width])
        out_ref[...] = rg_ref[...] + norm_back(hid * (1.0 + scale), normed, inv_std)

    return kernel_call(
        body,
        flags,
        [hid_long, hid_short, recv, tokens, resid_grad, mods],
        [shape_of((rows, width), F32)],
        pins=(0, 1, 3, 4, 5),
        flops=rows * width * 20,
        name="token_back",
    )[0]


def add_head_rows(flags, part, got, send, keep, order):
    half_blk, total, width = send.shape
    n_blk = 2 * half_blk
    rows = part.shape[1] // n_blk
    bit = order[0]

    def body(flag_ref, part_ref, got_ref, send_in, keep_in, send_ref, keep_ref):
        both = (part_ref[flag_ref[2]].astype(F32) + got_ref[...].astype(F32)).astype(BF)
        for target in range(n_blk):
            place = relative_place(target, flag_ref[4], n_blk)
            at = ((place >> (bit + 1)) << bit) | (place & ((1 << bit) - 1))
            value = both[target * rows : (target + 1) * rows]
            sent = (place >> bit) & 1

            @pl.when(sent == 1)
            def _(value=value, at=at):
                send_ref[at] = value

            @pl.when(sent == 0)
            def _(value=value, at=at):
                keep_ref[at] = value

    block = pl.BlockSpec((half_blk, rows, width), lambda i, f: (0, (total - rows) // rows, 0))
    return kernel_call(
        body,
        flags,
        [part, got, send, keep],
        [shape_of(send.shape, BF)] * 2,
        specs=[None, None, pl.BlockSpec(memory_space=pl.ANY), pl.BlockSpec(memory_space=pl.ANY)],
        out_specs=[block, block],
        pins=(2, 3),
        out_pins=(0, 1),
        aliases={3: 0, 4: 1},
        flops=rows * width * n_blk,
        name="add_head_rows",
    )


def group_spec(pair, rows, wide, moves, per):
    index = pair[1]
    if index is None:
        return pl.BlockSpec((rows, wide), lambda i, f: (0, i // per if moves else 0))
    return pl.BlockSpec((None, rows, wide), lambda i, f: (index, 0, i // per if moves else 0))


def split_weight_grads(flags, lefts, rights, n_blk, orders, extra, name):
    count = len(lefts)
    rows, depth = lefts[0][0].shape[-2:]
    pieces = len(orders)
    cols = rights[0][0].shape[-1] // pieces
    tall = depth // n_blk
    wide = max(tall, LANES)
    per = wide // tall

    def body(flag_ref, *refs):
        outs = refs[2 * count :]
        acc = dot_rows(refs[0][...], refs[count][...])
        for k in range(1, count):
            acc += dot_rows(refs[k][...], refs[count + k][...])
        low = acc.astype(BF)
        for member in range(per):
            part = low[member * tall : (member + 1) * tall]
            place = relative_place(pl.program_id(0) * per + member, flag_ref[4], n_blk)
            for piece, order in enumerate(orders):
                bit = order[0]
                at = ((place >> (bit + 1)) << bit) | (place & ((1 << bit) - 1))
                value = part[:, piece * cols : (piece + 1) * cols]
                sent = (place >> bit) & 1

                @pl.when(sent == 1)
                def _(value=value, at=at, piece=piece):
                    outs[2 * piece][at, :tall] = value

                @pl.when(sent == 0)
                def _(value=value, at=at, piece=piece):
                    outs[2 * piece + 1][at, :tall] = value

    return kernel_call(
        body,
        flags,
        [array for array, _ in [*lefts, *rights]],
        [shape_of((n_blk // 2, tall + extra, cols), BF)] * (2 * pieces),
        specs=[group_spec(pair, rows, wide, True, 1) for pair in lefts]
        + [group_spec(pair, rows, cols * pieces, False, 1) for pair in rights],
        grid=(depth // wide,),
        flops=2 * count * rows * depth * cols * pieces,
        name=name,
    )


def head_weight_grads(flags, longs, shorts, grad_own, grad_oth, lay):
    rows, width = grad_own.shape
    pairs = lay.heads // 2

    def body(flag_ref, l_ref, s_ref, go_ref, gt_ref, out_ref):
        own_long = flag_ref[0] == 1
        grads = jnp.where(own_long, go_ref[...], gt_ref[...]), jnp.where(own_long, gt_ref[...], go_ref[...])
        for pair in range(pairs):
            acc = 0.0
            for ref, grad in zip((l_ref, s_ref), grads):
                left = join_pair(ref[2 * pair].astype(F32), ref[2 * pair + 1].astype(F32), rows).astype(BF)
                acc = acc + dot_rows(left, grad)
            out_ref[pair * LANES : (pair + 1) * LANES, :] = acc.astype(BF)

    return kernel_call(
        body,
        flags,
        [longs, shorts, grad_own, grad_oth],
        [shape_of((lay.heads * DH, width), BF)],
        pins=(0, 1),
        flops=4 * rows * width * lay.heads * DH,
        name="head_weight_grads",
    )[0]


def relative_place(target, here, n_blk):
    relative = target ^ here
    return relative ^ ((relative >> 1) & (10 & (n_blk - 1)))


def hop_of(bit):
    return (1 << bit) if bit == 0 or bit % 2 == 1 else (1 << bit) | (1 << (bit - 1))


class CubeSum:
    def __init__(self, send, keep, n_blk, order):
        self.n_blk, self.order, self.at = n_blk, order, 0
        self.bits = n_blk.bit_length() - 1
        self.axes = [bit for bit in range(self.bits)[::-1] if bit != order[0]]
        self.send = send.reshape((2,) * (self.bits - 1) + send.shape[1:])
        self.keep = keep.reshape((2,) * (self.bits - 1) + keep.shape[1:])
        self.value = None

    def step(self, starts=(), ends=()):
        hop = hop_of(self.order[self.at])
        send = after(self.send, *starts) if starts else self.send
        got = lax.ppermute(send, "blk", [(i, i ^ hop) for i in range(self.n_blk)])
        if ends:
            got = after(got, *ends)
        value = self.keep.astype(F32) + got.astype(F32)
        self.at += 1
        if self.at < self.bits:
            axis = self.axes.index(self.order[self.at])
            self.axes.pop(axis)
            index = (slice(None),) * axis
            value = value.astype(BF)
            self.send, self.keep = value[index + (1,)], value[index + (0,)]
        self.value = value
        return value

    def finish(self):
        while self.at < self.bits:
            self.step()
        return self.value


def lay_out_rows(flags, gathered, split, ff, name):
    n_uly, rows, total = gathered.shape
    cols = (total - split) // 3

    def body(flag_ref, in_ref, up_ref, attn_ref):
        for u in range(n_uly):
            for i in range(split // LANES):
                at = (i * n_uly + u) * LANES
                up_ref[:, at : at + LANES] = in_ref[u, :, i * LANES : (i + 1) * LANES].astype(F32)
            for j in range(3):
                at = (j * n_uly + u) * cols
                attn_ref[:, at : at + cols] = in_ref[u, :, split + j * cols : split + (j + 1) * cols].astype(F32)

    return kernel_call(
        body,
        flags,
        [gathered],
        [shape_of((rows, ff), F32), shape_of((rows, 3 * n_uly * cols), F32)],
        flops=rows * total,
        name=name,
    )


def modulation_grads(flags, long_rows, gathered, row_out, name):
    total, width = gathered.shape
    quarter = total // 4

    def body(flag_ref, long_ref, g_ref, out_ref, sums_ref, part_ref):
        start = flag_ref[5]
        block = pl.multiple_of((start // LANES) * LANES, LANES)
        silu = g_ref[:, pl.ds(block, LANES)].astype(F32)
        parts = [silu[k * quarter : (k + 1) * quarter] for k in (1, 0, 3, 2)]
        mate = jnp.concatenate(parts, axis=0)
        own_long = long_ref[...] > 0.5

        def place_of(index):
            return index - PACK * ((index * 2731) >> 16)

        place = place_of(lax.broadcasted_iota(jnp.int32, (total, LANES), 0))

        def aligned(value, base):
            return jnp.where((place == base) | (place == base + 1), pltpu.roll(value, (base - 8) % total, 0), 0.0)

        def owner(base, is_long):
            return jnp.where(own_long == is_long, aligned(silu, base), aligned(mate, base))

        lefts = [
            owner(14, True) + owner(18, False),
            owner(16, True) + owner(20, False),
            aligned(silu, 0),
            aligned(silu, 2),
            aligned(silu, 4),
            aligned(silu, 6),
        ]
        for k, left in enumerate(lefts):
            part_ref[...] = dot_rows(left.astype(BF), g_ref[...])
            out_ref[:, k * width : (k + 1) * width] = part_ref[pl.ds(pl.multiple_of(start - block, row_out), row_out), :]
        row = lax.broadcasted_iota(jnp.int32, (32, quarter), 0)
        which = jnp.where(row == place_of(lax.broadcasted_iota(jnp.int32, (32, quarter), 1)), 1.0, 0.0).astype(BF)
        for u in range(4):
            sums_ref[u] = dot(which, g_ref[u * quarter : (u + 1) * quarter, :])

    return kernel_call(
        body,
        flags,
        [long_rows, gathered],
        [shape_of((row_out, 6 * width), F32), shape_of((4, 32, width), F32)],
        scratch=[pltpu.VMEM((LANES, width), F32)],
        vmem=max(16, 16 * total // 768),
        flops=total * width * LANES * 12,
        name=name,
    )


def after(value, *earlier):
    return lax.optimization_barrier((value,) + earlier)[0]


def rotary_static(frames):
    n_time, n_row = DH // 8, 3 * DH // 16
    cosine = np.zeros((frames * PATCH, LANES), np.float32)
    sine = np.zeros((frames * PATCH, LANES), np.float32)
    patch = np.arange(frames * PATCH) % PATCH
    for group, place in ((0, patch // GRID), (1, patch % GRID)):
        for j in range(n_row):
            freq = np.exp(np.float32(-math.log(10000.0)) * np.float32(j) / np.float32(n_row)).astype(np.float32)
            angle = (place.astype(np.float32) * freq).astype(np.float64)
            pair = n_time + group * n_row + j
            for head in (0, HALF):
                cosine[:, head + 2 * pair] = np.cos(angle)
                cosine[:, head + 2 * pair + 1] = np.cos(angle)
                sine[:, head + 2 * pair] = -np.sin(angle)
                sine[:, head + 2 * pair + 1] = np.sin(angle)
    return cosine, sine


def rotary_time(times):
    n_time = DH // 8
    lane = jnp.arange(LANES, dtype=jnp.int32)
    pair = (lane % HALF) // 2
    freq = jnp.exp(-math.log(10000.0) * pair.astype(F32) / float(n_time))
    angle = times.astype(F32)[:, None] * freq[None, :]
    live = (pair < n_time)[None, :]
    sign = jnp.where(lane % 2 == 0, -1.0, 1.0)[None, :]
    return jnp.where(live, jnp.cos(angle), 0.0), jnp.where(live, sign * jnp.sin(angle), 0.0)


class Layout:
    def __init__(self, rows, heads, parts):
        self.rows = rows
        self.heads = heads
        self.parts = parts
        self.top = round_up(-(-rows // 2), 16)
        self.vrow = round_up(rows, 16)


def on_device(
    tokens, cotangent, noise_embed, frame_clip, frame_index, mod_weight, mod_bias, attn_weight, attn_bias,
    proj_weight, proj_bias, up_weight, up_bias, down_weight, down_bias,
):
    n_uly = lax.axis_size("uly")
    n_blk = lax.axis_size("blk")
    blk = lax.axis_index("blk")
    uly = lax.axis_index("uly")
    rows, width = tokens.shape
    frames = noise_embed.shape[0]
    side, core = uly // 2, uly % 2
    heads = width // DH // 2
    parts = n_blk // heads
    lay = Layout(rows, heads, parts)
    dev = blk * n_uly + uly

    def swap_side(value):
        return lax.ppermute(value, "uly", [(i, i ^ 2) for i in range(n_uly)])

    def swap_core(value):
        return lax.ppermute(value, "uly", [(i, i ^ 1) for i in range(n_uly)])

    def spread(value):
        return lax.all_to_all(value, "blk", split_axis=0, concat_axis=0, tiled=True)

    def gather_rest(many):
        both = jnp.stack([many, swap_side(many)])
        return jnp.stack([both, swap_core(both)])

    long_first = frame_clip[::FB] == n_blk
    own_long_b = lax.dynamic_index_in_dim(long_first, blk, 0, False) == (side == 0)
    own_long = own_long_b.astype(jnp.int32)
    row_out = width // (n_blk * n_uly)
    flags = jnp.stack([own_long, side, core, blk // heads, blk, dev * row_out]).astype(jnp.int32)

    tok_oth = swap_side(tokens)
    silu = jax.nn.silu(noise_embed.astype(F32)).astype(BF)
    bias = mod_bias.astype(F32)
    first_mod = dot(silu, mod_weight[:, : 2 * width]) + bias[: 2 * width]
    first_mods = jnp.concatenate([first_mod, swap_side(first_mod)], axis=0)
    rest_mod = dot(after(silu, first_mod), mod_weight[:, 2 * width :]) + bias[2 * width :]
    first_mods, rest_mod = lax.optimization_barrier((first_mods, rest_mod))

    block_time = frame_index.reshape(n_blk, FB)
    head_time, tail_time = block_time[:, : FB // 2], block_time[:, FB // 2 :]
    long_times = lax.dynamic_slice_in_dim(jnp.where(long_first[:, None], head_time, tail_time), core * frames, frames, 1)
    short_times = lax.dynamic_slice_in_dim(jnp.where(long_first[:, None], tail_time, head_time), core * frames, frames, 1)
    short_times = lax.dynamic_index_in_dim(short_times, blk, 0, False)
    time_cos, time_sin = rotary_time(jnp.concatenate([lax.dynamic_index_in_dim(long_times, blk, 0, False), short_times]))
    long_cos, long_sin = rotary_time(long_times.reshape(-1))
    short_cos, short_sin = time_cos[frames:, None], time_sin[frames:, None]
    long_cos, long_sin = long_cos[:, None], long_sin[:, None]
    tab_cos, tab_sin = (jnp.asarray(t) for t in rotary_static(frames))

    gate2 = rest_mod[:, 3 * width :]
    mid_mods = jnp.concatenate([rest_mod[:, :width], rest_mod[:, width : 2 * width], rest_mod[:, 2 * width : 3 * width]], axis=0)
    mid_mods = jnp.concatenate([mid_mods, jnp.zeros((2, width), F32)], axis=0)
    hidden1, qkv_long, qkv_short = tokens_to_qkv(
        flags, tokens, tok_oth, first_mods, attn_weight, attn_bias.astype(F32)[None], tab_cos, tab_sin, time_cos, time_sin, lay
    )
    sent = jnp.concatenate([qkv_long] * parts, axis=0) if parts > 1 else qkv_long
    long_own = spread(sent)
    short_oth = swap_core(qkv_short)
    out_short, ot_short, lse_short = attend(flags, qkv_short, short_oth, lay, False)
    mlp_grad, down_b = scale_cotangent(flags, after(cotangent, qkv_long), gate2)
    mlp_grad_oth = swap_side(mlp_grad)
    long_own, out_short, mlp_grad = lax.optimization_barrier((long_own, out_short, mlp_grad))
    long_oth = swap_core(long_own)
    out_long_all, ot_long, lse_long = attend(flags, long_own, long_oth, lay, True)
    out_long_all, mlp_grad_oth = lax.optimization_barrier((out_long_all, mlp_grad_oth))

    def own_part(value):
        if parts == 1:
            return value
        return lax.dynamic_slice_in_dim(value, ((blk // 2) % parts) * heads, heads, 0)

    out_long = own_part(spread(out_long_all))
    out_recv = swap_side(jnp.where(own_long_b, out_short, out_long))
    branch, resid, normed2, inv2, hidden2 = project_and_norm(
        flags, out_long, out_short, out_recv, proj_weight, proj_bias.astype(F32)[None], tokens, mid_mods, lay
    )

    hidden2_oth = swap_side(hidden2)
    up_b = up_bias.astype(F32)[None]
    mine, send, bm, bt, mlp_own, hid_own = mlp_both(
        flags, hidden2, mlp_grad, up_weight, up_b, down_weight, lay, F32, "mlp_own"
    )
    hidden2_oth, mlp_own, hid_own = lax.optimization_barrier((hidden2_oth, mlp_own, hid_own))
    mine2, send2, bm2, bt2, mlp_oth, hid_oth = mlp_both(
        flags, hidden2_oth, mlp_grad_oth, up_weight, up_b, down_weight, lay, BF, "mlp_other"
    )
    hid_recv = swap_side(hid_oth)

    got, got2 = swap_core(send), swap_core(send2)
    hid_c, hid_c2, mg_c, mg_c2 = (swap_core(v) for v in (hidden2, hidden2_oth, mlp_grad, mlp_grad_oth))
    plain = lambda *arrays: [(v, None) for v in arrays]
    blocks = [mine, mine2, got, got2]
    bits = list(range(n_blk.bit_length() - 1))
    orders = [bits[k % len(bits) :] + bits[: k % len(bits)] for k in range(3)]
    down_order, up_order = [0, 2, 1] + bits[3:], [1, 0, 2] + bits[3:]
    down_send, down_keep = split_weight_grads(
        flags, [(v, 0) for v in blocks], plain(mlp_grad, mlp_grad_oth, mg_c, mg_c2), n_blk, [down_order], 0, "down_grads"
    )
    hid_recv, down_send, down_keep = lax.optimization_barrier((hid_recv, down_send, down_keep))

    resid_grad, branch_grad, do_keep, do_send, mid_sums = branch_back(
        flags, hid_own, hid_recv, cotangent, normed2, inv2, branch, mid_mods, proj_weight, lay
    )
    down_sum = CubeSum(down_send, down_keep, n_blk, down_order)
    do_recv = swap_side(do_send)
    hid_late = after(hidden2, do_send)
    up_send, up_keep = split_weight_grads(
        flags, plain(hid_late, hidden2_oth, hid_c, hid_c2), [(v, 1) for v in blocks], n_blk, [up_order], width // 4 // n_blk, "up_grads"
    )
    do_recv, up_send, up_keep = lax.optimization_barrier((do_recv, up_send, up_keep))
    do_long = jnp.where(own_long_b, do_keep, do_recv)
    if parts > 1:
        hot = (jnp.arange(parts) == (blk // 2) % parts)[:, None, None, None]
        do_sent = jnp.where(hot, do_long[None], 0).reshape((n_blk,) + do_long.shape[1:])
    else:
        do_sent = do_long
    do_all = spread(do_sent)
    dq_s, mine_s, theirs_s = attend_back(
        flags, qkv_short, short_oth, [do_keep, do_recv], ot_short, lse_short, tab_cos, tab_sin, short_cos, short_sin, lay, False
    )
    branch_grad_oth = swap_side(after(branch_grad, do_recv))
    mlp_recv = swap_side(after(mlp_oth, branch_grad_oth))
    do_all, dq_s, mine_s, theirs_s, branch_grad_oth = lax.optimization_barrier((do_all, dq_s, mine_s, theirs_s, branch_grad_oth))
    proj_part = head_weight_grads(flags, out_long, out_short, branch_grad, branch_grad_oth, lay)
    proj_part = proj_part.reshape(2, -1, width)
    proj_got = swap_core(jnp.where(core == 0, proj_part[1], proj_part[0]))
    up_send, up_keep = add_head_rows(flags, proj_part, proj_got, up_send, up_keep, up_order)
    up_sum = CubeSum(up_send, up_keep, n_blk, up_order)
    down_sum.step()
    do_all, up_sum.send, down_sum.send, down_sum.keep = lax.optimization_barrier(
        (do_all, up_sum.send, down_sum.send, down_sum.keep)
    )

    dq_l, mine_l, theirs_l = attend_back(
        flags, long_own, long_oth, [do_all], ot_long, lse_long, tab_cos, tab_sin, long_cos, long_sin, lay, True
    )
    grads_sent = finish_keys(flags, dq_l, mine_l, swap_core(theirs_l), tab_cos, tab_sin, long_cos, long_sin, lay, True)
    grads_all = spread(grads_sent)
    if parts > 1:
        grads_long = jnp.sum(grads_all.astype(F32).reshape((parts, heads) + grads_all.shape[1:]), axis=0).astype(BF)
    else:
        grads_long = grads_all

    theirs_s = swap_core(theirs_s)
    mlp_recv, dq_s, theirs_s, _ = lax.optimization_barrier((mlp_recv, dq_s, theirs_s, grads_sent))
    down_sum.step(ends=(grads_sent,))
    up_sum.step(ends=(grads_sent,))
    grads_short = finish_keys(flags, dq_s, mine_s, theirs_s, tab_cos, tab_sin, short_cos, short_sin, lay, False)
    hidS, hidS_low, gmS, gtS, abS, sumS = qkv_back(flags, grads_short, tokens, tok_oth, attn_weight, lay, False)
    output, gate2_sums = layer_output(flags, mlp_own, mlp_recv, down_bias.astype(F32)[None], resid, cotangent, gate2)
    h1_core = swap_core(hidden1)
    gtS_got = swap_core(gtS)
    grads_long, output, h1_core, gtS_got, hidS_low, up_sum.send, up_sum.keep, down_sum.send, down_sum.keep = lax.optimization_barrier(
        (grads_long, output, h1_core, gtS_got, hidS_low, up_sum.send, up_sum.keep, down_sum.send, down_sum.keep)
    )

    hidL, hidL_low, gmL, gtL, abL, sumL = qkv_back(flags, grads_long, tokens, tok_oth, attn_weight, lay, True)
    gtL_got = swap_core(gtL)
    hid1_recv = swap_side(jnp.where(own_long_b, hidS_low, hidL_low))
    pack = pack_rows(flags, n_blk, mid_sums, gate2_sums, silu, down_b, (bm, bm2, bt, bt2), sumL, sumS, abL, abS)
    halves = split_weight_grads(
        flags, [(hidden1, 0), (hidden1, 1), (h1_core, 0), (h1_core, 1)], plain(gmL, gmS, after(gtL_got, pack), gtS_got),
        n_blk, orders, 0, "attn_grads"
    )
    many = spread(pack)
    hid1_recv, many, *halves = lax.optimization_barrier((hid1_recv, many, *halves))
    packs = gather_rest(many).reshape(-1, width)
    attn_sums = [CubeSum(halves[2 * k], halves[2 * k + 1], n_blk, order) for k, order in enumerate(orders)]
    for part in attn_sums:
        part.step()
    up_sum.step(starts=(attn_sums[0].send,))
    down_sum.step(starts=(attn_sums[0].send,))
    attn_mine = [part.finish().astype(BF) for part in attn_sums]
    up_all, down_mine = up_sum.finish(), down_sum.finish()
    up_mine, proj_mine = up_all[: width // n_blk].astype(BF), up_all[width // n_blk :]
    token_grad = token_back(flags, hidL, hidS, hid1_recv, tokens, resid_grad, first_mod, lay)

    quarters = jnp.concatenate([up_mine] + attn_mine, axis=1)
    quarters = lax.all_to_all(quarters.reshape(n_uly, row_out, -1), "uly", 0, 0, tiled=True)
    ff = up_weight.shape[1]
    g_up_weight, g_attn_weight = lay_out_rows(flags, quarters, ff // n_uly, ff, "lay_out_rows")

    g = ff // (n_blk * n_uly)

    def down_home(index):
        b, u = divmod(index, n_uly)
        start = ((b * g // LANES) * n_uly + u) * LANES + (b * g) % LANES
        return start // g

    down_map = [(i, down_home(i)) for i in range(n_blk * n_uly)]
    g_down_weight = down_mine.astype(F32)
    if any(a != b for a, b in down_map):
        g_down_weight = lax.ppermute(g_down_weight, ("blk", "uly"), down_map)
    proj_map = [(b * n_uly + u, u * n_blk + b) for b in range(n_blk) for u in range(n_uly)]
    g_proj_weight = lax.ppermute(proj_mine.astype(F32), ("blk", "uly"), proj_map)

    own_long_all = (long_first[None, :] == ((side ^ jnp.arange(2)) == 0)[:, None]).astype(F32)
    long_rows = jnp.broadcast_to(own_long_all[None, :, :, None, None], (2, 2, n_blk, PACK, LANES)).reshape(-1, LANES)
    g_mod_weight, sums = modulation_grads(flags, long_rows, packs, row_out, "modulation_grads")

    def cut(vector, size):
        return lax.dynamic_slice_in_dim(vector, dev * size, size, 0)

    total_dev = n_blk * n_uly
    whole_sum = jnp.sum(sums, axis=0)
    mod_line = jnp.concatenate([whole_sum[14:16] + whole_sum[18:20], whole_sum[16:18] + whole_sum[20:22], whole_sum[0:8]], axis=0)
    g_mod_bias = cut(mod_line.reshape(6, 2, width).sum(axis=1).reshape(-1), 6 * width // total_dev)
    g_down_bias = cut(whole_sum[10], width // total_dev)
    g_proj_bias = cut(whole_sum[11], width // total_dev)
    first = dev * g
    steps = (first // LANES) % n_uly ^ uly
    core_step, side_step = steps % 2, steps // 2
    up_mine_sum = sums[2 * core_step + side_step, 12] + sums[2 * (1 - core_step) + side_step, 13]
    g_up_bias = lax.dynamic_slice_in_dim(up_mine_sum, first // (LANES * n_uly) * LANES + first % LANES, g, 0)
    by_step = (sums[0:2, 22:24] + sums[2:4, 22:24]).reshape(2, 2 * width)[:, : 3 * width // 2]
    by_side = jnp.where(side == 0, by_step, by_step[::-1])
    g_attn_bias = cut(jnp.swapaxes(by_side.reshape(2, 3, width // 2), 0, 1).reshape(-1), 3 * width // total_dev)
    return (
        output, token_grad, g_mod_weight, g_mod_bias, g_attn_weight, g_attn_bias,
        g_proj_weight, g_proj_bias, g_up_weight, g_up_bias, g_down_weight, g_down_bias,
    )


def solution(mesh):
    row = P(("blk", "uly"), None)
    flat = P(("blk", "uly"))
    in_specs = (row, row, row) + (P(),) * 12
    out_specs = (row, row, row, flat, row, flat, row, flat, row, flat, row, flat)
    return jax.shard_map(on_device, mesh=mesh, in_specs=in_specs, out_specs=out_specs, check_vma=False)
```

time: 448 us -> 314 us (0.70)
  local copies, waits for them, and re-layouts: 63.9 us -> 21.2 us
  other arithmetic: 39.4 us -> 11.4 us
  waiting for transfers between devices: 86.9 us -> 66.2 us
  starting transfers between devices: 78.1 us -> 59.3 us
  between operations: 16 us -> 2.21 us
  blocking collectives: 22 us -> 11.9 us
    unnamed x202 -> x115, local copies, waits for them, and re-layouts: 40.1 us -> 8.51 us
    ppermute x1 -> x16, waiting for transfers between devices: 3.45 us -> 30.2 us  [the longest x15 22.7 us: step(): got = lax.ppermute(send, 'blk', [(i, i ^ hop) for i in range(self.n_blk)])]
    all_to_all x6 -> x1, starting transfers between devices: 27.7 us -> 3.47 us  [on_device(): lax.all_to_all(quarters.reshape(n_uly, row_out, -1), 'uly', 0, 0, tiled=T...]
    all_to_all x5 -> x4, waiting for transfers between devices: 36.3 us -> 17.4 us  [spread(): return lax.all_to_all(value, 'blk', split_axis=0, concat_axis=0, tiled=True)]
    ppermute x1 -> x16, starting transfers between devices: 2.56 us -> 21.2 us  [the longest x15 17.8 us: step(): got = lax.ppermute(send, 'blk', [(i, i ^ hop) for i in range(self.n_blk)])]
    all_to_all x6 -> x1, waiting for transfers between devices: 15.7 us -> 0.01 us  [on_device(): lax.all_to_all(quarters.reshape(n_uly, row_out, -1), 'uly', 0, 0, tiled=T...]
    reduce_sum x9 -> x2, other arithmetic: 13.7 us -> 0.09 us  [the longest x1 0.06 us: on_device(): mod_line.reshape(6, 2, width).sum(axis=1).reshape(-1)]
    ppermute x10 -> x11, waiting for transfers between devices: 25.7 us -> 13.2 us  [swap_side(): return lax.ppermute(value, 'uly', [(i, i ^ 2) for i in range(n_uly)])]
  transfers between devices with their start and end apart: 39 -> 47, of which waited for: 14 -> 21; matrix products, arithmetic and copies ran while one was open for 16% -> 8% of each run, Pallas kernels for 28% -> 35%
where the time goes in v2:
time: 314 us; the launch traced here: 313 us
  Pallas kernels  133 us (42%)
  waiting for transfers between devices  66.2 us (21%)
  starting transfers between devices  59.3 us (19%)
  local copies, waits for them, and re-layouts  21.2 us (7%)
  blocking collectives  11.9 us (4%)
  other arithmetic  11.4 us (4%)
  matrix products  7.53 us (2%)
    pallas_call x24, Pallas kernels, kernel_call(): pl.pallas_call(body, grid_spec=pltpu.PrefetchScalarGridSpec(num_scalar_pr...  133 us
    ppermute x15, waiting for transfers between devices, step(): got = lax.ppermute(send, 'blk', [(i, i ^ hop) for i in range(self.n_blk)])  22.7 us
    all_to_all x4, starting transfers between devices, spread(): return lax.all_to_all(value, 'blk', split_axis=0, concat_axis=0, tiled=True)  21.9 us
    ppermute x15, starting transfers between devices, step(): got = lax.ppermute(send, 'blk', [(i, i ^ hop) for i in range(self.n_blk)])  17.8 us
    all_to_all x4, waiting for transfers between devices, spread(): return lax.all_to_all(value, 'blk', split_axis=0, concat_axis=0, tiled=True)  17.4 us
    ppermute x11, waiting for transfers between devices, swap_side(): return lax.ppermute(value, 'uly', [(i, i ^ 2) for i in range(n_uly)])  13.2 us
    all_to_all x1, blocking collectives, spread(): return lax.all_to_all(value, 'blk', split_axis=0, concat_axis=0, tiled=True)  11.9 us
    ppermute x11, starting transfers between devices, swap_side(): return lax.ppermute(value, 'uly', [(i, i ^ 2) for i in range(n_uly)])  9.91 us
  transfers between devices with their start and end apart: 47, of which 21 were waited for; matrix products, arithmetic and copies ran while one was open for 8% of the time, Pallas kernels for 35%

profile of v2, /device:TPU:4, one launch (start us, length us, event | category | flops | bytes accessed | tf_op | source)
XLA Modules:
  0.0 312.8 jit_solution(8073919013866525556)
XLA Ops:
  6.8 4.6 %fusion.2 = f32[2,4096]{1,0:T(2,128)S(1)} fusion(bf16[2,1024]{1,0:T(2,128)(2,1)S(1)} %fusion.24.s_ref, bf16[1024,6144]{1,0:T(8,128)(2,1)} %param.22, f32[4096]{0:T(1024)S(1)} %slice.192), kind=kOutput, calls=%fused_computation.2 | convolution fusion | flops 16785408 | bytes 8441856 | tf_op jit(solution)/shard_map/dot_general | solution.py:77
  13.0 3.8 %collective-permute-done.oth_ref = bf16[200,1024]{1,0:T(8,128)(2,1)S(1)} collective-permute-done((bf16[200,1024]{1,0:T(8,128)(2,1)S(1)}, bf16[200,1024]{1,0:T(8,128)(2,1)S(1)}, u32[]{:S(2)}, u32[]{:S(2)}) %collective-permute-start) | collective-permute-done | bytes 409632 | tf_op jit(solution)/shard_map/ppermute | solution.py:1098
  16.8 8.5 %tokens_to_qkv.1 = (bf16[2,200,1024]{2,1,0:T(8,128)(2,1)}, bf16[8,320,128]{2,1,0:T(8,128)(2,1)}, bf16[8,320,128]{2,1,0:T(8,128)(2,1)S(1)}) custom-call(s32[6]{0:T(128)S(1)} %stack.49.flag_ref, bf16[200,1024]{1,0:T(8,128)(2,1)S(1)} %copy-done, bf16[200,1024]{1,0:T(8,128)(2,1)S(1)} %collective-permute-done.oth_ref, f32[4,2048]{1,0:T(4,128)S(1)} %pad_maximum_fusion.4.mod_ref, ...), custom_call_target="tpu_custom_call" | custom-call | flops 307200 | bytes 4096 | tf_op jit(solution)/shard_map/tokens_to_qkv/pallas_call | solution.py:117
  25.3 6.3 %all-to-all-start = ((bf16[8,320,128]{2,1,0:T(8,128)(2,1)}), bf16[8,320,128]{2,1,0:T(8,128)(2,1)S(1)}, u32[]{:S(2)}, u32[]{:S(2)}) async-start(bf16[8,320,128]{2,1,0:T(8,128)(2,1)} %get-tuple-element.138), calls=%async_computation | async-start | bytes 1310720 | tf_op jit(solution)/shard_map/all_to_all | solution.py:1104
  33.7 5.9 %attend_short.1 = (bf16[8,112,128]{2,1,0:T(8,128)(2,1)S(1)}, f32[8,64,200]{2,1,0:T(8,128)}, f32[8,8,200]{2,1,0:T(8,128)}) custom-call(s32[6]{0:T(128)S(1)} %stack.49.flag_ref, bf16[8,320,128]{2,1,0:T(8,128)(2,1)S(1)} %get-tuple-element.139.own_ref, bf16[8,320,128]{2,1,0:T(8,128)(2,1)S(1)} %collective-permute-done.2.oth_ref), custom_call_target="tpu_custom_call" | custom-call | flops 160000 | bytes 4096 | tf_op jit(solution)/shard_map/attend_short/pallas_call | solution.py:117
  39.6 7.6 %all-to-all-done.own_ref = bf16[8,320,128]{2,1,0:T(8,128)(2,1)S(1)} async-done(((bf16[8,320,128]{2,1,0:T(8,128)(2,1)}), bf16[8,320,128]{2,1,0:T(8,128)(2,1)S(1)}, u32[]{:S(2)}, u32[]{:S(2)}) %all-to-all-start) | async-done | bytes 655392 | tf_op jit(solution)/shard_map/all_to_all | solution.py:1104
  49.3 11.4 %attend_long.1 = (bf16[8,112,128]{2,1,0:T(8,128)(2,1)S(1)}, f32[4,64,400]{2,1,0:T(8,128)}, f32[4,8,400]{2,1,0:T(8,128)}) custom-call(s32[6]{0:T(128)S(1)} %stack.49.flag_ref, bf16[8,320,128]{2,1,0:T(8,128)(2,1)S(1)} %all-to-all-done.own_ref, bf16[8,320,128]{2,1,0:T(8,128)(2,1)S(1)} %collective-permute-done.3.oth_ref), custom_call_target="tpu_custom_call" | custom-call | flops 800000 | bytes 4096 | tf_op jit(solution)/shard_map/attend_long/pallas_call | solution.py:117
  60.8 11.9 %all_to_all.30.long_ref.l_ref = bf16[8,112,128]{2,1,0:T(8,128)(2,1)S(1)} all-to-all(bf16[8,112,128]{2,1,0:T(8,128)(2,1)S(1)} %get-tuple-element.146), channel_id=1, replica_groups=mesh['blk'=8,'uly'=4] {'blk'}, dimensions={0} | all-to-all | bytes 458752 | tf_op jit(solution)/shard_map/all_to_all | solution.py:1104
  73.7 5.2 %collective-permute-done.5.recv_ref = bf16[8,112,128]{2,1,0:T(8,128)(2,1)S(1)} collective-permute-done((bf16[8,112,128]{2,1,0:T(8,128)(2,1)S(1)}, bf16[8,112,128]{2,1,0:T(8,128)(2,1)S(1)}, u32[]{:S(2)}, u32[]{:S(2)}) %collective-permute-start.5) | collective-permute-done | bytes 229408 | tf_op jit(solution)/shard_map/ppermute | solution.py:1098
  78.8 4.4 %project_and_norm.1 = (f32[200,1024]{1,0:T(8,128)}, f32[200,1024]{1,0:T(8,128)}, f32[200,1024]{1,0:T(8,128)}, f32[200,128]{1,0:T(8,128)}, bf16[200,1024]{1,0:T(8,128)(2,1)S(1)}) custom-call(s32[6]{0:T(128)S(1)} %stack.49.flag_ref, bf16[8,112,128]{2,1,0:T(8,128)(2,1)S(1)} %all_to_all.30.long_ref.l_ref, ...), custom_call_target="tpu_custom_call" | custom-call | flops 102400 | bytes 4096 | tf_op jit(solution)/shard_map/project_and_norm/pallas_call | solution.py:117
  84.0 9.0 %mlp_own.1 = (bf16[2,200,1024]{2,1,0:T(8,128)(2,1)S(1)}, bf16[2,200,1024]{2,1,0:T(8,128)(2,1)S(1)}, f32[8,1024]{1,0:T(8,128)S(1)}, f32[8,1024]{1,0:T(8,128)S(1)}...) custom-call(s32[6]{0:T(128)S(1)} %stack.49.flag_ref, bf16[200,1024]{1,0:T(8,128)(2,1)S(1)} %get-tuple-element.168.hid_ref.refs_0_, ...), custom_call_target="tpu_custom_call" | custom-call | flops 819200 | bytes 4096 | tf_op jit(solution)/shard_map/mlp_own/pallas_call | solution.py:117
  93.2 9.8 %mlp_other.1 = (bf16[2,200,1024]{2,1,0:T(8,128)(2,1)S(1)}, bf16[2,200,1024]{2,1,0:T(8,128)(2,1)S(1)}, f32[8,1024]{1,0:T(8,128)S(1)}, f32[8,1024]{1,0:T(8,128)S(1...) custom-call(s32[6]{0:T(128)S(1)} %stack.49.flag_ref, ...), custom_call_target="tpu_custom_call" | custom-call | flops 819200 | bytes 4096 | tf_op jit(solution)/shard_map/mlp_other/pallas_call | solution.py:117
  107.1 6.1 %down_grads.1 = (bf16[4,128,1024]{2,1,0:T(8,128)(2,1)}, bf16[4,128,1024]{2,1,0:T(8,128)(2,1)S(1)}) custom-call(s32[6]{0:T(128)S(1)} %stack.49.flag_ref, bf16[2,200,1024]{2,1,0:T(8,128)(2,1)S(1)} %get-tuple-element.156.refs_0_.refs_4_, bf16[2,200,1024]{2,1,0:T(8,128)(2,1)S(1)} %get-tuple-element.157.refs_1_.refs_5_, ...), custom_call_target="tpu_custom_call" | custom-call | flops 409600 | bytes 4096 | tf_op jit(solution)/shard_map/down_grads/pallas_call | solution.py:117
  115.6 4.8 %branch_back.1 = (f32[200,1024]{1,0:T(8,128)}, bf16[200,1024]{1,0:T(8,128)(2,1)S(1)}, bf16[8,112,128]{2,1,0:T(8,128)(2,1)S(1)}, bf16[8,112,128]{2,1,0:T(8,128)(2,1)S(1)}, f32[8,1024]{1,0:T(8,128)S(1)}) custom-call(s32[6]{0:T(128)S(1)} %stack.49.flag_ref, f32[200,1024]{1,0:T(8,128)} %copy-done.16, bf16[200,1024]{1,0:T(8,128)(2,1)S(1)} %collective-permute-done.7.b_ref, ...), custom_call_target="tpu_custom_call" | custom-call | flops 102400 | bytes 4096 | tf_op jit(solution)/shard_map/branch_back/pallas_call | solution.py:117
  122.6 5.0 %up_grads.1 = (bf16[4,160,1024]{2,1,0:T(8,128)(2,1)S(1)}, bf16[4,160,1024]{2,1,0:T(8,128)(2,1)S(1)}) custom-call(s32[6]{0:T(128)S(1)} %stack.49.flag_ref, bf16[200,1024]{1,0:T(8,128)(2,1)S(1)} %get-tuple-element.168.hid_ref.refs_0_, bf16[200,1024]{1,0:T(8,128)(2,1)S(1)} %collective-permute-done.6.hid_ref.refs_1_, ...), custom_call_target="tpu_custom_call" | custom-call | flops 409600 | bytes 4096 | tf_op jit(solution)/shard_map/up_grads/pallas_call | solution.py:117
  131.2 5.0 %all-to-all-start.2 = ((bf16[8,112,128]{2,1,0:T(8,128)(2,1)}), bf16[8,112,128]{2,1,0:T(8,128)(2,1)S(1)}, u32[]{:S(2)}, u32[]{:S(2)}) async-start(bf16[8,112,128]{2,1,0:T(8,128)(2,1)} %broadcast_select_fusion.1), calls=%async_computation.2 | async-start | bytes 458752 | tf_op jit(solution)/shard_map/all_to_all | solution.py:1104
  137.4 7.6 %attend_back_short.1 = (bf16[8,200,128]{2,1,0:T(8,128)(2,1)}, f32[8,200,128]{2,1,0:T(8,128)}, bf16[8,200,128]{2,1,0:T(8,128)(2,1)}) custom-call(s32[6]{0:T(128)S(1)} %stack.49.flag_ref, bf16[8,320,128]{2,1,0:T(8,128)(2,1)} %copy-done.9, bf16[8,320,128]{2,1,0:T(8,128)(2,1)} %copy-done.10, bf16[8,112,128]{2,1,0:T(8,128)(2,1)S(1)} %get-tuple-element.166.refs_0_, ...), custom_call_target="tpu_custom_call" | custom-call | flops 400000 | bytes 4096 | tf_op jit(solution)/shard_map/attend_back_short/pallas_call | solution.py:117
  162.0 17.4 %attend_back_long.1 = (bf16[8,200,128]{2,1,0:T(8,128)(2,1)}, f32[8,200,128]{2,1,0:T(8,128)}, bf16[8,200,128]{2,1,0:T(8,128)(2,1)S(1)}) custom-call(s32[6]{0:T(128)S(1)} %stack.49.flag_ref, bf16[8,320,128]{2,1,0:T(8,128)(2,1)} %copy-done.1, bf16[8,320,128]{2,1,0:T(8,128)(2,1)} %copy-done.8, bf16[8,112,128]{2,1,0:T(8,128)(2,1)S(1)} %all-to-all-done.2.refs_0_, ...), custom_call_target="tpu_custom_call" | custom-call | flops 2000000 | bytes 4096 | tf_op jit(solution)/shard_map/attend_back_long/pallas_call | solution.py:117
  181.3 3.8 %finish_keys.2 = bf16[8,320,128]{2,1,0:T(8,128)(2,1)} custom-call(s32[6]{0:T(128)S(1)} %stack.49.flag_ref, bf16[8,200,128]{2,1,0:T(8,128)(2,1)} %get-tuple-element.189.dq_ref, f32[8,200,128]{2,1,0:T(8,128)} %get-tuple-element.190.a_ref, bf16[8,200,128]{2,1,0:T(8,128)(2,1)S(1)} %collective-permute-done.18.b_ref, f32[200,128]{1,0:T(8,128)S(1)} %copy-done.12, ...), custom_call_target="tpu_custom_call" | custom-call | flops 500 | bytes 4096 | tf_op jit(solution)/shard_map/finish_keys/pallas_call | solution.py:117
  185.0 5.2 %all-to-all-start.3 = ((bf16[8,320,128]{2,1,0:T(8,128)(2,1)}), bf16[8,320,128]{2,1,0:T(8,128)(2,1)S(1)}, u32[]{:S(2)}, u32[]{:S(2)}) async-start(bf16[8,320,128]{2,1,0:T(8,128)(2,1)} %finish_keys.2), calls=%async_computation.3 | async-start | bytes 1310720 | tf_op jit(solution)/shard_map/all_to_all | solution.py:1104
  194.6 6.1 %qkv_back_short.1 = (f32[200,1024]{1,0:T(8,128)}, bf16[200,1024]{1,0:T(8,128)(2,1)S(1)}, bf16[200,768]{1,0:T(8,128)(2,1)S(1)}, bf16[200,768]{1,0:T(8,128)(2,1)S(...) custom-call(s32[6]{0:T(128)S(1)} %stack.49.flag_ref, bf16[8,320,128]{2,1,0:T(8,128)(2,1)S(1)} %finish_keys.3.g_ref, ...), custom_call_target="tpu_custom_call" | custom-call | flops 153600 | bytes 4096 | tf_op jit(solution)/shard_map/qkv_back_short/pallas_call | solution.py:117
  210.1 5.8 %all-to-all-done.3.g_ref = bf16[8,320,128]{2,1,0:T(8,128)(2,1)S(1)} async-done(((bf16[8,320,128]{2,1,0:T(8,128)(2,1)}), bf16[8,320,128]{2,1,0:T(8,128)(2,1)S(1)}, u32[]{:S(2)}, u32[]{:S(2)}) %all-to-all-start.3) | async-done | bytes 655392 | tf_op jit(solution)/shard_map/all_to_all | solution.py:1104
  215.9 6.1 %qkv_back_long.1 = (f32[200,1024]{1,0:T(8,128)}, bf16[200,1024]{1,0:T(8,128)(2,1)S(1)}, bf16[200,768]{1,0:T(8,128)(2,1)S(1)}, bf16[200,768]{1,0:T(8,128)(2,1)S(1...) custom-call(s32[6]{0:T(128)S(1)} %stack.49.flag_ref, bf16[8,320,128]{2,1,0:T(8,128)(2,1)S(1)} %all-to-all-done.3.g_ref, ...), custom_call_target="tpu_custom_call" | custom-call | flops 153600 | bytes 4096 | tf_op jit(solution)/shard_map/qkv_back_long/pallas_call | solution.py:117
  224.8 5.3 %all-to-all-start.4 = ((bf16[8,24,1024]{2,1,0:T(8,128)(2,1)}), bf16[8,24,1024]{2,1,0:T(8,128)(2,1)}, u32[]{:S(2)}, u32[]{:S(2)}) async-start(bf16[8,24,1024]{2,1,0:T(8,128)(2,1)} %pack_rows.1), calls=%async_computation.4 | async-start | bytes 786432 | tf_op jit(solution)/shard_map/all_to_all | solution.py:1104
  234.6 4.7 %attn_grads.1 = (bf16[4,128,256]{2,1,0:T(8,128)(2,1)S(1)}, bf16[4,128,256]{2,1,0:T(8,128)(2,1)S(1)}, bf16[4,128,256]{2,1,0:T(8,128)(2,1)S(1)}, bf16[4,128,256]{2...) custom-call(s32[6]{0:T(128)S(1)} %stack.49.flag_ref, ...), custom_call_target="tpu_custom_call" | custom-call | flops 307200 | bytes 4096 | tf_op jit(solution)/shard_map/attn_grads/pallas_call | solution.py:117
  248.0 3.8 %token_back.1 = f32[200,1024]{1,0:T(8,128)} custom-call(s32[6]{0:T(128)S(1)} %stack.49.flag_ref, f32[200,1024]{1,0:T(8,128)} %get-tuple-element.214.l_ref, f32[200,1024]{1,0:T(8,128)} %get-tuple-element.215.s_ref, bf16[200,1024]{1,0:T(8,128)(2,1)S(1)} %collective-permute-done.25.r_ref, bf16[200,1024]{1,0:T(8,128)(2,1)} %tok_ref.3, ...), custom_call_target="tpu_custom_call" | custom-call | flops 1000 | bytes 4096 | tf_op jit(solution)/shard_map/token_back/pallas_call | solution.py:117
  255.5 5.5 %collective-permute-done.37 = bf16[2,2,128,256]{3,2,0,1:T(8,128)(2,1)S(1)} collective-permute-done((bf16[2,2,128,256]{3,2,0,1:T(8,128)(2,1)S(1)}, bf16[2,2,128,256]{3,2,0,1:T(8,128)(2,1)S(1)}, u32[]{:S(2)}, u32[]{:S(2)}) %collective-permute-start.37) | collective-permute-done | bytes 262176 | tf_op jit(solution)/shard_map/ppermute | solution.py:945
  265.3 5.6 %collective-permute-done.35 = bf16[2,128,256]{2,1,0:T(8,128)(2,1)S(1)} collective-permute-done((bf16[2,128,256]{2,1,0:T(8,128)(2,1)S(1)}, bf16[2,128,256]{2,1,0:T(8,128)(2,1)S(1)}, u32[]{:S(2)}, u32[]{:S(2)}) %collective-permute-start.35) | collective-permute-done | bytes 131104 | tf_op jit(solution)/shard_map/ppermute | solution.py:945
  273.9 3.6 %collective-permute-done.33 = bf16[128,256]{1,0:T(8,128)(2,1)S(1)} collective-permute-done((bf16[128,256]{1,0:T(8,128)(2,1)S(1)}, bf16[128,256]{1,0:T(8,128)(2,1)S(1)}, u32[]{:S(2)}, u32[]{:S(2)}) %collective-permute-start.33) | collective-permute-done | bytes 65568 | tf_op jit(solution)/shard_map/ppermute | solution.py:945
  277.6 4.2 %collective-permute-done.39 = bf16[128,256]{1,0:T(8,128)(2,1)S(1)} collective-permute-done((bf16[128,256]{1,0:T(8,128)(2,1)S(1)}, bf16[128,256]{1,0:T(8,128)(2,1)S(1)}, u32[]{:S(2)}, u32[]{:S(2)}) %collective-permute-start.39) | collective-permute-done | bytes 65568 | tf_op jit(solution)/shard_map/ppermute | solution.py:945
  288.2 3.8 %collective-permute-done.31 = bf16[160,1024]{1,0:T(8,128)(2,1)S(1)} collective-permute-done((bf16[160,1024]{1,0:T(8,128)(2,1)S(1)}, bf16[160,1024]{1,0:T(8,128)(2,1)S(1)}, u32[]{:S(2)}, u32[]{:S(2)}) %collective-permute-start.31) | collective-permute-done | bytes 327712 | tf_op jit(solution)/shard_map/ppermute | solution.py:945
  303.0 7.5 %collective-permute-done.40 = f32[32,1024]{1,0:T(8,128)S(1)} collective-permute-done((f32[32,1024]{1,0:T(8,128)S(1)}, f32[32,1024]{1,0:T(8,128)S(1)}, u32[]{:S(2)}, u32[]{:S(2)}) %collective-permute-start.40) | collective-permute-done | bytes 131104 | tf_op jit(solution)/shard_map/ppermute | solution.py:1280
  (293 shorter events, 105.1 us)
Async XLA Ops:
  5.8 11.0 %collective-permute-start = (bf16[200,1024]{1,0:T(8,128)(2,1)S(1)}, bf16[200,1024]{1,0:T(8,128)(2,1)S(1)}, u32[]{:S(2)}, u32[]{:S(2)}) collective-permute-start(bf16[200,1024]{1,0:T(8,128)(2,1)S(1)} %copy-done), channel_id=1, source_target_pairs={{0,2},{1,3},{2,0},{3,1},{4,6},{5,7},{6,4},{7,5},{8,10},{9,11},{10,... | collective-permute-start | bytes 1228808 | tf_op jit(solution)/shard_map/ppermute | solution.py:1098
  25.3 22.0 %all-to-all-start = ((bf16[8,320,128]{2,1,0:T(8,128)(2,1)}), bf16[8,320,128]{2,1,0:T(8,128)(2,1)S(1)}, u32[]{:S(2)}, u32[]{:S(2)}) async-start(bf16[8,320,128]{2,1,0:T(8,128)(2,1)} %get-tuple-element.138), calls=%async_computation | async-start | bytes 1310720 | tf_op jit(solution)/shard_map/all_to_all | solution.py:1104
  47.2 13.5 %collective-permute-start.4 = (bf16[200,1024]{1,0:T(8,128)(2,1)S(1)}, bf16[200,1024]{1,0:T(8,128)(2,1)S(1)}, u32[]{:S(2)}, u32[]{:S(2)}) collective-permute-start(bf16[200,1024]{1,0:T(8,128)(2,1)S(1)} %get-tuple-element.149.mg_ref.refs_4_), channel_id=1, source_target_pairs={{0,2},{1,3},{2,0},{3,1},{4,6},{5,7},{6,4},{7,5},{8,10},{9,11},{10,... | collective-permute-start | bytes 1228808 | tf_op jit(solution)/shard_map/ppermute | solution.py:1098
  83.3 10.0 %collective-permute-start.6 = (bf16[200,1024]{1,0:T(8,128)(2,1)S(1)}, bf16[200,1024]{1,0:T(8,128)(2,1)S(1)}, u32[]{:S(2)}, u32[]{:S(2)}) collective-permute-start(bf16[200,1024]{1,0:T(8,128)(2,1)S(1)} %get-tuple-element.168.hid_ref.refs_0_), channel_id=1, source_target_pairs={{0,2},{1,3},{2,0},{3,1},{4,6},{5,7},{6,4},{7,5},{8,10},{9,11},{10,... | collective-permute-start | bytes 1228808 | tf_op jit(solution)/shard_map/ppermute | solution.py:1098
  93.1 14.0 %collective-permute-start.8 = (bf16[2,200,1024]{2,1,0:T(8,128)(2,1)S(1)}, bf16[2,200,1024]{2,1,0:T(8,128)(2,1)S(1)}, u32[]{:S(2)}, u32[]{:S(2)}) collective-permute-start(bf16[2,200,1024]{2,1,0:T(8,128)(2,1)S(1)} %get-tuple-element.158), channel_id=1, source_target_pairs={{0,1},{1,0},{2,3},{3,2},{4,5},{5,4},{6,7},{7,6},{8,9},{9,8},{10,11... | collective-permute-start | bytes 2457608 | tf_op jit(solution)/shard_map/ppermute | solution.py:1101
  104.1 11.4 %collective-permute-start.7 = (bf16[200,1024]{1,0:T(8,128)(2,1)S(1)}, bf16[200,1024]{1,0:T(8,128)(2,1)S(1)}, u32[]{:S(2)}, u32[]{:S(2)}) collective-permute-start(bf16[200,1024]{1,0:T(8,128)(2,1)S(1)} %get-tuple-element.155), channel_id=1, source_target_pairs={{0,2},{1,3},{2,0},{3,1},{4,6},{5,7},{6,4},{7,5},{8,10},{9,11},{10,... | collective-permute-start | bytes 1228808 | tf_op jit(solution)/shard_map/ppermute | solution.py:1098
  106.2 16.4 %collective-permute-start.13 = (bf16[200,1024]{1,0:T(8,128)(2,1)S(1)}, bf16[200,1024]{1,0:T(8,128)(2,1)S(1)}, u32[]{:S(2)}, u32[]{:S(2)}) collective-permute-start(bf16[200,1024]{1,0:T(8,128)(2,1)S(1)} %get-tuple-element.168.hid_ref.refs_0_), channel_id=1, source_target_pairs={{0,1},{1,0},{2,3},{3,2},{4,5},{5,4},{6,7},{7,6},{8,9},{9,8},{10,11... | collective-permute-start | bytes 1228808 | tf_op jit(solution)/shard_map/ppermute | solution.py:1101
  106.8 15.8 %collective-permute-start.14 = (bf16[200,1024]{1,0:T(8,128)(2,1)S(1)}, bf16[200,1024]{1,0:T(8,128)(2,1)S(1)}, u32[]{:S(2)}, u32[]{:S(2)}) collective-permute-start(bf16[200,1024]{1,0:T(8,128)(2,1)S(1)} %collective-permute-done.6.hid_ref.refs_1_), channel_id=1, source_target_pairs={{0,1},{1,0},{2,3},{3,2},{4,5},{5,4},{6,7},{7,6},{8,9},{9,8},{10,11... | collective-permute-start | bytes 1228808 | tf_op jit(solution)/shard_map/ppermute | solution.py:1101
  120.4 9.4 %collective-permute-start.12 = (bf16[8,112,128]{2,1,0:T(8,128)(2,1)S(1)}, bf16[8,112,128]{2,1,0:T(8,128)(2,1)S(1)}, u32[]{:S(2)}, u32[]{:S(2)}) collective-permute-start(bf16[8,112,128]{2,1,0:T(8,128)(2,1)S(1)} %get-tuple-element.167), channel_id=1, source_target_pairs={{0,2},{1,3},{2,0},{3,1},{4,6},{5,7},{6,4},{7,5},{8,10},{9,11},{10,... | collective-permute-start | bytes 688136 | tf_op jit(solution)/shard_map/ppermute | solution.py:1098
  121.7 29.5 %collective-permute-start.17 = (bf16[2,2,128,1024]{3,2,1,0:T(8,128)(2,1)}, bf16[2,2,128,1024]{3,2,1,0:T(8,128)(2,1)}, u32[]{:S(2)}, u32[]{:S(2)}) collective-permute-start(bf16[2,2,128,1024]{3,2,1,0:T(8,128)(2,1)} %bitcast.18), channel_id=1, source_target_pairs={{0,4},{4,0},{8,12},{12,8},{16,20},{20,16},{24,28},{28,24},{1,5},{5... | collective-permute-start | bytes 3145736 | tf_op jit(solution)/shard_map/ppermute | solution.py:945
  129.8 18.6 %collective-permute-start.15 = (bf16[200,1024]{1,0:T(8,128)(2,1)S(1)}, bf16[200,1024]{1,0:T(8,128)(2,1)S(1)}, u32[]{:S(2)}, u32[]{:S(2)}) collective-permute-start(bf16[200,1024]{1,0:T(8,128)(2,1)S(1)} %get-tuple-element.178.go_ref), channel_id=1, source_target_pairs={{0,2},{1,3},{2,0},{3,1},{4,6},{5,7},{6,4},{7,5},{8,10},{9,11},{10,... | collective-permute-start | bytes 1228808 | tf_op jit(solution)/shard_map/ppermute | solution.py:1098
  131.2 17.2 %all-to-all-start.2 = ((bf16[8,112,128]{2,1,0:T(8,128)(2,1)}), bf16[8,112,128]{2,1,0:T(8,128)(2,1)S(1)}, u32[]{:S(2)}, u32[]{:S(2)}) async-start(bf16[8,112,128]{2,1,0:T(8,128)(2,1)} %broadcast_select_fusion.1), calls=%async_computation.2 | async-start | bytes 458752 | tf_op jit(solution)/shard_map/all_to_all | solution.py:1104
  158.4 47.9 %collective-permute-start.23 = (bf16[2,2,160,1024]{3,2,0,1:T(8,128)(2,1)}, bf16[2,2,160,1024]{3,2,0,1:T(8,128)(2,1)}, u32[]{:S(2)}, u32[]{:S(2)}) collective-permute-start(bf16[2,2,160,1024]{3,2,0,1:T(8,128)(2,1)} %copy.41), channel_id=1, source_target_pairs={{0,8},{4,12},{8,0},{12,4},{16,24},{20,28},{24,16},{28,20},{1,9},{5... | collective-permute-start | bytes 3932168 | tf_op jit(solution)/shard_map/ppermute | solution.py:945
  159.0 45.2 %collective-permute-start.24 = (bf16[2,128,1024]{2,1,0:T(8,128)(2,1)}, bf16[2,128,1024]{2,1,0:T(8,128)(2,1)}, u32[]{:S(2)}, u32[]{:S(2)}) collective-permute-start(bf16[2,128,1024]{2,1,0:T(8,128)(2,1)} %get-tuple-element.210), channel_id=1, source_target_pairs={{0,24},{4,28},{8,16},{12,20},{16,8},{20,12},{24,0},{28,4},{1,25},{... | collective-permute-start | bytes 1572872 | tf_op jit(solution)/shard_map/ppermute | solution.py:945
  179.7 11.9 %collective-permute-start.19 = (bf16[200,1024]{1,0:T(8,128)(2,1)}, bf16[200,1024]{1,0:T(8,128)(2,1)S(1)}, u32[]{:S(2)}, u32[]{:S(2)}) collective-permute-start(bf16[200,1024]{1,0:T(8,128)(2,1)} %get-tuple-element.194), channel_id=1, source_target_pairs={{0,2},{1,3},{2,0},{3,1},{4,6},{5,7},{6,4},{7,5},{8,10},{9,11},{10,... | collective-permute-start | bytes 1228808 | tf_op jit(solution)/shard_map/ppermute | solution.py:1098
  180.5 11.1 %collective-permute-start.20 = (bf16[8,200,128]{2,1,0:T(8,128)(2,1)}, bf16[8,200,128]{2,1,0:T(8,128)(2,1)S(1)}, u32[]{:S(2)}, u32[]{:S(2)}) collective-permute-start(bf16[8,200,128]{2,1,0:T(8,128)(2,1)} %get-tuple-element.196), channel_id=1, source_target_pairs={{0,1},{1,0},{2,3},{3,2},{4,5},{5,4},{6,7},{7,6},{8,9},{9,8},{10,11... | collective-permute-start | bytes 1228808 | tf_op jit(solution)/shard_map/ppermute | solution.py:1101
  185.0 30.9 %all-to-all-start.3 = ((bf16[8,320,128]{2,1,0:T(8,128)(2,1)}), bf16[8,320,128]{2,1,0:T(8,128)(2,1)S(1)}, u32[]{:S(2)}, u32[]{:S(2)}) async-start(bf16[8,320,128]{2,1,0:T(8,128)(2,1)} %finish_keys.2), calls=%async_computation.3 | async-start | bytes 1310720 | tf_op jit(solution)/shard_map/all_to_all | solution.py:1104
  194.5 14.8 %collective-permute-start.21 = (bf16[2,200,1024]{2,1,0:T(8,128)(2,1)S(1)}, bf16[2,200,1024]{2,1,0:T(8,128)(2,1)S(1)}, u32[]{:S(2)}, u32[]{:S(2)}) collective-permute-start(bf16[2,200,1024]{2,1,0:T(8,128)(2,1)S(1)} %copy-done.7), channel_id=1, source_target_pairs={{0,1},{1,0},{2,3},{3,2},{4,5},{5,4},{6,7},{7,6},{8,9},{9,8},{10,11... | collective-permute-start | bytes 2457608 | tf_op jit(solution)/shard_map/ppermute | solution.py:1101
  224.8 17.0 %all-to-all-start.4 = ((bf16[8,24,1024]{2,1,0:T(8,128)(2,1)}), bf16[8,24,1024]{2,1,0:T(8,128)(2,1)}, u32[]{:S(2)}, u32[]{:S(2)}) async-start(bf16[8,24,1024]{2,1,0:T(8,128)(2,1)} %pack_rows.1), calls=%async_computation.4 | async-start | bytes 786432 | tf_op jit(solution)/shard_map/all_to_all | solution.py:1104
  230.1 11.2 %collective-permute-start.25 = (bf16[200,1024]{1,0:T(8,128)(2,1)S(1)}, bf16[200,1024]{1,0:T(8,128)(2,1)S(1)}, u32[]{:S(2)}, u32[]{:S(2)}) collective-permute-start(bf16[200,1024]{1,0:T(8,128)(2,1)S(1)} %broadcast_select_fusion), channel_id=1, source_target_pairs={{0,2},{1,3},{2,0},{3,1},{4,6},{5,7},{6,4},{7,5},{8,10},{9,11},{10,... | collective-permute-start | bytes 1228808 | tf_op jit(solution)/shard_map/ppermute | solution.py:1098
  242.8 9.0 %collective-permute-start.29 = (bf16[2,2,128,256]{3,2,0,1:T(8,128)(2,1)S(1)}, bf16[2,2,128,256]{3,2,0,1:T(8,128)(2,1)S(1)}, u32[]{:S(2)}, u32[]{:S(2)}) collective-permute-start(bf16[2,2,128,256]{3,2,0,1:T(8,128)(2,1)S(1)} %copy.43), channel_id=1, source_target_pairs={{0,4},{4,0},{8,12},{12,8},{16,20},{20,16},{24,28},{28,24},{1,5},{5... | collective-permute-start | bytes 786440 | tf_op jit(solution)/shard_map/ppermute | solution.py:945
  243.6 19.2 %collective-permute-start.27 = (bf16[8,24,1024]{2,1,0:T(8,128)(2,1)}, bf16[8,24,1024]{2,1,0:T(8,128)(2,1)S(1)}, u32[]{:S(2)}, u32[]{:S(2)}) collective-permute-start(bf16[8,24,1024]{2,1,0:T(8,128)(2,1)} %all-to-all-done.4), channel_id=1, source_target_pairs={{0,2},{1,3},{2,0},{3,1},{4,6},{5,7},{6,4},{7,5},{8,10},{9,11},{10,... | collective-permute-start | bytes 1179656 | tf_op jit(solution)/shard_map/ppermute | solution.py:1098
  244.4 9.6 %collective-permute-start.34 = (bf16[2,2,128,256]{3,2,1,0:T(8,128)(2,1)}, bf16[2,2,128,256]{3,2,1,0:T(8,128)(2,1)S(1)}, u32[]{:S(2)}, u32[]{:S(2)}) collective-permute-start(bf16[2,2,128,256]{3,2,1,0:T(8,128)(2,1)} %bitcast.142), channel_id=1, source_target_pairs={{0,8},{4,12},{8,0},{12,4},{16,24},{20,28},{24,16},{28,20},{1,9},{5... | collective-permute-start | bytes 786440 | tf_op jit(solution)/shard_map/ppermute | solution.py:945
  245.5 15.5 %collective-permute-start.37 = (bf16[2,2,128,256]{3,2,0,1:T(8,128)(2,1)S(1)}, bf16[2,2,128,256]{3,2,0,1:T(8,128)(2,1)S(1)}, u32[]{:S(2)}, u32[]{:S(2)}) collective-permute-start(bf16[2,2,128,256]{3,2,0,1:T(8,128)(2,1)S(1)} %copy.45), channel_id=1, source_target_pairs={{0,24},{4,28},{8,16},{12,20},{16,8},{20,12},{24,0},{28,4},{1,25},{... | collective-permute-start | bytes 786440 | tf_op jit(solution)/shard_map/ppermute | solution.py:945
  251.9 13.3 %collective-permute-start.32 = (bf16[2,128,256]{2,1,0:T(8,128)(2,1)S(1)}, bf16[2,128,256]{2,1,0:T(8,128)(2,1)S(1)}, u32[]{:S(2)}, u32[]{:S(2)}) collective-permute-start(bf16[2,128,256]{2,1,0:T(8,128)(2,1)S(1)} %slice_bitcast_fusion.13), channel_id=1, source_target_pairs={{0,8},{4,12},{8,0},{12,4},{16,24},{20,28},{24,16},{28,20},{1,9},{5... | collective-permute-start | bytes 393224 | tf_op jit(solution)/shard_map/ppermute | solution.py:945
  252.5 29.3 %collective-permute-start.41 = (bf16[128,1024]{1,0:T(8,128)(2,1)S(1)}, bf16[128,1024]{1,0:T(8,128)(2,1)S(1)}, u32[]{:S(2)}, u32[]{:S(2)}) collective-permute-start(bf16[128,1024]{1,0:T(8,128)(2,1)S(1)} %copy-done.46), channel_id=1, source_target_pairs={{0,8},{4,12},{8,0},{12,4},{16,24},{20,28},{24,16},{28,20},{1,9},{5... | collective-permute-start | bytes 786440 | tf_op jit(solution)/shard_map/ppermute | solution.py:945
  254.0 28.7 %collective-permute-start.30 = (bf16[2,160,1024]{2,1,0:T(8,128)(2,1)S(1)}, bf16[2,160,1024]{2,1,0:T(8,128)(2,1)S(1)}, u32[]{:S(2)}, u32[]{:S(2)}) collective-permute-start(bf16[2,160,1024]{2,1,0:T(8,128)(2,1)S(1)} %copy-done.45), channel_id=1, source_target_pairs={{0,4},{4,0},{8,12},{12,8},{16,20},{20,16},{24,28},{28,24},{1,5},{5... | collective-permute-start | bytes 1966088 | tf_op jit(solution)/shard_map/ppermute | solution.py:945
  261.0 9.9 %collective-permute-start.35 = (bf16[2,128,256]{2,1,0:T(8,128)(2,1)S(1)}, bf16[2,128,256]{2,1,0:T(8,128)(2,1)S(1)}, u32[]{:S(2)}, u32[]{:S(2)}) collective-permute-start(bf16[2,128,256]{2,1,0:T(8,128)(2,1)S(1)} %slice_bitcast_fusion.10), channel_id=1, source_target_pairs={{0,24},{4,28},{8,16},{12,20},{16,8},{20,12},{24,0},{28,4},{1,25},{... | collective-permute-start | bytes 393224 | tf_op jit(solution)/shard_map/ppermute | solution.py:945
  262.9 9.5 %collective-permute-start.38 = (bf16[2,128,256]{2,1,0:T(8,128)(2,1)S(1)}, bf16[2,128,256]{2,1,0:T(8,128)(2,1)S(1)}, u32[]{:S(2)}, u32[]{:S(2)}) collective-permute-start(bf16[2,128,256]{2,1,0:T(8,128)(2,1)S(1)} %slice_bitcast_fusion.8), channel_id=1, source_target_pairs={{0,4},{4,0},{8,12},{12,8},{16,20},{20,16},{24,28},{28,24},{1,5},{5... | collective-permute-start | bytes 393224 | tf_op jit(solution)/shard_map/ppermute | solution.py:945
  265.2 18.7 %collective-permute-start.28 = (bf16[2,8,24,1024]{3,2,1,0:T(8,128)(2,1)S(1)}, bf16[2,8,24,1024]{3,2,1,0:T(8,128)(2,1)S(1)}, u32[]{:S(2)}, u32[]{:S(2)}) collective-permute-start(bf16[2,8,24,1024]{3,2,1,0:T(8,128)(2,1)S(1)} %get-tuple-element.265), channel_id=1, source_target_pairs={{0,1},{1,0},{2,3},{3,2},{4,5},{5,4},{6,7},{7,6},{8,9},{9,8},{10,11... | collective-permute-start | bytes 2359304 | tf_op jit(solution)/shard_map/ppermute | solution.py:1101
  293.0 17.6 %all-to-all-start.5 = ((bf16[4,32,1792]{2,1,0:T(8,128)(2,1)}), bf16[4,32,1792]{2,1,0:T(8,128)(2,1)S(1)}, u32[]{:S(2)}, u32[]{:S(2)}) async-start(bf16[4,32,1792]{2,1,0:T(8,128)(2,1)} %bitcast.53), calls=%async_computation.5 | async-start | bytes 917504 | tf_op jit(solution)/shard_map/all_to_all | solution.py:1264
  297.1 13.5 %collective-permute-start.40 = (f32[32,1024]{1,0:T(8,128)S(1)}, f32[32,1024]{1,0:T(8,128)S(1)}, u32[]{:S(2)}, u32[]{:S(2)}) collective-permute-start(f32[32,1024]{1,0:T(8,128)S(1)} %slice.222), channel_id=1, source_target_pairs={{0,0},{1,8},{2,16},{3,24},{4,1},{5,9},{6,17},{7,25},{8,2},{9,10},{... | collective-permute-start | bytes 393224 | tf_op jit(solution)/shard_map/ppermute | solution.py:1280
  (71 other events, 734.8 us)

commit v3 on v2

--- a/solution.py
+++ b/solution.py
@@ -139,22 +139,30 @@
     rows, width = tok_own.shape
     cols = lay.heads * DH
 
-    def body(flag_ref, own_ref, oth_ref, mod_ref, w_ref, b_ref, tc_ref, ts_ref, qc_ref, qs_ref, hid_ref, long_ref, short_ref):
+    def body(flag_ref, own_ref, oth_ref, mod_ref, w_ref, b_ref, tc_ref, ts_ref, qc_ref, qs_ref, hid_ref, long_ref, short_ref, both_ref):
         step = pl.program_id(0)
         own_long = flag_ref[0]
 
         @pl.when(step == 0)
         def _():
-            for src, base, slot in ((own_ref, 0, 1 - own_long), (oth_ref, 2, own_long)):
+            hidden = []
+            for src, base in ((own_ref, 0), (oth_ref, 2)):
                 normed, _ = norm_rows(src[...].astype(F32))
                 shift = per_frame(normed.shape, mod_ref[base : base + 1, :width], mod_ref[base + 1 : base + 2, :width])
                 scale = per_frame(
                     normed.shape, mod_ref[base : base + 1, width : 2 * width], mod_ref[base + 1 : base + 2, width : 2 * width]
                 )
-                hid_ref[slot] = (normed * (1.0 + scale) + shift).astype(BF)
-
+                hidden.append(normed * (1.0 + scale) + shift)
+            swapped = own_long == 0
+            first = jnp.where(swapped, hidden[1], hidden[0])
+            second = jnp.where(swapped, hidden[0], hidden[1])
+            hid_ref[0] = first.astype(BF)
+            hid_ref[1] = second.astype(BF)
+            both_ref[...] = jnp.concatenate([first, second], axis=0).astype(BF)
+
+        result = dot(both_ref[...], w_ref[...]) + b_ref[...]
         for slot, out_ref in ((0, long_ref), (1, short_ref)):
-            acc = dot(hid_ref[slot], w_ref[...]) + b_ref[...]
+            acc = result[slot * rows : (slot + 1) * rows]
 
             def rotated(pair):
                 value = acc[:, pair * LANES : (pair + 1) * LANES]
@@ -195,6 +203,7 @@
             pl.BlockSpec((1, cols), lambda j, f: (0, 2 * j + f[1])),
             None, None, None, None,
         ],
+        scratch=[pltpu.VMEM((2 * rows, width), BF)],
         out_pins=(0,),
         grid=(3,),
         flops=12 * rows * width * cols,
@@ -535,28 +544,60 @@
     )
 
 
-def mlp_both(flags, hidden, mlp_grad, up_weight, up_bias, down_weight, lay, out_dtype, name):
+def hidden_blocks(width, wide, chunks, weight_rows):
+    def pick(k):
+        def at(i, f):
+            block = 2 * (chunks * i + k) + f[1]
+            return (block, 0) if weight_rows else (0, block)
+        return at
+
+    return [pl.BlockSpec((wide, width) if weight_rows else (width, wide), pick(k)) for k in range(chunks)]
+
+
+def ahead_grads(flags, mlp_grad, down_weight, name):
+    rows, width = mlp_grad.shape
+    ff = down_weight.shape[0]
+    wide, chunks = 2 * LANES, 2
+
+    def body(flag_ref, mg_ref, *refs):
+        out_ref = refs[-1]
+        for k in range(chunks):
+            out_ref[:, k * wide : (k + 1) * wide] = dot_lanes(mg_ref[...], refs[k][...])
+
+    return kernel_call(
+        body,
+        flags,
+        [mlp_grad] + [down_weight] * chunks,
+        [shape_of((rows, ff // 2), F32)],
+        specs=[None] + hidden_blocks(width, wide, chunks, True),
+        out_specs=[pl.BlockSpec((rows, chunks * wide), lambda i, f: (0, i))],
+        out_pins=(0,),
+        grid=(ff // (2 * wide * chunks),),
+        flops=rows * width * ff,
+        name=name,
+    )[0]
+
+
+def hidden_grads(flags, hidden, ahead, up_weight, up_bias, lay, out_dtype, name):
     rows, width = hidden.shape
     ff = up_weight.shape[1]
-    wide = 2 * LANES
-    chunks = 2
+    wide, chunks = 2 * LANES, 2
     steps = ff // (2 * wide * chunks)
     quarter = ff // 4
 
-    def body(flag_ref, hid_ref, mg_ref, *refs):
-        weights, outs = refs[: 3 * chunks], refs[3 * chunks :]
-        mine_ref, send_ref, bm_ref, bt_ref, mlp_ref, hg_ref, macc, hacc = outs
+    def body(flag_ref, hid_ref, ahead_ref, *refs):
+        weights, outs = refs[: 2 * chunks], refs[2 * chunks :]
+        mine_ref, send_ref, bm_ref, bt_ref, hg_ref, hacc = outs
         step = pl.program_id(0)
         first = flag_ref[2] == 0
-        mlp, back = 0.0, 0.0
+        back = 0.0
         for k in range(chunks):
-            up_ref, ub_ref, dn_ref = weights[3 * k : 3 * k + 3]
+            up_ref, ub_ref = weights[k], weights[chunks + k]
             pre = dot(hid_ref[...], up_ref[...]) + ub_ref[...]
             tanh = jnp.tanh(GELU_C * (pre + GELU_K * pre * pre * pre))
             act = (0.5 * pre * (1.0 + tanh)).astype(BF)
             slope = 0.5 * (1.0 + tanh) + 0.5 * pre * (1.0 - tanh * tanh) * GELU_C * (1.0 + 3.0 * GELU_K * pre * pre)
-            pre_low = (dot_lanes(mg_ref[...], dn_ref[...]) * slope).astype(BF)
-            mlp = mlp + dot(act, dn_ref[...])
+            pre_low = (ahead_ref[:, k * wide : (k + 1) * wide] * slope).astype(BF)
             back = back + dot_lanes(pre_low, up_ref[...])
             sums = jnp.sum(pre_low.astype(F32), axis=0, keepdims=True)
             lanes = slice(k * LANES, (k + 1) * LANES)
@@ -568,41 +609,78 @@
 
         @pl.when(step == 0)
         def _():
-            macc[...] = mlp
             hacc[...] = back
 
         @pl.when(step > 0)
         def _():
-            macc[...] += mlp
             hacc[...] += back
 
         @pl.when(step == steps - 1)
         def _():
-            mlp_ref[...] = macc[...].astype(mlp_ref.dtype)
             hg_ref[...] = hacc[...].astype(hg_ref.dtype)
 
     chunk = pl.BlockSpec((2, rows, chunks * LANES), lambda i, f: (0, 0, i))
     bchunk = pl.BlockSpec((8, chunks * LANES), lambda i, f: (0, i))
-    weight_args, weight_specs = [], []
-    for k in range(chunks):
-        weight_args += [up_weight, up_bias, down_weight]
-        weight_specs += [
-            pl.BlockSpec((width, wide), lambda i, f, k=k: (0, 2 * (chunks * i + k) + f[1])),
-            pl.BlockSpec((1, wide), lambda i, f, k=k: (0, 2 * (chunks * i + k) + f[1])),
-            pl.BlockSpec((wide, width), lambda i, f, k=k: (2 * (chunks * i + k) + f[1], 0)),
-        ]
-    return kernel_call(
-        body,
-        flags,
-        [hidden, mlp_grad, *weight_args],
-        [shape_of((2, rows, quarter), BF)] * 2 + [shape_of((8, quarter), F32)] * 2 + [shape_of((rows, width), out_dtype)] * 2,
-        specs=[None, None] + weight_specs,
-        out_specs=[chunk, chunk, bchunk, bchunk, None, None],
+    return kernel_call(
+        body,
+        flags,
+        [hidden, ahead] + [up_weight] * chunks + [up_bias] * chunks,
+        [shape_of((2, rows, quarter), BF)] * 2 + [shape_of((8, quarter), F32)] * 2 + [shape_of((rows, width), out_dtype)],
+        specs=[None, pl.BlockSpec((rows, chunks * wide), lambda i, f: (0, i))]
+        + hidden_blocks(width, wide, chunks, False)
+        + hidden_blocks(1, wide, chunks, False),
+        out_specs=[chunk, chunk, bchunk, bchunk, None],
         grid=(steps,),
-        scratch=[pltpu.VMEM((rows, width), F32), pltpu.VMEM((rows, width), F32)],
-        vmem=20,
-        flops=4 * rows * width * ff,
+        scratch=[pltpu.VMEM((rows, width), F32)],
+        pins=(1,),
+        flops=2 * rows * width * ff,
         name=name,
+    )
+
+
+def forward_rows(flags, mine, send, mine2, send2, down_weight):
+    _, rows, quarter = mine.shape
+    ff, width = down_weight.shape
+    wide, chunks = 2 * LANES, 2
+    steps = ff // (2 * wide * chunks)
+
+    def body(flag_ref, m_ref, s_ref, m2_ref, s2_ref, *refs):
+        own_ref, oth_ref, acc_ref = refs[chunks:]
+        first = flag_ref[2] == 0
+        step = pl.program_id(0)
+        for at, (a_ref, b_ref) in enumerate(((m_ref, s_ref), (m2_ref, s2_ref))):
+            total = 0.0
+            for k in range(chunks):
+                lanes = slice(k * LANES, (k + 1) * LANES)
+                a, b = a_ref[:, lanes], b_ref[:, lanes]
+                act = jnp.concatenate([jnp.where(first, a, b), jnp.where(first, b, a)], axis=1)
+                total = total + dot(act, refs[k][...])
+
+            @pl.when(step == 0)
+            def _(total=total, at=at):
+                acc_ref[at] = total
+
+            @pl.when(step > 0)
+            def _(total=total, at=at):
+                acc_ref[at] += total
+
+        @pl.when(step == steps - 1)
+        def _():
+            own_ref[...] = acc_ref[0]
+            oth_ref[...] = acc_ref[1].astype(BF)
+
+    chunk = pl.BlockSpec((None, rows, chunks * LANES), lambda i, f: (0, 0, i))
+    return kernel_call(
+        body,
+        flags,
+        [mine, send, mine2, send2] + [down_weight] * chunks,
+        [shape_of((rows, width), F32), shape_of((rows, width), BF)],
+        specs=[chunk] * 4 + hidden_blocks(width, wide, chunks, True),
+        scratch=[pltpu.VMEM((2, rows, width), F32)],
+        out_pins=(0,),
+        grid=(steps,),
+        flops=2 * rows * width * ff,
+        name="forward_rows",
     )
 
 
@@ -806,92 +884,79 @@
     )[0]
 
 
-def add_head_rows(flags, part, got, send, keep, order):
-    half_blk, total, width = send.shape
-    n_blk = 2 * half_blk
-    rows = part.shape[1] // n_blk
-    bit = order[0]
-
-    def body(flag_ref, part_ref, got_ref, send_in, keep_in, send_ref, keep_ref):
-        both = (part_ref[flag_ref[2]].astype(F32) + got_ref[...].astype(F32)).astype(BF)
-        for target in range(n_blk):
-            place = relative_place(target, flag_ref[4], n_blk)
-            at = ((place >> (bit + 1)) << bit) | (place & ((1 << bit) - 1))
-            value = both[target * rows : (target + 1) * rows]
-            sent = (place >> bit) & 1
-
-            @pl.when(sent == 1)
-            def _(value=value, at=at):
-                send_ref[at] = value
-
-            @pl.when(sent == 0)
-            def _(value=value, at=at):
-                keep_ref[at] = value
-
-    block = pl.BlockSpec((half_blk, rows, width), lambda i, f: (0, (total - rows) // rows, 0))
-    return kernel_call(
-        body,
-        flags,
-        [part, got, send, keep],
-        [shape_of(send.shape, BF)] * 2,
-        specs=[None, None, pl.BlockSpec(memory_space=pl.ANY), pl.BlockSpec(memory_space=pl.ANY)],
-        out_specs=[block, block],
-        pins=(2, 3),
-        out_pins=(0, 1),
-        aliases={3: 0, 4: 1},
-        flops=rows * width * n_blk,
-        name="add_head_rows",
-    )
-
-
-def group_spec(pair, rows, wide, moves, per):
+def group_spec(pair, rows, wide, moves):
     index = pair[1]
     if index is None:
-        return pl.BlockSpec((rows, wide), lambda i, f: (0, i // per if moves else 0))
-    return pl.BlockSpec((None, rows, wide), lambda i, f: (index, 0, i // per if moves else 0))
-
-
-def split_weight_grads(flags, lefts, rights, n_blk, orders, extra, name):
-    count = len(lefts)
-    rows, depth = lefts[0][0].shape[-2:]
-    pieces = len(orders)
-    cols = rights[0][0].shape[-1] // pieces
+        return pl.BlockSpec((rows, wide), lambda i, f: (0, i if moves else 0))
+    return pl.BlockSpec((None, rows, wide), lambda i, f: (index, 0, i if moves else 0))
+
+
+def width_of(jobs):
+    return sum(rights[0][0].shape[-1] for _, rights in jobs)
+
+
+def split_weight_grads(flags, jobs, n_blk, cuts, head_rows, name):
+    count = len(jobs[0][0])
+    rows, depth = jobs[0][0][0][0].shape[-2:]
+    pieces = [(job, *cut) for job, many in enumerate(cuts) for cut in many]
     tall = depth // n_blk
     wide = max(tall, LANES)
     per = wide // tall
+    operands = [pair for lefts, rights in jobs for pair in [*lefts, *rights]]
+    extra = 0
+    if head_rows:
+        head = head_rows[0].shape[1] // n_blk
+        turns = head_rows[0].shape[2] // cuts[0][-1][1]
+        extra = head * turns
 
     def body(flag_ref, *refs):
-        outs = refs[2 * count :]
-        acc = dot_rows(refs[0][...], refs[count][...])
-        for k in range(1, count):
-            acc += dot_rows(refs[k][...], refs[count + k][...])
-        low = acc.astype(BF)
+        outs = refs[len(operands) + len(head_rows) :]
+        step = pl.program_id(0)
+        results = []
+        for job in range(len(jobs)):
+            mine = refs[2 * count * job : 2 * count * (job + 1)]
+            acc = dot_rows(mine[0][...], mine[count][...])
+            for k in range(1, count):
+                acc += dot_rows(mine[k][...], mine[count + k][...])
+            results.append(acc.astype(BF))
         for member in range(per):
-            part = low[member * tall : (member + 1) * tall]
-            place = relative_place(pl.program_id(0) * per + member, flag_ref[4], n_blk)
-            for piece, order in enumerate(orders):
-                bit = order[0]
-                at = ((place >> (bit + 1)) << bit) | (place & ((1 << bit) - 1))
-                value = part[:, piece * cols : (piece + 1) * cols]
-                sent = (place >> bit) & 1
-
-                @pl.when(sent == 1)
-                def _(value=value, at=at, piece=piece):
-                    outs[2 * piece][at, :tall] = value
-
-                @pl.when(sent == 0)
-                def _(value=value, at=at, piece=piece):
-                    outs[2 * piece + 1][at, :tall] = value
-
-    return kernel_call(
-        body,
-        flags,
-        [array for array, _ in [*lefts, *rights]],
-        [shape_of((n_blk // 2, tall + extra, cols), BF)] * (2 * pieces),
-        specs=[group_spec(pair, rows, wide, True, 1) for pair in lefts]
-        + [group_spec(pair, rows, cols * pieces, False, 1) for pair in rights],
+            place = relative_place(step * per + member, flag_ref[4], n_blk)
+            if head_rows:
+                part_ref, got_ref = refs[len(operands) : len(operands) + 2]
+                at = pl.ds(pl.multiple_of((step * per + member) * head, head), head)
+                both = (part_ref[flag_ref[2], at].astype(F32) + got_ref[at].astype(F32)).astype(BF)
+            for out, (job, start, cols, order) in enumerate(pieces):
+                sent, at = half_place(place, order)
+                values = [results[job][member * tall : (member + 1) * tall, start : start + cols]]
+                if head_rows and out == len(pieces) - 1:
+                    values += [both[:, turn * cols : (turn + 1) * cols] for turn in range(turns)]
+
+                def store(out_ref, values=values, at=at):
+                    row = 0
+                    for value in values:
+                        out_ref[at, row : row + value.shape[0]] = value
+                        row += value.shape[0]
+
+                pl.when(sent == 1)(functools.partial(store, outs[2 * out]))
+                pl.when(sent == 0)(functools.partial(store, outs[2 * out + 1]))
+
+    specs = []
+    for lefts, rights in jobs:
+        specs += [group_spec(pair, rows, wide, True) for pair in lefts]
+        specs += [group_spec(pair, rows, pair[0].shape[-1], False) for pair in rights]
+    outs = []
+    for out, (job, start, cols, order) in enumerate(pieces):
+        outs += [shape_of((n_blk // 2, tall + (extra if out == len(pieces) - 1 else 0), cols), BF)] * 2
+    return kernel_call(
+        body,
+        flags,
+        [array for array, _ in operands] + list(head_rows),
+        outs,
+        specs=specs + [None] * len(head_rows),
         grid=(depth // wide,),
-        flops=2 * count * rows * depth * cols * pieces,
+        vmem=24,
+        pins=tuple(range(len(operands))) if head_rows else (),
+        flops=2 * count * rows * depth * width_of(jobs),
         name=name,
     )
 
@@ -926,6 +991,13 @@
     return relative ^ ((relative >> 1) & (10 & (n_blk - 1)))
 
 
+def half_place(place, order):
+    at = 0
+    for bit in order[1:]:
+        at = 2 * at + ((place >> bit) & 1)
+    return (place >> order[0]) & 1, at
+
+
 def hop_of(bit):
     return (1 << bit) if bit == 0 or bit % 2 == 1 else (1 << bit) | (1 << (bit - 1))
 
@@ -934,31 +1006,26 @@
     def __init__(self, send, keep, n_blk, order):
         self.n_blk, self.order, self.at = n_blk, order, 0
         self.bits = n_blk.bit_length() - 1
-        self.axes = [bit for bit in range(self.bits)[::-1] if bit != order[0]]
-        self.send = send.reshape((2,) * (self.bits - 1) + send.shape[1:])
-        self.keep = keep.reshape((2,) * (self.bits - 1) + keep.shape[1:])
-        self.value = None
-
-    def step(self, starts=(), ends=()):
+        self.send, self.keep, self.value, self.got = send, keep, None, None
+
+    def move(self, *starts):
         hop = hop_of(self.order[self.at])
         send = after(self.send, *starts) if starts else self.send
-        got = lax.ppermute(send, "blk", [(i, i ^ hop) for i in range(self.n_blk)])
-        if ends:
-            got = after(got, *ends)
-        value = self.keep.astype(F32) + got.astype(F32)
+        self.got = lax.ppermute(send, "blk", [(i, i ^ hop) for i in range(self.n_blk)])
+
+    def add(self):
         self.at += 1
-        if self.at < self.bits:
-            axis = self.axes.index(self.order[self.at])
-            self.axes.pop(axis)
-            index = (slice(None),) * axis
-            value = value.astype(BF)
-            self.send, self.keep = value[index + (1,)], value[index + (0,)]
-        self.value = value
-        return value
+        half = self.keep.shape[0] // 2
+        if self.at == self.bits:
+            self.value = (self.keep.astype(F32) + self.got.astype(F32))[0]
+        else:
+            low = [(self.keep[k].astype(F32) + self.got[k].astype(F32)).astype(BF) for k in (slice(half), slice(half, None))]
+            self.keep, self.send = low
 
     def finish(self):
         while self.at < self.bits:
-            self.step()
+            self.move()
+            self.add()
         return self.value
 
 
@@ -1103,10 +1170,6 @@
     def spread(value):
         return lax.all_to_all(value, "blk", split_axis=0, concat_axis=0, tiled=True)
 
-    def gather_rest(many):
-        both = jnp.stack([many, swap_side(many)])
-        return jnp.stack([both, swap_core(both)])
-
     long_first = frame_clip[::FB] == n_blk
     own_long_b = lax.dynamic_index_in_dim(long_first, blk, 0, False) == (side == 0)
     own_long = own_long_b.astype(jnp.int32)
@@ -1119,7 +1182,6 @@
     first_mod = dot(silu, mod_weight[:, : 2 * width]) + bias[: 2 * width]
     first_mods = jnp.concatenate([first_mod, swap_side(first_mod)], axis=0)
     rest_mod = dot(after(silu, first_mod), mod_weight[:, 2 * width :]) + bias[2 * width :]
-    first_mods, rest_mod = lax.optimization_barrier((first_mods, rest_mod))
 
     block_time = frame_index.reshape(n_blk, FB)
     head_time, tail_time = block_time[:, : FB // 2], block_time[:, FB // 2 :]
@@ -1131,6 +1193,11 @@
     short_cos, short_sin = time_cos[frames:, None], time_sin[frames:, None]
     long_cos, long_sin = long_cos[:, None], long_sin[:, None]
     tab_cos, tab_sin = (jnp.asarray(t) for t in rotary_static(frames))
+    own_long_all = (long_first[None, :] == ((side ^ jnp.arange(2)) == 0)[:, None]).astype(F32)
+    long_rows = jnp.broadcast_to(own_long_all[None, :, :, None, None], (2, 2, n_blk, PACK, LANES)).reshape(-1, LANES)
+    first_mods, rest_mod, long_cos, long_sin, short_cos, short_sin, long_rows = lax.optimization_barrier(
+        (first_mods, rest_mod, long_cos, long_sin, short_cos, short_sin, long_rows)
+    )
 
     gate2 = rest_mod[:, 3 * width :]
     mid_mods = jnp.concatenate([rest_mod[:, :width], rest_mod[:, width : 2 * width], rest_mod[:, 2 * width : 3 * width]], axis=0)
@@ -1144,7 +1211,8 @@
     out_short, ot_short, lse_short = attend(flags, qkv_short, short_oth, lay, False)
     mlp_grad, down_b = scale_cotangent(flags, after(cotangent, qkv_long), gate2)
     mlp_grad_oth = swap_side(mlp_grad)
-    long_own, out_short, mlp_grad = lax.optimization_barrier((long_own, out_short, mlp_grad))
+    ahead_own = ahead_grads(flags, mlp_grad, down_weight, "ahead_own")
+    long_own, out_short, mlp_grad, ahead_own = lax.optimization_barrier((long_own, out_short, mlp_grad, ahead_own))
     long_oth = swap_core(long_own)
     out_long_all, ot_long, lse_long = attend(flags, long_own, long_oth, lay, True)
     out_long_all, mlp_grad_oth = lax.optimization_barrier((out_long_all, mlp_grad_oth))
@@ -1154,7 +1222,9 @@
             return value
         return lax.dynamic_slice_in_dim(value, ((blk // 2) % parts) * heads, heads, 0)
 
+    ahead_oth = ahead_grads(flags, mlp_grad_oth, down_weight, "ahead_other")
     out_long = own_part(spread(out_long_all))
+    out_long, ahead_oth = lax.optimization_barrier((out_long, ahead_oth))
     out_recv = swap_side(jnp.where(own_long_b, out_short, out_long))
     branch, resid, normed2, inv2, hidden2 = project_and_norm(
         flags, out_long, out_short, out_recv, proj_weight, proj_bias.astype(F32)[None], tokens, mid_mods, lay
@@ -1162,13 +1232,9 @@
 
     hidden2_oth = swap_side(hidden2)
     up_b = up_bias.astype(F32)[None]
-    mine, send, bm, bt, mlp_own, hid_own = mlp_both(
-        flags, hidden2, mlp_grad, up_weight, up_b, down_weight, lay, F32, "mlp_own"
-    )
-    hidden2_oth, mlp_own, hid_own = lax.optimization_barrier((hidden2_oth, mlp_own, hid_own))
-    mine2, send2, bm2, bt2, mlp_oth, hid_oth = mlp_both(
-        flags, hidden2_oth, mlp_grad_oth, up_weight, up_b, down_weight, lay, BF, "mlp_other"
-    )
+    mine, send, bm, bt, hid_own = hidden_grads(flags, hidden2, ahead_own, up_weight, up_b, lay, F32, "hidden_own")
+    hidden2_oth, hid_own = lax.optimization_barrier((hidden2_oth, hid_own))
+    mine2, send2, bm2, bt2, hid_oth = hidden_grads(flags, hidden2_oth, ahead_oth, up_weight, up_b, lay, BF, "hidden_other")
     hid_recv = swap_side(hid_oth)
 
     got, got2 = swap_core(send), swap_core(send2)
@@ -1176,23 +1242,27 @@
     plain = lambda *arrays: [(v, None) for v in arrays]
     blocks = [mine, mine2, got, got2]
     bits = list(range(n_blk.bit_length() - 1))
-    orders = [bits[k % len(bits) :] + bits[: k % len(bits)] for k in range(3)]
-    down_order, up_order = [0, 2, 1] + bits[3:], [1, 0, 2] + bits[3:]
-    down_send, down_keep = split_weight_grads(
-        flags, [(v, 0) for v in blocks], plain(mlp_grad, mlp_grad_oth, mg_c, mg_c2), n_blk, [down_order], 0, "down_grads"
-    )
-    hid_recv, down_send, down_keep = lax.optimization_barrier((hid_recv, down_send, down_keep))
+    orders = [bits, [1, 0] + bits[2:]]
+    down_order, up_order = ([0, 2, 1], [1, 0, 2]) if len(bits) == 3 else (bits, bits)
+    mlp_halves = split_weight_grads(
+        flags,
+        [
+            ([(v, 0) for v in blocks], plain(mlp_grad, mlp_grad_oth, mg_c, mg_c2)),
+            (plain(hidden2, hidden2_oth, hid_c, hid_c2), [(v, 1) for v in blocks]),
+        ],
+        n_blk, [[(0, width, down_order)], [(0, width, up_order)]], [], "mlp_grads",
+    )
+    hid_recv, *mlp_halves = lax.optimization_barrier((hid_recv, *mlp_halves))
 
     resid_grad, branch_grad, do_keep, do_send, mid_sums = branch_back(
         flags, hid_own, hid_recv, cotangent, normed2, inv2, branch, mid_mods, proj_weight, lay
     )
-    down_sum = CubeSum(down_send, down_keep, n_blk, down_order)
+    mlp_sums = [CubeSum(*mlp_halves[:2], n_blk, down_order), CubeSum(*mlp_halves[2:], n_blk, up_order)]
+    for part in mlp_sums:
+        part.move()
     do_recv = swap_side(do_send)
-    hid_late = after(hidden2, do_send)
-    up_send, up_keep = split_weight_grads(
-        flags, plain(hid_late, hidden2_oth, hid_c, hid_c2), [(v, 1) for v in blocks], n_blk, [up_order], width // 4 // n_blk, "up_grads"
-    )
-    do_recv, up_send, up_keep = lax.optimization_barrier((do_recv, up_send, up_keep))
+    mlp_own, mlp_oth = forward_rows(flags, mine, send, mine2, after(send2, do_send), down_weight)
+    do_recv, mlp_own, mlp_oth = lax.optimization_barrier((do_recv, mlp_own, mlp_oth))
     do_long = jnp.where(own_long_b, do_keep, do_recv)
     if parts > 1:
         hot = (jnp.arange(parts) == (blk // 2) % parts)[:, None, None, None]
@@ -1205,21 +1275,22 @@
     )
     branch_grad_oth = swap_side(after(branch_grad, do_recv))
     mlp_recv = swap_side(after(mlp_oth, branch_grad_oth))
-    do_all, dq_s, mine_s, theirs_s, branch_grad_oth = lax.optimization_barrier((do_all, dq_s, mine_s, theirs_s, branch_grad_oth))
-    proj_part = head_weight_grads(flags, out_long, out_short, branch_grad, branch_grad_oth, lay)
-    proj_part = proj_part.reshape(2, -1, width)
-    proj_got = swap_core(jnp.where(core == 0, proj_part[1], proj_part[0]))
-    up_send, up_keep = add_head_rows(flags, proj_part, proj_got, up_send, up_keep, up_order)
-    up_sum = CubeSum(up_send, up_keep, n_blk, up_order)
-    down_sum.step()
-    do_all, up_sum.send, down_sum.send, down_sum.keep = lax.optimization_barrier(
-        (do_all, up_sum.send, down_sum.send, down_sum.keep)
-    )
+    do_all, dq_s, mine_s, theirs_s, branch_grad_oth, mlp_sums[0].got, mlp_sums[1].got = lax.optimization_barrier(
+        (do_all, dq_s, mine_s, theirs_s, branch_grad_oth, mlp_sums[0].got, mlp_sums[1].got)
+    )
+    for part in mlp_sums:
+        part.add()
+    do_all, mlp_sums[0].send, mlp_sums[1].send = lax.optimization_barrier((do_all, mlp_sums[0].send, mlp_sums[1].send))
+    for part in mlp_sums:
+        part.move()
 
     dq_l, mine_l, theirs_l = attend_back(
         flags, long_own, long_oth, [do_all], ot_long, lse_long, tab_cos, tab_sin, long_cos, long_sin, lay, True
     )
-    grads_sent = finish_keys(flags, dq_l, mine_l, swap_core(theirs_l), tab_cos, tab_sin, long_cos, long_sin, lay, True)
+    theirs_l, mlp_sums[0].got, mlp_sums[1].got = lax.optimization_barrier(
+        (swap_core(theirs_l), mlp_sums[0].got, mlp_sums[1].got)
+    )
+    grads_sent = finish_keys(flags, dq_l, mine_l, theirs_l, tab_cos, tab_sin, long_cos, long_sin, lay, True)
     grads_all = spread(grads_sent)
     if parts > 1:
         grads_long = jnp.sum(grads_all.astype(F32).reshape((parts, heads) + grads_all.shape[1:]), axis=0).astype(BF)
@@ -1227,43 +1298,77 @@
         grads_long = grads_all
 
     theirs_s = swap_core(theirs_s)
-    mlp_recv, dq_s, theirs_s, _ = lax.optimization_barrier((mlp_recv, dq_s, theirs_s, grads_sent))
-    down_sum.step(ends=(grads_sent,))
-    up_sum.step(ends=(grads_sent,))
+    branch_grad_oth, dq_s, theirs_s, mlp_sums[0].got, mlp_sums[1].got, _ = lax.optimization_barrier(
+        (branch_grad_oth, dq_s, theirs_s, mlp_sums[0].got, mlp_sums[1].got, grads_sent)
+    )
+    for part in mlp_sums:
+        part.add()
     grads_short = finish_keys(flags, dq_s, mine_s, theirs_s, tab_cos, tab_sin, short_cos, short_sin, lay, False)
     hidS, hidS_low, gmS, gtS, abS, sumS = qkv_back(flags, grads_short, tokens, tok_oth, attn_weight, lay, False)
-    output, gate2_sums = layer_output(flags, mlp_own, mlp_recv, down_bias.astype(F32)[None], resid, cotangent, gate2)
+    output, gate2_sums = layer_output(flags, mlp_own, after(mlp_recv, grads_sent), down_bias.astype(F32)[None], resid, cotangent, gate2)
+    proj_part = head_weight_grads(flags, out_long, out_short, branch_grad, branch_grad_oth, lay).reshape(2, -1, width)
+    proj_got = swap_core(jnp.where(core == 0, proj_part[1], proj_part[0]))
     h1_core = swap_core(hidden1)
     gtS_got = swap_core(gtS)
-    grads_long, output, h1_core, gtS_got, hidS_low, up_sum.send, up_sum.keep, down_sum.send, down_sum.keep = lax.optimization_barrier(
-        (grads_long, output, h1_core, gtS_got, hidS_low, up_sum.send, up_sum.keep, down_sum.send, down_sum.keep)
-    )
+    grads_long, hidS_low, gate2_sums, mlp_sums[0].send, mlp_sums[1].send = lax.optimization_barrier(
+        (grads_long, hidS_low, gate2_sums, mlp_sums[0].send, mlp_sums[1].send)
+    )
+    for part in mlp_sums:
+        part.move()
 
     hidL, hidL_low, gmL, gtL, abL, sumL = qkv_back(flags, grads_long, tokens, tok_oth, attn_weight, lay, True)
     gtL_got = swap_core(gtL)
     hid1_recv = swap_side(jnp.where(own_long_b, hidS_low, hidL_low))
     pack = pack_rows(flags, n_blk, mid_sums, gate2_sums, silu, down_b, (bm, bm2, bt, bt2), sumL, sumS, abL, abS)
+    many = spread(pack)
+    quarter = 3 * width // n_uly
+    split = 2 * quarter // 3
     halves = split_weight_grads(
-        flags, [(hidden1, 0), (hidden1, 1), (h1_core, 0), (h1_core, 1)], plain(gmL, gmS, after(gtL_got, pack), gtS_got),
-        n_blk, orders, 0, "attn_grads"
-    )
-    many = spread(pack)
-    hid1_recv, many, *halves = lax.optimization_barrier((hid1_recv, many, *halves))
-    packs = gather_rest(many).reshape(-1, width)
-    attn_sums = [CubeSum(halves[2 * k], halves[2 * k + 1], n_blk, order) for k, order in enumerate(orders)]
+        flags,
+        [([(hidden1, 0), (hidden1, 1), (h1_core, 0), (h1_core, 1)], plain(gmL, gmS, after(gtL_got, pack), gtS_got))],
+        n_blk, [[(0, split, orders[0]), (split, quarter - split, orders[1])]], [proj_part, proj_got], "attn_grads",
+    )
+    hid1_recv, mlp_sums[0].got, mlp_sums[1].got, *halves = lax.optimization_barrier(
+        (hid1_recv, mlp_sums[0].got, mlp_sums[1].got, *halves)
+    )
+    attn_sums = [CubeSum(*halves[2 * k : 2 * k + 2], n_blk, order) for k, order in enumerate(orders)]
     for part in attn_sums:
-        part.step()
-    up_sum.step(starts=(attn_sums[0].send,))
-    down_sum.step(starts=(attn_sums[0].send,))
-    attn_mine = [part.finish().astype(BF) for part in attn_sums]
-    up_all, down_mine = up_sum.finish(), down_sum.finish()
-    up_mine, proj_mine = up_all[: width // n_blk].astype(BF), up_all[width // n_blk :]
+        part.move()
     token_grad = token_back(flags, hidL, hidS, hid1_recv, tokens, resid_grad, first_mod, lay)
+    many, token_grad, *gots = lax.optimization_barrier((many, token_grad, *[part.got for part in attn_sums]))
+    both = swap_side(many)
+    for part, got in zip(attn_sums, gots):
+        part.got = got
+        part.add()
+        part.move()
+    for part in mlp_sums:
+        part.add()
+    down_mine, up_mine = mlp_sums[0].finish(), mlp_sums[1].finish().astype(BF)
+    both, down_mine, up_mine, *gots = lax.optimization_barrier((both, down_mine, up_mine, *[part.got for part in attn_sums]))
+    for part, got in zip(attn_sums, gots):
+        part.got = got
+        part.add()
+        part.move()
+    both = jnp.stack([many, both])
+    packs = jnp.stack([both, swap_core(both)]).reshape(-1, width)
+    g_mod_weight, sums = modulation_grads(flags, long_rows, packs, row_out, "modulation_grads")
+    if len(bits) == 3:
+        sums, *gots = lax.optimization_barrier((sums, *[part.got for part in attn_sums]))
+        for part, got in zip(attn_sums, gots):
+            part.got = got
+    for part in attn_sums:
+        part.add()
+    attn_mine = [part.finish() for part in attn_sums]
+    attn_rows = width // n_blk
+    head = proj_part.shape[1] // n_blk
+    proj_mine = jnp.concatenate(
+        [attn_mine[1][attn_rows + k * head : attn_rows + (k + 1) * head] for k in range(width // (quarter - split))], axis=1
+    )
+    attn_mine = [part[:attn_rows].astype(BF) for part in attn_mine]
 
     quarters = jnp.concatenate([up_mine] + attn_mine, axis=1)
     quarters = lax.all_to_all(quarters.reshape(n_uly, row_out, -1), "uly", 0, 0, tiled=True)
     ff = up_weight.shape[1]
-    g_up_weight, g_attn_weight = lay_out_rows(flags, quarters, ff // n_uly, ff, "lay_out_rows")
 
     g = ff // (n_blk * n_uly)
 
@@ -1279,9 +1384,6 @@
     proj_map = [(b * n_uly + u, u * n_blk + b) for b in range(n_blk) for u in range(n_uly)]
     g_proj_weight = lax.ppermute(proj_mine.astype(F32), ("blk", "uly"), proj_map)
 
-    own_long_all = (long_first[None, :] == ((side ^ jnp.arange(2)) == 0)[:, None]).astype(F32)
-    long_rows = jnp.broadcast_to(own_long_all[None, :, :, None, None], (2, 2, n_blk, PACK, LANES)).reshape(-1, LANES)
-    g_mod_weight, sums = modulation_grads(flags, long_rows, packs, row_out, "modulation_grads")
 
     def cut(vector, size):
         return lax.dynamic_slice_in_dim(vector, dev * size, size, 0)
@@ -1300,6 +1402,10 @@
     by_step = (sums[0:2, 22:24] + sums[2:4, 22:24]).reshape(2, 2 * width)[:, : 3 * width // 2]
     by_side = jnp.where(side == 0, by_step, by_step[::-1])
     g_attn_bias = cut(jnp.swapaxes(by_side.reshape(2, 3, width // 2), 0, 1).reshape(-1), 3 * width // total_dev)
+    quarters, g_mod_bias, g_down_bias, g_proj_bias, g_up_bias, g_attn_bias, g_down_weight = lax.optimization_barrier(
+        (quarters, g_mod_bias, g_down_bias, g_proj_bias, g_up_bias, g_attn_bias, g_down_weight)
+    )
+    g_up_weight, g_attn_weight = lay_out_rows(flags, quarters, ff // n_uly, ff, "lay_out_rows")
     return (
         output, token_grad, g_mod_weight, g_mod_bias, g_attn_weight, g_attn_bias,
         g_proj_weight, g_proj_bias, g_up_weight, g_up_bias, g_down_weight, g_down_bias,

time: 314 us -> 303 us (0.965)
  waiting for transfers between devices: 66.2 us -> 39.5 us
  Pallas kernels: 133 us -> 146 us
  other arithmetic: 11.4 us -> 23.4 us
  blocking collectives: 11.9 us -> 0 us
  starting transfers between devices: 59.3 us -> 66 us
  local copies, waits for them, and re-layouts: 21.2 us -> 15.9 us
    all_to_all x4 -> x5, waiting for transfers between devices: 17.4 us -> 4.67 us  [spread(): return lax.all_to_all(value, 'blk', split_axis=0, concat_axis=0, tiled=True)]
    pallas_call x24 -> x25, Pallas kernels: 133 us -> 146 us  [kernel_call(): pl.pallas_call(body, grid_spec=pltpu.PrefetchScalarGridSpec(num_scalar_pr...]
    all_to_all x1 -> x0, blocking collectives: 11.9 us -> none  [spread(): return lax.all_to_all(value, 'blk', split_axis=0, concat_axis=0, tiled=True)]
    ppermute x15 -> x12, waiting for transfers between devices: 22.7 us -> 13.6 us  [move(): lax.ppermute(send, 'blk', [(i, i ^ hop) for i in range(self.n_blk)])]
    convert_element_type x13 -> x10, other arithmetic: 5.3 us -> 11.8 us  [the longest x8 9.7 us: add(): (self.keep[k].astype(F32) + self.got[k].astype(F32)).astype(BF)]
    ppermute x11, waiting for transfers between devices: 13.2 us -> 8.1 us  [swap_side(): return lax.ppermute(value, 'uly', [(i, i ^ 2) for i in range(n_uly)])]
    all_to_all x4 -> x5, starting transfers between devices: 21.9 us -> 25.4 us  [spread(): return lax.all_to_all(value, 'blk', split_axis=0, concat_axis=0, tiled=True)]
    squeeze x10 -> x0, local copies, waits for them, and re-layouts: 3.14 us -> none  [step(): self.send, self.keep = (value[index + (1,)], value[index + (0,)])]
  transfers between devices with their start and end apart: 47 -> 45, of which waited for: 21 -> 16; matrix products, arithmetic and copies ran while one was open for 8% -> 10% of each run, Pallas kernels for 35% -> 44%
where the time goes in v3:
time: 303 us; the launch traced here: 300 us
  Pallas kernels  146 us (48%)
  starting transfers between devices  66 us (22%)
  waiting for transfers between devices  39.5 us (13%)
  other arithmetic  23.4 us (8%)
  local copies, waits for them, and re-layouts  15.9 us (5%)
  matrix products  7.49 us (2%)
    pallas_call x25, Pallas kernels, kernel_call(): pl.pallas_call(body, grid_spec=pltpu.PrefetchScalarGridSpec(num_scalar_pr...  146 us
    all_to_all x5, starting transfers between devices, spread(): return lax.all_to_all(value, 'blk', split_axis=0, concat_axis=0, tiled=True)  25.4 us
    ppermute x12, starting transfers between devices, move(): lax.ppermute(send, 'blk', [(i, i ^ hop) for i in range(self.n_blk)])  17.6 us
    ppermute x12, waiting for transfers between devices, move(): lax.ppermute(send, 'blk', [(i, i ^ hop) for i in range(self.n_blk)])  13.6 us
    ppermute x11, starting transfers between devices, swap_side(): return lax.ppermute(value, 'uly', [(i, i ^ 2) for i in range(n_uly)])  12.8 us
    convert_element_type x8, other arithmetic, add(): (self.keep[k].astype(F32) + self.got[k].astype(F32)).astype(BF)  9.7 us
    ppermute x1, waiting for transfers between devices, on_device(): lax.ppermute(proj_mine.astype(F32), ('blk', 'uly'), proj_map)  8.27 us
    ppermute x11, waiting for transfers between devices, swap_side(): return lax.ppermute(value, 'uly', [(i, i ^ 2) for i in range(n_uly)])  8.1 us
  transfers between devices with their start and end apart: 45, of which 16 were waited for; matrix products, arithmetic and copies ran while one was open for 10% of the time, Pallas kernels for 44%

profile of v3, /device:TPU:4, one launch (start us, length us, event | category | flops | bytes accessed | tf_op | source)
XLA Modules:
  0.0 299.9 jit_solution(10199770939958879584)
XLA Ops:
  11.3 4.6 %fusion.2 = f32[2,4096]{1,0:T(2,128)S(1)} fusion(bf16[2,1024]{1,0:T(2,128)(2,1)S(1)} %fusion.16.s_ref, bf16[1024,6144]{1,0:T(8,128)(2,1)} %param.22, f32[4096]{0:T(1024)S(1)} %slice.269), kind=kOutput, calls=%fused_computation.2 | convolution fusion | flops 16785408 | bytes 8441856 | tf_op jit(solution)/shard_map/dot_general | solution.py:77
  19.1 7.7 %tokens_to_qkv.1 = (bf16[2,200,1024]{2,1,0:T(8,128)(2,1)}, bf16[8,320,128]{2,1,0:T(8,128)(2,1)S(1)}, bf16[8,320,128]{2,1,0:T(8,128)(2,1)S(1)}) custom-call(s32[6]{0:T(128)S(1)} %stack.49.flag_ref, bf16[200,1024]{1,0:T(8,128)(2,1)S(1)} %copy-done, bf16[200,1024]{1,0:T(8,128)(2,1)S(1)} %collective-permute-done.oth_ref, ...), custom_call_target="tpu_custom_call" | custom-call | flops 307200 | bytes 4096 | tf_op jit(solution)/shard_map/tokens_to_qkv/pallas_call | solution.py:117
  27.6 6.3 %all-to-all-start = ((bf16[8,320,128]{2,1,0:T(8,128)(2,1)}), bf16[8,320,128]{2,1,0:T(8,128)(2,1)S(1)}, u32[]{:S(2)}, u32[]{:S(2)}) async-start(bf16[8,320,128]{2,1,0:T(8,128)(2,1)} %copy-done.17), calls=%async_computation | async-start | bytes 1310720 | tf_op jit(solution)/shard_map/all_to_all | solution.py:1171
  35.7 5.6 %ahead_own.1.ahead_ref = f32[200,2048]{1,0:T(8,128)} custom-call(s32[6]{0:T(128)S(1)} %stack.49.flag_ref, bf16[200,1024]{1,0:T(8,128)(2,1)S(1)} %get-tuple-element.183.mg_ref.refs_4_, bf16[4096,1024]{1,0:T(8,128)(2,1)} %refs_1_.9, bf16[4096,1024]{1,0:T(8,128)(2,1)} %refs_1_.9), custom_call_target="tpu_custom_call" | custom-call | flops 204800 | bytes 4096 | tf_op jit(solution)/shard_map/ahead_own/pallas_call | solution.py:117
  41.3 5.9 %attend_short.1 = (bf16[8,112,128]{2,1,0:T(8,128)(2,1)S(1)}, f32[8,64,200]{2,1,0:T(8,128)}, f32[8,8,200]{2,1,0:T(8,128)}) custom-call(s32[6]{0:T(128)S(1)} %stack.49.flag_ref, bf16[8,320,128]{2,1,0:T(8,128)(2,1)S(1)} %get-tuple-element.161.own_ref, bf16[8,320,128]{2,1,0:T(8,128)(2,1)S(1)} %collective-permute-done.2.oth_ref), custom_call_target="tpu_custom_call" | custom-call | flops 160000 | bytes 4096 | tf_op jit(solution)/shard_map/attend_short/pallas_call | solution.py:117
  52.2 11.4 %attend_long.1 = (bf16[8,112,128]{2,1,0:T(8,128)(2,1)S(1)}, f32[4,64,400]{2,1,0:T(8,128)}, f32[4,8,400]{2,1,0:T(8,128)}) custom-call(s32[6]{0:T(128)S(1)} %stack.49.flag_ref, bf16[8,320,128]{2,1,0:T(8,128)(2,1)S(1)} %all-to-all-done.own_ref, bf16[8,320,128]{2,1,0:T(8,128)(2,1)S(1)} %collective-permute-done.3.oth_ref), custom_call_target="tpu_custom_call" | custom-call | flops 800000 | bytes 4096 | tf_op jit(solution)/shard_map/attend_long/pallas_call | solution.py:117
  65.1 4.2 %all-to-all-start.1 = ((bf16[8,112,128]{2,1,0:T(8,128)(2,1)}), bf16[8,112,128]{2,1,0:T(8,128)(2,1)S(1)}, u32[]{:S(2)}, u32[]{:S(2)}) async-start(bf16[8,112,128]{2,1,0:T(8,128)(2,1)} %copy-done.21), calls=%async_computation.1 | async-start | bytes 458752 | tf_op jit(solution)/shard_map/all_to_all | solution.py:1171
  70.4 5.6 %ahead_other.1.ahead_ref = f32[200,2048]{1,0:T(8,128)} custom-call(s32[6]{0:T(128)S(1)} %stack.49.flag_ref, bf16[200,1024]{1,0:T(8,128)(2,1)S(1)} %copy-done.13, bf16[4096,1024]{1,0:T(8,128)(2,1)} %refs_1_.9, bf16[4096,1024]{1,0:T(8,128)(2,1)} %refs_1_.9), custom_call_target="tpu_custom_call" | custom-call | flops 204800 | bytes 4096 | tf_op jit(solution)/shard_map/ahead_other/pallas_call | solution.py:117
  79.0 4.4 %collective-permute-done.5.recv_ref = bf16[8,112,128]{2,1,0:T(8,128)(2,1)S(1)} collective-permute-done((bf16[8,112,128]{2,1,0:T(8,128)(2,1)S(1)}, bf16[8,112,128]{2,1,0:T(8,128)(2,1)S(1)}, u32[]{:S(2)}, u32[]{:S(2)}) %collective-permute-start.5) | collective-permute-done | bytes 229408 | tf_op jit(solution)/shard_map/ppermute | solution.py:1165
  83.4 4.5 %project_and_norm.1 = (f32[200,1024]{1,0:T(8,128)}, f32[200,1024]{1,0:T(8,128)}, f32[200,1024]{1,0:T(8,128)}, f32[200,128]{1,0:T(8,128)}, bf16[200,1024]{1,0:T(8,128)(2,1)S(1)}) custom-call(s32[6]{0:T(128)S(1)} %stack.49.flag_ref, bf16[8,112,128]{2,1,0:T(8,128)(2,1)S(1)} %all-to-all-done.1.long_ref.l_ref, ...), custom_call_target="tpu_custom_call" | custom-call | flops 102400 | bytes 4096 | tf_op jit(solution)/shard_map/project_and_norm/pallas_call | solution.py:117
  89.4 6.9 %hidden_own.1 = (bf16[2,200,1024]{2,1,0:T(8,128)(2,1)S(1)}, bf16[2,200,1024]{2,1,0:T(8,128)(2,1)S(1)}, f32[8,1024]{1,0:T(8,128)S(1)}, f32[8,1024]{1,0:T(8,128)S(1)}, f32[200,1024]{1,0:T(8,128)S(1)}) custom-call(s32[6]{0:T(128)S(1)} %stack.49.flag_ref, bf16[200,1024]{1,0:T(8,128)(2,1)S(1)} %get-tuple-element.172.hid_ref.refs_8_, ...), custom_call_target="tpu_custom_call" | custom-call | flops 409600 | bytes 4096 | tf_op jit(solution)/shard_map/hidden_own/pallas_call | solution.py:117
  97.7 6.8 %hidden_other.1 = (bf16[2,200,1024]{2,1,0:T(8,128)(2,1)S(1)}, bf16[2,200,1024]{2,1,0:T(8,128)(2,1)S(1)}, f32[8,1024]{1,0:T(8,128)S(1)}, f32[8,1024]{1,0:T(8,128)S(1)}, bf16[200,1024]{1,0:T(8,128)(2,1)S(1)}) custom-call(s32[6]{0:T(128)S(1)} %stack.49.flag_ref, bf16[200,1024]{1,0:T(8,128)(2,1)S(1)} %collective-permute-done.6.hid_ref.refs_9_, ...), custom_call_target="tpu_custom_call" | custom-call | flops 409600 | bytes 4096 | tf_op jit(solution)/shard_map/hidden_other/pallas_call | solution.py:117
  109.2 9.4 %mlp_grads.1 = (bf16[4,128,1024]{2,1,0:T(8,128)(2,1)}, bf16[4,128,1024]{2,1,0:T(8,128)(2,1)S(1)}, bf16[4,128,1024]{2,1,0:T(8,128)(2,1)}, bf16[4,128,1024]{2,1,0:T(8,128)(2,1)S(1)}) custom-call(s32[6]{0:T(128)S(1)} %stack.49.flag_ref, bf16[2,200,1024]{2,1,0:T(8,128)(2,1)S(1)} %get-tuple-element.179.refs_0_.refs_12_.m_ref, ...), custom_call_target="tpu_custom_call" | custom-call | flops 819200 | bytes 4096 | tf_op jit(solution)/shard_map/mlp_grads/pallas_call | solution.py:117
  121.3 4.8 %branch_back.1 = (f32[200,1024]{1,0:T(8,128)}, bf16[200,1024]{1,0:T(8,128)(2,1)S(1)}, bf16[8,112,128]{2,1,0:T(8,128)(2,1)S(1)}, bf16[8,112,128]{2,1,0:T(8,128)(2,1)S(1)}, f32[8,1024]{1,0:T(8,128)S(1)}) custom-call(s32[6]{0:T(128)S(1)} %stack.49.flag_ref, f32[200,1024]{1,0:T(8,128)} %copy-done.16, bf16[200,1024]{1,0:T(8,128)(2,1)S(1)} %collective-permute-done.7.b_ref, ...), custom_call_target="tpu_custom_call" | custom-call | flops 102400 | bytes 4096 | tf_op jit(solution)/shard_map/branch_back/pallas_call | solution.py:117
  127.2 7.1 %forward_rows.1 = (f32[200,1024]{1,0:T(8,128)}, bf16[200,1024]{1,0:T(8,128)(2,1)S(1)}) custom-call(s32[6]{0:T(128)S(1)} %stack.49.flag_ref, bf16[2,200,1024]{2,1,0:T(8,128)(2,1)S(1)} %get-tuple-element.179.refs_0_.refs_12_.m_ref, bf16[2,200,1024]{2,1,0:T(8,128)(2,1)S(1)} %get-tuple-element.181.s_ref, ...), custom_call_target="tpu_custom_call" | custom-call | flops 409600 | bytes 4096 | tf_op jit(solution)/shard_map/forward_rows/pallas_call | solution.py:117
  136.8 5.4 %all-to-all-start.2 = ((bf16[8,112,128]{2,1,0:T(8,128)(2,1)}), bf16[8,112,128]{2,1,0:T(8,128)(2,1)S(1)}, u32[]{:S(2)}, u32[]{:S(2)}) async-start(bf16[8,112,128]{2,1,0:T(8,128)(2,1)} %broadcast_select_fusion.1), calls=%async_computation.2 | async-start | bytes 458752 | tf_op jit(solution)/shard_map/all_to_all | solution.py:1171
  142.1 7.5 %attend_back_short.1 = (bf16[8,200,128]{2,1,0:T(8,128)(2,1)}, f32[8,200,128]{2,1,0:T(8,128)}, bf16[8,200,128]{2,1,0:T(8,128)(2,1)}) custom-call(s32[6]{0:T(128)S(1)} %stack.49.flag_ref, bf16[8,320,128]{2,1,0:T(8,128)(2,1)} %copy-done.5, bf16[8,320,128]{2,1,0:T(8,128)(2,1)} %copy-done.6, bf16[8,112,128]{2,1,0:T(8,128)(2,1)S(1)} %get-tuple-element.202.refs_0_, ...), custom_call_target="tpu_custom_call" | custom-call | flops 400000 | bytes 4096 | tf_op jit(solution)/shard_map/attend_back_short/pallas_call | solution.py:117
  154.6 3.3 %collective-permute-start.20 = (bf16[2,128,1024]{2,1,0:T(8,128)(2,1)S(1)}, bf16[2,128,1024]{2,1,0:T(8,128)(2,1)S(1)}, u32[]{:S(2)}, u32[]{:S(2)}) collective-permute-start(bf16[2,128,1024]{2,1,0:T(8,128)(2,1)S(1)} %get-tuple-element.225), channel_id=1, source_target_pairs={{0,24},{4,28},{8,16},{12,20},{16,8},{20,12},{24,0},{28,4},{1,25},{... | collective-permute-start | bytes 1572872 | tf_op jit(solution)/shard_map/ppermute | solution.py:1014
  158.4 17.4 %attend_back_long.1 = (bf16[8,200,128]{2,1,0:T(8,128)(2,1)}, f32[8,200,128]{2,1,0:T(8,128)}, bf16[8,200,128]{2,1,0:T(8,128)(2,1)S(1)}) custom-call(s32[6]{0:T(128)S(1)} %stack.49.flag_ref, bf16[8,320,128]{2,1,0:T(8,128)(2,1)} %copy-done.1, bf16[8,320,128]{2,1,0:T(8,128)(2,1)} %copy-done.4, bf16[8,112,128]{2,1,0:T(8,128)(2,1)S(1)} %all-to-all-done.2.refs_0_, ...), custom_call_target="tpu_custom_call" | custom-call | flops 2000000 | bytes 4096 | tf_op jit(solution)/shard_map/attend_back_long/pallas_call | solution.py:117
  178.2 3.8 %finish_keys.2 = bf16[8,320,128]{2,1,0:T(8,128)(2,1)} custom-call(s32[6]{0:T(128)S(1)} %stack.49.flag_ref, bf16[8,200,128]{2,1,0:T(8,128)(2,1)} %get-tuple-element.222.dq_ref, f32[8,200,128]{2,1,0:T(8,128)} %get-tuple-element.223.a_ref, bf16[8,200,128]{2,1,0:T(8,128)(2,1)S(1)} %collective-permute-done.19.b_ref, f32[200,128]{1,0:T(8,128)S(1)} %copy-done.8, ...), custom_call_target="tpu_custom_call" | custom-call | flops 500 | bytes 4096 | tf_op jit(solution)/shard_map/finish_keys/pallas_call | solution.py:117
  181.9 4.9 %all-to-all-start.3 = ((bf16[8,320,128]{2,1,0:T(8,128)(2,1)}), bf16[8,320,128]{2,1,0:T(8,128)(2,1)S(1)}, u32[]{:S(2)}, u32[]{:S(2)}) async-start(bf16[8,320,128]{2,1,0:T(8,128)(2,1)} %finish_keys.2), calls=%async_computation.3 | async-start | bytes 1310720 | tf_op jit(solution)/shard_map/all_to_all | solution.py:1171
  198.4 3.2 %layer_output.1 = (bf16[200,1024]{1,0:T(8,128)(2,1)}, f32[8,1024]{1,0:T(8,128)S(1)}) custom-call(s32[6]{0:T(128)S(1)} %stack.49.flag_ref, f32[200,1024]{1,0:T(8,128)} %get-tuple-element.196.a_ref, bf16[200,1024]{1,0:T(8,128)(2,1)} %collective-permute-done.16.b_ref, f32[1,1024]{1,0:T(1,128)S(1)} %bitcast.68, f32[200,1024]{1,0:T(8,128)} %get-tuple-element.229.r_ref, ...), custom_call_target="tpu_custom_call" | custom-call | flops 200 | bytes 4096 | tf_op jit(solution)/shard_map/layer_output/pallas_call | solution.py:117
  201.5 6.1 %qkv_back_short.1 = (f32[200,1024]{1,0:T(8,128)}, bf16[200,1024]{1,0:T(8,128)(2,1)S(1)}, bf16[200,768]{1,0:T(8,128)(2,1)S(1)}, bf16[200,768]{1,0:T(8,128)(2,1)},...) custom-call(s32[6]{0:T(128)S(1)} %stack.49.flag_ref, bf16[8,320,128]{2,1,0:T(8,128)(2,1)S(1)} %finish_keys.3.g_ref, ...), custom_call_target="tpu_custom_call" | custom-call | flops 153600 | bytes 4096 | tf_op jit(solution)/shard_map/qkv_back_short/pallas_call | solution.py:117
  209.2 6.1 %qkv_back_long.1 = (f32[200,1024]{1,0:T(8,128)}, bf16[200,1024]{1,0:T(8,128)(2,1)S(1)}, bf16[200,768]{1,0:T(8,128)(2,1)S(1)}, bf16[200,768]{1,0:T(8,128)(2,1)S(1...) custom-call(s32[6]{0:T(128)S(1)} %stack.49.flag_ref, bf16[8,320,128]{2,1,0:T(8,128)(2,1)S(1)} %all-to-all-done.3.g_ref, ...), custom_call_target="tpu_custom_call" | custom-call | flops 153600 | bytes 4096 | tf_op jit(solution)/shard_map/qkv_back_long/pallas_call | solution.py:117
  223.1 4.5 %all-to-all-start.4 = ((bf16[8,24,1024]{2,1,0:T(8,128)(2,1)}), bf16[8,24,1024]{2,1,0:T(8,128)(2,1)}, u32[]{:S(2)}, u32[]{:S(2)}) async-start(bf16[8,24,1024]{2,1,0:T(8,128)(2,1)} %pack_rows.1), calls=%async_computation.4 | async-start | bytes 786432 | tf_op jit(solution)/shard_map/all_to_all | solution.py:1171
  228.4 8.0 %attn_grads.1 = (bf16[4,128,512]{2,1,0:T(8,128)(2,1)}, bf16[4,128,512]{2,1,0:T(8,128)(2,1)S(1)}, bf16[4,256,256]{2,1,0:T(8,128)(2,1)}, bf16[4,256,256]{2,1,0:T(8,128)(2,1)S(1)}) custom-call(s32[6]{0:T(128)S(1)} %stack.49.flag_ref, bf16[2,200,1024]{2,1,0:T(8,128)(2,1)} %get-tuple-element.261.refs_0_.refs_1_, ...), custom_call_target="tpu_custom_call" | custom-call | flops 307200 | bytes 4096 | tf_op jit(solution)/shard_map/attn_grads/pallas_call | solution.py:117
  238.5 3.8 %token_back.1 = f32[200,1024]{1,0:T(8,128)} custom-call(s32[6]{0:T(128)S(1)} %stack.49.flag_ref, f32[200,1024]{1,0:T(8,128)} %get-tuple-element.255.l_ref, f32[200,1024]{1,0:T(8,128)} %get-tuple-element.256.s_ref, bf16[200,1024]{1,0:T(8,128)(2,1)S(1)} %collective-permute-done.23.r_ref, bf16[200,1024]{1,0:T(8,128)(2,1)} %tok_ref.3, ...), custom_call_target="tpu_custom_call" | custom-call | flops 1000 | bytes 4096 | tf_op jit(solution)/shard_map/token_back/pallas_call | solution.py:117
  242.7 8.4 %collective-permute-done.30 = bf16[4,128,512]{2,1,0:T(8,128)(2,1)} collective-permute-done((bf16[4,128,512]{2,1,0:T(8,128)(2,1)}, bf16[4,128,512]{2,1,0:T(8,128)(2,1)}, u32[]{:S(2)}, u32[]{:S(2)}) %collective-permute-start.30) | collective-permute-done | bytes 524320 | tf_op jit(solution)/shard_map/ppermute | solution.py:1014
  270.3 3.5 %modulation_grads.1 = (f32[32,6144]{1,0:T(8,128)}, f32[4,32,1024]{2,1,0:T(8,128)S(1)}) custom-call(s32[6]{0:T(128)S(1)} %stack.49.flag_ref, f32[768,128]{1,0:T(8,128)S(1)} %copy-done.15, bf16[768,1024]{1,0:T(8,128)(2,1)S(1)} %bitcast.62), custom_call_target="tpu_custom_call" | custom-call | flops 294912 | bytes 4096 | tf_op jit(solution)/shard_map/modulation_grads/pallas_call | solution.py:117
  278.5 3.5 %all-to-all-start.5 = ((bf16[4,32,1792]{2,1,0:T(8,128)(2,1)}), bf16[4,32,1792]{2,1,0:T(8,128)(2,1)S(1)}, u32[]{:S(2)}, u32[]{:S(2)}) async-start(bf16[4,32,1792]{2,1,0:T(8,128)(2,1)} %bitcast.27), calls=%async_computation.5 | async-start | bytes 917504 | tf_op jit(solution)/shard_map/all_to_all | solution.py:1370
  282.4 3.9 %collective-permute-start.38 = (f32[32,1024]{1,0:T(8,128)S(1)}, f32[32,1024]{1,0:T(8,128)S(1)}, u32[]{:S(2)}, u32[]{:S(2)}) collective-permute-start(f32[32,1024]{1,0:T(8,128)S(1)} %pad_maximum_fusion.3), channel_id=1, source_target_pairs={{0,0},{1,8},{2,16},{3,24},{4,1},{5,9},{6,17},{7,25},{8,2},{9,10},{... | collective-permute-start | bytes 393224 | tf_op jit(solution)/shard_map/ppermute | solution.py:1385
  289.5 8.3 %collective-permute-done.38 = f32[32,1024]{1,0:T(8,128)S(1)} collective-permute-done((f32[32,1024]{1,0:T(8,128)S(1)}, f32[32,1024]{1,0:T(8,128)S(1)}, u32[]{:S(2)}, u32[]{:S(2)}) %collective-permute-start.38) | collective-permute-done | bytes 131104 | tf_op jit(solution)/shard_map/ppermute | solution.py:1385
  (266 shorter events, 101.0 us)
Async XLA Ops:
  0.6 18.4 %collective-permute-start = (bf16[200,1024]{1,0:T(8,128)(2,1)}, bf16[200,1024]{1,0:T(8,128)(2,1)S(1)}, u32[]{:S(2)}, u32[]{:S(2)}) collective-permute-start(bf16[200,1024]{1,0:T(8,128)(2,1)} %tok_ref.3), channel_id=1, source_target_pairs={{0,2},{1,3},{2,0},{3,1},{4,6},{5,7},{6,4},{7,5},{8,10},{9,11},{10,... | collective-permute-start | bytes 1228808 | tf_op jit(solution)/shard_map/ppermute | solution.py:1165
  5.8 12.3 %collective-permute-start.1 = (f32[2,2048]{1,0:T(2,128)S(1)}, f32[2,2048]{1,0:T(2,128)S(1)}, u32[]{:S(2)}, u32[]{:S(2)}) collective-permute-start(f32[2,2048]{1,0:T(2,128)S(1)} %fusion.7.mod_ref), channel_id=1, source_target_pairs={{0,2},{1,3},{2,0},{3,1},{4,6},{5,7},{6,4},{7,5},{8,10},{9,11},{10,... | collective-permute-start | bytes 49160 | tf_op jit(solution)/shard_map/ppermute | solution.py:1165
  27.6 22.5 %all-to-all-start = ((bf16[8,320,128]{2,1,0:T(8,128)(2,1)}), bf16[8,320,128]{2,1,0:T(8,128)(2,1)S(1)}, u32[]{:S(2)}, u32[]{:S(2)}) async-start(bf16[8,320,128]{2,1,0:T(8,128)(2,1)} %copy-done.17), calls=%async_computation | async-start | bytes 1310720 | tf_op jit(solution)/shard_map/all_to_all | solution.py:1171
  50.1 13.5 %collective-permute-start.4 = (bf16[200,1024]{1,0:T(8,128)(2,1)S(1)}, bf16[200,1024]{1,0:T(8,128)(2,1)S(1)}, u32[]{:S(2)}, u32[]{:S(2)}) collective-permute-start(bf16[200,1024]{1,0:T(8,128)(2,1)S(1)} %get-tuple-element.183.mg_ref.refs_4_), channel_id=1, source_target_pairs={{0,2},{1,3},{2,0},{3,1},{4,6},{5,7},{6,4},{7,5},{8,10},{9,11},{10,... | collective-permute-start | bytes 1228808 | tf_op jit(solution)/shard_map/ppermute | solution.py:1165
  65.1 12.1 %all-to-all-start.1 = ((bf16[8,112,128]{2,1,0:T(8,128)(2,1)}), bf16[8,112,128]{2,1,0:T(8,128)(2,1)S(1)}, u32[]{:S(2)}, u32[]{:S(2)}) async-start(bf16[8,112,128]{2,1,0:T(8,128)(2,1)} %copy-done.21), calls=%async_computation.1 | async-start | bytes 458752 | tf_op jit(solution)/shard_map/all_to_all | solution.py:1171
  87.9 9.8 %collective-permute-start.6 = (bf16[200,1024]{1,0:T(8,128)(2,1)S(1)}, bf16[200,1024]{1,0:T(8,128)(2,1)S(1)}, u32[]{:S(2)}, u32[]{:S(2)}) collective-permute-start(bf16[200,1024]{1,0:T(8,128)(2,1)S(1)} %get-tuple-element.172.hid_ref.refs_8_), channel_id=1, source_target_pairs={{0,2},{1,3},{2,0},{3,1},{4,6},{5,7},{6,4},{7,5},{8,10},{9,11},{10,... | collective-permute-start | bytes 1228808 | tf_op jit(solution)/shard_map/ppermute | solution.py:1165
  89.4 16.3 %collective-permute-start.10 = (bf16[200,1024]{1,0:T(8,128)(2,1)S(1)}, bf16[200,1024]{1,0:T(8,128)(2,1)S(1)}, u32[]{:S(2)}, u32[]{:S(2)}) collective-permute-start(bf16[200,1024]{1,0:T(8,128)(2,1)S(1)} %get-tuple-element.183.mg_ref.refs_4_), channel_id=1, source_target_pairs={{0,1},{1,0},{2,3},{3,2},{4,5},{5,4},{6,7},{7,6},{8,9},{9,8},{10,11... | collective-permute-start | bytes 1228808 | tf_op jit(solution)/shard_map/ppermute | solution.py:1168
  97.2 11.5 %collective-permute-start.8 = (bf16[2,200,1024]{2,1,0:T(8,128)(2,1)S(1)}, bf16[2,200,1024]{2,1,0:T(8,128)(2,1)S(1)}, u32[]{:S(2)}, u32[]{:S(2)}) collective-permute-start(bf16[2,200,1024]{2,1,0:T(8,128)(2,1)S(1)} %get-tuple-element.181.s_ref), channel_id=1, source_target_pairs={{0,1},{1,0},{2,3},{3,2},{4,5},{5,4},{6,7},{7,6},{8,9},{9,8},{10,11... | collective-permute-start | bytes 2457608 | tf_op jit(solution)/shard_map/ppermute | solution.py:1168
  108.0 11.5 %collective-permute-start.7 = (bf16[200,1024]{1,0:T(8,128)(2,1)S(1)}, bf16[200,1024]{1,0:T(8,128)(2,1)S(1)}, u32[]{:S(2)}, u32[]{:S(2)}) collective-permute-start(bf16[200,1024]{1,0:T(8,128)(2,1)S(1)} %get-tuple-element.178), channel_id=1, source_target_pairs={{0,2},{1,3},{2,0},{3,1},{4,6},{5,7},{6,4},{7,5},{8,10},{9,11},{10,... | collective-permute-start | bytes 1228808 | tf_op jit(solution)/shard_map/ppermute | solution.py:1165
  119.5 30.2 %collective-permute-start.17 = (bf16[4,128,1024]{2,1,0:T(8,128)(2,1)}, bf16[4,128,1024]{2,1,0:T(8,128)(2,1)}, u32[]{:S(2)}, u32[]{:S(2)}) collective-permute-start(bf16[4,128,1024]{2,1,0:T(8,128)(2,1)} %get-tuple-element.210), channel_id=1, source_target_pairs={{0,4},{4,0},{8,12},{12,8},{16,20},{20,16},{24,28},{28,24},{1,5},{5... | collective-permute-start | bytes 3145736 | tf_op jit(solution)/shard_map/ppermute | solution.py:1014
  120.4 29.3 %collective-permute-start.18 = (bf16[4,128,1024]{2,1,0:T(8,128)(2,1)}, bf16[4,128,1024]{2,1,0:T(8,128)(2,1)}, u32[]{:S(2)}, u32[]{:S(2)}) collective-permute-start(bf16[4,128,1024]{2,1,0:T(8,128)(2,1)} %get-tuple-element.211), channel_id=1, source_target_pairs={{0,8},{4,12},{8,0},{12,4},{16,24},{20,28},{24,16},{28,20},{1,9},{5... | collective-permute-start | bytes 3145736 | tf_op jit(solution)/shard_map/ppermute | solution.py:1014
  126.2 8.3 %collective-permute-start.14 = (bf16[8,112,128]{2,1,0:T(8,128)(2,1)S(1)}, bf16[8,112,128]{2,1,0:T(8,128)(2,1)S(1)}, u32[]{:S(2)}, u32[]{:S(2)}) collective-permute-start(bf16[8,112,128]{2,1,0:T(8,128)(2,1)S(1)} %get-tuple-element.192), channel_id=1, source_target_pairs={{0,2},{1,3},{2,0},{3,1},{4,6},{5,7},{6,4},{7,5},{8,10},{9,11},{10,... | collective-permute-start | bytes 688136 | tf_op jit(solution)/shard_map/ppermute | solution.py:1165
  135.1 14.5 %collective-permute-start.15 = (bf16[200,1024]{1,0:T(8,128)(2,1)S(1)}, bf16[200,1024]{1,0:T(8,128)(2,1)}, u32[]{:S(2)}, u32[]{:S(2)}) collective-permute-start(bf16[200,1024]{1,0:T(8,128)(2,1)S(1)} %get-tuple-element.200.go_ref), channel_id=1, source_target_pairs={{0,2},{1,3},{2,0},{3,1},{4,6},{5,7},{6,4},{7,5},{8,10},{9,11},{10,... | collective-permute-start | bytes 1228808 | tf_op jit(solution)/shard_map/ppermute | solution.py:1165
  136.8 12.9 %all-to-all-start.2 = ((bf16[8,112,128]{2,1,0:T(8,128)(2,1)}), bf16[8,112,128]{2,1,0:T(8,128)(2,1)S(1)}, u32[]{:S(2)}, u32[]{:S(2)}) async-start(bf16[8,112,128]{2,1,0:T(8,128)(2,1)} %broadcast_select_fusion.1), calls=%async_computation.2 | async-start | bytes 458752 | tf_op jit(solution)/shard_map/all_to_all | solution.py:1171
  154.6 23.6 %collective-permute-start.20 = (bf16[2,128,1024]{2,1,0:T(8,128)(2,1)S(1)}, bf16[2,128,1024]{2,1,0:T(8,128)(2,1)S(1)}, u32[]{:S(2)}, u32[]{:S(2)}) collective-permute-start(bf16[2,128,1024]{2,1,0:T(8,128)(2,1)S(1)} %get-tuple-element.225), channel_id=1, source_target_pairs={{0,24},{4,28},{8,16},{12,20},{16,8},{20,12},{24,0},{28,4},{1,25},{... | collective-permute-start | bytes 1572872 | tf_op jit(solution)/shard_map/ppermute | solution.py:1014
  157.8 20.3 %collective-permute-start.21 = (bf16[2,128,1024]{2,1,0:T(8,128)(2,1)S(1)}, bf16[2,128,1024]{2,1,0:T(8,128)(2,1)S(1)}, u32[]{:S(2)}, u32[]{:S(2)}) collective-permute-start(bf16[2,128,1024]{2,1,0:T(8,128)(2,1)S(1)} %get-tuple-element.226), channel_id=1, source_target_pairs={{0,4},{4,0},{8,12},{12,8},{16,20},{20,16},{24,28},{28,24},{1,5},{5... | collective-permute-start | bytes 1572872 | tf_op jit(solution)/shard_map/ppermute | solution.py:1014
  175.8 12.5 %collective-permute-start.22 = (bf16[8,200,128]{2,1,0:T(8,128)(2,1)}, bf16[8,200,128]{2,1,0:T(8,128)(2,1)S(1)}, u32[]{:S(2)}, u32[]{:S(2)}) collective-permute-start(bf16[8,200,128]{2,1,0:T(8,128)(2,1)} %get-tuple-element.234), channel_id=1, source_target_pairs={{0,1},{1,0},{2,3},{3,2},{4,5},{5,4},{6,7},{7,6},{8,9},{9,8},{10,11... | collective-permute-start | bytes 1228808 | tf_op jit(solution)/shard_map/ppermute | solution.py:1168
  181.9 27.3 %all-to-all-start.3 = ((bf16[8,320,128]{2,1,0:T(8,128)(2,1)}), bf16[8,320,128]{2,1,0:T(8,128)(2,1)S(1)}, u32[]{:S(2)}, u32[]{:S(2)}) async-start(bf16[8,320,128]{2,1,0:T(8,128)(2,1)} %finish_keys.2), calls=%async_computation.3 | async-start | bytes 1310720 | tf_op jit(solution)/shard_map/all_to_all | solution.py:1171
  186.8 11.5 %collective-permute-start.16 = (bf16[200,1024]{1,0:T(8,128)(2,1)}, bf16[200,1024]{1,0:T(8,128)(2,1)}, u32[]{:S(2)}, u32[]{:S(2)}) collective-permute-start(bf16[200,1024]{1,0:T(8,128)(2,1)} %copy-done.32), channel_id=1, source_target_pairs={{0,2},{1,3},{2,0},{3,1},{4,6},{5,7},{6,4},{7,5},{8,10},{9,11},{10,... | collective-permute-start | bytes 1228808 | tf_op jit(solution)/shard_map/ppermute | solution.py:1165
  188.3 29.5 %collective-permute-start.26 = (bf16[2,200,1024]{2,1,0:T(8,128)(2,1)}, bf16[2,200,1024]{2,1,0:T(8,128)(2,1)}, u32[]{:S(2)}, u32[]{:S(2)}) collective-permute-start(bf16[2,200,1024]{2,1,0:T(8,128)(2,1)} %get-tuple-element.261.refs_0_.refs_1_), channel_id=1, source_target_pairs={{0,1},{1,0},{2,3},{3,2},{4,5},{5,4},{6,7},{7,6},{8,9},{9,8},{10,11... | collective-permute-start | bytes 2457608 | tf_op jit(solution)/shard_map/ppermute | solution.py:1168
  192.1 35.5 %collective-permute-start.29 = (bf16[256,1024]{1,0:T(8,128)(2,1)}, bf16[256,1024]{1,0:T(8,128)(2,1)S(1)}, u32[]{:S(2)}, u32[]{:S(2)}) collective-permute-start(bf16[256,1024]{1,0:T(8,128)(2,1)} %slice_select_fusion), channel_id=1, source_target_pairs={{0,1},{1,0},{2,3},{3,2},{4,5},{5,4},{6,7},{7,6},{8,9},{9,8},{10,11... | collective-permute-start | bytes 1572872 | tf_op jit(solution)/shard_map/ppermute | solution.py:1168
  216.2 20.2 %collective-permute-start.23 = (bf16[200,1024]{1,0:T(8,128)(2,1)}, bf16[200,1024]{1,0:T(8,128)(2,1)S(1)}, u32[]{:S(2)}, u32[]{:S(2)}) collective-permute-start(bf16[200,1024]{1,0:T(8,128)(2,1)} %broadcast_select_fusion), channel_id=1, source_target_pairs={{0,2},{1,3},{2,0},{3,1},{4,6},{5,7},{6,4},{7,5},{8,10},{9,11},{10,... | collective-permute-start | bytes 1228808 | tf_op jit(solution)/shard_map/ppermute | solution.py:1165
  217.7 10.0 %collective-permute-start.28 = (bf16[200,768]{1,0:T(8,128)(2,1)}, bf16[200,768]{1,0:T(8,128)(2,1)S(1)}, u32[]{:S(2)}, u32[]{:S(2)}) collective-permute-start(bf16[200,768]{1,0:T(8,128)(2,1)} %get-tuple-element.266), channel_id=1, source_target_pairs={{0,1},{1,0},{2,3},{3,2},{4,5},{5,4},{6,7},{7,6},{8,9},{9,8},{10,11... | collective-permute-start | bytes 921608 | tf_op jit(solution)/shard_map/ppermute | solution.py:1168
  217.9 18.5 %collective-permute-start.24 = (bf16[1,128,1024]{2,1,0:T(8,128)(2,1)}, bf16[1,128,1024]{2,1,0:T(8,128)(2,1)}, u32[]{:S(2)}, u32[]{:S(2)}) collective-permute-start(bf16[1,128,1024]{2,1,0:T(8,128)(2,1)} %add_convert_fusion.12), channel_id=1, source_target_pairs={{0,8},{4,12},{8,0},{12,4},{16,24},{20,28},{24,16},{28,20},{1,9},{5... | collective-permute-start | bytes 786440 | tf_op jit(solution)/shard_map/ppermute | solution.py:1014
  219.3 17.0 %collective-permute-start.25 = (bf16[1,128,1024]{2,1,0:T(8,128)(2,1)}, bf16[1,128,1024]{2,1,0:T(8,128)(2,1)}, u32[]{:S(2)}, u32[]{:S(2)}) collective-permute-start(bf16[1,128,1024]{2,1,0:T(8,128)(2,1)} %add_convert_fusion.11), channel_id=1, source_target_pairs={{0,24},{4,28},{8,16},{12,20},{16,8},{20,12},{24,0},{28,4},{1,25},{... | collective-permute-start | bytes 786440 | tf_op jit(solution)/shard_map/ppermute | solution.py:1014
  223.1 19.6 %all-to-all-start.4 = ((bf16[8,24,1024]{2,1,0:T(8,128)(2,1)}), bf16[8,24,1024]{2,1,0:T(8,128)(2,1)}, u32[]{:S(2)}, u32[]{:S(2)}) async-start(bf16[8,24,1024]{2,1,0:T(8,128)(2,1)} %pack_rows.1), calls=%async_computation.4 | async-start | bytes 786432 | tf_op jit(solution)/shard_map/all_to_all | solution.py:1171
  236.4 14.8 %collective-permute-start.30 = (bf16[4,128,512]{2,1,0:T(8,128)(2,1)}, bf16[4,128,512]{2,1,0:T(8,128)(2,1)}, u32[]{:S(2)}, u32[]{:S(2)}) collective-permute-start(bf16[4,128,512]{2,1,0:T(8,128)(2,1)} %get-tuple-element.274), channel_id=1, source_target_pairs={{0,4},{4,0},{8,12},{12,8},{16,20},{20,16},{24,28},{28,24},{1,5},{5... | collective-permute-start | bytes 1572872 | tf_op jit(solution)/shard_map/ppermute | solution.py:1014
  236.9 15.1 %collective-permute-start.31 = (bf16[4,256,256]{2,1,0:T(8,128)(2,1)}, bf16[4,256,256]{2,1,0:T(8,128)(2,1)}, u32[]{:S(2)}, u32[]{:S(2)}) collective-permute-start(bf16[4,256,256]{2,1,0:T(8,128)(2,1)} %get-tuple-element.275), channel_id=1, source_target_pairs={{0,8},{4,12},{8,0},{12,4},{16,24},{20,28},{24,16},{28,20},{1,9},{5... | collective-permute-start | bytes 1572872 | tf_op jit(solution)/shard_map/ppermute | solution.py:1014
  252.0 10.7 %collective-permute-start.32 = (bf16[8,24,1024]{2,1,0:T(8,128)(2,1)}, bf16[8,24,1024]{2,1,0:T(8,128)(2,1)S(1)}, u32[]{:S(2)}, u32[]{:S(2)}) collective-permute-start(bf16[8,24,1024]{2,1,0:T(8,128)(2,1)} %all-to-all-done.4), channel_id=1, source_target_pairs={{0,2},{1,3},{2,0},{3,1},{4,6},{5,7},{6,4},{7,5},{8,10},{9,11},{10,... | collective-permute-start | bytes 1179656 | tf_op jit(solution)/shard_map/ppermute | solution.py:1165
  265.0 8.9 %collective-permute-start.36 = (bf16[1,128,512]{2,1,0:T(8,128)(2,1)S(1)}, bf16[1,128,512]{2,1,0:T(8,128)(2,1)S(1)}, u32[]{:S(2)}, u32[]{:S(2)}) collective-permute-start(bf16[1,128,512]{2,1,0:T(8,128)(2,1)S(1)} %add_convert_fusion.16), channel_id=1, source_target_pairs={{0,24},{4,28},{8,16},{12,20},{16,8},{20,12},{24,0},{28,4},{1,25},{... | collective-permute-start | bytes 393224 | tf_op jit(solution)/shard_map/ppermute | solution.py:1014
  278.5 19.2 %all-to-all-start.5 = ((bf16[4,32,1792]{2,1,0:T(8,128)(2,1)}), bf16[4,32,1792]{2,1,0:T(8,128)(2,1)S(1)}, u32[]{:S(2)}, u32[]{:S(2)}) async-start(bf16[4,32,1792]{2,1,0:T(8,128)(2,1)} %bitcast.27), calls=%async_computation.5 | async-start | bytes 917504 | tf_op jit(solution)/shard_map/all_to_all | solution.py:1370
  282.4 15.4 %collective-permute-start.38 = (f32[32,1024]{1,0:T(8,128)S(1)}, f32[32,1024]{1,0:T(8,128)S(1)}, u32[]{:S(2)}, u32[]{:S(2)}) collective-permute-start(f32[32,1024]{1,0:T(8,128)S(1)} %pad_maximum_fusion.3), channel_id=1, source_target_pairs={{0,0},{1,8},{2,16},{3,24},{4,1},{5,9},{6,17},{7,25},{8,2},{9,10},{... | collective-permute-start | bytes 393224 | tf_op jit(solution)/shard_map/ppermute | solution.py:1385
  (65 other events, 930.6 us)

commit v4 on v3

--- a/solution.py
+++ b/solution.py
@@ -793,20 +793,37 @@
     cols = lay.heads * DH
     half = cols // 2
 
-    def body(flag_ref, g_ref, own_ref, oth_ref, w_ref, hid_ref, low_ref, gm_ref, gt_ref, bias_ref, sums_ref, q_ref, acc_ref):
+    def body(flag_ref, *refs):
+        g_refs, refs = refs[: len(grads)], refs[len(grads) :]
+        own_ref, oth_ref, w_ref, hid_ref, low_ref, gm_ref, gt_ref, bias_ref, sums_ref, q_ref, acc_ref = refs
         step = pl.program_id(0)
         core = flag_ref[2]
 
         @pl.when(step == 0)
         def _():
+            if not is_long:
+                dq_ref, a_ref, b_ref, tc_ref, ts_ref, qc_ref, qs_ref = g_refs
+                table = (rows, LANES)
+                cosine = tc_ref[...] + per_frame(table, qc_ref[0], qc_ref[1])
+                sine = ts_ref[...] + per_frame(table, qs_ref[0], qs_ref[1])
             for pair in range(lay.heads // 2):
-                one, two = g_ref[2 * pair, :rows, :].astype(F32), g_ref[2 * pair + 1, :rows, :].astype(F32)
-                low = lane_low(one.shape)
                 lanes = slice(pair * LANES, (pair + 1) * LANES)
-                q_ref[0, :, lanes] = jnp.where(low, one, swap_halves(two)).astype(BF)
-                q_ref[1, :, lanes] = jnp.where(low, swap_halves(one), two).astype(BF)
-                one, two = g_ref[2 * pair, lay.vrow :, :].astype(F32), g_ref[2 * pair + 1, lay.vrow :, :].astype(F32)
-                q_ref[2, :, lanes] = join_pair(one, two, rows).astype(BF)
+                low = lane_low((rows, LANES))
+                if is_long:
+                    g_ref = g_refs[0]
+                    one, two = (g_ref[2 * pair + k, :rows, :].astype(F32) for k in (0, 1))
+                    query, key = jnp.where(low, one, swap_halves(two)), jnp.where(low, swap_halves(one), two)
+                    value = join_pair(*(g_ref[2 * pair + k, lay.vrow :, :].astype(F32) for k in (0, 1)), rows)
+                else:
+                    one, two = (dq_ref[2 * pair + k].astype(F32) for k in (0, 1))
+                    query = jnp.where(low, one, swap_halves(two))
+                    one, two = (a_ref[2 * pair + k] + b_ref[2 * pair + k].astype(F32) for k in (0, 1))
+                    value = jnp.where(low, one, swap_halves(two))
+                    one, two = (v * cosine - swap_pairs(v) * sine for v in (one, two))
+                    key = jnp.where(low, swap_halves(one), two)
+                q_ref[0, :, lanes] = query.astype(BF)
+                q_ref[1, :, lanes] = key.astype(BF)
+                q_ref[2, :, lanes] = value.astype(BF)
 
         value = q_ref[step]
         part = dot_lanes(value, w_ref[...])
@@ -838,7 +855,7 @@
     return kernel_call(
         body,
         flags,
-        [grads, tok_own, tok_oth, weight],
+        [*grads, tok_own, tok_oth, weight],
         [
             shape_of((rows, width), F32),
             shape_of((rows, width), BF),
@@ -847,7 +864,7 @@
             shape_of((8, 3 * cols), F32),
             shape_of((8, width), F32),
         ],
-        specs=[None, None, None, pl.BlockSpec((width, cols), lambda j, f: (0, 2 * j + f[1]))],
+        specs=[None] * (len(grads) + 2) + [pl.BlockSpec((width, cols), lambda j, f: (0, 2 * j + f[1]))],
         out_specs=[
             None, None,
             pl.BlockSpec((rows, half), lambda j, f: (0, j)),
@@ -855,7 +872,7 @@
             pl.BlockSpec((8, cols), lambda j, f: (0, j)),
             None,
         ],
-        pins=(1, 2),
+        pins=(len(grads), len(grads) + 1) + (() if is_long else (0, 1)),
         out_pins=(0,),
         grid=(3,),
         scratch=[pltpu.VMEM((3, rows, cols), BF), pltpu.VMEM((rows, width), F32)],
@@ -1303,39 +1320,45 @@
     )
     for part in mlp_sums:
         part.add()
-    grads_short = finish_keys(flags, dq_s, mine_s, theirs_s, tab_cos, tab_sin, short_cos, short_sin, lay, False)
-    hidS, hidS_low, gmS, gtS, abS, sumS = qkv_back(flags, grads_short, tokens, tok_oth, attn_weight, lay, False)
-    output, gate2_sums = layer_output(flags, mlp_own, after(mlp_recv, grads_sent), down_bias.astype(F32)[None], resid, cotangent, gate2)
+    hidS, hidS_low, gmS, gtS, abS, sumS = qkv_back(
+        flags, [dq_s, mine_s, theirs_s, tab_cos, tab_sin, short_cos, short_sin], tokens, tok_oth, attn_weight, lay, False
+    )
     proj_part = head_weight_grads(flags, out_long, out_short, branch_grad, branch_grad_oth, lay).reshape(2, -1, width)
     proj_got = swap_core(jnp.where(core == 0, proj_part[1], proj_part[0]))
     h1_core = swap_core(hidden1)
     gtS_got = swap_core(gtS)
-    grads_long, hidS_low, gate2_sums, mlp_sums[0].send, mlp_sums[1].send = lax.optimization_barrier(
-        (grads_long, hidS_low, gate2_sums, mlp_sums[0].send, mlp_sums[1].send)
+    grads_long, hidS_low, mlp_sums[0].send, mlp_sums[1].send = lax.optimization_barrier(
+        (grads_long, hidS_low, mlp_sums[0].send, mlp_sums[1].send)
     )
     for part in mlp_sums:
         part.move()
 
-    hidL, hidL_low, gmL, gtL, abL, sumL = qkv_back(flags, grads_long, tokens, tok_oth, attn_weight, lay, True)
+    hidL, hidL_low, gmL, gtL, abL, sumL = qkv_back(flags, [grads_long], tokens, tok_oth, attn_weight, lay, True)
     gtL_got = swap_core(gtL)
     hid1_recv = swap_side(jnp.where(own_long_b, hidS_low, hidL_low))
-    pack = pack_rows(flags, n_blk, mid_sums, gate2_sums, silu, down_b, (bm, bm2, bt, bt2), sumL, sumS, abL, abS)
-    many = spread(pack)
     quarter = 3 * width // n_uly
     split = 2 * quarter // 3
     halves = split_weight_grads(
         flags,
-        [([(hidden1, 0), (hidden1, 1), (h1_core, 0), (h1_core, 1)], plain(gmL, gmS, after(gtL_got, pack), gtS_got))],
+        [([(hidden1, 0), (hidden1, 1), (h1_core, 0), (h1_core, 1)], plain(gmL, gmS, gtL_got, gtS_got))],
         n_blk, [[(0, split, orders[0]), (split, quarter - split, orders[1])]], [proj_part, proj_got], "attn_grads",
     )
-    hid1_recv, mlp_sums[0].got, mlp_sums[1].got, *halves = lax.optimization_barrier(
-        (hid1_recv, mlp_sums[0].got, mlp_sums[1].got, *halves)
+    hid1_recv, mlp_recv, mlp_sums[0].got, mlp_sums[1].got, *halves = lax.optimization_barrier(
+        (hid1_recv, mlp_recv, mlp_sums[0].got, mlp_sums[1].got, *halves)
     )
     attn_sums = [CubeSum(*halves[2 * k : 2 * k + 2], n_blk, order) for k, order in enumerate(orders)]
     for part in attn_sums:
         part.move()
     token_grad = token_back(flags, hidL, hidS, hid1_recv, tokens, resid_grad, first_mod, lay)
-    many, token_grad, *gots = lax.optimization_barrier((many, token_grad, *[part.got for part in attn_sums]))
+    output, gate2_sums = layer_output(flags, mlp_own, mlp_recv, down_bias.astype(F32)[None], resid, cotangent, gate2)
+    gate2_sums, token_grad, *gots = lax.optimization_barrier((gate2_sums, token_grad, *[part.got for part in attn_sums]))
+    pack = pack_rows(flags, n_blk, mid_sums, gate2_sums, silu, down_b, (bm, bm2, bt, bt2), sumL, sumS, abL, abS)
+    many = spread(pack)
+    for part, got in zip(attn_sums, gots):
+        part.got = got
+        part.add()
+        part.move()
+    many, *gots = lax.optimization_barrier((many, *[part.got for part in attn_sums]))
     both = swap_side(many)
     for part, got in zip(attn_sums, gots):
         part.got = got
@@ -1347,15 +1370,9 @@
     both, down_mine, up_mine, *gots = lax.optimization_barrier((both, down_mine, up_mine, *[part.got for part in attn_sums]))
     for part, got in zip(attn_sums, gots):
         part.got = got
-        part.add()
-        part.move()
     both = jnp.stack([many, both])
     packs = jnp.stack([both, swap_core(both)]).reshape(-1, width)
     g_mod_weight, sums = modulation_grads(flags, long_rows, packs, row_out, "modulation_grads")
-    if len(bits) == 3:
-        sums, *gots = lax.optimization_barrier((sums, *[part.got for part in attn_sums]))
-        for part, got in zip(attn_sums, gots):
-            part.got = got
     for part in attn_sums:
         part.add()
     attn_mine = [part.finish() for part in attn_sums]

time: 303 us -> 297 us (0.980)
  Pallas kernels: 146 us -> 142 us
    ppermute x12, waiting for transfers between devices: 13.6 us -> 20.4 us  [move(): lax.ppermute(send, 'blk', [(i, i ^ hop) for i in range(self.n_blk)])]
    ppermute x1, waiting for transfers between devices: 8.27 us -> 2.81 us  [on_device(): lax.ppermute(proj_mine.astype(F32), ('blk', 'uly'), proj_map)]
    pallas_call x25 -> x24, Pallas kernels: 146 us -> 142 us  [kernel_call(): pl.pallas_call(body, grid_spec=pltpu.PrefetchScalarGridSpec(num_scalar_pr...]
    unnamed x107 -> x117, local copies, waits for them, and re-layouts: 7.02 us -> 9.02 us
  transfers between devices with their start and end apart: 45 -> 45, of which waited for: 16 -> 17; matrix products, arithmetic and copies ran while one was open for 10% -> 11% of each run, Pallas kernels for 44% -> 43%
where the time goes in v4:
time: 297 us; the launch traced here: 294 us
  Pallas kernels  142 us (48%)
  starting transfers between devices  65.7 us (22%)
  waiting for transfers between devices  37.8 us (13%)
  other arithmetic  21.1 us (7%)
  local copies, waits for them, and re-layouts  17.9 us (6%)
  matrix products  7.49 us (3%)
    pallas_call x24, Pallas kernels, kernel_call(): pl.pallas_call(body, grid_spec=pltpu.PrefetchScalarGridSpec(num_scalar_pr...  142 us
    all_to_all x5, starting transfers between devices, spread(): return lax.all_to_all(value, 'blk', split_axis=0, concat_axis=0, tiled=True)  25.4 us
    ppermute x12, waiting for transfers between devices, move(): lax.ppermute(send, 'blk', [(i, i ^ hop) for i in range(self.n_blk)])  20.4 us
    ppermute x12, starting transfers between devices, move(): lax.ppermute(send, 'blk', [(i, i ^ hop) for i in range(self.n_blk)])  15.9 us
    ppermute x11, starting transfers between devices, swap_side(): return lax.ppermute(value, 'uly', [(i, i ^ 2) for i in range(n_uly)])  13.2 us
    convert_element_type x8, other arithmetic, add(): (self.keep[k].astype(F32) + self.got[k].astype(F32)).astype(BF)  10.1 us
    unnamed x117, local copies, waits for them, and re-layouts  9.02 us
    dot_general x2, matrix products, dot(): return jnp.dot(left, right, preferred_element_type=F32)  7.49 us
  transfers between devices with their start and end apart: 45, of which 17 were waited for; matrix products, arithmetic and copies ran while one was open for 11% of the time, Pallas kernels for 43%

profile of v4, /device:TPU:4, one launch (start us, length us, event | category | flops | bytes accessed | tf_op | source)
XLA Modules:
  0.0 294.3 jit_solution(3442518381587780910)
XLA Ops:
  11.3 4.6 %fusion.2 = f32[2,4096]{1,0:T(2,128)S(1)} fusion(bf16[2,1024]{1,0:T(2,128)(2,1)S(1)} %fusion.16.s_ref, bf16[1024,6144]{1,0:T(8,128)(2,1)} %param.22, f32[4096]{0:T(1024)S(1)} %slice.269), kind=kOutput, calls=%fused_computation.2 | convolution fusion | flops 16785408 | bytes 8441856 | tf_op jit(solution)/shard_map/dot_general | solution.py:77
  19.1 7.7 %tokens_to_qkv.1 = (bf16[2,200,1024]{2,1,0:T(8,128)(2,1)}, bf16[8,320,128]{2,1,0:T(8,128)(2,1)S(1)}, bf16[8,320,128]{2,1,0:T(8,128)(2,1)S(1)}) custom-call(s32[6]{0:T(128)S(1)} %stack.49.flag_ref, bf16[200,1024]{1,0:T(8,128)(2,1)S(1)} %copy-done, bf16[200,1024]{1,0:T(8,128)(2,1)S(1)} %collective-permute-done.oth_ref.refs_8_.refs_2_, ...), custom_call_target="tpu_custom_call" | custom-call | flops 307200 | bytes 4096 | tf_op jit(solution)/shard_map/tokens_to_qkv/pallas_call | solution.py:117
  27.6 6.3 %all-to-all-start = ((bf16[8,320,128]{2,1,0:T(8,128)(2,1)}), bf16[8,320,128]{2,1,0:T(8,128)(2,1)S(1)}, u32[]{:S(2)}, u32[]{:S(2)}) async-start(bf16[8,320,128]{2,1,0:T(8,128)(2,1)} %copy-done.17), calls=%async_computation | async-start | bytes 1310720 | tf_op jit(solution)/shard_map/all_to_all | solution.py:1188
  35.7 5.6 %ahead_own.1.ahead_ref = f32[200,2048]{1,0:T(8,128)} custom-call(s32[6]{0:T(128)S(1)} %stack.49.flag_ref, bf16[200,1024]{1,0:T(8,128)(2,1)S(1)} %get-tuple-element.181.mg_ref.refs_4_, bf16[4096,1024]{1,0:T(8,128)(2,1)} %refs_1_.10, bf16[4096,1024]{1,0:T(8,128)(2,1)} %refs_1_.10), custom_call_target="tpu_custom_call" | custom-call | flops 204800 | bytes 4096 | tf_op jit(solution)/shard_map/ahead_own/pallas_call | solution.py:117
  41.3 5.9 %attend_short.1 = (bf16[8,112,128]{2,1,0:T(8,128)(2,1)S(1)}, f32[8,64,200]{2,1,0:T(8,128)}, f32[8,8,200]{2,1,0:T(8,128)}) custom-call(s32[6]{0:T(128)S(1)} %stack.49.flag_ref, bf16[8,320,128]{2,1,0:T(8,128)(2,1)S(1)} %get-tuple-element.159.own_ref, bf16[8,320,128]{2,1,0:T(8,128)(2,1)S(1)} %collective-permute-done.2.oth_ref), custom_call_target="tpu_custom_call" | custom-call | flops 160000 | bytes 4096 | tf_op jit(solution)/shard_map/attend_short/pallas_call | solution.py:117
  52.3 11.4 %attend_long.1 = (bf16[8,112,128]{2,1,0:T(8,128)(2,1)S(1)}, f32[4,64,400]{2,1,0:T(8,128)}, f32[4,8,400]{2,1,0:T(8,128)}) custom-call(s32[6]{0:T(128)S(1)} %stack.49.flag_ref, bf16[8,320,128]{2,1,0:T(8,128)(2,1)S(1)} %all-to-all-done.own_ref, bf16[8,320,128]{2,1,0:T(8,128)(2,1)S(1)} %collective-permute-done.3.oth_ref), custom_call_target="tpu_custom_call" | custom-call | flops 800000 | bytes 4096 | tf_op jit(solution)/shard_map/attend_long/pallas_call | solution.py:117
  65.1 4.2 %all-to-all-start.1 = ((bf16[8,112,128]{2,1,0:T(8,128)(2,1)}), bf16[8,112,128]{2,1,0:T(8,128)(2,1)S(1)}, u32[]{:S(2)}, u32[]{:S(2)}) async-start(bf16[8,112,128]{2,1,0:T(8,128)(2,1)} %copy-done.23), calls=%async_computation.1 | async-start | bytes 458752 | tf_op jit(solution)/shard_map/all_to_all | solution.py:1188
  70.4 5.6 %ahead_other.1.ahead_ref = f32[200,2048]{1,0:T(8,128)} custom-call(s32[6]{0:T(128)S(1)} %stack.49.flag_ref, bf16[200,1024]{1,0:T(8,128)(2,1)S(1)} %copy-done.13, bf16[4096,1024]{1,0:T(8,128)(2,1)} %refs_1_.10, bf16[4096,1024]{1,0:T(8,128)(2,1)} %refs_1_.10), custom_call_target="tpu_custom_call" | custom-call | flops 204800 | bytes 4096 | tf_op jit(solution)/shard_map/ahead_other/pallas_call | solution.py:117
  79.0 4.4 %collective-permute-done.5.recv_ref = bf16[8,112,128]{2,1,0:T(8,128)(2,1)S(1)} collective-permute-done((bf16[8,112,128]{2,1,0:T(8,128)(2,1)S(1)}, bf16[8,112,128]{2,1,0:T(8,128)(2,1)S(1)}, u32[]{:S(2)}, u32[]{:S(2)}) %collective-permute-start.5) | collective-permute-done | bytes 229408 | tf_op jit(solution)/shard_map/ppermute | solution.py:1182
  83.4 4.5 %project_and_norm.1 = (f32[200,1024]{1,0:T(8,128)}, f32[200,1024]{1,0:T(8,128)}, f32[200,1024]{1,0:T(8,128)}, f32[200,128]{1,0:T(8,128)}, bf16[200,1024]{1,0:T(8,128)(2,1)S(1)}) custom-call(s32[6]{0:T(128)S(1)} %stack.49.flag_ref, bf16[8,112,128]{2,1,0:T(8,128)(2,1)S(1)} %all-to-all-done.1.long_ref.l_ref, ...), custom_call_target="tpu_custom_call" | custom-call | flops 102400 | bytes 4096 | tf_op jit(solution)/shard_map/project_and_norm/pallas_call | solution.py:117
  89.4 6.9 %hidden_own.1 = (bf16[2,200,1024]{2,1,0:T(8,128)(2,1)S(1)}, bf16[2,200,1024]{2,1,0:T(8,128)(2,1)S(1)}, f32[8,1024]{1,0:T(8,128)S(1)}, f32[8,1024]{1,0:T(8,128)S(1)}, f32[200,1024]{1,0:T(8,128)S(1)}) custom-call(s32[6]{0:T(128)S(1)} %stack.49.flag_ref, bf16[200,1024]{1,0:T(8,128)(2,1)S(1)} %get-tuple-element.170.hid_ref.refs_8_, ...), custom_call_target="tpu_custom_call" | custom-call | flops 409600 | bytes 4096 | tf_op jit(solution)/shard_map/hidden_own/pallas_call | solution.py:117
  97.7 6.8 %hidden_other.1 = (bf16[2,200,1024]{2,1,0:T(8,128)(2,1)S(1)}, bf16[2,200,1024]{2,1,0:T(8,128)(2,1)S(1)}, f32[8,1024]{1,0:T(8,128)S(1)}, f32[8,1024]{1,0:T(8,128)S(1)}, bf16[200,1024]{1,0:T(8,128)(2,1)S(1)}) custom-call(s32[6]{0:T(128)S(1)} %stack.49.flag_ref, bf16[200,1024]{1,0:T(8,128)(2,1)S(1)} %collective-permute-done.6.hid_ref.refs_9_, ...), custom_call_target="tpu_custom_call" | custom-call | flops 409600 | bytes 4096 | tf_op jit(solution)/shard_map/hidden_other/pallas_call | solution.py:117
  109.3 9.4 %mlp_grads.1 = (bf16[4,128,1024]{2,1,0:T(8,128)(2,1)}, bf16[4,128,1024]{2,1,0:T(8,128)(2,1)S(1)}, bf16[4,128,1024]{2,1,0:T(8,128)(2,1)}, bf16[4,128,1024]{2,1,0:T(8,128)(2,1)S(1)}) custom-call(s32[6]{0:T(128)S(1)} %stack.49.flag_ref, bf16[2,200,1024]{2,1,0:T(8,128)(2,1)S(1)} %get-tuple-element.177.refs_0_.refs_12_.m_ref, ...), custom_call_target="tpu_custom_call" | custom-call | flops 819200 | bytes 4096 | tf_op jit(solution)/shard_map/mlp_grads/pallas_call | solution.py:117
  121.4 4.8 %branch_back.1 = (f32[200,1024]{1,0:T(8,128)}, bf16[200,1024]{1,0:T(8,128)(2,1)S(1)}, bf16[8,112,128]{2,1,0:T(8,128)(2,1)S(1)}, bf16[8,112,128]{2,1,0:T(8,128)(2,1)S(1)}, f32[8,1024]{1,0:T(8,128)S(1)}) custom-call(s32[6]{0:T(128)S(1)} %stack.49.flag_ref, f32[200,1024]{1,0:T(8,128)} %copy-done.16, bf16[200,1024]{1,0:T(8,128)(2,1)S(1)} %collective-permute-done.7.b_ref, ...), custom_call_target="tpu_custom_call" | custom-call | flops 102400 | bytes 4096 | tf_op jit(solution)/shard_map/branch_back/pallas_call | solution.py:117
  127.3 7.2 %forward_rows.1 = (f32[200,1024]{1,0:T(8,128)}, bf16[200,1024]{1,0:T(8,128)(2,1)}) custom-call(s32[6]{0:T(128)S(1)} %stack.49.flag_ref, bf16[2,200,1024]{2,1,0:T(8,128)(2,1)S(1)} %get-tuple-element.177.refs_0_.refs_12_.m_ref, bf16[2,200,1024]{2,1,0:T(8,128)(2,1)S(1)} %get-tuple-element.179.s_ref, ...), custom_call_target="tpu_custom_call" | custom-call | flops 409600 | bytes 4096 | tf_op jit(solution)/shard_map/forward_rows/pallas_call | solution.py:117
  136.3 5.3 %all-to-all-start.2 = ((bf16[8,112,128]{2,1,0:T(8,128)(2,1)}), bf16[8,112,128]{2,1,0:T(8,128)(2,1)S(1)}, u32[]{:S(2)}, u32[]{:S(2)}) async-start(bf16[8,112,128]{2,1,0:T(8,128)(2,1)} %broadcast_select_fusion.1), calls=%async_computation.2 | async-start | bytes 458752 | tf_op jit(solution)/shard_map/all_to_all | solution.py:1188
  141.7 7.4 %attend_back_short.1 = (bf16[8,200,128]{2,1,0:T(8,128)(2,1)}, f32[8,200,128]{2,1,0:T(8,128)}, bf16[8,200,128]{2,1,0:T(8,128)(2,1)S(1)}) custom-call(s32[6]{0:T(128)S(1)} %stack.49.flag_ref, bf16[8,320,128]{2,1,0:T(8,128)(2,1)} %copy-done.5, bf16[8,320,128]{2,1,0:T(8,128)(2,1)} %copy-done.6, bf16[8,112,128]{2,1,0:T(8,128)(2,1)S(1)} %get-tuple-element.195.refs_0_, ...), custom_call_target="tpu_custom_call" | custom-call | flops 400000 | bytes 4096 | tf_op jit(solution)/shard_map/attend_back_short/pallas_call | solution.py:117
  154.7 3.3 %collective-permute-start.19 = (bf16[2,128,1024]{2,1,0:T(8,128)(2,1)S(1)}, bf16[2,128,1024]{2,1,0:T(8,128)(2,1)S(1)}, u32[]{:S(2)}, u32[]{:S(2)}) collective-permute-start(bf16[2,128,1024]{2,1,0:T(8,128)(2,1)S(1)} %get-tuple-element.221), channel_id=1, source_target_pairs={{0,24},{4,28},{8,16},{12,20},{16,8},{20,12},{24,0},{28,4},{1,25},{... | collective-permute-start | bytes 1572872 | tf_op jit(solution)/shard_map/ppermute | solution.py:1031
  158.5 17.4 %attend_back_long.1 = (bf16[8,200,128]{2,1,0:T(8,128)(2,1)}, f32[8,200,128]{2,1,0:T(8,128)}, bf16[8,200,128]{2,1,0:T(8,128)(2,1)S(1)}) custom-call(s32[6]{0:T(128)S(1)} %stack.49.flag_ref, bf16[8,320,128]{2,1,0:T(8,128)(2,1)} %copy-done.1, bf16[8,320,128]{2,1,0:T(8,128)(2,1)} %copy-done.4, bf16[8,112,128]{2,1,0:T(8,128)(2,1)S(1)} %all-to-all-done.2.refs_0_, ...), custom_call_target="tpu_custom_call" | custom-call | flops 2000000 | bytes 4096 | tf_op jit(solution)/shard_map/attend_back_long/pallas_call | solution.py:117
  177.8 3.8 %finish_keys.1 = bf16[8,320,128]{2,1,0:T(8,128)(2,1)} custom-call(s32[6]{0:T(128)S(1)} %stack.49.flag_ref, bf16[8,200,128]{2,1,0:T(8,128)(2,1)} %get-tuple-element.218.dq_ref, f32[8,200,128]{2,1,0:T(8,128)} %get-tuple-element.219.a_ref, bf16[8,200,128]{2,1,0:T(8,128)(2,1)S(1)} %collective-permute-done.18.b_ref, f32[200,128]{1,0:T(8,128)S(1)} %copy-done.8, ...), custom_call_target="tpu_custom_call" | custom-call | flops 500 | bytes 4096 | tf_op jit(solution)/shard_map/finish_keys/pallas_call | solution.py:117
  181.5 4.9 %all-to-all-start.3 = ((bf16[8,320,128]{2,1,0:T(8,128)(2,1)}), bf16[8,320,128]{2,1,0:T(8,128)(2,1)S(1)}, u32[]{:S(2)}, u32[]{:S(2)}) async-start(bf16[8,320,128]{2,1,0:T(8,128)(2,1)} %finish_keys.1), calls=%async_computation.3 | async-start | bytes 1310720 | tf_op jit(solution)/shard_map/all_to_all | solution.py:1188
  188.1 6.9 %qkv_back_short.1 = (f32[200,1024]{1,0:T(8,128)}, bf16[200,1024]{1,0:T(8,128)(2,1)S(1)}, bf16[200,768]{1,0:T(8,128)(2,1)S(1)}, bf16[200,768]{1,0:T(8,128)(2,1)},...) custom-call(s32[6]{0:T(128)S(1)} %stack.49.flag_ref, bf16[8,200,128]{2,1,0:T(8,128)(2,1)} %get-tuple-element.229.refs_0_, ...), custom_call_target="tpu_custom_call" | custom-call | flops 153600 | bytes 4096 | tf_op jit(solution)/shard_map/qkv_back_short/pallas_call | solution.py:117
  203.8 6.0 %qkv_back_long.1 = (f32[200,1024]{1,0:T(8,128)}, bf16[200,1024]{1,0:T(8,128)(2,1)S(1)}, bf16[200,768]{1,0:T(8,128)(2,1)S(1)}, bf16[200,768]{1,0:T(8,128)(2,1)S(1...) custom-call(s32[6]{0:T(128)S(1)} %stack.49.flag_ref, bf16[8,320,128]{2,1,0:T(8,128)(2,1)S(1)} %all-to-all-done.3.refs_0_, ...), custom_call_target="tpu_custom_call" | custom-call | flops 153600 | bytes 4096 | tf_op jit(solution)/shard_map/qkv_back_long/pallas_call | solution.py:117
  214.7 7.0 %attn_grads.1 = (bf16[4,128,512]{2,1,0:T(8,128)(2,1)S(1)}, bf16[4,128,512]{2,1,0:T(8,128)(2,1)S(1)}, bf16[4,256,256]{2,1,0:T(8,128)(2,1)S(1)}, bf16[4,256,256]{2,1,0:T(8,128)(2,1)S(1)}) custom-call(s32[6]{0:T(128)S(1)} %stack.49.flag_ref, bf16[2,200,1024]{2,1,0:T(8,128)(2,1)} %get-tuple-element.242.refs_0_.refs_1_, ...), custom_call_target="tpu_custom_call" | custom-call | flops 307200 | bytes 4096 | tf_op jit(solution)/shard_map/attn_grads/pallas_call | solution.py:117
  221.7 4.6 %collective-permute-done.25 = bf16[1,128,1024]{2,1,0:T(8,128)(2,1)S(1)} collective-permute-done((bf16[1,128,1024]{2,1,0:T(8,128)(2,1)S(1)}, bf16[1,128,1024]{2,1,0:T(8,128)(2,1)S(1)}, u32[]{:S(2)}, u32[]{:S(2)}) %collective-permute-start.25) | collective-permute-done | bytes 262176 | tf_op jit(solution)/shard_map/ppermute | solution.py:1031
  228.1 3.1 %layer_output.1 = (bf16[200,1024]{1,0:T(8,128)(2,1)}, f32[8,1024]{1,0:T(8,128)S(1)}) custom-call(s32[6]{0:T(128)S(1)} %stack.49.flag_ref, f32[200,1024]{1,0:T(8,128)} %get-tuple-element.194.a_ref, bf16[200,1024]{1,0:T(8,128)(2,1)} %collective-permute-done.23.b_ref, f32[1,1024]{1,0:T(1,128)S(1)} %bitcast.69, f32[200,1024]{1,0:T(8,128)} %get-tuple-element.253.r_ref, ...), custom_call_target="tpu_custom_call" | custom-call | flops 200 | bytes 4096 | tf_op jit(solution)/shard_map/layer_output/pallas_call | solution.py:117
  231.3 3.8 %token_back.1 = f32[200,1024]{1,0:T(8,128)} custom-call(s32[6]{0:T(128)S(1)} %stack.49.flag_ref, f32[200,1024]{1,0:T(8,128)} %get-tuple-element.256.l_ref, f32[200,1024]{1,0:T(8,128)} %get-tuple-element.257.s_ref, bf16[200,1024]{1,0:T(8,128)(2,1)S(1)} %collective-permute-done.22.r_ref, bf16[200,1024]{1,0:T(8,128)(2,1)} %tok_ref.3, ...), custom_call_target="tpu_custom_call" | custom-call | flops 1000 | bytes 4096 | tf_op jit(solution)/shard_map/token_back/pallas_call | solution.py:117
  235.1 4.7 %collective-permute-done.30 = bf16[4,128,512]{2,1,0:T(8,128)(2,1)S(1)} collective-permute-done((bf16[4,128,512]{2,1,0:T(8,128)(2,1)S(1)}, bf16[4,128,512]{2,1,0:T(8,128)(2,1)S(1)}, u32[]{:S(2)}, u32[]{:S(2)}) %collective-permute-start.30) | collective-permute-done | bytes 524320 | tf_op jit(solution)/shard_map/ppermute | solution.py:1031
  241.9 4.6 %all-to-all-start.4 = ((bf16[8,24,1024]{2,1,0:T(8,128)(2,1)}), bf16[8,24,1024]{2,1,0:T(8,128)(2,1)S(1)}, u32[]{:S(2)}, u32[]{:S(2)}) async-start(bf16[8,24,1024]{2,1,0:T(8,128)(2,1)} %pack_rows.1), calls=%async_computation.4 | async-start | bytes 786432 | tf_op jit(solution)/shard_map/all_to_all | solution.py:1188
  253.2 6.7 %collective-permute-done.32 = bf16[2,128,512]{2,1,0:T(8,128)(2,1)S(1)} collective-permute-done((bf16[2,128,512]{2,1,0:T(8,128)(2,1)}, bf16[2,128,512]{2,1,0:T(8,128)(2,1)S(1)}, u32[]{:S(2)}, u32[]{:S(2)}) %collective-permute-start.32) | collective-permute-done | bytes 262176 | tf_op jit(solution)/shard_map/ppermute | solution.py:1031
  275.1 5.7 %all-to-all-start.5 = ((bf16[4,32,1792]{2,1,0:T(8,128)(2,1)}), bf16[4,32,1792]{2,1,0:T(8,128)(2,1)S(1)}, u32[]{:S(2)}, u32[]{:S(2)}) async-start(bf16[4,32,1792]{2,1,0:T(8,128)(2,1)} %bitcast.27), calls=%async_computation.5 | async-start | bytes 917504 | tf_op jit(solution)/shard_map/all_to_all | solution.py:1387
  284.9 3.5 %modulation_grads.1 = (f32[32,6144]{1,0:T(8,128)}, f32[4,32,1024]{2,1,0:T(8,128)S(1)}) custom-call(s32[6]{0:T(128)S(1)} %stack.49.flag_ref, f32[768,128]{1,0:T(8,128)S(1)} %copy-done.15, bf16[768,1024]{1,0:T(8,128)(2,1)S(1)} %bitcast.62), custom_call_target="tpu_custom_call" | custom-call | flops 294912 | bytes 4096 | tf_op jit(solution)/shard_map/modulation_grads/pallas_call | solution.py:117
  (275 shorter events, 98.0 us)
Async XLA Ops:
  0.6 18.4 %collective-permute-start = (bf16[200,1024]{1,0:T(8,128)(2,1)}, bf16[200,1024]{1,0:T(8,128)(2,1)S(1)}, u32[]{:S(2)}, u32[]{:S(2)}) collective-permute-start(bf16[200,1024]{1,0:T(8,128)(2,1)} %tok_ref.3), channel_id=1, source_target_pairs={{0,2},{1,3},{2,0},{3,1},{4,6},{5,7},{6,4},{7,5},{8,10},{9,11},{10,... | collective-permute-start | bytes 1228808 | tf_op jit(solution)/shard_map/ppermute | solution.py:1182
  5.8 12.3 %collective-permute-start.1 = (f32[2,2048]{1,0:T(2,128)S(1)}, f32[2,2048]{1,0:T(2,128)S(1)}, u32[]{:S(2)}, u32[]{:S(2)}) collective-permute-start(f32[2,2048]{1,0:T(2,128)S(1)} %fusion.7.mod_ref), channel_id=1, source_target_pairs={{0,2},{1,3},{2,0},{3,1},{4,6},{5,7},{6,4},{7,5},{8,10},{9,11},{10,... | collective-permute-start | bytes 49160 | tf_op jit(solution)/shard_map/ppermute | solution.py:1182
  27.6 22.5 %all-to-all-start = ((bf16[8,320,128]{2,1,0:T(8,128)(2,1)}), bf16[8,320,128]{2,1,0:T(8,128)(2,1)S(1)}, u32[]{:S(2)}, u32[]{:S(2)}) async-start(bf16[8,320,128]{2,1,0:T(8,128)(2,1)} %copy-done.17), calls=%async_computation | async-start | bytes 1310720 | tf_op jit(solution)/shard_map/all_to_all | solution.py:1188
  50.2 13.5 %collective-permute-start.4 = (bf16[200,1024]{1,0:T(8,128)(2,1)S(1)}, bf16[200,1024]{1,0:T(8,128)(2,1)S(1)}, u32[]{:S(2)}, u32[]{:S(2)}) collective-permute-start(bf16[200,1024]{1,0:T(8,128)(2,1)S(1)} %get-tuple-element.181.mg_ref.refs_4_), channel_id=1, source_target_pairs={{0,2},{1,3},{2,0},{3,1},{4,6},{5,7},{6,4},{7,5},{8,10},{9,11},{10,... | collective-permute-start | bytes 1228808 | tf_op jit(solution)/shard_map/ppermute | solution.py:1182
  65.1 12.1 %all-to-all-start.1 = ((bf16[8,112,128]{2,1,0:T(8,128)(2,1)}), bf16[8,112,128]{2,1,0:T(8,128)(2,1)S(1)}, u32[]{:S(2)}, u32[]{:S(2)}) async-start(bf16[8,112,128]{2,1,0:T(8,128)(2,1)} %copy-done.23), calls=%async_computation.1 | async-start | bytes 458752 | tf_op jit(solution)/shard_map/all_to_all | solution.py:1188
  87.9 9.8 %collective-permute-start.6 = (bf16[200,1024]{1,0:T(8,128)(2,1)S(1)}, bf16[200,1024]{1,0:T(8,128)(2,1)S(1)}, u32[]{:S(2)}, u32[]{:S(2)}) collective-permute-start(bf16[200,1024]{1,0:T(8,128)(2,1)S(1)} %get-tuple-element.170.hid_ref.refs_8_), channel_id=1, source_target_pairs={{0,2},{1,3},{2,0},{3,1},{4,6},{5,7},{6,4},{7,5},{8,10},{9,11},{10,... | collective-permute-start | bytes 1228808 | tf_op jit(solution)/shard_map/ppermute | solution.py:1182
  89.4 16.4 %collective-permute-start.10 = (bf16[200,1024]{1,0:T(8,128)(2,1)S(1)}, bf16[200,1024]{1,0:T(8,128)(2,1)S(1)}, u32[]{:S(2)}, u32[]{:S(2)}) collective-permute-start(bf16[200,1024]{1,0:T(8,128)(2,1)S(1)} %get-tuple-element.181.mg_ref.refs_4_), channel_id=1, source_target_pairs={{0,1},{1,0},{2,3},{3,2},{4,5},{5,4},{6,7},{7,6},{8,9},{9,8},{10,11... | collective-permute-start | bytes 1228808 | tf_op jit(solution)/shard_map/ppermute | solution.py:1185
  97.2 11.5 %collective-permute-start.8 = (bf16[2,200,1024]{2,1,0:T(8,128)(2,1)S(1)}, bf16[2,200,1024]{2,1,0:T(8,128)(2,1)S(1)}, u32[]{:S(2)}, u32[]{:S(2)}) collective-permute-start(bf16[2,200,1024]{2,1,0:T(8,128)(2,1)S(1)} %get-tuple-element.179.s_ref), channel_id=1, source_target_pairs={{0,1},{1,0},{2,3},{3,2},{4,5},{5,4},{6,7},{7,6},{8,9},{9,8},{10,11... | collective-permute-start | bytes 2457608 | tf_op jit(solution)/shard_map/ppermute | solution.py:1185
  108.1 11.5 %collective-permute-start.7 = (bf16[200,1024]{1,0:T(8,128)(2,1)S(1)}, bf16[200,1024]{1,0:T(8,128)(2,1)S(1)}, u32[]{:S(2)}, u32[]{:S(2)}) collective-permute-start(bf16[200,1024]{1,0:T(8,128)(2,1)S(1)} %get-tuple-element.176), channel_id=1, source_target_pairs={{0,2},{1,3},{2,0},{3,1},{4,6},{5,7},{6,4},{7,5},{8,10},{9,11},{10,... | collective-permute-start | bytes 1228808 | tf_op jit(solution)/shard_map/ppermute | solution.py:1182
  119.6 30.2 %collective-permute-start.16 = (bf16[4,128,1024]{2,1,0:T(8,128)(2,1)}, bf16[4,128,1024]{2,1,0:T(8,128)(2,1)}, u32[]{:S(2)}, u32[]{:S(2)}) collective-permute-start(bf16[4,128,1024]{2,1,0:T(8,128)(2,1)} %get-tuple-element.206), channel_id=1, source_target_pairs={{0,4},{4,0},{8,12},{12,8},{16,20},{20,16},{24,28},{28,24},{1,5},{5... | collective-permute-start | bytes 3145736 | tf_op jit(solution)/shard_map/ppermute | solution.py:1031
  120.4 29.4 %collective-permute-start.17 = (bf16[4,128,1024]{2,1,0:T(8,128)(2,1)}, bf16[4,128,1024]{2,1,0:T(8,128)(2,1)}, u32[]{:S(2)}, u32[]{:S(2)}) collective-permute-start(bf16[4,128,1024]{2,1,0:T(8,128)(2,1)} %get-tuple-element.207), channel_id=1, source_target_pairs={{0,8},{4,12},{8,0},{12,4},{16,24},{20,28},{24,16},{28,20},{1,9},{5... | collective-permute-start | bytes 3145736 | tf_op jit(solution)/shard_map/ppermute | solution.py:1031
  134.5 15.3 %collective-permute-start.15 = (bf16[200,1024]{1,0:T(8,128)(2,1)S(1)}, bf16[200,1024]{1,0:T(8,128)(2,1)}, u32[]{:S(2)}, u32[]{:S(2)}) collective-permute-start(bf16[200,1024]{1,0:T(8,128)(2,1)S(1)} %get-tuple-element.205.go_ref), channel_id=1, source_target_pairs={{0,2},{1,3},{2,0},{3,1},{4,6},{5,7},{6,4},{7,5},{8,10},{9,11},{10,... | collective-permute-start | bytes 1228808 | tf_op jit(solution)/shard_map/ppermute | solution.py:1182
  136.3 13.5 %all-to-all-start.2 = ((bf16[8,112,128]{2,1,0:T(8,128)(2,1)}), bf16[8,112,128]{2,1,0:T(8,128)(2,1)S(1)}, u32[]{:S(2)}, u32[]{:S(2)}) async-start(bf16[8,112,128]{2,1,0:T(8,128)(2,1)} %broadcast_select_fusion.1), calls=%async_computation.2 | async-start | bytes 458752 | tf_op jit(solution)/shard_map/all_to_all | solution.py:1188
  154.7 23.0 %collective-permute-start.19 = (bf16[2,128,1024]{2,1,0:T(8,128)(2,1)S(1)}, bf16[2,128,1024]{2,1,0:T(8,128)(2,1)S(1)}, u32[]{:S(2)}, u32[]{:S(2)}) collective-permute-start(bf16[2,128,1024]{2,1,0:T(8,128)(2,1)S(1)} %get-tuple-element.221), channel_id=1, source_target_pairs={{0,24},{4,28},{8,16},{12,20},{16,8},{20,12},{24,0},{28,4},{1,25},{... | collective-permute-start | bytes 1572872 | tf_op jit(solution)/shard_map/ppermute | solution.py:1031
  158.0 19.8 %collective-permute-start.20 = (bf16[2,128,1024]{2,1,0:T(8,128)(2,1)S(1)}, bf16[2,128,1024]{2,1,0:T(8,128)(2,1)}, u32[]{:S(2)}, u32[]{:S(2)}) collective-permute-start(bf16[2,128,1024]{2,1,0:T(8,128)(2,1)S(1)} %get-tuple-element.222), channel_id=1, source_target_pairs={{0,4},{4,0},{8,12},{12,8},{16,20},{20,16},{24,28},{28,24},{1,5},{5... | collective-permute-start | bytes 1572872 | tf_op jit(solution)/shard_map/ppermute | solution.py:1031
  176.0 12.1 %collective-permute-start.21 = (bf16[8,200,128]{2,1,0:T(8,128)(2,1)S(1)}, bf16[8,200,128]{2,1,0:T(8,128)(2,1)S(1)}, u32[]{:S(2)}, u32[]{:S(2)}) collective-permute-start(bf16[8,200,128]{2,1,0:T(8,128)(2,1)S(1)} %copy-done.39), channel_id=1, source_target_pairs={{0,1},{1,0},{2,3},{3,2},{4,5},{5,4},{6,7},{7,6},{8,9},{9,8},{10,11... | collective-permute-start | bytes 1228808 | tf_op jit(solution)/shard_map/ppermute | solution.py:1185
  181.5 22.3 %all-to-all-start.3 = ((bf16[8,320,128]{2,1,0:T(8,128)(2,1)}), bf16[8,320,128]{2,1,0:T(8,128)(2,1)S(1)}, u32[]{:S(2)}, u32[]{:S(2)}) async-start(bf16[8,320,128]{2,1,0:T(8,128)(2,1)} %finish_keys.1), calls=%async_computation.3 | async-start | bytes 1310720 | tf_op jit(solution)/shard_map/all_to_all | solution.py:1188
  186.5 24.9 %collective-permute-start.26 = (bf16[2,200,1024]{2,1,0:T(8,128)(2,1)}, bf16[2,200,1024]{2,1,0:T(8,128)(2,1)}, u32[]{:S(2)}, u32[]{:S(2)}) collective-permute-start(bf16[2,200,1024]{2,1,0:T(8,128)(2,1)} %get-tuple-element.242.refs_0_.refs_1_), channel_id=1, source_target_pairs={{0,1},{1,0},{2,3},{3,2},{4,5},{5,4},{6,7},{7,6},{8,9},{9,8},{10,11... | collective-permute-start | bytes 2457608 | tf_op jit(solution)/shard_map/ppermute | solution.py:1185
  186.6 35.2 %collective-permute-start.23 = (bf16[200,1024]{1,0:T(8,128)(2,1)}, bf16[200,1024]{1,0:T(8,128)(2,1)}, u32[]{:S(2)}, u32[]{:S(2)}) collective-permute-start(bf16[200,1024]{1,0:T(8,128)(2,1)} %get-tuple-element.239), channel_id=1, source_target_pairs={{0,2},{1,3},{2,0},{3,1},{4,6},{5,7},{6,4},{7,5},{8,10},{9,11},{10,... | collective-permute-start | bytes 1228808 | tf_op jit(solution)/shard_map/ppermute | solution.py:1182
  196.4 15.0 %collective-permute-start.28 = (bf16[200,768]{1,0:T(8,128)(2,1)}, bf16[200,768]{1,0:T(8,128)(2,1)S(1)}, u32[]{:S(2)}, u32[]{:S(2)}) collective-permute-start(bf16[200,768]{1,0:T(8,128)(2,1)} %get-tuple-element.246), channel_id=1, source_target_pairs={{0,1},{1,0},{2,3},{3,2},{4,5},{5,4},{6,7},{7,6},{8,9},{9,8},{10,11... | collective-permute-start | bytes 921608 | tf_op jit(solution)/shard_map/ppermute | solution.py:1185
  200.3 11.2 %collective-permute-start.29 = (bf16[256,1024]{1,0:T(8,128)(2,1)}, bf16[256,1024]{1,0:T(8,128)(2,1)S(1)}, u32[]{:S(2)}, u32[]{:S(2)}) collective-permute-start(bf16[256,1024]{1,0:T(8,128)(2,1)} %slice_select_fusion), channel_id=1, source_target_pairs={{0,1},{1,0},{2,3},{3,2},{4,5},{5,4},{6,7},{7,6},{8,9},{9,8},{10,11... | collective-permute-start | bytes 1572872 | tf_op jit(solution)/shard_map/ppermute | solution.py:1185
  209.9 16.4 %collective-permute-start.22 = (bf16[200,1024]{1,0:T(8,128)(2,1)S(1)}, bf16[200,1024]{1,0:T(8,128)(2,1)S(1)}, u32[]{:S(2)}, u32[]{:S(2)}) collective-permute-start(bf16[200,1024]{1,0:T(8,128)(2,1)S(1)} %broadcast_select_fusion), channel_id=1, source_target_pairs={{0,2},{1,3},{2,0},{3,1},{4,6},{5,7},{6,4},{7,5},{8,10},{9,11},{10,... | collective-permute-start | bytes 1228808 | tf_op jit(solution)/shard_map/ppermute | solution.py:1182
  211.4 10.3 %collective-permute-start.24 = (bf16[1,128,1024]{2,1,0:T(8,128)(2,1)S(1)}, bf16[1,128,1024]{2,1,0:T(8,128)(2,1)S(1)}, u32[]{:S(2)}, u32[]{:S(2)}) collective-permute-start(bf16[1,128,1024]{2,1,0:T(8,128)(2,1)S(1)} %copy-done.50), channel_id=1, source_target_pairs={{0,8},{4,12},{8,0},{12,4},{16,24},{20,28},{24,16},{28,20},{1,9},{5... | collective-permute-start | bytes 786440 | tf_op jit(solution)/shard_map/ppermute | solution.py:1031
  211.5 14.8 %collective-permute-start.25 = (bf16[1,128,1024]{2,1,0:T(8,128)(2,1)S(1)}, bf16[1,128,1024]{2,1,0:T(8,128)(2,1)S(1)}, u32[]{:S(2)}, u32[]{:S(2)}) collective-permute-start(bf16[1,128,1024]{2,1,0:T(8,128)(2,1)S(1)} %copy-done.49), channel_id=1, source_target_pairs={{0,24},{4,28},{8,16},{12,20},{16,8},{20,12},{24,0},{28,4},{1,25},{... | collective-permute-start | bytes 786440 | tf_op jit(solution)/shard_map/ppermute | solution.py:1031
  226.3 13.5 %collective-permute-start.30 = (bf16[4,128,512]{2,1,0:T(8,128)(2,1)S(1)}, bf16[4,128,512]{2,1,0:T(8,128)(2,1)S(1)}, u32[]{:S(2)}, u32[]{:S(2)}) collective-permute-start(bf16[4,128,512]{2,1,0:T(8,128)(2,1)S(1)} %get-tuple-element.260), channel_id=1, source_target_pairs={{0,4},{4,0},{8,12},{12,8},{16,20},{20,16},{24,28},{28,24},{1,5},{5... | collective-permute-start | bytes 1572872 | tf_op jit(solution)/shard_map/ppermute | solution.py:1031
  226.9 13.2 %collective-permute-start.31 = (bf16[4,256,256]{2,1,0:T(8,128)(2,1)S(1)}, bf16[4,256,256]{2,1,0:T(8,128)(2,1)S(1)}, u32[]{:S(2)}, u32[]{:S(2)}) collective-permute-start(bf16[4,256,256]{2,1,0:T(8,128)(2,1)S(1)} %get-tuple-element.261), channel_id=1, source_target_pairs={{0,8},{4,12},{8,0},{12,4},{16,24},{20,28},{24,16},{28,20},{1,9},{5... | collective-permute-start | bytes 1572872 | tf_op jit(solution)/shard_map/ppermute | solution.py:1031
  241.9 18.0 %all-to-all-start.4 = ((bf16[8,24,1024]{2,1,0:T(8,128)(2,1)}), bf16[8,24,1024]{2,1,0:T(8,128)(2,1)S(1)}, u32[]{:S(2)}, u32[]{:S(2)}) async-start(bf16[8,24,1024]{2,1,0:T(8,128)(2,1)} %pack_rows.1), calls=%async_computation.4 | async-start | bytes 786432 | tf_op jit(solution)/shard_map/all_to_all | solution.py:1188
  248.4 11.5 %collective-permute-start.32 = (bf16[2,128,512]{2,1,0:T(8,128)(2,1)}, bf16[2,128,512]{2,1,0:T(8,128)(2,1)S(1)}, u32[]{:S(2)}, u32[]{:S(2)}) collective-permute-start(bf16[2,128,512]{2,1,0:T(8,128)(2,1)} %get-tuple-element.307), channel_id=1, source_target_pairs={{0,8},{4,12},{8,0},{12,4},{16,24},{20,28},{24,16},{28,20},{1,9},{5... | collective-permute-start | bytes 786440 | tf_op jit(solution)/shard_map/ppermute | solution.py:1031
  260.0 10.3 %collective-permute-start.34 = (bf16[8,24,1024]{2,1,0:T(8,128)(2,1)S(1)}, bf16[8,24,1024]{2,1,0:T(8,128)(2,1)S(1)}, u32[]{:S(2)}, u32[]{:S(2)}) collective-permute-start(bf16[8,24,1024]{2,1,0:T(8,128)(2,1)S(1)} %all-to-all-done.4), channel_id=1, source_target_pairs={{0,2},{1,3},{2,0},{3,1},{4,6},{5,7},{6,4},{7,5},{8,10},{9,11},{10,... | collective-permute-start | bytes 1179656 | tf_op jit(solution)/shard_map/ppermute | solution.py:1182
  271.3 12.4 %collective-permute-start.37 = (bf16[2,8,24,1024]{3,2,1,0:T(8,128)(2,1)}, bf16[2,8,24,1024]{3,2,1,0:T(8,128)(2,1)}, u32[]{:S(2)}, u32[]{:S(2)}) collective-permute-start(bf16[2,8,24,1024]{3,2,1,0:T(8,128)(2,1)} %get-tuple-element.309), channel_id=1, source_target_pairs={{0,1},{1,0},{2,3},{3,2},{4,5},{5,4},{6,7},{7,6},{8,9},{9,8},{10,11... | collective-permute-start | bytes 2359304 | tf_op jit(solution)/shard_map/ppermute | solution.py:1185
  271.3 12.3 %collective-permute-start.38 = (f32[32,1024]{1,0:T(8,128)S(1)}, f32[32,1024]{1,0:T(8,128)S(1)}, u32[]{:S(2)}, u32[]{:S(2)}) collective-permute-start(f32[32,1024]{1,0:T(8,128)S(1)} %pad_maximum_fusion.3), channel_id=1, source_target_pairs={{0,0},{1,8},{2,16},{3,24},{4,1},{5,9},{6,17},{7,25},{8,2},{9,10},{... | collective-permute-start | bytes 393224 | tf_op jit(solution)/shard_map/ppermute | solution.py:1402
  275.1 17.0 %all-to-all-start.5 = ((bf16[4,32,1792]{2,1,0:T(8,128)(2,1)}), bf16[4,32,1792]{2,1,0:T(8,128)(2,1)S(1)}, u32[]{:S(2)}, u32[]{:S(2)}) async-start(bf16[4,32,1792]{2,1,0:T(8,128)(2,1)} %bitcast.27), calls=%async_computation.5 | async-start | bytes 917504 | tf_op jit(solution)/shard_map/all_to_all | solution.py:1387
  (70 other events, 1026.9 us)

commit v5 on v4

--- a/solution.py
+++ b/solution.py
@@ -20,7 +20,7 @@
 GELU_K = 0.044715
 NEG_BIG = -1e30
 MIB = 1 << 20
-UNROLL = 2
+UNROLL = 8
 PACK = 24
 
 BF = jnp.bfloat16
@@ -507,7 +507,7 @@
     rows, width = tokens.shape
     half = lay.heads * DH
 
-    def body(flag_ref, long_ref, short_ref, recv_ref, w_ref, b_ref, tok_ref, mod_ref, branch_ref, resid_ref, normed_ref, inv_ref, hid_ref, att_ref):
+    def body(flag_ref, long_ref, short_ref, recv_ref, w_ref, b_ref, tok_ref, mod_ref, branch_ref, resid_ref, hid_ref, att_ref):
         own_long = flag_ref[0]
         side = flag_ref[1]
         for pair in range(lay.heads // 2):
@@ -523,9 +523,7 @@
         gate = per_frame(branch.shape, mod_ref[0:1], mod_ref[1:2])
         resid = tok_ref[...].astype(F32) + gate * branch
         resid_ref[...] = resid
-        normed, inv_std = norm_rows(resid)
-        normed_ref[...] = normed
-        inv_ref[...] = jnp.broadcast_to(inv_std, inv_ref.shape)
+        normed, _ = norm_rows(resid)
         shift = per_frame(branch.shape, mod_ref[2:3], mod_ref[3:4])
         scale = per_frame(branch.shape, mod_ref[4:5], mod_ref[5:6])
         hid_ref[...] = (normed * (1.0 + scale) + shift).astype(BF)
@@ -535,9 +533,9 @@
         body,
         flags,
         [long_out, short_out, recv, weight, bias, tokens, mods],
-        [full, full, full, shape_of((rows, LANES), F32), shape_of((rows, width), BF)],
+        [full, full, shape_of((rows, width), BF)],
         scratch=[pltpu.VMEM((2, rows, half), BF)],
-        out_pins=(0, 1, 2, 3),
+        out_pins=(0, 1),
         vmem=24,
         flops=2 * rows * width * width,
         name="project_and_norm",
@@ -748,16 +746,16 @@
     )[0]
 
 
-def branch_back(flags, hid_own, hid_recv, cotangent, normed, inv_std, branch, mods, weight, lay):
-    rows, width = normed.shape
+def branch_back(flags, hid_own, hid_recv, cotangent, resid, branch, mods, weight, lay):
+    rows, width = resid.shape
     half = lay.heads * DH
 
-    def body(flag_ref, a_ref, b_ref, dy_ref, n_ref, inv_ref, br_ref, mod_ref, w_ref, rg_ref, bg_ref, keep_ref, send_ref, sums_ref):
+    def body(flag_ref, a_ref, b_ref, dy_ref, r_ref, br_ref, mod_ref, w_ref, rg_ref, bg_ref, keep_ref, send_ref, sums_ref):
         side = flag_ref[1]
         hid = a_ref[...] + b_ref[...].astype(F32)
-        norm = n_ref[...]
+        norm, inv_std = norm_rows(r_ref[...])
         scale = per_frame(hid.shape, mod_ref[4:5], mod_ref[5:6])
-        resid = dy_ref[...].astype(F32) + norm_back(hid * (1.0 + scale), norm, inv_ref[:, 0:1])
+        resid = dy_ref[...].astype(F32) + norm_back(hid * (1.0 + scale), norm, inv_std)
         rg_ref[...] = resid
         gate = per_frame(hid.shape, mod_ref[0:1], mod_ref[1:2])
         low = (gate * resid).astype(BF)
@@ -778,9 +776,9 @@
     return kernel_call(
         body,
         flags,
-        [hid_own, hid_recv, cotangent, normed, inv_std, branch, mods, weight],
+        [hid_own, hid_recv, cotangent, resid, branch, mods, weight],
         [shape_of((rows, width), F32), shape_of((rows, width), BF), packed, packed, shape_of((8, width), F32)],
-        pins=(0, 2, 3, 4, 5, 6),
+        pins=(0, 2, 3, 4, 5),
         out_pins=(0,),
         vmem=24,
         flops=2 * rows * width * width,
@@ -972,7 +970,7 @@
         specs=specs + [None] * len(head_rows),
         grid=(depth // wide,),
         vmem=24,
-        pins=tuple(range(len(operands))) if head_rows else (),
+        pins=(0, 1, 2, 3, 5, 7) if head_rows else (),
         flops=2 * count * rows * depth * width_of(jobs),
         name=name,
     )
@@ -1069,11 +1067,14 @@
     )
 
 
-def modulation_grads(flags, long_rows, gathered, row_out, name):
-    total, width = gathered.shape
+def modulation_grads(flags, long_rows, mine, got, row_out, name):
+    half, width = mine.shape
+    total = 2 * half
     quarter = total // 4
 
-    def body(flag_ref, long_ref, g_ref, out_ref, sums_ref, part_ref):
+    def body(flag_ref, long_ref, mine_ref, got_ref, out_ref, sums_ref, part_ref, g_ref):
+        g_ref[:half] = mine_ref[...]
+        g_ref[half:] = got_ref[...]
         start = flag_ref[5]
         block = pl.multiple_of((start // LANES) * LANES, LANES)
         silu = g_ref[:, pl.ds(block, LANES)].astype(F32)
@@ -1111,10 +1112,10 @@
     return kernel_call(
         body,
         flags,
-        [long_rows, gathered],
+        [long_rows, mine, got],
         [shape_of((row_out, 6 * width), F32), shape_of((4, 32, width), F32)],
-        scratch=[pltpu.VMEM((LANES, width), F32)],
-        vmem=max(16, 16 * total // 768),
+        scratch=[pltpu.VMEM((LANES, width), F32), pltpu.VMEM((total, width), BF)],
+        vmem=max(20, 20 * total // 768),
         flops=total * width * LANES * 12,
         name=name,
     )
@@ -1243,7 +1244,7 @@
     out_long = own_part(spread(out_long_all))
     out_long, ahead_oth = lax.optimization_barrier((out_long, ahead_oth))
     out_recv = swap_side(jnp.where(own_long_b, out_short, out_long))
-    branch, resid, normed2, inv2, hidden2 = project_and_norm(
+    branch, resid, hidden2 = project_and_norm(
         flags, out_long, out_short, out_recv, proj_weight, proj_bias.astype(F32)[None], tokens, mid_mods, lay
     )
 
@@ -1272,7 +1273,7 @@
     hid_recv, *mlp_halves = lax.optimization_barrier((hid_recv, *mlp_halves))
 
     resid_grad, branch_grad, do_keep, do_send, mid_sums = branch_back(
-        flags, hid_own, hid_recv, cotangent, normed2, inv2, branch, mid_mods, proj_weight, lay
+        flags, hid_own, hid_recv, cotangent, resid, branch, mid_mods, proj_weight, lay
     )
     mlp_sums = [CubeSum(*mlp_halves[:2], n_blk, down_order), CubeSum(*mlp_halves[2:], n_blk, up_order)]
     for part in mlp_sums:
@@ -1371,8 +1372,9 @@
     for part, got in zip(attn_sums, gots):
         part.got = got
     both = jnp.stack([many, both])
-    packs = jnp.stack([both, swap_core(both)]).reshape(-1, width)
-    g_mod_weight, sums = modulation_grads(flags, long_rows, packs, row_out, "modulation_grads")
+    g_mod_weight, sums = modulation_grads(
+        flags, long_rows, both.reshape(-1, width), swap_core(both).reshape(-1, width), row_out, "modulation_grads"
+    )
     for part in attn_sums:
         part.add()
     attn_mine = [part.finish() for part in attn_sums]

time: 297 us -> 296 us (level)
  Pallas kernels: 142 us -> 139 us
    pallas_call x24, Pallas kernels: 142 us -> 139 us  [kernel_call(): pl.pallas_call(body, grid_spec=pltpu.PrefetchScalarGridSpec(num_scalar_pr...]
    unnamed x117 -> x111, local copies, waits for them, and re-layouts: 9.02 us -> 7.61 us
  transfers between devices with their start and end apart: 45 -> 45, of which waited for: 17 -> 18; matrix products, arithmetic and copies ran while one was open for 11% -> 12% of each run, Pallas kernels for 43% -> 42%
where the time goes in v5:
time: 296 us; the launch traced here: 293 us
  Pallas kernels  139 us (47%)
  starting transfers between devices  65.3 us (22%)
  waiting for transfers between devices  40 us (14%)
  other arithmetic  23.7 us (8%)
  local copies, waits for them, and re-layouts  16.4 us (6%)
  matrix products  7.43 us (3%)
    pallas_call x24, Pallas kernels, kernel_call(): pl.pallas_call(body, grid_spec=pltpu.PrefetchScalarGridSpec(num_scalar_pr...  139 us
    all_to_all x5, starting transfers between devices, spread(): return lax.all_to_all(value, 'blk', split_axis=0, concat_axis=0, tiled=True)  24.9 us
    ppermute x12, waiting for transfers between devices, move(): lax.ppermute(send, 'blk', [(i, i ^ hop) for i in range(self.n_blk)])  20.5 us
    ppermute x12, starting transfers between devices, move(): lax.ppermute(send, 'blk', [(i, i ^ hop) for i in range(self.n_blk)])  15.4 us
    ppermute x11, starting transfers between devices, swap_side(): return lax.ppermute(value, 'uly', [(i, i ^ 2) for i in range(n_uly)])  13.5 us
    convert_element_type x8, other arithmetic, add(): (self.keep[k].astype(F32) + self.got[k].astype(F32)).astype(BF)  12.2 us
    all_to_all x5, waiting for transfers between devices, spread(): return lax.all_to_all(value, 'blk', split_axis=0, concat_axis=0, tiled=True)  7.75 us
    unnamed x111, local copies, waits for them, and re-layouts  7.61 us
  transfers between devices with their start and end apart: 45, of which 18 were waited for; matrix products, arithmetic and copies ran while one was open for 12% of the time, Pallas kernels for 42%

profile of v5, /device:TPU:4, one launch (start us, length us, event | category | flops | bytes accessed | tf_op | source)
XLA Modules:
  0.0 293.5 jit_solution(73713821111108496)
XLA Ops:
  11.3 4.6 %fusion.2 = f32[2,4096]{1,0:T(2,128)S(1)} fusion(bf16[2,1024]{1,0:T(2,128)(2,1)S(1)} %fusion.16.s_ref, bf16[1024,6144]{1,0:T(8,128)(2,1)} %param.22, f32[4096]{0:T(1024)S(1)} %slice.269), kind=kOutput, calls=%fused_computation.2 | convolution fusion | flops 16785408 | bytes 8441856 | tf_op jit(solution)/shard_map/dot_general | solution.py:77
  19.0 7.7 %tokens_to_qkv.1 = (bf16[2,200,1024]{2,1,0:T(8,128)(2,1)}, bf16[8,320,128]{2,1,0:T(8,128)(2,1)S(1)}, bf16[8,320,128]{2,1,0:T(8,128)(2,1)S(1)}) custom-call(s32[6]{0:T(128)S(1)} %stack.40.flag_ref, bf16[200,1024]{1,0:T(8,128)(2,1)S(1)} %copy-done, bf16[200,1024]{1,0:T(8,128)(2,1)S(1)} %collective-permute-done.oth_ref.refs_8_.refs_2_, ...), custom_call_target="tpu_custom_call" | custom-call | flops 307200 | bytes 4096 | tf_op jit(solution)/shard_map/tokens_to_qkv/pallas_call | solution.py:117
  27.6 6.3 %all-to-all-start = ((bf16[8,320,128]{2,1,0:T(8,128)(2,1)}), bf16[8,320,128]{2,1,0:T(8,128)(2,1)S(1)}, u32[]{:S(2)}, u32[]{:S(2)}) async-start(bf16[8,320,128]{2,1,0:T(8,128)(2,1)} %copy-done.17), calls=%async_computation | async-start | bytes 1310720 | tf_op jit(solution)/shard_map/all_to_all | solution.py:1189
  35.6 5.6 %ahead_own.1.ahead_ref = f32[200,2048]{1,0:T(8,128)} custom-call(s32[6]{0:T(128)S(1)} %stack.40.flag_ref, bf16[200,1024]{1,0:T(8,128)(2,1)S(1)} %get-tuple-element.179.mg_ref.refs_4_, bf16[4096,1024]{1,0:T(8,128)(2,1)} %refs_1_.10, bf16[4096,1024]{1,0:T(8,128)(2,1)} %refs_1_.10), custom_call_target="tpu_custom_call" | custom-call | flops 204800 | bytes 4096 | tf_op jit(solution)/shard_map/ahead_own/pallas_call | solution.py:117
  41.2 3.8 %attend_short.1 = (bf16[8,112,128]{2,1,0:T(8,128)(2,1)S(1)}, f32[8,64,200]{2,1,0:T(8,128)}, f32[8,8,200]{2,1,0:T(8,128)}) custom-call(s32[6]{0:T(128)S(1)} %stack.40.flag_ref, bf16[8,320,128]{2,1,0:T(8,128)(2,1)S(1)} %get-tuple-element.157.own_ref, bf16[8,320,128]{2,1,0:T(8,128)(2,1)S(1)} %collective-permute-done.2.oth_ref), custom_call_target="tpu_custom_call" | custom-call | flops 160000 | bytes 4096 | tf_op jit(solution)/shard_map/attend_short/pallas_call | solution.py:117
  45.1 5.0 %all-to-all-done.own_ref = bf16[8,320,128]{2,1,0:T(8,128)(2,1)S(1)} async-done(((bf16[8,320,128]{2,1,0:T(8,128)(2,1)}), bf16[8,320,128]{2,1,0:T(8,128)(2,1)S(1)}, u32[]{:S(2)}, u32[]{:S(2)}) %all-to-all-start) | async-done | bytes 655392 | tf_op jit(solution)/shard_map/all_to_all | solution.py:1189
  52.2 11.4 %attend_long.1 = (bf16[8,112,128]{2,1,0:T(8,128)(2,1)S(1)}, f32[4,64,400]{2,1,0:T(8,128)}, f32[4,8,400]{2,1,0:T(8,128)}) custom-call(s32[6]{0:T(128)S(1)} %stack.40.flag_ref, bf16[8,320,128]{2,1,0:T(8,128)(2,1)S(1)} %all-to-all-done.own_ref, bf16[8,320,128]{2,1,0:T(8,128)(2,1)S(1)} %collective-permute-done.3.oth_ref), custom_call_target="tpu_custom_call" | custom-call | flops 800000 | bytes 4096 | tf_op jit(solution)/shard_map/attend_long/pallas_call | solution.py:117
  65.1 4.3 %all-to-all-start.1 = ((bf16[8,112,128]{2,1,0:T(8,128)(2,1)}), bf16[8,112,128]{2,1,0:T(8,128)(2,1)S(1)}, u32[]{:S(2)}, u32[]{:S(2)}) async-start(bf16[8,112,128]{2,1,0:T(8,128)(2,1)} %copy-done.20), calls=%async_computation.1 | async-start | bytes 458752 | tf_op jit(solution)/shard_map/all_to_all | solution.py:1189
  70.3 5.6 %ahead_other.1.ahead_ref = f32[200,2048]{1,0:T(8,128)} custom-call(s32[6]{0:T(128)S(1)} %stack.40.flag_ref, bf16[200,1024]{1,0:T(8,128)(2,1)S(1)} %copy-done.13, bf16[4096,1024]{1,0:T(8,128)(2,1)} %refs_1_.10, bf16[4096,1024]{1,0:T(8,128)(2,1)} %refs_1_.10), custom_call_target="tpu_custom_call" | custom-call | flops 204800 | bytes 4096 | tf_op jit(solution)/shard_map/ahead_other/pallas_call | solution.py:117
  79.0 4.4 %collective-permute-done.5.recv_ref = bf16[8,112,128]{2,1,0:T(8,128)(2,1)S(1)} collective-permute-done((bf16[8,112,128]{2,1,0:T(8,128)(2,1)S(1)}, bf16[8,112,128]{2,1,0:T(8,128)(2,1)S(1)}, u32[]{:S(2)}, u32[]{:S(2)}) %collective-permute-start.5) | collective-permute-done | bytes 229408 | tf_op jit(solution)/shard_map/ppermute | solution.py:1183
  83.3 4.1 %project_and_norm.1 = (f32[200,1024]{1,0:T(8,128)}, f32[200,1024]{1,0:T(8,128)}, bf16[200,1024]{1,0:T(8,128)(2,1)S(1)}) custom-call(s32[6]{0:T(128)S(1)} %stack.40.flag_ref, bf16[8,112,128]{2,1,0:T(8,128)(2,1)S(1)} %all-to-all-done.1.long_ref.l_ref, bf16[8,112,128]{2,1,0:T(8,128)(2,1)S(1)} %get-tuple-element.167.short_ref.s_ref, ...), custom_call_target="tpu_custom_call" | custom-call | flops 102400 | bytes 4096 | tf_op jit(solution)/shard_map/project_and_norm/pallas_call | solution.py:117
  89.0 6.9 %hidden_own.1 = (bf16[2,200,1024]{2,1,0:T(8,128)(2,1)S(1)}, bf16[2,200,1024]{2,1,0:T(8,128)(2,1)S(1)}, f32[8,1024]{1,0:T(8,128)S(1)}, f32[8,1024]{1,0:T(8,128)S(1)}, f32[200,1024]{1,0:T(8,128)S(1)}) custom-call(s32[6]{0:T(128)S(1)} %stack.40.flag_ref, bf16[200,1024]{1,0:T(8,128)(2,1)S(1)} %get-tuple-element.168.hid_ref.refs_8_, ...), custom_call_target="tpu_custom_call" | custom-call | flops 409600 | bytes 4096 | tf_op jit(solution)/shard_map/hidden_own/pallas_call | solution.py:117
  97.4 6.8 %hidden_other.1 = (bf16[2,200,1024]{2,1,0:T(8,128)(2,1)S(1)}, bf16[2,200,1024]{2,1,0:T(8,128)(2,1)S(1)}, f32[8,1024]{1,0:T(8,128)S(1)}, f32[8,1024]{1,0:T(8,128)S(1)}, bf16[200,1024]{1,0:T(8,128)(2,1)S(1)}) custom-call(s32[6]{0:T(128)S(1)} %stack.40.flag_ref, bf16[200,1024]{1,0:T(8,128)(2,1)S(1)} %collective-permute-done.6.hid_ref.refs_9_, ...), custom_call_target="tpu_custom_call" | custom-call | flops 409600 | bytes 4096 | tf_op jit(solution)/shard_map/hidden_other/pallas_call | solution.py:117
  108.9 9.5 %mlp_grads.1 = (bf16[4,128,1024]{2,1,0:T(8,128)(2,1)}, bf16[4,128,1024]{2,1,0:T(8,128)(2,1)S(1)}, bf16[4,128,1024]{2,1,0:T(8,128)(2,1)}, bf16[4,128,1024]{2,1,0:T(8,128)(2,1)S(1)}) custom-call(s32[6]{0:T(128)S(1)} %stack.40.flag_ref, bf16[2,200,1024]{2,1,0:T(8,128)(2,1)S(1)} %get-tuple-element.175.refs_0_.refs_12_.m_ref, ...), custom_call_target="tpu_custom_call" | custom-call | flops 819200 | bytes 4096 | tf_op jit(solution)/shard_map/mlp_grads/pallas_call | solution.py:117
  121.1 4.9 %branch_back.1 = (f32[200,1024]{1,0:T(8,128)}, bf16[200,1024]{1,0:T(8,128)(2,1)S(1)}, bf16[8,112,128]{2,1,0:T(8,128)(2,1)S(1)}, bf16[8,112,128]{2,1,0:T(8,128)(2,1)S(1)}, f32[8,1024]{1,0:T(8,128)S(1)}) custom-call(s32[6]{0:T(128)S(1)} %stack.40.flag_ref, f32[200,1024]{1,0:T(8,128)} %copy-done.16, bf16[200,1024]{1,0:T(8,128)(2,1)S(1)} %collective-permute-done.7.b_ref, ...), custom_call_target="tpu_custom_call" | custom-call | flops 102400 | bytes 4096 | tf_op jit(solution)/shard_map/branch_back/pallas_call | solution.py:117
  127.0 7.2 %forward_rows.1 = (f32[200,1024]{1,0:T(8,128)}, bf16[200,1024]{1,0:T(8,128)(2,1)}) custom-call(s32[6]{0:T(128)S(1)} %stack.40.flag_ref, bf16[2,200,1024]{2,1,0:T(8,128)(2,1)S(1)} %get-tuple-element.175.refs_0_.refs_12_.m_ref, bf16[2,200,1024]{2,1,0:T(8,128)(2,1)S(1)} %get-tuple-element.177.s_ref, ...), custom_call_target="tpu_custom_call" | custom-call | flops 409600 | bytes 4096 | tf_op jit(solution)/shard_map/forward_rows/pallas_call | solution.py:117
  136.1 5.2 %all-to-all-start.2 = ((bf16[8,112,128]{2,1,0:T(8,128)(2,1)}), bf16[8,112,128]{2,1,0:T(8,128)(2,1)S(1)}, u32[]{:S(2)}, u32[]{:S(2)}) async-start(bf16[8,112,128]{2,1,0:T(8,128)(2,1)} %broadcast_select_fusion.1), calls=%async_computation.2 | async-start | bytes 458752 | tf_op jit(solution)/shard_map/all_to_all | solution.py:1189
  141.3 6.2 %attend_back_short.1 = (bf16[8,200,128]{2,1,0:T(8,128)(2,1)}, f32[8,200,128]{2,1,0:T(8,128)}, bf16[8,200,128]{2,1,0:T(8,128)(2,1)S(1)}) custom-call(s32[6]{0:T(128)S(1)} %stack.40.flag_ref, bf16[8,320,128]{2,1,0:T(8,128)(2,1)} %copy-done.5, bf16[8,320,128]{2,1,0:T(8,128)(2,1)} %copy-done.6, bf16[8,112,128]{2,1,0:T(8,128)(2,1)S(1)} %get-tuple-element.192.refs_0_, ...), custom_call_target="tpu_custom_call" | custom-call | flops 400000 | bytes 4096 | tf_op jit(solution)/shard_map/attend_back_short/pallas_call | solution.py:117
  157.4 17.4 %attend_back_long.1 = (bf16[8,200,128]{2,1,0:T(8,128)(2,1)}, f32[8,200,128]{2,1,0:T(8,128)}, bf16[8,200,128]{2,1,0:T(8,128)(2,1)S(1)}) custom-call(s32[6]{0:T(128)S(1)} %stack.40.flag_ref, bf16[8,320,128]{2,1,0:T(8,128)(2,1)} %copy-done.1, bf16[8,320,128]{2,1,0:T(8,128)(2,1)} %copy-done.4, bf16[8,112,128]{2,1,0:T(8,128)(2,1)S(1)} %all-to-all-done.2.refs_0_, ...), custom_call_target="tpu_custom_call" | custom-call | flops 2000000 | bytes 4096 | tf_op jit(solution)/shard_map/attend_back_long/pallas_call | solution.py:117
  176.6 3.8 %finish_keys.1 = bf16[8,320,128]{2,1,0:T(8,128)(2,1)} custom-call(s32[6]{0:T(128)S(1)} %stack.40.flag_ref, bf16[8,200,128]{2,1,0:T(8,128)(2,1)} %get-tuple-element.215.dq_ref, f32[8,200,128]{2,1,0:T(8,128)} %get-tuple-element.216.a_ref, bf16[8,200,128]{2,1,0:T(8,128)(2,1)S(1)} %collective-permute-done.18.b_ref, f32[200,128]{1,0:T(8,128)S(1)} %copy-done.8, ...), custom_call_target="tpu_custom_call" | custom-call | flops 500 | bytes 4096 | tf_op jit(solution)/shard_map/finish_keys/pallas_call | solution.py:117
  180.4 4.7 %all-to-all-start.3 = ((bf16[8,320,128]{2,1,0:T(8,128)(2,1)}), bf16[8,320,128]{2,1,0:T(8,128)(2,1)S(1)}, u32[]{:S(2)}, u32[]{:S(2)}) async-start(bf16[8,320,128]{2,1,0:T(8,128)(2,1)} %finish_keys.1), calls=%async_computation.3 | async-start | bytes 1310720 | tf_op jit(solution)/shard_map/all_to_all | solution.py:1189
  186.6 6.9 %qkv_back_short.1 = (f32[200,1024]{1,0:T(8,128)}, bf16[200,1024]{1,0:T(8,128)(2,1)S(1)}, bf16[200,768]{1,0:T(8,128)(2,1)S(1)}, bf16[200,768]{1,0:T(8,128)(2,1)S(...) custom-call(s32[6]{0:T(128)S(1)} %stack.40.flag_ref, bf16[8,200,128]{2,1,0:T(8,128)(2,1)} %get-tuple-element.226.refs_0_, ...), custom_call_target="tpu_custom_call" | custom-call | flops 153600 | bytes 4096 | tf_op jit(solution)/shard_map/qkv_back_short/pallas_call | solution.py:117
  202.3 6.0 %qkv_back_long.1 = (f32[200,1024]{1,0:T(8,128)}, bf16[200,1024]{1,0:T(8,128)(2,1)S(1)}, bf16[200,768]{1,0:T(8,128)(2,1)S(1)}, bf16[200,768]{1,0:T(8,128)(2,1)S(1...) custom-call(s32[6]{0:T(128)S(1)} %stack.40.flag_ref, bf16[8,320,128]{2,1,0:T(8,128)(2,1)S(1)} %all-to-all-done.3.refs_0_, ...), custom_call_target="tpu_custom_call" | custom-call | flops 153600 | bytes 4096 | tf_op jit(solution)/shard_map/qkv_back_long/pallas_call | solution.py:117
  212.6 6.8 %attn_grads.1 = (bf16[4,128,512]{2,1,0:T(8,128)(2,1)S(1)}, bf16[4,128,512]{2,1,0:T(8,128)(2,1)S(1)}, bf16[4,256,256]{2,1,0:T(8,128)(2,1)S(1)}, bf16[4,256,256]{2,1,0:T(8,128)(2,1)S(1)}) custom-call(s32[6]{0:T(128)S(1)} %stack.40.flag_ref, bf16[2,200,1024]{2,1,0:T(8,128)(2,1)} %get-tuple-element.239.refs_0_.refs_1_, ...), custom_call_target="tpu_custom_call" | custom-call | flops 307200 | bytes 4096 | tf_op jit(solution)/shard_map/attn_grads/pallas_call | solution.py:117
  219.5 5.7 %collective-permute-done.25 = bf16[1,128,1024]{2,1,0:T(8,128)(2,1)S(1)} collective-permute-done((bf16[1,128,1024]{2,1,0:T(8,128)(2,1)}, bf16[1,128,1024]{2,1,0:T(8,128)(2,1)S(1)}, u32[]{:S(2)}, u32[]{:S(2)}) %collective-permute-start.25) | collective-permute-done | bytes 262176 | tf_op jit(solution)/shard_map/ppermute | solution.py:1029
  226.9 3.2 %layer_output.1 = (bf16[200,1024]{1,0:T(8,128)(2,1)}, f32[8,1024]{1,0:T(8,128)S(1)}) custom-call(s32[6]{0:T(128)S(1)} %stack.40.flag_ref, f32[200,1024]{1,0:T(8,128)} %get-tuple-element.191.a_ref, bf16[200,1024]{1,0:T(8,128)(2,1)} %collective-permute-done.23.b_ref, f32[1,1024]{1,0:T(1,128)S(1)} %bitcast.68, f32[200,1024]{1,0:T(8,128)} %get-tuple-element.185.r_ref, ...), custom_call_target="tpu_custom_call" | custom-call | flops 200 | bytes 4096 | tf_op jit(solution)/shard_map/layer_output/pallas_call | solution.py:117
  230.0 3.8 %token_back.1 = f32[200,1024]{1,0:T(8,128)} custom-call(s32[6]{0:T(128)S(1)} %stack.40.flag_ref, f32[200,1024]{1,0:T(8,128)} %get-tuple-element.252.l_ref, f32[200,1024]{1,0:T(8,128)} %get-tuple-element.253.s_ref, bf16[200,1024]{1,0:T(8,128)(2,1)S(1)} %collective-permute-done.22.r_ref, bf16[200,1024]{1,0:T(8,128)(2,1)} %tok_ref.3, ...), custom_call_target="tpu_custom_call" | custom-call | flops 1000 | bytes 4096 | tf_op jit(solution)/shard_map/token_back/pallas_call | solution.py:117
  233.8 4.7 %collective-permute-done.30 = bf16[4,128,512]{2,1,0:T(8,128)(2,1)S(1)} collective-permute-done((bf16[4,128,512]{2,1,0:T(8,128)(2,1)S(1)}, bf16[4,128,512]{2,1,0:T(8,128)(2,1)S(1)}, u32[]{:S(2)}, u32[]{:S(2)}) %collective-permute-start.30) | collective-permute-done | bytes 524320 | tf_op jit(solution)/shard_map/ppermute | solution.py:1029
  240.7 4.4 %all-to-all-start.4 = ((bf16[8,24,1024]{2,1,0:T(8,128)(2,1)}), bf16[8,24,1024]{2,1,0:T(8,128)(2,1)S(1)}, u32[]{:S(2)}, u32[]{:S(2)}) async-start(bf16[8,24,1024]{2,1,0:T(8,128)(2,1)} %pack_rows.1), calls=%async_computation.4 | async-start | bytes 786432 | tf_op jit(solution)/shard_map/all_to_all | solution.py:1189
  252.9 5.6 %collective-permute-done.32 = bf16[2,128,512]{2,1,0:T(8,128)(2,1)S(1)} collective-permute-done((bf16[2,128,512]{2,1,0:T(8,128)(2,1)}, bf16[2,128,512]{2,1,0:T(8,128)(2,1)S(1)}, u32[]{:S(2)}, u32[]{:S(2)}) %collective-permute-start.32) | collective-permute-done | bytes 262176 | tf_op jit(solution)/shard_map/ppermute | solution.py:1029
  275.9 6.0 %all-to-all-start.5 = ((bf16[4,32,1792]{2,1,0:T(8,128)(2,1)}), bf16[4,32,1792]{2,1,0:T(8,128)(2,1)S(1)}, u32[]{:S(2)}, u32[]{:S(2)}) async-start(bf16[4,32,1792]{2,1,0:T(8,128)(2,1)} %bitcast.26), calls=%async_computation.5 | async-start | bytes 917504 | tf_op jit(solution)/shard_map/all_to_all | solution.py:1389
  284.1 3.5 %modulation_grads.1 = (f32[32,6144]{1,0:T(8,128)}, f32[4,32,1024]{2,1,0:T(8,128)S(1)}) custom-call(s32[6]{0:T(128)S(1)} %stack.40.flag_ref, f32[768,128]{1,0:T(8,128)S(1)} %copy-done.15, bf16[384,1024]{1,0:T(8,128)(2,1)S(1)} %bitcast.60, bf16[384,1024]{1,0:T(8,128)(2,1)S(1)} %bitcast.61), custom_call_target="tpu_custom_call" | custom-call | flops 294912 | bytes 4096 | tf_op jit(solution)/shard_map/modulation_grads/pallas_call | solution.py:117
  (268 shorter events, 99.3 us)
Async XLA Ops:
  0.7 18.3 %collective-permute-start = (bf16[200,1024]{1,0:T(8,128)(2,1)}, bf16[200,1024]{1,0:T(8,128)(2,1)S(1)}, u32[]{:S(2)}, u32[]{:S(2)}) collective-permute-start(bf16[200,1024]{1,0:T(8,128)(2,1)} %tok_ref.3), channel_id=1, source_target_pairs={{0,2},{1,3},{2,0},{3,1},{4,6},{5,7},{6,4},{7,5},{8,10},{9,11},{10,... | collective-permute-start | bytes 1228808 | tf_op jit(solution)/shard_map/ppermute | solution.py:1183
  5.8 12.3 %collective-permute-start.1 = (f32[2,2048]{1,0:T(2,128)S(1)}, f32[2,2048]{1,0:T(2,128)S(1)}, u32[]{:S(2)}, u32[]{:S(2)}) collective-permute-start(f32[2,2048]{1,0:T(2,128)S(1)} %fusion.7.mod_ref), channel_id=1, source_target_pairs={{0,2},{1,3},{2,0},{3,1},{4,6},{5,7},{6,4},{7,5},{8,10},{9,11},{10,... | collective-permute-start | bytes 49160 | tf_op jit(solution)/shard_map/ppermute | solution.py:1183
  27.6 22.5 %all-to-all-start = ((bf16[8,320,128]{2,1,0:T(8,128)(2,1)}), bf16[8,320,128]{2,1,0:T(8,128)(2,1)S(1)}, u32[]{:S(2)}, u32[]{:S(2)}) async-start(bf16[8,320,128]{2,1,0:T(8,128)(2,1)} %copy-done.17), calls=%async_computation | async-start | bytes 1310720 | tf_op jit(solution)/shard_map/all_to_all | solution.py:1189
  50.1 13.5 %collective-permute-start.4 = (bf16[200,1024]{1,0:T(8,128)(2,1)S(1)}, bf16[200,1024]{1,0:T(8,128)(2,1)S(1)}, u32[]{:S(2)}, u32[]{:S(2)}) collective-permute-start(bf16[200,1024]{1,0:T(8,128)(2,1)S(1)} %get-tuple-element.179.mg_ref.refs_4_), channel_id=1, source_target_pairs={{0,2},{1,3},{2,0},{3,1},{4,6},{5,7},{6,4},{7,5},{8,10},{9,11},{10,... | collective-permute-start | bytes 1228808 | tf_op jit(solution)/shard_map/ppermute | solution.py:1183
  65.1 12.2 %all-to-all-start.1 = ((bf16[8,112,128]{2,1,0:T(8,128)(2,1)}), bf16[8,112,128]{2,1,0:T(8,128)(2,1)S(1)}, u32[]{:S(2)}, u32[]{:S(2)}) async-start(bf16[8,112,128]{2,1,0:T(8,128)(2,1)} %copy-done.20), calls=%async_computation.1 | async-start | bytes 458752 | tf_op jit(solution)/shard_map/all_to_all | solution.py:1189
  87.5 9.9 %collective-permute-start.6 = (bf16[200,1024]{1,0:T(8,128)(2,1)S(1)}, bf16[200,1024]{1,0:T(8,128)(2,1)S(1)}, u32[]{:S(2)}, u32[]{:S(2)}) collective-permute-start(bf16[200,1024]{1,0:T(8,128)(2,1)S(1)} %get-tuple-element.168.hid_ref.refs_8_), channel_id=1, source_target_pairs={{0,2},{1,3},{2,0},{3,1},{4,6},{5,7},{6,4},{7,5},{8,10},{9,11},{10,... | collective-permute-start | bytes 1228808 | tf_op jit(solution)/shard_map/ppermute | solution.py:1183
  89.0 16.5 %collective-permute-start.10 = (bf16[200,1024]{1,0:T(8,128)(2,1)S(1)}, bf16[200,1024]{1,0:T(8,128)(2,1)S(1)}, u32[]{:S(2)}, u32[]{:S(2)}) collective-permute-start(bf16[200,1024]{1,0:T(8,128)(2,1)S(1)} %get-tuple-element.179.mg_ref.refs_4_), channel_id=1, source_target_pairs={{0,1},{1,0},{2,3},{3,2},{4,5},{5,4},{6,7},{7,6},{8,9},{9,8},{10,11... | collective-permute-start | bytes 1228808 | tf_op jit(solution)/shard_map/ppermute | solution.py:1186
  96.9 11.5 %collective-permute-start.8 = (bf16[2,200,1024]{2,1,0:T(8,128)(2,1)S(1)}, bf16[2,200,1024]{2,1,0:T(8,128)(2,1)S(1)}, u32[]{:S(2)}, u32[]{:S(2)}) collective-permute-start(bf16[2,200,1024]{2,1,0:T(8,128)(2,1)S(1)} %get-tuple-element.177.s_ref), channel_id=1, source_target_pairs={{0,1},{1,0},{2,3},{3,2},{4,5},{5,4},{6,7},{7,6},{8,9},{9,8},{10,11... | collective-permute-start | bytes 2457608 | tf_op jit(solution)/shard_map/ppermute | solution.py:1186
  107.8 11.5 %collective-permute-start.7 = (bf16[200,1024]{1,0:T(8,128)(2,1)S(1)}, bf16[200,1024]{1,0:T(8,128)(2,1)S(1)}, u32[]{:S(2)}, u32[]{:S(2)}) collective-permute-start(bf16[200,1024]{1,0:T(8,128)(2,1)S(1)} %get-tuple-element.174), channel_id=1, source_target_pairs={{0,2},{1,3},{2,0},{3,1},{4,6},{5,7},{6,4},{7,5},{8,10},{9,11},{10,... | collective-permute-start | bytes 1228808 | tf_op jit(solution)/shard_map/ppermute | solution.py:1183
  119.3 30.0 %collective-permute-start.16 = (bf16[4,128,1024]{2,1,0:T(8,128)(2,1)}, bf16[4,128,1024]{2,1,0:T(8,128)(2,1)}, u32[]{:S(2)}, u32[]{:S(2)}) collective-permute-start(bf16[4,128,1024]{2,1,0:T(8,128)(2,1)} %get-tuple-element.203), channel_id=1, source_target_pairs={{0,4},{4,0},{8,12},{12,8},{16,20},{20,16},{24,28},{28,24},{1,5},{5... | collective-permute-start | bytes 3145736 | tf_op jit(solution)/shard_map/ppermute | solution.py:1029
  120.1 29.2 %collective-permute-start.17 = (bf16[4,128,1024]{2,1,0:T(8,128)(2,1)}, bf16[4,128,1024]{2,1,0:T(8,128)(2,1)}, u32[]{:S(2)}, u32[]{:S(2)}) collective-permute-start(bf16[4,128,1024]{2,1,0:T(8,128)(2,1)} %get-tuple-element.204), channel_id=1, source_target_pairs={{0,8},{4,12},{8,0},{12,4},{16,24},{20,28},{24,16},{28,20},{1,9},{5... | collective-permute-start | bytes 3145736 | tf_op jit(solution)/shard_map/ppermute | solution.py:1029
  134.3 15.0 %collective-permute-start.15 = (bf16[200,1024]{1,0:T(8,128)(2,1)S(1)}, bf16[200,1024]{1,0:T(8,128)(2,1)}, u32[]{:S(2)}, u32[]{:S(2)}) collective-permute-start(bf16[200,1024]{1,0:T(8,128)(2,1)S(1)} %get-tuple-element.202.go_ref), channel_id=1, source_target_pairs={{0,2},{1,3},{2,0},{3,1},{4,6},{5,7},{6,4},{7,5},{8,10},{9,11},{10,... | collective-permute-start | bytes 1228808 | tf_op jit(solution)/shard_map/ppermute | solution.py:1183
  136.1 13.2 %all-to-all-start.2 = ((bf16[8,112,128]{2,1,0:T(8,128)(2,1)}), bf16[8,112,128]{2,1,0:T(8,128)(2,1)S(1)}, u32[]{:S(2)}, u32[]{:S(2)}) async-start(bf16[8,112,128]{2,1,0:T(8,128)(2,1)} %broadcast_select_fusion.1), calls=%async_computation.2 | async-start | bytes 458752 | tf_op jit(solution)/shard_map/all_to_all | solution.py:1189
  154.2 22.4 %collective-permute-start.19 = (bf16[2,128,1024]{2,1,0:T(8,128)(2,1)S(1)}, bf16[2,128,1024]{2,1,0:T(8,128)(2,1)S(1)}, u32[]{:S(2)}, u32[]{:S(2)}) collective-permute-start(bf16[2,128,1024]{2,1,0:T(8,128)(2,1)S(1)} %get-tuple-element.218), channel_id=1, source_target_pairs={{0,24},{4,28},{8,16},{12,20},{16,8},{20,12},{24,0},{28,4},{1,25},{... | collective-permute-start | bytes 1572872 | tf_op jit(solution)/shard_map/ppermute | solution.py:1029
  156.5 20.1 %collective-permute-start.20 = (bf16[2,128,1024]{2,1,0:T(8,128)(2,1)S(1)}, bf16[2,128,1024]{2,1,0:T(8,128)(2,1)}, u32[]{:S(2)}, u32[]{:S(2)}) collective-permute-start(bf16[2,128,1024]{2,1,0:T(8,128)(2,1)S(1)} %get-tuple-element.219), channel_id=1, source_target_pairs={{0,4},{4,0},{8,12},{12,8},{16,20},{20,16},{24,28},{28,24},{1,5},{5... | collective-permute-start | bytes 1572872 | tf_op jit(solution)/shard_map/ppermute | solution.py:1029
  174.8 11.7 %collective-permute-start.21 = (bf16[8,200,128]{2,1,0:T(8,128)(2,1)S(1)}, bf16[8,200,128]{2,1,0:T(8,128)(2,1)S(1)}, u32[]{:S(2)}, u32[]{:S(2)}) collective-permute-start(bf16[8,200,128]{2,1,0:T(8,128)(2,1)S(1)} %copy-done.36), channel_id=1, source_target_pairs={{0,1},{1,0},{2,3},{3,2},{4,5},{5,4},{6,7},{7,6},{8,9},{9,8},{10,11... | collective-permute-start | bytes 1228808 | tf_op jit(solution)/shard_map/ppermute | solution.py:1186
  180.4 21.9 %all-to-all-start.3 = ((bf16[8,320,128]{2,1,0:T(8,128)(2,1)}), bf16[8,320,128]{2,1,0:T(8,128)(2,1)S(1)}, u32[]{:S(2)}, u32[]{:S(2)}) async-start(bf16[8,320,128]{2,1,0:T(8,128)(2,1)} %finish_keys.1), calls=%async_computation.3 | async-start | bytes 1310720 | tf_op jit(solution)/shard_map/all_to_all | solution.py:1189
  185.1 24.9 %collective-permute-start.26 = (bf16[2,200,1024]{2,1,0:T(8,128)(2,1)}, bf16[2,200,1024]{2,1,0:T(8,128)(2,1)}, u32[]{:S(2)}, u32[]{:S(2)}) collective-permute-start(bf16[2,200,1024]{2,1,0:T(8,128)(2,1)} %get-tuple-element.239.refs_0_.refs_1_), channel_id=1, source_target_pairs={{0,1},{1,0},{2,3},{3,2},{4,5},{5,4},{6,7},{7,6},{8,9},{9,8},{10,11... | collective-permute-start | bytes 2457608 | tf_op jit(solution)/shard_map/ppermute | solution.py:1186
  185.1 34.4 %collective-permute-start.23 = (bf16[200,1024]{1,0:T(8,128)(2,1)}, bf16[200,1024]{1,0:T(8,128)(2,1)}, u32[]{:S(2)}, u32[]{:S(2)}) collective-permute-start(bf16[200,1024]{1,0:T(8,128)(2,1)} %get-tuple-element.236), channel_id=1, source_target_pairs={{0,2},{1,3},{2,0},{3,1},{4,6},{5,7},{6,4},{7,5},{8,10},{9,11},{10,... | collective-permute-start | bytes 1228808 | tf_op jit(solution)/shard_map/ppermute | solution.py:1183
  194.1 15.9 %collective-permute-start.28 = (bf16[200,768]{1,0:T(8,128)(2,1)S(1)}, bf16[200,768]{1,0:T(8,128)(2,1)}, u32[]{:S(2)}, u32[]{:S(2)}) collective-permute-start(bf16[200,768]{1,0:T(8,128)(2,1)S(1)} %get-tuple-element.243), channel_id=1, source_target_pairs={{0,1},{1,0},{2,3},{3,2},{4,5},{5,4},{6,7},{7,6},{8,9},{9,8},{10,11... | collective-permute-start | bytes 921608 | tf_op jit(solution)/shard_map/ppermute | solution.py:1186
  198.0 12.3 %collective-permute-start.29 = (bf16[256,1024]{1,0:T(8,128)(2,1)}, bf16[256,1024]{1,0:T(8,128)(2,1)S(1)}, u32[]{:S(2)}, u32[]{:S(2)}) collective-permute-start(bf16[256,1024]{1,0:T(8,128)(2,1)} %slice_select_fusion), channel_id=1, source_target_pairs={{0,1},{1,0},{2,3},{3,2},{4,5},{5,4},{6,7},{7,6},{8,9},{9,8},{10,11... | collective-permute-start | bytes 1572872 | tf_op jit(solution)/shard_map/ppermute | solution.py:1186
  208.4 16.7 %collective-permute-start.22 = (bf16[200,1024]{1,0:T(8,128)(2,1)S(1)}, bf16[200,1024]{1,0:T(8,128)(2,1)S(1)}, u32[]{:S(2)}, u32[]{:S(2)}) collective-permute-start(bf16[200,1024]{1,0:T(8,128)(2,1)S(1)} %broadcast_select_fusion), channel_id=1, source_target_pairs={{0,2},{1,3},{2,0},{3,1},{4,6},{5,7},{6,4},{7,5},{8,10},{9,11},{10,... | collective-permute-start | bytes 1228808 | tf_op jit(solution)/shard_map/ppermute | solution.py:1183
  210.0 9.5 %collective-permute-start.24 = (bf16[1,128,1024]{2,1,0:T(8,128)(2,1)}, bf16[1,128,1024]{2,1,0:T(8,128)(2,1)S(1)}, u32[]{:S(2)}, u32[]{:S(2)}) collective-permute-start(bf16[1,128,1024]{2,1,0:T(8,128)(2,1)} %add_convert_fusion.12), channel_id=1, source_target_pairs={{0,8},{4,12},{8,0},{12,4},{16,24},{20,28},{24,16},{28,20},{1,9},{5... | collective-permute-start | bytes 786440 | tf_op jit(solution)/shard_map/ppermute | solution.py:1029
  210.2 14.9 %collective-permute-start.25 = (bf16[1,128,1024]{2,1,0:T(8,128)(2,1)}, bf16[1,128,1024]{2,1,0:T(8,128)(2,1)S(1)}, u32[]{:S(2)}, u32[]{:S(2)}) collective-permute-start(bf16[1,128,1024]{2,1,0:T(8,128)(2,1)} %add_convert_fusion.11), channel_id=1, source_target_pairs={{0,24},{4,28},{8,16},{12,20},{16,8},{20,12},{24,0},{28,4},{1,25},{... | collective-permute-start | bytes 786440 | tf_op jit(solution)/shard_map/ppermute | solution.py:1029
  225.2 13.4 %collective-permute-start.30 = (bf16[4,128,512]{2,1,0:T(8,128)(2,1)S(1)}, bf16[4,128,512]{2,1,0:T(8,128)(2,1)S(1)}, u32[]{:S(2)}, u32[]{:S(2)}) collective-permute-start(bf16[4,128,512]{2,1,0:T(8,128)(2,1)S(1)} %get-tuple-element.256), channel_id=1, source_target_pairs={{0,4},{4,0},{8,12},{12,8},{16,20},{20,16},{24,28},{28,24},{1,5},{5... | collective-permute-start | bytes 1572872 | tf_op jit(solution)/shard_map/ppermute | solution.py:1029
  225.7 13.1 %collective-permute-start.31 = (bf16[4,256,256]{2,1,0:T(8,128)(2,1)S(1)}, bf16[4,256,256]{2,1,0:T(8,128)(2,1)S(1)}, u32[]{:S(2)}, u32[]{:S(2)}) collective-permute-start(bf16[4,256,256]{2,1,0:T(8,128)(2,1)S(1)} %get-tuple-element.257), channel_id=1, source_target_pairs={{0,8},{4,12},{8,0},{12,4},{16,24},{20,28},{24,16},{28,20},{1,9},{5... | collective-permute-start | bytes 1572872 | tf_op jit(solution)/shard_map/ppermute | solution.py:1029
  240.7 17.7 %all-to-all-start.4 = ((bf16[8,24,1024]{2,1,0:T(8,128)(2,1)}), bf16[8,24,1024]{2,1,0:T(8,128)(2,1)S(1)}, u32[]{:S(2)}, u32[]{:S(2)}) async-start(bf16[8,24,1024]{2,1,0:T(8,128)(2,1)} %pack_rows.1), calls=%async_computation.4 | async-start | bytes 786432 | tf_op jit(solution)/shard_map/all_to_all | solution.py:1189
  247.0 11.4 %collective-permute-start.32 = (bf16[2,128,512]{2,1,0:T(8,128)(2,1)}, bf16[2,128,512]{2,1,0:T(8,128)(2,1)S(1)}, u32[]{:S(2)}, u32[]{:S(2)}) collective-permute-start(bf16[2,128,512]{2,1,0:T(8,128)(2,1)} %get-tuple-element.303), channel_id=1, source_target_pairs={{0,8},{4,12},{8,0},{12,4},{16,24},{20,28},{24,16},{28,20},{1,9},{5... | collective-permute-start | bytes 786440 | tf_op jit(solution)/shard_map/ppermute | solution.py:1029
  258.5 10.6 %collective-permute-start.34 = (bf16[8,24,1024]{2,1,0:T(8,128)(2,1)S(1)}, bf16[8,24,1024]{2,1,0:T(8,128)(2,1)S(1)}, u32[]{:S(2)}, u32[]{:S(2)}) collective-permute-start(bf16[8,24,1024]{2,1,0:T(8,128)(2,1)S(1)} %all-to-all-done.4), channel_id=1, source_target_pairs={{0,2},{1,3},{2,0},{3,1},{4,6},{5,7},{6,4},{7,5},{8,10},{9,11},{10,... | collective-permute-start | bytes 1179656 | tf_op jit(solution)/shard_map/ppermute | solution.py:1183
  270.2 13.9 %collective-permute-start.37 = (bf16[2,8,24,1024]{3,2,1,0:T(8,128)(2,1)S(1)}, bf16[2,8,24,1024]{3,2,1,0:T(8,128)(2,1)S(1)}, u32[]{:S(2)}, u32[]{:S(2)}) collective-permute-start(bf16[2,8,24,1024]{3,2,1,0:T(8,128)(2,1)S(1)} %pad_maximum_fusion), channel_id=1, source_target_pairs={{0,1},{1,0},{2,3},{3,2},{4,5},{5,4},{6,7},{7,6},{8,9},{9,8},{10,11... | collective-permute-start | bytes 2359304 | tf_op jit(solution)/shard_map/ppermute | solution.py:1186
  271.2 12.9 %collective-permute-start.38 = (f32[32,1024]{1,0:T(8,128)S(1)}, f32[32,1024]{1,0:T(8,128)S(1)}, u32[]{:S(2)}, u32[]{:S(2)}) collective-permute-start(f32[32,1024]{1,0:T(8,128)S(1)} %pad_maximum_fusion.2), channel_id=1, source_target_pairs={{0,0},{1,8},{2,16},{3,24},{4,1},{5,9},{6,17},{7,25},{8,2},{9,10},{... | collective-permute-start | bytes 393224 | tf_op jit(solution)/shard_map/ppermute | solution.py:1404
  275.9 15.3 %all-to-all-start.5 = ((bf16[4,32,1792]{2,1,0:T(8,128)(2,1)}), bf16[4,32,1792]{2,1,0:T(8,128)(2,1)S(1)}, u32[]{:S(2)}, u32[]{:S(2)}) async-start(bf16[4,32,1792]{2,1,0:T(8,128)(2,1)} %bitcast.26), calls=%async_computation.5 | async-start | bytes 917504 | tf_op jit(solution)/shard_map/all_to_all | solution.py:1389
  (67 other events, 1156.3 us)

commit v6 on v5

--- a/solution.py
+++ b/solution.py
@@ -416,7 +416,7 @@
 
         def flush(tile, slot):
             for k in range(per):
-                down_ref[per * tile + k] = acc_ref[slot, 2 * k * lay.rows : (2 * k + 1) * lay.rows]
+                down_ref[per * tile + k] = acc_ref[slot, 2 * k * lay.rows : (2 * k + 1) * lay.rows].astype(BF)
                 doth_ref[per * tile + k] = acc_ref[slot, (2 * k + 1) * lay.rows : (2 * k + 2) * lay.rows].astype(BF)
 
         if long_clip:
@@ -459,7 +459,7 @@
         [own, oth, *d_outs, ot, lse, tab_cos, tab_sin, time_cos, time_sin],
         [
             shape_of((groups, lay.rows, LANES), BF),
-            shape_of((groups, lay.rows, LANES), F32),
+            shape_of((groups, lay.rows, LANES), BF),
             shape_of((groups, lay.rows, LANES), BF),
         ],
         scratch=[
@@ -480,7 +480,7 @@
 
     def body(flag_ref, dq_ref, a_ref, b_ref, tc_ref, ts_ref, qc_ref, qs_ref, out_ref):
         def one(group, _):
-            both = a_ref[group] + b_ref[group].astype(F32)
+            both = a_ref[group].astype(F32) + b_ref[group].astype(F32)
             tab = group if long_clip else 0
             cosine = tc_ref[...] + per_frame(both.shape, qc_ref[2 * tab], qc_ref[2 * tab + 1])
             sine = ts_ref[...] + per_frame(both.shape, qs_ref[2 * tab], qs_ref[2 * tab + 1])
@@ -815,7 +815,7 @@
                 else:
                     one, two = (dq_ref[2 * pair + k].astype(F32) for k in (0, 1))
                     query = jnp.where(low, one, swap_halves(two))
-                    one, two = (a_ref[2 * pair + k] + b_ref[2 * pair + k].astype(F32) for k in (0, 1))
+                    one, two = (a_ref[2 * pair + k].astype(F32) + b_ref[2 * pair + k].astype(F32) for k in (0, 1))
                     value = jnp.where(low, one, swap_halves(two))
                     one, two = (v * cosine - swap_pairs(v) * sine for v in (one, two))
                     key = jnp.where(low, swap_halves(one), two)
@@ -1261,7 +1261,7 @@
     blocks = [mine, mine2, got, got2]
     bits = list(range(n_blk.bit_length() - 1))
     orders = [bits, [1, 0] + bits[2:]]
-    down_order, up_order = ([0, 2, 1], [1, 0, 2]) if len(bits) == 3 else (bits, bits)
+    down_order, up_order = ([0, 1, 2], [1, 2, 0]) if len(bits) == 3 else (bits, bits)
     mlp_halves = split_weight_grads(
         flags,
         [

time: 296 us -> 297 us (level)
  starting transfers between devices: 65.3 us -> 70.7 us
  waiting for transfers between devices: 40 us -> 36.3 us
    ppermute x12, starting transfers between devices: 15.4 us -> 19.3 us  [move(): lax.ppermute(send, 'blk', [(i, i ^ hop) for i in range(self.n_blk)])]
    ppermute x12, waiting for transfers between devices: 20.5 us -> 17 us  [move(): lax.ppermute(send, 'blk', [(i, i ^ hop) for i in range(self.n_blk)])]
  transfers between devices with their start and end apart: 45 -> 45, of which waited for: 18 -> 19; matrix products, arithmetic and copies ran while one was open for 12% -> 12% of each run, Pallas kernels for 42% -> 42%
where the time goes in v6:
time: 297 us; the launch traced here: 294 us
  Pallas kernels  138 us (46%)
  starting transfers between devices  70.7 us (24%)
  waiting for transfers between devices  36.3 us (12%)
  other arithmetic  23.8 us (8%)
  local copies, waits for them, and re-layouts  15.9 us (5%)
  matrix products  7.43 us (3%)
    pallas_call x24, Pallas kernels, kernel_call(): pl.pallas_call(body, grid_spec=pltpu.PrefetchScalarGridSpec(num_scalar_pr...  138 us
    all_to_all x5, starting transfers between devices, spread(): return lax.all_to_all(value, 'blk', split_axis=0, concat_axis=0, tiled=True)  26.9 us
    ppermute x12, starting transfers between devices, move(): lax.ppermute(send, 'blk', [(i, i ^ hop) for i in range(self.n_blk)])  19.3 us
    ppermute x12, waiting for transfers between devices, move(): lax.ppermute(send, 'blk', [(i, i ^ hop) for i in range(self.n_blk)])  17 us
    ppermute x11, starting transfers between devices, swap_side(): return lax.ppermute(value, 'uly', [(i, i ^ 2) for i in range(n_uly)])  12.9 us
    convert_element_type x8, other arithmetic, add(): (self.keep[k].astype(F32) + self.got[k].astype(F32)).astype(BF)  12.3 us
    dot_general x2, matrix products, dot(): return jnp.dot(left, right, preferred_element_type=F32)  7.43 us
    all_to_all x5, waiting for transfers between devices, spread(): return lax.all_to_all(value, 'blk', split_axis=0, concat_axis=0, tiled=True)  7.38 us
  transfers between devices with their start and end apart: 45, of which 19 were waited for; matrix products, arithmetic and copies ran while one was open for 12% of the time, Pallas kernels for 42%

profile of v6, /device:TPU:4, one launch (start us, length us, event | category | flops | bytes accessed | tf_op | source)
XLA Modules:
  0.0 294.2 jit_solution(8407319200709764794)
XLA Ops:
  11.3 4.6 %fusion.2 = f32[2,4096]{1,0:T(2,128)S(1)} fusion(bf16[2,1024]{1,0:T(2,128)(2,1)S(1)} %fusion.16.s_ref, bf16[1024,6144]{1,0:T(8,128)(2,1)} %param.22, f32[4096]{0:T(1024)S(1)} %slice.269), kind=kOutput, calls=%fused_computation.2 | convolution fusion | flops 16785408 | bytes 8441856 | tf_op jit(solution)/shard_map/dot_general | solution.py:77
  19.0 7.7 %tokens_to_qkv.1 = (bf16[2,200,1024]{2,1,0:T(8,128)(2,1)}, bf16[8,320,128]{2,1,0:T(8,128)(2,1)S(1)}, bf16[8,320,128]{2,1,0:T(8,128)(2,1)S(1)}) custom-call(s32[6]{0:T(128)S(1)} %stack.40.flag_ref, bf16[200,1024]{1,0:T(8,128)(2,1)S(1)} %copy-done, bf16[200,1024]{1,0:T(8,128)(2,1)S(1)} %collective-permute-done.oth_ref.refs_8_.refs_2_, ...), custom_call_target="tpu_custom_call" | custom-call | flops 307200 | bytes 4096 | tf_op jit(solution)/shard_map/tokens_to_qkv/pallas_call | solution.py:117
  27.6 6.3 %all-to-all-start = ((bf16[8,320,128]{2,1,0:T(8,128)(2,1)}), bf16[8,320,128]{2,1,0:T(8,128)(2,1)S(1)}, u32[]{:S(2)}, u32[]{:S(2)}) async-start(bf16[8,320,128]{2,1,0:T(8,128)(2,1)} %copy-done.17), calls=%async_computation | async-start | bytes 1310720 | tf_op jit(solution)/shard_map/all_to_all | solution.py:1189
  35.6 5.6 %ahead_own.1.ahead_ref = f32[200,2048]{1,0:T(8,128)} custom-call(s32[6]{0:T(128)S(1)} %stack.40.flag_ref, bf16[200,1024]{1,0:T(8,128)(2,1)S(1)} %get-tuple-element.179.mg_ref.refs_4_, bf16[4096,1024]{1,0:T(8,128)(2,1)} %refs_1_.10, bf16[4096,1024]{1,0:T(8,128)(2,1)} %refs_1_.10), custom_call_target="tpu_custom_call" | custom-call | flops 204800 | bytes 4096 | tf_op jit(solution)/shard_map/ahead_own/pallas_call | solution.py:117
  41.2 3.8 %attend_short.1 = (bf16[8,112,128]{2,1,0:T(8,128)(2,1)S(1)}, f32[8,64,200]{2,1,0:T(8,128)}, f32[8,8,200]{2,1,0:T(8,128)}) custom-call(s32[6]{0:T(128)S(1)} %stack.40.flag_ref, bf16[8,320,128]{2,1,0:T(8,128)(2,1)S(1)} %get-tuple-element.157.own_ref, bf16[8,320,128]{2,1,0:T(8,128)(2,1)S(1)} %collective-permute-done.2.oth_ref), custom_call_target="tpu_custom_call" | custom-call | flops 160000 | bytes 4096 | tf_op jit(solution)/shard_map/attend_short/pallas_call | solution.py:117
  45.1 5.0 %all-to-all-done.own_ref = bf16[8,320,128]{2,1,0:T(8,128)(2,1)S(1)} async-done(((bf16[8,320,128]{2,1,0:T(8,128)(2,1)}), bf16[8,320,128]{2,1,0:T(8,128)(2,1)S(1)}, u32[]{:S(2)}, u32[]{:S(2)}) %all-to-all-start) | async-done | bytes 655392 | tf_op jit(solution)/shard_map/all_to_all | solution.py:1189
  52.2 11.4 %attend_long.1 = (bf16[8,112,128]{2,1,0:T(8,128)(2,1)S(1)}, f32[4,64,400]{2,1,0:T(8,128)}, f32[4,8,400]{2,1,0:T(8,128)}) custom-call(s32[6]{0:T(128)S(1)} %stack.40.flag_ref, bf16[8,320,128]{2,1,0:T(8,128)(2,1)S(1)} %all-to-all-done.own_ref, bf16[8,320,128]{2,1,0:T(8,128)(2,1)S(1)} %collective-permute-done.3.oth_ref), custom_call_target="tpu_custom_call" | custom-call | flops 800000 | bytes 4096 | tf_op jit(solution)/shard_map/attend_long/pallas_call | solution.py:117
  65.1 4.2 %all-to-all-start.1 = ((bf16[8,112,128]{2,1,0:T(8,128)(2,1)}), bf16[8,112,128]{2,1,0:T(8,128)(2,1)S(1)}, u32[]{:S(2)}, u32[]{:S(2)}) async-start(bf16[8,112,128]{2,1,0:T(8,128)(2,1)} %copy-done.20), calls=%async_computation.1 | async-start | bytes 458752 | tf_op jit(solution)/shard_map/all_to_all | solution.py:1189
  70.3 5.6 %ahead_other.1.ahead_ref = f32[200,2048]{1,0:T(8,128)} custom-call(s32[6]{0:T(128)S(1)} %stack.40.flag_ref, bf16[200,1024]{1,0:T(8,128)(2,1)S(1)} %copy-done.13, bf16[4096,1024]{1,0:T(8,128)(2,1)} %refs_1_.10, bf16[4096,1024]{1,0:T(8,128)(2,1)} %refs_1_.10), custom_call_target="tpu_custom_call" | custom-call | flops 204800 | bytes 4096 | tf_op jit(solution)/shard_map/ahead_other/pallas_call | solution.py:117
  79.0 4.4 %collective-permute-done.5.recv_ref = bf16[8,112,128]{2,1,0:T(8,128)(2,1)S(1)} collective-permute-done((bf16[8,112,128]{2,1,0:T(8,128)(2,1)S(1)}, bf16[8,112,128]{2,1,0:T(8,128)(2,1)S(1)}, u32[]{:S(2)}, u32[]{:S(2)}) %collective-permute-start.5) | collective-permute-done | bytes 229408 | tf_op jit(solution)/shard_map/ppermute | solution.py:1183
  83.3 4.1 %project_and_norm.1 = (f32[200,1024]{1,0:T(8,128)}, f32[200,1024]{1,0:T(8,128)}, bf16[200,1024]{1,0:T(8,128)(2,1)S(1)}) custom-call(s32[6]{0:T(128)S(1)} %stack.40.flag_ref, bf16[8,112,128]{2,1,0:T(8,128)(2,1)S(1)} %all-to-all-done.1.long_ref.l_ref, bf16[8,112,128]{2,1,0:T(8,128)(2,1)S(1)} %get-tuple-element.167.short_ref.s_ref, ...), custom_call_target="tpu_custom_call" | custom-call | flops 102400 | bytes 4096 | tf_op jit(solution)/shard_map/project_and_norm/pallas_call | solution.py:117
  89.0 6.9 %hidden_own.1 = (bf16[2,200,1024]{2,1,0:T(8,128)(2,1)S(1)}, bf16[2,200,1024]{2,1,0:T(8,128)(2,1)S(1)}, f32[8,1024]{1,0:T(8,128)S(1)}, f32[8,1024]{1,0:T(8,128)S(1)}, f32[200,1024]{1,0:T(8,128)S(1)}) custom-call(s32[6]{0:T(128)S(1)} %stack.40.flag_ref, bf16[200,1024]{1,0:T(8,128)(2,1)S(1)} %get-tuple-element.168.hid_ref.refs_8_, ...), custom_call_target="tpu_custom_call" | custom-call | flops 409600 | bytes 4096 | tf_op jit(solution)/shard_map/hidden_own/pallas_call | solution.py:117
  97.4 6.8 %hidden_other.1 = (bf16[2,200,1024]{2,1,0:T(8,128)(2,1)S(1)}, bf16[2,200,1024]{2,1,0:T(8,128)(2,1)S(1)}, f32[8,1024]{1,0:T(8,128)S(1)}, f32[8,1024]{1,0:T(8,128)S(1)}, bf16[200,1024]{1,0:T(8,128)(2,1)S(1)}) custom-call(s32[6]{0:T(128)S(1)} %stack.40.flag_ref, bf16[200,1024]{1,0:T(8,128)(2,1)S(1)} %collective-permute-done.6.hid_ref.refs_9_, ...), custom_call_target="tpu_custom_call" | custom-call | flops 409600 | bytes 4096 | tf_op jit(solution)/shard_map/hidden_other/pallas_call | solution.py:117
  108.9 9.5 %mlp_grads.1 = (bf16[4,128,1024]{2,1,0:T(8,128)(2,1)}, bf16[4,128,1024]{2,1,0:T(8,128)(2,1)S(1)}, bf16[4,128,1024]{2,1,0:T(8,128)(2,1)}, bf16[4,128,1024]{2,1,0:T(8,128)(2,1)S(1)}) custom-call(s32[6]{0:T(128)S(1)} %stack.40.flag_ref, bf16[2,200,1024]{2,1,0:T(8,128)(2,1)S(1)} %get-tuple-element.175.refs_0_.refs_12_.m_ref, ...), custom_call_target="tpu_custom_call" | custom-call | flops 819200 | bytes 4096 | tf_op jit(solution)/shard_map/mlp_grads/pallas_call | solution.py:117
  121.1 4.9 %branch_back.1 = (f32[200,1024]{1,0:T(8,128)}, bf16[200,1024]{1,0:T(8,128)(2,1)S(1)}, bf16[8,112,128]{2,1,0:T(8,128)(2,1)S(1)}, bf16[8,112,128]{2,1,0:T(8,128)(2,1)S(1)}, f32[8,1024]{1,0:T(8,128)S(1)}) custom-call(s32[6]{0:T(128)S(1)} %stack.40.flag_ref, f32[200,1024]{1,0:T(8,128)} %copy-done.16, bf16[200,1024]{1,0:T(8,128)(2,1)S(1)} %collective-permute-done.7.b_ref, ...), custom_call_target="tpu_custom_call" | custom-call | flops 102400 | bytes 4096 | tf_op jit(solution)/shard_map/branch_back/pallas_call | solution.py:117
  127.0 7.2 %forward_rows.1 = (f32[200,1024]{1,0:T(8,128)}, bf16[200,1024]{1,0:T(8,128)(2,1)}) custom-call(s32[6]{0:T(128)S(1)} %stack.40.flag_ref, bf16[2,200,1024]{2,1,0:T(8,128)(2,1)S(1)} %get-tuple-element.175.refs_0_.refs_12_.m_ref, bf16[2,200,1024]{2,1,0:T(8,128)(2,1)S(1)} %get-tuple-element.177.s_ref, ...), custom_call_target="tpu_custom_call" | custom-call | flops 409600 | bytes 4096 | tf_op jit(solution)/shard_map/forward_rows/pallas_call | solution.py:117
  136.1 5.2 %all-to-all-start.2 = ((bf16[8,112,128]{2,1,0:T(8,128)(2,1)}), bf16[8,112,128]{2,1,0:T(8,128)(2,1)S(1)}, u32[]{:S(2)}, u32[]{:S(2)}) async-start(bf16[8,112,128]{2,1,0:T(8,128)(2,1)} %broadcast_select_fusion.1), calls=%async_computation.2 | async-start | bytes 458752 | tf_op jit(solution)/shard_map/all_to_all | solution.py:1189
  141.3 6.1 %attend_back_short.1 = (bf16[8,200,128]{2,1,0:T(8,128)(2,1)}, bf16[8,200,128]{2,1,0:T(8,128)(2,1)}, bf16[8,200,128]{2,1,0:T(8,128)(2,1)S(1)}) custom-call(s32[6]{0:T(128)S(1)} %stack.40.flag_ref, bf16[8,320,128]{2,1,0:T(8,128)(2,1)} %copy-done.5, bf16[8,320,128]{2,1,0:T(8,128)(2,1)} %copy-done.6, bf16[8,112,128]{2,1,0:T(8,128)(2,1)S(1)} %get-tuple-element.192.refs_0_, ...), custom_call_target="tpu_custom_call" | custom-call | flops 400000 | bytes 4096 | tf_op jit(solution)/shard_map/attend_back_short/pallas_call | solution.py:117
  157.1 17.3 %attend_back_long.1 = (bf16[8,200,128]{2,1,0:T(8,128)(2,1)}, bf16[8,200,128]{2,1,0:T(8,128)(2,1)}, bf16[8,200,128]{2,1,0:T(8,128)(2,1)S(1)}) custom-call(s32[6]{0:T(128)S(1)} %stack.40.flag_ref, bf16[8,320,128]{2,1,0:T(8,128)(2,1)} %copy-done.1, bf16[8,320,128]{2,1,0:T(8,128)(2,1)} %copy-done.4, bf16[8,112,128]{2,1,0:T(8,128)(2,1)S(1)} %all-to-all-done.2.refs_0_, ...), custom_call_target="tpu_custom_call" | custom-call | flops 2000000 | bytes 4096 | tf_op jit(solution)/shard_map/attend_back_long/pallas_call | solution.py:117
  177.9 3.6 %finish_keys.1 = bf16[8,320,128]{2,1,0:T(8,128)(2,1)} custom-call(s32[6]{0:T(128)S(1)} %stack.40.flag_ref, bf16[8,200,128]{2,1,0:T(8,128)(2,1)} %get-tuple-element.215.dq_ref, bf16[8,200,128]{2,1,0:T(8,128)(2,1)} %get-tuple-element.216.a_ref, bf16[8,200,128]{2,1,0:T(8,128)(2,1)S(1)} %collective-permute-done.18.b_ref, f32[200,128]{1,0:T(8,128)S(1)} %copy-done.8, ...), custom_call_target="tpu_custom_call" | custom-call | flops 500 | bytes 4096 | tf_op jit(solution)/shard_map/finish_keys/pallas_call | solution.py:117
  181.4 5.2 %all-to-all-start.3 = ((bf16[8,320,128]{2,1,0:T(8,128)(2,1)}), bf16[8,320,128]{2,1,0:T(8,128)(2,1)S(1)}, u32[]{:S(2)}, u32[]{:S(2)}) async-start(bf16[8,320,128]{2,1,0:T(8,128)(2,1)} %finish_keys.1), calls=%async_computation.3 | async-start | bytes 1310720 | tf_op jit(solution)/shard_map/all_to_all | solution.py:1189
  188.1 6.8 %qkv_back_short.1 = (f32[200,1024]{1,0:T(8,128)}, bf16[200,1024]{1,0:T(8,128)(2,1)S(1)}, bf16[200,768]{1,0:T(8,128)(2,1)S(1)}, bf16[200,768]{1,0:T(8,128)(2,1)S(...) custom-call(s32[6]{0:T(128)S(1)} %stack.40.flag_ref, bf16[8,200,128]{2,1,0:T(8,128)(2,1)} %get-tuple-element.226.refs_0_, ...), custom_call_target="tpu_custom_call" | custom-call | flops 153600 | bytes 4096 | tf_op jit(solution)/shard_map/qkv_back_short/pallas_call | solution.py:117
  203.3 6.0 %qkv_back_long.1 = (f32[200,1024]{1,0:T(8,128)}, bf16[200,1024]{1,0:T(8,128)(2,1)S(1)}, bf16[200,768]{1,0:T(8,128)(2,1)S(1)}, bf16[200,768]{1,0:T(8,128)(2,1)S(1...) custom-call(s32[6]{0:T(128)S(1)} %stack.40.flag_ref, bf16[8,320,128]{2,1,0:T(8,128)(2,1)S(1)} %all-to-all-done.3.refs_0_, ...), custom_call_target="tpu_custom_call" | custom-call | flops 153600 | bytes 4096 | tf_op jit(solution)/shard_map/qkv_back_long/pallas_call | solution.py:117
  210.1 3.3 %collective-permute-start.24 = (bf16[1,128,1024]{2,1,0:T(8,128)(2,1)}, bf16[1,128,1024]{2,1,0:T(8,128)(2,1)S(1)}, u32[]{:S(2)}, u32[]{:S(2)}) collective-permute-start(bf16[1,128,1024]{2,1,0:T(8,128)(2,1)} %add_convert_fusion.12), channel_id=1, source_target_pairs={{0,24},{4,28},{8,16},{12,20},{16,8},{20,12},{24,0},{28,4},{1,25},{... | collective-permute-start | bytes 786440 | tf_op jit(solution)/shard_map/ppermute | solution.py:1029
  214.0 6.8 %attn_grads.1 = (bf16[4,128,512]{2,1,0:T(8,128)(2,1)S(1)}, bf16[4,128,512]{2,1,0:T(8,128)(2,1)S(1)}, bf16[4,256,256]{2,1,0:T(8,128)(2,1)S(1)}, bf16[4,256,256]{2,1,0:T(8,128)(2,1)S(1)}) custom-call(s32[6]{0:T(128)S(1)} %stack.40.flag_ref, bf16[2,200,1024]{2,1,0:T(8,128)(2,1)} %get-tuple-element.239.refs_0_.refs_1_, ...), custom_call_target="tpu_custom_call" | custom-call | flops 307200 | bytes 4096 | tf_op jit(solution)/shard_map/attn_grads/pallas_call | solution.py:117
  222.6 4.2 %collective-permute-start.31 = (bf16[4,256,256]{2,1,0:T(8,128)(2,1)S(1)}, bf16[4,256,256]{2,1,0:T(8,128)(2,1)S(1)}, u32[]{:S(2)}, u32[]{:S(2)}) collective-permute-start(bf16[4,256,256]{2,1,0:T(8,128)(2,1)S(1)} %get-tuple-element.257), channel_id=1, source_target_pairs={{0,8},{4,12},{8,0},{12,4},{16,24},{20,28},{24,16},{28,20},{1,9},{5... | collective-permute-start | bytes 1572872 | tf_op jit(solution)/shard_map/ppermute | solution.py:1029
  226.7 3.2 %layer_output.1 = (bf16[200,1024]{1,0:T(8,128)(2,1)}, f32[8,1024]{1,0:T(8,128)S(1)}) custom-call(s32[6]{0:T(128)S(1)} %stack.40.flag_ref, f32[200,1024]{1,0:T(8,128)} %get-tuple-element.191.a_ref, bf16[200,1024]{1,0:T(8,128)(2,1)} %collective-permute-done.23.b_ref, f32[1,1024]{1,0:T(1,128)S(1)} %bitcast.68, f32[200,1024]{1,0:T(8,128)} %get-tuple-element.185.r_ref, ...), custom_call_target="tpu_custom_call" | custom-call | flops 200 | bytes 4096 | tf_op jit(solution)/shard_map/layer_output/pallas_call | solution.py:117
  229.9 3.8 %token_back.1 = f32[200,1024]{1,0:T(8,128)} custom-call(s32[6]{0:T(128)S(1)} %stack.40.flag_ref, f32[200,1024]{1,0:T(8,128)} %get-tuple-element.252.l_ref, f32[200,1024]{1,0:T(8,128)} %get-tuple-element.253.s_ref, bf16[200,1024]{1,0:T(8,128)(2,1)S(1)} %collective-permute-done.22.r_ref, bf16[200,1024]{1,0:T(8,128)(2,1)} %tok_ref.3, ...), custom_call_target="tpu_custom_call" | custom-call | flops 1000 | bytes 4096 | tf_op jit(solution)/shard_map/token_back/pallas_call | solution.py:117
  239.6 5.9 %all-to-all-start.4 = ((bf16[8,24,1024]{2,1,0:T(8,128)(2,1)}), bf16[8,24,1024]{2,1,0:T(8,128)(2,1)S(1)}, u32[]{:S(2)}, u32[]{:S(2)}) async-start(bf16[8,24,1024]{2,1,0:T(8,128)(2,1)} %pack_rows.1), calls=%async_computation.4 | async-start | bytes 786432 | tf_op jit(solution)/shard_map/all_to_all | solution.py:1189
  253.2 5.5 %collective-permute-done.32 = bf16[2,128,512]{2,1,0:T(8,128)(2,1)S(1)} collective-permute-done((bf16[2,128,512]{2,1,0:T(8,128)(2,1)}, bf16[2,128,512]{2,1,0:T(8,128)(2,1)S(1)}, u32[]{:S(2)}, u32[]{:S(2)}) %collective-permute-start.32) | collective-permute-done | bytes 262176 | tf_op jit(solution)/shard_map/ppermute | solution.py:1029
  276.4 6.2 %all-to-all-start.5 = ((bf16[4,32,1792]{2,1,0:T(8,128)(2,1)}), bf16[4,32,1792]{2,1,0:T(8,128)(2,1)S(1)}, u32[]{:S(2)}, u32[]{:S(2)}) async-start(bf16[4,32,1792]{2,1,0:T(8,128)(2,1)} %bitcast.26), calls=%async_computation.5 | async-start | bytes 917504 | tf_op jit(solution)/shard_map/all_to_all | solution.py:1389
  284.8 3.5 %modulation_grads.1 = (f32[32,6144]{1,0:T(8,128)}, f32[4,32,1024]{2,1,0:T(8,128)S(1)}) custom-call(s32[6]{0:T(128)S(1)} %stack.40.flag_ref, f32[768,128]{1,0:T(8,128)S(1)} %copy-done.15, bf16[384,1024]{1,0:T(8,128)(2,1)S(1)} %bitcast.60, bf16[384,1024]{1,0:T(8,128)(2,1)S(1)} %bitcast.61), custom_call_target="tpu_custom_call" | custom-call | flops 294912 | bytes 4096 | tf_op jit(solution)/shard_map/modulation_grads/pallas_call | solution.py:117
  (268 shorter events, 101.5 us)
Async XLA Ops:
  0.7 18.3 %collective-permute-start = (bf16[200,1024]{1,0:T(8,128)(2,1)}, bf16[200,1024]{1,0:T(8,128)(2,1)S(1)}, u32[]{:S(2)}, u32[]{:S(2)}) collective-permute-start(bf16[200,1024]{1,0:T(8,128)(2,1)} %tok_ref.3), channel_id=1, source_target_pairs={{0,2},{1,3},{2,0},{3,1},{4,6},{5,7},{6,4},{7,5},{8,10},{9,11},{10,... | collective-permute-start | bytes 1228808 | tf_op jit(solution)/shard_map/ppermute | solution.py:1183
  5.8 12.3 %collective-permute-start.1 = (f32[2,2048]{1,0:T(2,128)S(1)}, f32[2,2048]{1,0:T(2,128)S(1)}, u32[]{:S(2)}, u32[]{:S(2)}) collective-permute-start(f32[2,2048]{1,0:T(2,128)S(1)} %fusion.7.mod_ref), channel_id=1, source_target_pairs={{0,2},{1,3},{2,0},{3,1},{4,6},{5,7},{6,4},{7,5},{8,10},{9,11},{10,... | collective-permute-start | bytes 49160 | tf_op jit(solution)/shard_map/ppermute | solution.py:1183
  27.6 22.5 %all-to-all-start = ((bf16[8,320,128]{2,1,0:T(8,128)(2,1)}), bf16[8,320,128]{2,1,0:T(8,128)(2,1)S(1)}, u32[]{:S(2)}, u32[]{:S(2)}) async-start(bf16[8,320,128]{2,1,0:T(8,128)(2,1)} %copy-done.17), calls=%async_computation | async-start | bytes 1310720 | tf_op jit(solution)/shard_map/all_to_all | solution.py:1189
  50.1 13.5 %collective-permute-start.4 = (bf16[200,1024]{1,0:T(8,128)(2,1)S(1)}, bf16[200,1024]{1,0:T(8,128)(2,1)S(1)}, u32[]{:S(2)}, u32[]{:S(2)}) collective-permute-start(bf16[200,1024]{1,0:T(8,128)(2,1)S(1)} %get-tuple-element.179.mg_ref.refs_4_), channel_id=1, source_target_pairs={{0,2},{1,3},{2,0},{3,1},{4,6},{5,7},{6,4},{7,5},{8,10},{9,11},{10,... | collective-permute-start | bytes 1228808 | tf_op jit(solution)/shard_map/ppermute | solution.py:1183
  65.1 12.2 %all-to-all-start.1 = ((bf16[8,112,128]{2,1,0:T(8,128)(2,1)}), bf16[8,112,128]{2,1,0:T(8,128)(2,1)S(1)}, u32[]{:S(2)}, u32[]{:S(2)}) async-start(bf16[8,112,128]{2,1,0:T(8,128)(2,1)} %copy-done.20), calls=%async_computation.1 | async-start | bytes 458752 | tf_op jit(solution)/shard_map/all_to_all | solution.py:1189
  87.5 9.9 %collective-permute-start.6 = (bf16[200,1024]{1,0:T(8,128)(2,1)S(1)}, bf16[200,1024]{1,0:T(8,128)(2,1)S(1)}, u32[]{:S(2)}, u32[]{:S(2)}) collective-permute-start(bf16[200,1024]{1,0:T(8,128)(2,1)S(1)} %get-tuple-element.168.hid_ref.refs_8_), channel_id=1, source_target_pairs={{0,2},{1,3},{2,0},{3,1},{4,6},{5,7},{6,4},{7,5},{8,10},{9,11},{10,... | collective-permute-start | bytes 1228808 | tf_op jit(solution)/shard_map/ppermute | solution.py:1183
  89.0 16.5 %collective-permute-start.10 = (bf16[200,1024]{1,0:T(8,128)(2,1)S(1)}, bf16[200,1024]{1,0:T(8,128)(2,1)S(1)}, u32[]{:S(2)}, u32[]{:S(2)}) collective-permute-start(bf16[200,1024]{1,0:T(8,128)(2,1)S(1)} %get-tuple-element.179.mg_ref.refs_4_), channel_id=1, source_target_pairs={{0,1},{1,0},{2,3},{3,2},{4,5},{5,4},{6,7},{7,6},{8,9},{9,8},{10,11... | collective-permute-start | bytes 1228808 | tf_op jit(solution)/shard_map/ppermute | solution.py:1186
  96.9 11.5 %collective-permute-start.8 = (bf16[2,200,1024]{2,1,0:T(8,128)(2,1)S(1)}, bf16[2,200,1024]{2,1,0:T(8,128)(2,1)S(1)}, u32[]{:S(2)}, u32[]{:S(2)}) collective-permute-start(bf16[2,200,1024]{2,1,0:T(8,128)(2,1)S(1)} %get-tuple-element.177.s_ref), channel_id=1, source_target_pairs={{0,1},{1,0},{2,3},{3,2},{4,5},{5,4},{6,7},{7,6},{8,9},{9,8},{10,11... | collective-permute-start | bytes 2457608 | tf_op jit(solution)/shard_map/ppermute | solution.py:1186
  107.8 11.5 %collective-permute-start.7 = (bf16[200,1024]{1,0:T(8,128)(2,1)S(1)}, bf16[200,1024]{1,0:T(8,128)(2,1)S(1)}, u32[]{:S(2)}, u32[]{:S(2)}) collective-permute-start(bf16[200,1024]{1,0:T(8,128)(2,1)S(1)} %get-tuple-element.174), channel_id=1, source_target_pairs={{0,2},{1,3},{2,0},{3,1},{4,6},{5,7},{6,4},{7,5},{8,10},{9,11},{10,... | collective-permute-start | bytes 1228808 | tf_op jit(solution)/shard_map/ppermute | solution.py:1183
  119.3 30.0 %collective-permute-start.16 = (bf16[4,128,1024]{2,1,0:T(8,128)(2,1)}, bf16[4,128,1024]{2,1,0:T(8,128)(2,1)}, u32[]{:S(2)}, u32[]{:S(2)}) collective-permute-start(bf16[4,128,1024]{2,1,0:T(8,128)(2,1)} %get-tuple-element.203), channel_id=1, source_target_pairs={{0,4},{4,0},{8,12},{12,8},{16,20},{20,16},{24,28},{28,24},{1,5},{5... | collective-permute-start | bytes 3145736 | tf_op jit(solution)/shard_map/ppermute | solution.py:1029
  120.1 29.1 %collective-permute-start.17 = (bf16[4,128,1024]{2,1,0:T(8,128)(2,1)}, bf16[4,128,1024]{2,1,0:T(8,128)(2,1)}, u32[]{:S(2)}, u32[]{:S(2)}) collective-permute-start(bf16[4,128,1024]{2,1,0:T(8,128)(2,1)} %get-tuple-element.204), channel_id=1, source_target_pairs={{0,8},{4,12},{8,0},{12,4},{16,24},{20,28},{24,16},{28,20},{1,9},{5... | collective-permute-start | bytes 3145736 | tf_op jit(solution)/shard_map/ppermute | solution.py:1029
  134.3 15.0 %collective-permute-start.15 = (bf16[200,1024]{1,0:T(8,128)(2,1)S(1)}, bf16[200,1024]{1,0:T(8,128)(2,1)}, u32[]{:S(2)}, u32[]{:S(2)}) collective-permute-start(bf16[200,1024]{1,0:T(8,128)(2,1)S(1)} %get-tuple-element.202.go_ref), channel_id=1, source_target_pairs={{0,2},{1,3},{2,0},{3,1},{4,6},{5,7},{6,4},{7,5},{8,10},{9,11},{10,... | collective-permute-start | bytes 1228808 | tf_op jit(solution)/shard_map/ppermute | solution.py:1183
  136.1 13.1 %all-to-all-start.2 = ((bf16[8,112,128]{2,1,0:T(8,128)(2,1)}), bf16[8,112,128]{2,1,0:T(8,128)(2,1)S(1)}, u32[]{:S(2)}, u32[]{:S(2)}) async-start(bf16[8,112,128]{2,1,0:T(8,128)(2,1)} %broadcast_select_fusion.1), calls=%async_computation.2 | async-start | bytes 458752 | tf_op jit(solution)/shard_map/all_to_all | solution.py:1189
  154.2 21.9 %collective-permute-start.19 = (bf16[2,128,1024]{2,1,0:T(8,128)(2,1)S(1)}, bf16[2,128,1024]{2,1,0:T(8,128)(2,1)S(1)}, u32[]{:S(2)}, u32[]{:S(2)}) collective-permute-start(bf16[2,128,1024]{2,1,0:T(8,128)(2,1)S(1)} %get-tuple-element.218), channel_id=1, source_target_pairs={{0,8},{4,12},{8,0},{12,4},{16,24},{20,28},{24,16},{28,20},{1,9},{5... | collective-permute-start | bytes 1572872 | tf_op jit(solution)/shard_map/ppermute | solution.py:1029
  155.7 22.2 %collective-permute-start.20 = (bf16[2,128,1024]{2,1,0:T(8,128)(2,1)S(1)}, bf16[2,128,1024]{2,1,0:T(8,128)(2,1)}, u32[]{:S(2)}, u32[]{:S(2)}) collective-permute-start(bf16[2,128,1024]{2,1,0:T(8,128)(2,1)S(1)} %get-tuple-element.219), channel_id=1, source_target_pairs={{0,24},{4,28},{8,16},{12,20},{16,8},{20,12},{24,0},{28,4},{1,25},{... | collective-permute-start | bytes 1572872 | tf_op jit(solution)/shard_map/ppermute | solution.py:1029
  174.4 13.8 %collective-permute-start.21 = (bf16[8,200,128]{2,1,0:T(8,128)(2,1)S(1)}, bf16[8,200,128]{2,1,0:T(8,128)(2,1)S(1)}, u32[]{:S(2)}, u32[]{:S(2)}) collective-permute-start(bf16[8,200,128]{2,1,0:T(8,128)(2,1)S(1)} %copy-done.36), channel_id=1, source_target_pairs={{0,1},{1,0},{2,3},{3,2},{4,5},{5,4},{6,7},{7,6},{8,9},{9,8},{10,11... | collective-permute-start | bytes 1228808 | tf_op jit(solution)/shard_map/ppermute | solution.py:1186
  181.4 21.8 %all-to-all-start.3 = ((bf16[8,320,128]{2,1,0:T(8,128)(2,1)}), bf16[8,320,128]{2,1,0:T(8,128)(2,1)S(1)}, u32[]{:S(2)}, u32[]{:S(2)}) async-start(bf16[8,320,128]{2,1,0:T(8,128)(2,1)} %finish_keys.1), calls=%async_computation.3 | async-start | bytes 1310720 | tf_op jit(solution)/shard_map/all_to_all | solution.py:1189
  186.6 23.5 %collective-permute-start.26 = (bf16[2,200,1024]{2,1,0:T(8,128)(2,1)}, bf16[2,200,1024]{2,1,0:T(8,128)(2,1)}, u32[]{:S(2)}, u32[]{:S(2)}) collective-permute-start(bf16[2,200,1024]{2,1,0:T(8,128)(2,1)} %get-tuple-element.239.refs_0_.refs_1_), channel_id=1, source_target_pairs={{0,1},{1,0},{2,3},{3,2},{4,5},{5,4},{6,7},{7,6},{8,9},{9,8},{10,11... | collective-permute-start | bytes 2457608 | tf_op jit(solution)/shard_map/ppermute | solution.py:1186
  186.6 34.2 %collective-permute-start.23 = (bf16[200,1024]{1,0:T(8,128)(2,1)}, bf16[200,1024]{1,0:T(8,128)(2,1)}, u32[]{:S(2)}, u32[]{:S(2)}) collective-permute-start(bf16[200,1024]{1,0:T(8,128)(2,1)} %get-tuple-element.236), channel_id=1, source_target_pairs={{0,2},{1,3},{2,0},{3,1},{4,6},{5,7},{6,4},{7,5},{8,10},{9,11},{10,... | collective-permute-start | bytes 1228808 | tf_op jit(solution)/shard_map/ppermute | solution.py:1183
  195.5 14.6 %collective-permute-start.28 = (bf16[200,768]{1,0:T(8,128)(2,1)S(1)}, bf16[200,768]{1,0:T(8,128)(2,1)}, u32[]{:S(2)}, u32[]{:S(2)}) collective-permute-start(bf16[200,768]{1,0:T(8,128)(2,1)S(1)} %get-tuple-element.243), channel_id=1, source_target_pairs={{0,1},{1,0},{2,3},{3,2},{4,5},{5,4},{6,7},{7,6},{8,9},{9,8},{10,11... | collective-permute-start | bytes 921608 | tf_op jit(solution)/shard_map/ppermute | solution.py:1186
  199.4 14.0 %collective-permute-start.29 = (bf16[256,1024]{1,0:T(8,128)(2,1)}, bf16[256,1024]{1,0:T(8,128)(2,1)S(1)}, u32[]{:S(2)}, u32[]{:S(2)}) collective-permute-start(bf16[256,1024]{1,0:T(8,128)(2,1)} %slice_select_fusion), channel_id=1, source_target_pairs={{0,1},{1,0},{2,3},{3,2},{4,5},{5,4},{6,7},{7,6},{8,9},{9,8},{10,11... | collective-permute-start | bytes 1572872 | tf_op jit(solution)/shard_map/ppermute | solution.py:1186
  209.4 12.6 %collective-permute-start.22 = (bf16[200,1024]{1,0:T(8,128)(2,1)S(1)}, bf16[200,1024]{1,0:T(8,128)(2,1)S(1)}, u32[]{:S(2)}, u32[]{:S(2)}) collective-permute-start(bf16[200,1024]{1,0:T(8,128)(2,1)S(1)} %broadcast_select_fusion), channel_id=1, source_target_pairs={{0,2},{1,3},{2,0},{3,1},{4,6},{5,7},{6,4},{7,5},{8,10},{9,11},{10,... | collective-permute-start | bytes 1228808 | tf_op jit(solution)/shard_map/ppermute | solution.py:1183
  210.1 10.8 %collective-permute-start.24 = (bf16[1,128,1024]{2,1,0:T(8,128)(2,1)}, bf16[1,128,1024]{2,1,0:T(8,128)(2,1)S(1)}, u32[]{:S(2)}, u32[]{:S(2)}) collective-permute-start(bf16[1,128,1024]{2,1,0:T(8,128)(2,1)} %add_convert_fusion.12), channel_id=1, source_target_pairs={{0,24},{4,28},{8,16},{12,20},{16,8},{20,12},{24,0},{28,4},{1,25},{... | collective-permute-start | bytes 786440 | tf_op jit(solution)/shard_map/ppermute | solution.py:1029
  213.4 8.6 %collective-permute-start.25 = (bf16[1,128,1024]{2,1,0:T(8,128)(2,1)}, bf16[1,128,1024]{2,1,0:T(8,128)(2,1)S(1)}, u32[]{:S(2)}, u32[]{:S(2)}) collective-permute-start(bf16[1,128,1024]{2,1,0:T(8,128)(2,1)} %add_convert_fusion.11), channel_id=1, source_target_pairs={{0,4},{4,0},{8,12},{12,8},{16,20},{20,16},{24,28},{28,24},{1,5},{5... | collective-permute-start | bytes 786440 | tf_op jit(solution)/shard_map/ppermute | solution.py:1029
  222.0 13.2 %collective-permute-start.30 = (bf16[4,128,512]{2,1,0:T(8,128)(2,1)S(1)}, bf16[4,128,512]{2,1,0:T(8,128)(2,1)S(1)}, u32[]{:S(2)}, u32[]{:S(2)}) collective-permute-start(bf16[4,128,512]{2,1,0:T(8,128)(2,1)S(1)} %get-tuple-element.256), channel_id=1, source_target_pairs={{0,4},{4,0},{8,12},{12,8},{16,20},{20,16},{24,28},{28,24},{1,5},{5... | collective-permute-start | bytes 1572872 | tf_op jit(solution)/shard_map/ppermute | solution.py:1029
  222.6 15.6 %collective-permute-start.31 = (bf16[4,256,256]{2,1,0:T(8,128)(2,1)S(1)}, bf16[4,256,256]{2,1,0:T(8,128)(2,1)S(1)}, u32[]{:S(2)}, u32[]{:S(2)}) collective-permute-start(bf16[4,256,256]{2,1,0:T(8,128)(2,1)S(1)} %get-tuple-element.257), channel_id=1, source_target_pairs={{0,8},{4,12},{8,0},{12,4},{16,24},{20,28},{24,16},{28,20},{1,9},{5... | collective-permute-start | bytes 1572872 | tf_op jit(solution)/shard_map/ppermute | solution.py:1029
  239.6 19.1 %all-to-all-start.4 = ((bf16[8,24,1024]{2,1,0:T(8,128)(2,1)}), bf16[8,24,1024]{2,1,0:T(8,128)(2,1)S(1)}, u32[]{:S(2)}, u32[]{:S(2)}) async-start(bf16[8,24,1024]{2,1,0:T(8,128)(2,1)} %pack_rows.1), calls=%async_computation.4 | async-start | bytes 786432 | tf_op jit(solution)/shard_map/all_to_all | solution.py:1189
  247.4 11.4 %collective-permute-start.32 = (bf16[2,128,512]{2,1,0:T(8,128)(2,1)}, bf16[2,128,512]{2,1,0:T(8,128)(2,1)S(1)}, u32[]{:S(2)}, u32[]{:S(2)}) collective-permute-start(bf16[2,128,512]{2,1,0:T(8,128)(2,1)} %get-tuple-element.303), channel_id=1, source_target_pairs={{0,8},{4,12},{8,0},{12,4},{16,24},{20,28},{24,16},{28,20},{1,9},{5... | collective-permute-start | bytes 786440 | tf_op jit(solution)/shard_map/ppermute | solution.py:1029
  258.7 10.8 %collective-permute-start.34 = (bf16[8,24,1024]{2,1,0:T(8,128)(2,1)S(1)}, bf16[8,24,1024]{2,1,0:T(8,128)(2,1)S(1)}, u32[]{:S(2)}, u32[]{:S(2)}) collective-permute-start(bf16[8,24,1024]{2,1,0:T(8,128)(2,1)S(1)} %all-to-all-done.4), channel_id=1, source_target_pairs={{0,2},{1,3},{2,0},{3,1},{4,6},{5,7},{6,4},{7,5},{8,10},{9,11},{10,... | collective-permute-start | bytes 1179656 | tf_op jit(solution)/shard_map/ppermute | solution.py:1183
  270.6 14.2 %collective-permute-start.37 = (bf16[2,8,24,1024]{3,2,1,0:T(8,128)(2,1)S(1)}, bf16[2,8,24,1024]{3,2,1,0:T(8,128)(2,1)S(1)}, u32[]{:S(2)}, u32[]{:S(2)}) collective-permute-start(bf16[2,8,24,1024]{3,2,1,0:T(8,128)(2,1)S(1)} %pad_maximum_fusion), channel_id=1, source_target_pairs={{0,1},{1,0},{2,3},{3,2},{4,5},{5,4},{6,7},{7,6},{8,9},{9,8},{10,11... | collective-permute-start | bytes 2359304 | tf_op jit(solution)/shard_map/ppermute | solution.py:1186
  271.7 13.1 %collective-permute-start.38 = (f32[32,1024]{1,0:T(8,128)S(1)}, f32[32,1024]{1,0:T(8,128)S(1)}, u32[]{:S(2)}, u32[]{:S(2)}) collective-permute-start(f32[32,1024]{1,0:T(8,128)S(1)} %pad_maximum_fusion.2), channel_id=1, source_target_pairs={{0,0},{1,8},{2,16},{3,24},{4,1},{5,9},{6,17},{7,25},{8,2},{9,10},{... | collective-permute-start | bytes 393224 | tf_op jit(solution)/shard_map/ppermute | solution.py:1404
  276.4 15.6 %all-to-all-start.5 = ((bf16[4,32,1792]{2,1,0:T(8,128)(2,1)}), bf16[4,32,1792]{2,1,0:T(8,128)(2,1)S(1)}, u32[]{:S(2)}, u32[]{:S(2)}) async-start(bf16[4,32,1792]{2,1,0:T(8,128)(2,1)} %bitcast.26), calls=%async_computation.5 | async-start | bytes 917504 | tf_op jit(solution)/shard_map/all_to_all | solution.py:1389
  (67 other events, 1156.5 us)
